TPU v7x, 128 devices: a whole 4x4x4 slice. The times are simulated.
128 devices in a mesh: face: 8 (over x_lo, z), tile: 16 (over y, x_hi, core).
Axes of the slice: x: 4 (x_hi: 2, x_lo: 2; x = x_hi * 2 + x_lo), y: 4, z: 4, core: 2. Of those that a mesh axis runs over, the one named last changes fastest.
Arguments:
- state: bfloat16 [8, 16, 2, 4, 512, 128], P('face', 'tile'), may hold values from -6 to 6
- obs_values: bfloat16 [131072, 256], P(('face', 'tile')), may hold values from -6 to 6
- obs_dest: int32 [131072, 1], P(('face', 'tile')), may hold values from 0 to 127; in each aligned block of 1024 rows (0 to 1023, 1024 to 2047, ...) at most 16 rows name the same one
- obs_pixel: int32 [131072], P(('face', 'tile')), may hold values from 0 to 4095
- matching: int32 [8, 2, 3], replicated, may hold values from 0 to 7, as said below
- kernel_one: bfloat16 [9, 128, 256], replicated, may hold values from -0.1875 to 0.1875
- bias_one: float32 [256], replicated, may hold values from -3 to 3
- kernel_two: bfloat16 [9, 256, 128], replicated, may hold values from -0.125 to 0.125
- bias_two: float32 [128], replicated, may hold values from -3 to 3
- cotangent: bfloat16 [8, 16, 2, 4, 512, 128], P('face', 'tile'), may hold values from -6 to 6
Outputs:
- analysis: bfloat16 [8, 16, 2, 4, 512, 128], P('face', 'tile')
- grad_state: float32 [8, 16, 2, 4, 512, 128], P('face', 'tile')
Inputs may be any that keep to these rules, and one draw needn't show every extreme that they name: `obs_dest`: of the rows of one device, at most 16 name the same pixel tile, and in every draw some device names some tile exactly 16 times. The matching pairs sides: if side s of face block f is matched with side s2 of block g and flag r, then side s2 of g is matched with side s of f and the same flag. A block may be matched with itself on its other side.
All inputs are finite; a program needn't handle non-finite values.
Results may differ from a plain program's by a relative error of at most 0.0034.
Values may be sent and summed in bfloat16 or wider, within the bound.
A program may use at most 192 MiB of HBM per device.

v0:
```python
import functools

import jax
import jax.numpy as jnp
from jax import lax
from jax.experimental import pallas as pl
from jax.experimental.pallas import tpu as pltpu
from jax.sharding import PartitionSpec as P

MESH_IDS = pl.DeviceIdType.MESH


def activation(values):
    return jax.nn.gelu(values, approximate=True)


def tap_index(band, row_tap, col_tap, backward):
    if backward:
        row = 2 - row_tap if band == 0 else row_tap
        return 3 * row + 2 - col_tap
    row = row_tap if band == 0 else 2 - row_tap
    return 3 * row + col_tap


def conv_kernel(backward, first, width, src_ref, before_ref, after_ref, side_ref, k_ref, out_ref, margin_ref):
    bands, rows, cols, cout = out_ref.shape
    pixels = rows * cols
    lanes = slice(first, first + width)
    col = lax.broadcasted_iota(jnp.int32, (rows, cols, cout), 1).reshape(pixels, cout)
    for band in range(bands):
        ext = jnp.concatenate(
            [before_ref[band, :, :, lanes], src_ref[band, :, :, lanes], after_ref[band, :, :, lanes]],
            axis=0,
        )
        lhs = jnp.concatenate(
            [ext[dy : dy + rows].reshape(pixels, width) for dy in range(3)], axis=1
        )
        stacks = []
        for col_tap in range(3):
            taps = [k_ref[tap_index(band, dy, col_tap, backward)] for dy in range(3)]
            if backward:
                stacks.append(jnp.concatenate(taps, axis=1))
            else:
                stacks.append(jnp.concatenate(taps, axis=0))

        def product(values, stack):
            if backward:
                return lax.dot_general(
                    values, stack, (((1,), (1,)), ((), ())), preferred_element_type=jnp.float32
                )
            return jnp.dot(values, stack, preferred_element_type=jnp.float32)

        z_left = product(lhs, stacks[0])
        z_mid = product(lhs, stacks[1])
        z_right = product(lhs, stacks[2])
        if backward:
            left_full = jnp.zeros((pixels, cout), jnp.float32)
            right_full = left_full
        else:
            sides = side_ref[band]
            left = jnp.concatenate([sides[0, dy : dy + rows] for dy in range(3)], axis=1)
            right = jnp.concatenate([sides[1, dy : dy + rows] for dy in range(3)], axis=1)
            left_term = product(left, stacks[0])
            right_term = product(right, stacks[2])
            left_full = jnp.broadcast_to(left_term[:, None, :], (rows, cols, cout)).reshape(pixels, cout)
            right_full = jnp.broadcast_to(right_term[:, None, :], (rows, cols, cout)).reshape(pixels, cout)
        from_left = jnp.where(col == 0, left_full, pltpu.roll(z_left, 1, 0))
        from_right = jnp.where(col == cols - 1, right_full, pltpu.roll(z_right, pixels - 1, 0))
        out_ref[band] = (z_mid + from_left + from_right).reshape(rows, cols, cout)
        if backward:
            margin_ref[band, 0] = z_right.reshape(rows, cols, cout)[:, 0, :]
            margin_ref[band, 1] = z_left.reshape(rows, cols, cout)[:, cols - 1, :]


def conv_pallas(pieces, first, width, sides, kernel, backward):
    source, before, after = pieces
    bands, rows, cols, _ = source.shape
    cout = kernel.shape[1] if backward else kernel.shape[2]
    if sides is None:
        sides = jnp.zeros((bands, 2, rows + 2, width), jnp.bfloat16)
    vmem = pl.BlockSpec(memory_space=pltpu.VMEM)
    out, margins = pl.pallas_call(
        functools.partial(conv_kernel, backward, first, width),
        in_specs=[vmem] * 5,
        out_specs=[vmem, vmem],
        out_shape=[
            jax.ShapeDtypeStruct((bands, rows, cols, cout), jnp.float32),
            jax.ShapeDtypeStruct((bands, 2, rows, cout), jnp.float32),
        ],
        compiler_params=pltpu.CompilerParams(vmem_limit_bytes=60 * 1024 * 1024),
    )(source, before, after, sides, kernel)
    return out, margins


def extend_rows(source, last_tile):
    count = lax.axis_size("tile")
    band_rows = source.shape[1]
    head = source[:, 0:1]
    tail = source[:, band_rows - 1 : band_rows]
    before = lax.ppermute(tail, "tile", [(i, i + 1) for i in range(count - 1)])
    after = lax.ppermute(head, "tile", [(i + 1, i) for i in range(count - 1)])
    after = jnp.where(last_tile, tail[::-1], after)
    return source, before, after


def edge_cols(pieces, first, width):
    extended = jnp.concatenate([piece[..., first : first + width] for piece in (pieces[1], pieces[0], pieces[2])], axis=1)
    return jnp.stack([extended[:, :, 0], extended[:, :, -1]], axis=2)


def pick_partner(gathered, matching_row):
    picked_sides = []
    for side_number in range(2):
        partner = matching_row[side_number, 0]
        their_side = matching_row[side_number, 1]
        flipped = matching_row[side_number, 2]
        chosen = lax.dynamic_index_in_dim(gathered, partner, 0, keepdims=False)
        column = jnp.where(their_side == 0, chosen[:, :, 0], chosen[:, :, 1])
        column = jnp.where(flipped == 1, column[::-1], column)
        picked_sides.append(column)
    return picked_sides


def face_gather_kernel(count, block_ref, out_ref, landed, send_sems, recv_sems):
    face = lax.axis_index("face")
    tile = lax.axis_index("tile")
    barrier = pltpu.get_barrier_semaphore()
    for step in range(1, count):
        peer = lax.rem(face + step, count)
        pl.semaphore_signal(barrier, inc=1, device_id=(peer, tile), device_id_type=MESH_IDS)
    pl.semaphore_wait(barrier, count - 1)
    copies = []
    for step in range(1, count):
        peer = lax.rem(face + step, count)
        copy = pltpu.make_async_remote_copy(
            src_ref=block_ref,
            dst_ref=landed.at[step],
            send_sem=send_sems.at[step],
            recv_sem=recv_sems.at[step],
            device_id=(peer, tile),
            device_id_type=MESH_IDS,
        )
        copy.start()
        copies.append(copy)
    out_ref[0] = block_ref[...]
    for copy in copies:
        copy.wait()
    for step in range(1, count):
        out_ref[step] = landed[step]


def face_gather(block, count, gather_id):
    rows, lanes = block.shape
    return pl.pallas_call(
        functools.partial(face_gather_kernel, count),
        out_shape=jax.ShapeDtypeStruct((count, rows, lanes), block.dtype),
        in_specs=[pl.BlockSpec(memory_space=pltpu.VMEM)],
        out_specs=pl.BlockSpec(memory_space=pltpu.VMEM),
        scratch_shapes=[
            pltpu.VMEM((count, rows, lanes), block.dtype),
            pltpu.SemaphoreType.DMA((count,)),
            pltpu.SemaphoreType.DMA((count,)),
        ],
        compiler_params=pltpu.CompilerParams(collective_id=gather_id, has_side_effects=True),
    )(block)


def gather_faces(parts, gather_id):
    flat = jnp.concatenate([part.astype(jnp.float32).reshape(-1) for part in parts])
    face_count = lax.axis_size("face")
    face_at = lax.axis_index("face")
    landed = face_gather(flat.reshape(-1, 128), face_count, gather_id).reshape(face_count, -1)
    slot_of_face = lax.rem(face_at - lax.iota(jnp.int32, face_count) + face_count, face_count)
    gathered = jnp.take(landed, slot_of_face, axis=0)
    pieces = []
    offset = 0
    for part in parts:
        size = part.size
        piece = gathered[:, offset : offset + size].reshape((face_count,) + part.shape)
        pieces.append(piece)
        offset += size
    return pieces


def side_columns(gathered_edges, matching_row):
    left_side, right_side = pick_partner(gathered_edges, matching_row)
    return jnp.stack([left_side, right_side], axis=1).astype(jnp.bfloat16)


def add_ends(field, first_add, last_add, axis):
    length = field.shape[axis]
    head = lax.slice_in_dim(field, 0, 1, axis=axis) + jnp.expand_dims(first_add, axis)
    middle = lax.slice_in_dim(field, 1, length - 1, axis=axis)
    tail = lax.slice_in_dim(field, length - 1, length, axis=axis) + jnp.expand_dims(last_add, axis)
    return jnp.concatenate([head, middle, tail], axis=axis)


def return_sides(inside, gathered_margins, matching_row):
    left_back, right_back = pick_partner(gathered_margins, matching_row)
    inside = inside.at[:, :, 0].add(left_back)
    return inside.at[:, :, inside.shape[2] - 1].add(right_back)


def route_observations(obs_values, obs_dest, obs_pixel, device_count):
    obs_rows = obs_values.shape[0]
    obs_width = obs_values.shape[1]
    capacity = 2 * obs_rows // device_count
    target = obs_dest[:, 0]
    positions = lax.iota(jnp.int32, obs_rows)
    same_target = (target[:, None] == target[None, :]) & (positions[None, :] < positions[:, None])
    rank_within = jnp.sum(same_target.astype(jnp.int32), axis=1)
    slot_index = target * capacity + rank_within
    slot_ids = lax.iota(jnp.int32, device_count * capacity)
    hits = slot_ids[:, None] == slot_index[None, :]
    value_slots = jnp.dot(
        hits.astype(jnp.bfloat16), obs_values, preferred_element_type=jnp.float32
    ).astype(jnp.bfloat16)
    pixel_slots = jnp.sum(jnp.where(hits, obs_pixel[None, :], 0), axis=1)
    high = (pixel_slots // 16).astype(jnp.bfloat16).reshape(device_count, capacity)
    low = (pixel_slots % 16).astype(jnp.bfloat16).reshape(device_count, capacity)
    pixel_row = jnp.concatenate(
        [high, low, jnp.zeros((device_count, obs_width - 2 * capacity), jnp.bfloat16)], axis=1
    )
    payload = jnp.concatenate(
        [value_slots.reshape(device_count, capacity, obs_width), pixel_row[:, None]], axis=1
    )
    arrived = lax.all_to_all(payload, ("face", "tile"), split_axis=0, concat_axis=0, tiled=True)
    got_values = arrived[:, :capacity].reshape(-1, obs_width)
    got_high = arrived[:, capacity, 0:capacity].astype(jnp.int32)
    got_low = arrived[:, capacity, capacity : 2 * capacity].astype(jnp.int32)
    got_pixels = (got_high * 16 + got_low).reshape(-1)
    return got_values, got_pixels


def per_device(
    state,
    obs_values,
    obs_dest,
    obs_pixel,
    matching,
    kernel_one,
    bias_one,
    kernel_two,
    bias_two,
    cotangent,
):
    base_field = state[0, 0]
    cot_field = cotangent[0, 0]
    band_rows = base_field.shape[1]
    column_count = base_field.shape[2]
    channels = base_field.shape[3]
    tile_count = lax.axis_size("tile")
    face_count = lax.axis_size("face")
    tile_at = lax.axis_index("tile")
    face_at = lax.axis_index("face")
    device_count = tile_count * face_count
    obs_width = obs_values.shape[1]

    got_values, got_pixels = route_observations(obs_values, obs_dest, obs_pixel, device_count)
    pixel_count = 2 * band_rows * column_count
    pixel_ids = lax.iota(jnp.int32, pixel_count)
    onehot = (pixel_ids[:, None] == got_pixels[None, :]).astype(jnp.bfloat16)
    gridded = jnp.dot(onehot, got_values, preferred_element_type=jnp.float32)
    gridded = gridded.reshape(2, band_rows, column_count, obs_width)

    last_tile = tile_at == tile_count - 1
    matching_row = lax.dynamic_index_in_dim(matching, face_at, 0, keepdims=False)

    lifted = kernel_one.shape[2]
    both = extend_rows(jnp.concatenate([base_field, cot_field], axis=3), last_tile)
    cot_back, cot_margins = conv_pallas(both, channels, channels, None, kernel_two, True)
    base_edges, cot_gathered = gather_faces(
        [edge_cols(both, 0, channels), jnp.swapaxes(cot_margins, 1, 2)], 0
    )

    first_out = conv_pallas(both, 0, channels, side_columns(base_edges, matching_row), kernel_one, False)[0]
    pre_act = first_out + bias_one + gridded
    inner = activation(pre_act).astype(jnp.bfloat16)
    grad_inner = return_sides(cot_back, cot_gathered, matching_row)
    grad_pre = jax.vjp(activation, pre_act)[1](grad_inner)[0].astype(jnp.bfloat16)

    pair = extend_rows(jnp.concatenate([inner, grad_pre], axis=3), last_tile)
    pre_back, pre_margins = conv_pallas(pair, lifted, lifted, None, kernel_one, True)
    inner_edges, pre_gathered = gather_faces(
        [edge_cols(pair, 0, lifted), jnp.swapaxes(pre_margins, 1, 2)], 1
    )

    second_out = conv_pallas(pair, 0, lifted, side_columns(inner_edges, matching_row), kernel_two, False)[0]
    analysis = (base_field.astype(jnp.float32) + second_out + bias_two).astype(jnp.bfloat16)
    grad_base = cot_field.astype(jnp.float32) + return_sides(pre_back, pre_gathered, matching_row)
    return (analysis[None, None], grad_base[None, None])


def solution(mesh):
    return jax.shard_map(
        per_device,
        mesh=mesh,
        in_specs=(
            P("face", "tile", None, None, None, None),
            P(("face", "tile"), None),
            P(("face", "tile"), None),
            P(("face", "tile")),
            P(),
            P(),
            P(),
            P(),
            P(),
            P("face", "tile", None, None, None, None),
        ),
        out_specs=(
            P("face", "tile", None, None, None, None),
            P("face", "tile", None, None, None, None),
        ),
        check_vma=False,
    )
```

profile of v0, /device:TPU:24, one launch (start us, length us, event | category | flops | bytes accessed | tf_op | source)
XLA Modules:
  0.0 158.5 jit_solution(4298443967883181365)
XLA Ops:
  0.6 2.3 %fusion.19 = (bf16[2,1,512,256]{3,2,1,0:T(8,128)(2,1)}, bf16[2,1,512,256]{3,2,1,0:T(8,128)(2,1)}) fusion(bf16[2,4,512,128]{3,2,1,0:T(8,128)(2,1)} %bitcast.101, bf16[2,4,512,128]{3,2,1,0:T(8,128)(2,1)} %bitcast.104), kind=kLoop, calls=%fused_computation.43 | loop fusion | flops 2097152 | bytes 3145728 | tf_op jit(solution)/shard_map/concatenate | solution.py:270
  3.0 4.5 %collective-permute-start.1 = (bf16[2,1,512,256]{3,2,1,0:T(8,128)(2,1)}, bf16[2,1,512,256]{3,2,1,0:T(8,128)(2,1)}, u32[]{:S(2)}, u32[]{:S(2)}) collective-permute-start(bf16[2,1,512,256]{3,2,1,0:T(8,128)(2,1)} %get-tuple-element.66), channel_id=1, source_target_pairs={{1,0},{2,1},{3,2},{4,3},{5,4},{6,5},{7,6},{8,7},{9,8},{10,9},{11,1... | collective-permute-start | bytes 1572872 | tf_op jit(solution)/shard_map/ppermute | solution.py:101
  7.5 1.9 %collective-permute-start = (bf16[2,1,512,256]{3,2,1,0:T(8,128)(2,1)}, bf16[2,1,512,256]{3,2,1,0:T(8,128)(2,1)S(1)}, u32[]{:S(2)}, u32[]{:S(2)}) collective-permute-start(bf16[2,1,512,256]{3,2,1,0:T(8,128)(2,1)} %get-tuple-element.67), channel_id=1, source_target_pairs={{0,1},{1,2},{2,3},{3,4},{4,5},{5,6},{6,7},{7,8},{8,9},{9,10},{10,1... | collective-permute-start | bytes 1572872 | tf_op jit(solution)/shard_map/ppermute | solution.py:100
  9.5 1.3 convert_reduce_fusion
  10.7 0.7 multiply_add_fusion.1
  11.4 1.6 %select_reduce_fusion = s32[2048]{0:T(1024)S(1)} fusion(s32[1024]{0:T(1024)} %param.21, s32[1024]{0:T(1024)S(1)} %multiply_add_fusion.1), kind=kLoop, calls=%fused_computation.6 | loop fusion | flops 6289408 | bytes 16384 | tf_op jit(solution)/shard_map/reduce_sum | solution.py:218
  13.1 0.1 reduce_sum.22
  13.1 0.1 fusion.20
  13.2 0.1 pad.23.clone
  13.3 0.1 maximum_bitcast_fusion
  13.4 0.1 copy.50
  13.5 1.6 %fusion.14 = bf16[2048,256]{1,0:T(8,128)(2,1)S(1)} fusion(bf16[1024,256]{1,0:T(8,128)(2,1)S(1)} %copy-done, s32[1024]{0:T(1024)S(1)} %multiply_add_fusion.1), kind=kOutput, calls=%fused_computation.34 | convolution fusion | flops 1076363264 | bytes 1576960 | tf_op jit(solution)/shard_map/dot_general | solution.py:215
  15.2 1.4 pad_maximum_fusion.2
  16.5 11.6 %all-to-all-start = ((bf16[128,17,256]{2,1,0:T(8,128)(2,1)}), bf16[128,17,256]{2,1,0:T(8,128)(2,1)}, u32[]{:S(2)}, u32[]{:S(2)}) async-start(bf16[128,17,256]{2,1,0:T(8,128)(2,1)} %pad_maximum_fusion.2), calls=%async_computation | async-start | bytes 3145728 | tf_op jit(solution)/shard_map/all_to_all | solution.py:227
  28.2 0.1 constant_dynamic-slice_fusion.8
  28.3 0.1 copy.46
  28.4 0.7 fusion.67
  35.5 1.5 pad_maximum_fusion.1.src_ref
  37.1 1.3 reverse_select_fusion.1.after_ref
  38.5 0.7 broadcast_in_dim.59.side_ref
  39.2 0.2 copy-done.9
  39.4 7.4 %shard_map.113 = (f32[2,4,512,256]{3,2,1,0:T(8,128)}, f32[2,2,4,256]{3,2,1,0:T(4,128)}) custom-call(bf16[2,4,512,256]{3,2,1,0:T(8,128)(2,1)} %pad_maximum_fusion.1.src_ref, bf16[2,1,512,256]{3,2,1,0:T(8,128)(2,1)} %copy-done.9, bf16[2,1,512,256]{3,2,1,0:T(8,128)(2,1)} %copy-done.6, bf16[2,2,6,128]{3,2,1,0:T(8,128)(2,1)} %broadcast_in_dim.59.side_ref, ...), custom_call_target="tpu_custom_call" | custom-call | tf_op jit(solution)/shard_map/pallas_call | solution.py:82
  46.8 0.7 copy.47
  47.6 1.0 slice.302
  48.6 0.6 maximum_bitcast_fusion.2.block_ref
  49.2 10.3 %shard_map.114 = f32[8,56,128]{2,1,0:T(8,128)} custom-call(f32[56,128]{1,0:T(8,128)} %maximum_bitcast_fusion.2.block_ref), custom_call_target="tpu_custom_call" | custom-call | tf_op jit(solution)/shard_map/pallas_call | solution.py:154
  59.5 1.0 copy.82
  60.5 0.6 gather_fusion
  61.1 0.1 broadcast_select_fusion.1
  61.3 0.9 reshape_add_fusion
  62.2 1.5 scatter-add.14
  63.8 0.9 slice_add_fusion
  64.6 1.5 scatter-add.15
  66.2 0.6 pad_maximum_fusion.4.side_ref
  66.8 7.6 %shard_map.115 = (f32[2,4,512,256]{3,2,1,0:T(8,128)}, f32[2,2,4,256]{3,2,1,0:T(4,128)}) custom-call(bf16[2,4,512,256]{3,2,1,0:T(8,128)(2,1)} %pad_maximum_fusion.1.src_ref, bf16[2,1,512,256]{3,2,1,0:T(8,128)(2,1)} %copy-done.9, bf16[2,1,512,256]{3,2,1,0:T(8,128)(2,1)} %copy-done.6, bf16[2,2,6,128]{3,2,1,0:T(8,128)(2,1)} %pad_maximum_fusion.4.side_ref, ...), custom_call_target="tpu_custom_call" | custom-call | tf_op jit(solution)/shard_map/pallas_call | solution.py:82
  74.4 1.5 fusion.23
  75.9 0.1 add.160
  75.9 1.3 slice.311
  77.3 5.3 %fusion = f32[2,4,512,256]{3,2,1,0:T(8,128)S(1)} fusion(bf16[2048,256,1,1]{1,0,3,2:T(8,128)(2,1)S(1)} %bitcast.106, s32[2048]{0:T(1024)S(1)} %add.160, s32[2,4,512]{2,1,0:T(4,128)S(1)} %multiply_add_fusion), kind=kOutput, calls=%fused_computation.2 | convolution fusion | flops 4303355904 | bytes 5267456 | tf_op jit(solution)/shard_map/dot_general | solution.py:263
  82.7 3.5 %multiply_convert_fusion = (bf16[2,4,512,256]{3,2,1,0:T(8,128)(2,1)S(1)}, bf16[2,4,512,256]{3,2,1,0:T(8,128)(2,1)S(1)}) fusion(f32[2,4,512,256]{3,2,1,0:T(8,128)S(1)} %fusion, f32[2,4,512,256]{3,2,1,0:T(8,128)S(1)} %copy-done.8, f32[256]{0:T(256)S(1)} %copy-done.11, f32[2,4,512,256]{3,2,1,0:T(8,128)S(1)} %copy-done.7), kind=kLoop, calls=%fused_computation.23 | loop fusion | flops 25165824 | bytes 16778240 | tf_op jit(solution)/shard_map/convert_element_type | solution.py:278
  86.1 0.2 fusion.17
  86.3 3.5 %collective-permute-start.3 = (bf16[2,1,512,512]{3,2,1,0:T(8,128)(2,1)S(1)}, bf16[2,1,512,512]{3,2,1,0:T(8,128)(2,1)S(1)}, u32[]{:S(2)}, u32[]{:S(2)}) collective-permute-start(bf16[2,1,512,512]{3,2,1,0:T(8,128)(2,1)S(1)} %get-tuple-element.64), channel_id=1, source_target_pairs={{1,0},{2,1},{3,2},{4,3},{5,4},{6,5},{7,6},{8,7},{9,8},{10,9},{11,1... | collective-permute-start | bytes 3145736 | tf_op jit(solution)/shard_map/ppermute | solution.py:101
  89.8 2.1 %collective-permute-start.2 = (bf16[2,1,512,512]{3,2,1,0:T(8,128)(2,1)S(1)}, bf16[2,1,512,512]{3,2,1,0:T(8,128)(2,1)S(1)}, u32[]{:S(2)}, u32[]{:S(2)}) collective-permute-start(bf16[2,1,512,512]{3,2,1,0:T(8,128)(2,1)S(1)} %get-tuple-element.65), channel_id=1, source_target_pairs={{0,1},{1,2},{2,3},{3,4},{4,5},{5,6},{6,7},{7,8},{8,9},{9,10},{10,1... | collective-permute-start | bytes 3145736 | tf_op jit(solution)/shard_map/ppermute | solution.py:100
  91.9 2.3 %pad_maximum_fusion.src_ref = bf16[2,4,512,512]{3,2,1,0:T(8,128)(2,1)} fusion(bf16[2,4,512,256]{3,2,1,0:T(8,128)(2,1)S(1)} %get-tuple-element.63, bf16[2,4,512,256]{3,2,1,0:T(8,128)(2,1)S(1)} %get-tuple-element.62), kind=kLoop, calls=%fused_computation.13 | loop fusion | flops 8388608 | bytes 8388608 | tf_op jit(solution)/shard_map/concatenate | solution.py:282
  94.2 16.6 %collective-permute-done.3 = bf16[2,1,512,512]{3,2,1,0:T(8,128)(2,1)S(1)} collective-permute-done((bf16[2,1,512,512]{3,2,1,0:T(8,128)(2,1)S(1)}, bf16[2,1,512,512]{3,2,1,0:T(8,128)(2,1)S(1)}, u32[]{:S(2)}, u32[]{:S(2)}) %collective-permute-start.3) | collective-permute-done | bytes 1048608 | tf_op jit(solution)/shard_map/ppermute | solution.py:101
  110.8 0.3 reverse_select_fusion.after_ref
  111.2 4.0 %collective-permute-done.2.before_ref = bf16[2,1,512,512]{3,2,1,0:T(8,128)(2,1)S(1)} collective-permute-done((bf16[2,1,512,512]{3,2,1,0:T(8,128)(2,1)S(1)}, bf16[2,1,512,512]{3,2,1,0:T(8,128)(2,1)S(1)}, u32[]{:S(2)}, u32[]{:S(2)}) %collective-permute-start.2) | collective-permute-done | bytes 1048608 | tf_op jit(solution)/shard_map/ppermute | solution.py:100
  115.2 0.9 copy-done.5
  116.1 0.6 broadcast_in_dim.66.side_ref
  116.7 9.3 %shard_map.116 = (f32[2,4,512,128]{3,2,1,0:T(8,128)}, f32[2,2,4,128]{3,2,1,0:T(4,128)}) custom-call(bf16[2,4,512,512]{3,2,1,0:T(8,128)(2,1)} %pad_maximum_fusion.src_ref, bf16[2,1,512,512]{3,2,1,0:T(8,128)(2,1)} %copy-done.5, bf16[2,1,512,512]{3,2,1,0:T(8,128)(2,1)} %copy-done.2, bf16[2,2,6,256]{3,2,1,0:T(8,128)(2,1)} %broadcast_in_dim.66.side_ref, ...), custom_call_target="tpu_custom_call" | custom-call | tf_op jit(solution)/shard_map/pallas_call | solution.py:82
  126.1 0.8 copy.53
  126.9 0.6 maximum_bitcast_fusion.1.block_ref
  127.5 8.6 %shard_map.117 = f32[8,64,128]{2,1,0:T(8,128)} custom-call(f32[64,128]{1,0:T(8,128)} %maximum_bitcast_fusion.1.block_ref), custom_call_target="tpu_custom_call" | custom-call | tf_op jit(solution)/shard_map/pallas_call | solution.py:154
  136.1 1.1 copy.81
  137.2 0.6 gather_fusion.1
  137.8 0.1 broadcast_select_fusion
  138.0 0.8 slice_add_fusion.2
  138.8 1.4 scatter-add.16
  140.2 0.8 slice_add_fusion.1
  141.0 1.4 scatter-add.19
  142.4 3.1 %add_bitcast_fusion = f32[1,1,2,4,512,128]{5,4,3,2,1,0:T(8,128)} fusion(f32[2,4,512,128]{3,2,1,0:T(8,128)} %scatter-add.19, bf16[1,1,2,4,512,128]{5,4,3,2,1,0:T(8,128)(2,1)S(1)} %copy-done.4), kind=kLoop, calls=%fused_computation.35 | loop fusion | flops 1048576 | bytes 5242880 | tf_op jit(solution)/shard_map/broadcast_in_dim | solution.py:291
  145.6 0.6 pad_maximum_fusion.3.side_ref
  146.2 9.5 %shard_map.118 = (f32[2,4,512,128]{3,2,1,0:T(8,128)}, f32[2,2,4,128]{3,2,1,0:T(4,128)}) custom-call(bf16[2,4,512,512]{3,2,1,0:T(8,128)(2,1)} %pad_maximum_fusion.src_ref, bf16[2,1,512,512]{3,2,1,0:T(8,128)(2,1)} %copy-done.5, bf16[2,1,512,512]{3,2,1,0:T(8,128)(2,1)} %copy-done.2, bf16[2,2,6,256]{3,2,1,0:T(8,128)(2,1)} %pad_maximum_fusion.3.side_ref, ...), custom_call_target="tpu_custom_call" | custom-call | tf_op jit(solution)/shard_map/pallas_call | solution.py:82
  155.7 2.8 %fusion.15 = bf16[1,1,2,4,512,128]{5,4,3,2,1,0:T(8,128)(2,1)} fusion(f32[2,4,512,128]{3,2,1,0:T(8,128)} %get-tuple-element.60, f32[128]{0:T(128)S(1)} %copy-done.12, bf16[1,1,2,4,512,128]{5,4,3,2,1,0:T(8,128)(2,1)S(1)} %copy-done.1), kind=kLoop, calls=%fused_computation.38 | loop fusion | flops 2097152 | bytes 4194816 | tf_op jit(solution)/shard_map/broadcast_in_dim | solution.py:291
  (70 shorter events, 0.6 us)
Async XLA Ops:
  0.6 12.9 %copy-start = (bf16[1024,256]{1,0:T(8,128)(2,1)S(1)}, bf16[1024,256]{1,0:T(8,128)(2,1)}, u32[]{:S(2)}) copy-start(bf16[1024,256]{1,0:T(8,128)(2,1)} %param.19) | copy-start | bytes 1572868
  3.0 34.1 %collective-permute-start.1 = (bf16[2,1,512,256]{3,2,1,0:T(8,128)(2,1)}, bf16[2,1,512,256]{3,2,1,0:T(8,128)(2,1)}, u32[]{:S(2)}, u32[]{:S(2)}) collective-permute-start(bf16[2,1,512,256]{3,2,1,0:T(8,128)(2,1)} %get-tuple-element.66), channel_id=1, source_target_pairs={{1,0},{2,1},{3,2},{4,3},{5,4},{6,5},{7,6},{8,7},{9,8},{10,9},{11,1... | collective-permute-start | bytes 1572872 | tf_op jit(solution)/shard_map/ppermute | solution.py:101
  7.5 30.9 %collective-permute-start = (bf16[2,1,512,256]{3,2,1,0:T(8,128)(2,1)}, bf16[2,1,512,256]{3,2,1,0:T(8,128)(2,1)S(1)}, u32[]{:S(2)}, u32[]{:S(2)}) collective-permute-start(bf16[2,1,512,256]{3,2,1,0:T(8,128)(2,1)} %get-tuple-element.67), channel_id=1, source_target_pairs={{0,1},{1,2},{2,3},{3,4},{4,5},{5,6},{6,7},{7,8},{8,9},{9,10},{10,1... | collective-permute-start | bytes 1572872 | tf_op jit(solution)/shard_map/ppermute | solution.py:100
  15.1 13.0 %copy-start.10 = (s32[8,2,3]{0,1,2:T(2,128)S(1)}, s32[8,2,3]{0,1,2:T(2,128)}, u32[]{:S(2)}) copy-start(s32[8,2,3]{0,1,2:T(2,128)} %param.22) | copy-start | bytes 580
  15.2 20.3 %copy-start.1 = (bf16[1,1,2,4,512,128]{5,4,3,2,1,0:T(8,128)(2,1)S(1)}, bf16[1,1,2,4,512,128]{5,4,3,2,1,0:T(8,128)(2,1)}, u32[]{:S(2)}) copy-start(bf16[1,1,2,4,512,128]{5,4,3,2,1,0:T(8,128)(2,1)} %param.18) | copy-start | bytes 3145732
  15.2 20.3 %copy-start.3 = (bf16[1,1,2,4,512,128]{5,4,3,2,1,0:T(8,128)(2,1)S(1)}, bf16[1,1,2,4,512,128]{5,4,3,2,1,0:T(8,128)(2,1)}, u32[]{:S(2)}) copy-start(bf16[1,1,2,4,512,128]{5,4,3,2,1,0:T(8,128)(2,1)} %param.27) | copy-start | bytes 3145732
  16.5 57.8 %all-to-all-start = ((bf16[128,17,256]{2,1,0:T(8,128)(2,1)}), bf16[128,17,256]{2,1,0:T(8,128)(2,1)}, u32[]{:S(2)}, u32[]{:S(2)}) async-start(bf16[128,17,256]{2,1,0:T(8,128)(2,1)} %pad_maximum_fusion.2), calls=%async_computation | async-start | bytes 3145728 | tf_op jit(solution)/shard_map/all_to_all | solution.py:227
  38.4 0.8 copy-start.6
  38.5 0.9 copy-start.9
  77.3 5.4 %copy-start.7 = (f32[2,4,512,256]{3,2,1,0:T(8,128)S(1)}, f32[2,4,512,256]{3,2,1,0:T(8,128)}, u32[]{:S(2)}) copy-start(f32[2,4,512,256]{3,2,1,0:T(8,128)} %scatter-add.15) | copy-start | bytes 12582916
  77.3 5.4 %copy-start.8 = (f32[2,4,512,256]{3,2,1,0:T(8,128)S(1)}, f32[2,4,512,256]{3,2,1,0:T(8,128)}, u32[]{:S(2)}) copy-start(f32[2,4,512,256]{3,2,1,0:T(8,128)} %get-tuple-element.57) | copy-start | bytes 12582916
  77.3 5.4 %copy-start.11 = (f32[256]{0:T(256)S(1)}, f32[256]{0:T(256)}, u32[]{:S(2)}) copy-start(f32[256]{0:T(256)} %param.24) | copy-start | bytes 3076
  86.3 24.5 %collective-permute-start.3 = (bf16[2,1,512,512]{3,2,1,0:T(8,128)(2,1)S(1)}, bf16[2,1,512,512]{3,2,1,0:T(8,128)(2,1)S(1)}, u32[]{:S(2)}, u32[]{:S(2)}) collective-permute-start(bf16[2,1,512,512]{3,2,1,0:T(8,128)(2,1)S(1)} %get-tuple-element.64), channel_id=1, source_target_pairs={{1,0},{2,1},{3,2},{4,3},{5,4},{6,5},{7,6},{8,7},{9,8},{10,9},{11,1... | collective-permute-start | bytes 3145736 | tf_op jit(solution)/shard_map/ppermute | solution.py:101
  89.8 25.4 %collective-permute-start.2 = (bf16[2,1,512,512]{3,2,1,0:T(8,128)(2,1)S(1)}, bf16[2,1,512,512]{3,2,1,0:T(8,128)(2,1)S(1)}, u32[]{:S(2)}, u32[]{:S(2)}) collective-permute-start(bf16[2,1,512,512]{3,2,1,0:T(8,128)(2,1)S(1)} %get-tuple-element.65), channel_id=1, source_target_pairs={{0,1},{1,2},{2,3},{3,4},{4,5},{5,6},{6,7},{7,8},{8,9},{9,10},{10,1... | collective-permute-start | bytes 3145736 | tf_op jit(solution)/shard_map/ppermute | solution.py:100
  111.1 5.6 %copy-start.2 = (bf16[2,1,512,512]{3,2,1,0:T(8,128)(2,1)}, bf16[2,1,512,512]{3,2,1,0:T(8,128)(2,1)S(1)}, u32[]{:S(2)}) copy-start(bf16[2,1,512,512]{3,2,1,0:T(8,128)(2,1)S(1)} %reverse_select_fusion.after_ref) | copy-start | bytes 3145732
  115.2 1.0 copy-start.5
  126.1 16.3 %copy-start.4 = (bf16[1,1,2,4,512,128]{5,4,3,2,1,0:T(8,128)(2,1)S(1)}, bf16[1,1,2,4,512,128]{5,4,3,2,1,0:T(8,128)(2,1)}, u32[]{:S(2)}) copy-start(bf16[1,1,2,4,512,128]{5,4,3,2,1,0:T(8,128)(2,1)} %param.27) | copy-start | bytes 3145732
  145.5 10.3 %copy-start.12 = (f32[128]{0:T(128)S(1)}, f32[128]{0:T(128)}, u32[]{:S(2)}) copy-start(f32[128]{0:T(128)} %param.26) | copy-start | bytes 1540
where the time goes:
time: 160 us; the launch traced here: 159 us
  Pallas kernels  52.8 us (33%)
  other arithmetic  29.9 us (19%)
  starting transfers between devices  23.7 us (15%)
  waiting for transfers between devices  20.6 us (13%)
  local copies, waits for them, and re-layouts  16.9 us (11%)
  between operations  7.63 us (5%)
  matrix products  6.97 us (4%)
    pallas_call x4, Pallas kernels, conv_pallas(): pl.pallas_call(functools.partial(conv_kernel, backward, first, width), in...  33.9 us
    pallas_call x2, Pallas kernels, face_gather(): pl.pallas_call(functools.partial(face_gather_kernel, count), out_shape=ja...  18.9 us
    ppermute x2, waiting for transfers between devices, extend_rows(): after = lax.ppermute(head, 'tile', [(i + 1, i) for i in range(count - 1)])  16.6 us
    all_to_all x1, starting transfers between devices, route_observations(): lax.all_to_all(payload, ('face', 'tile'), split_axis=0, concat_axis=0, ti...  11.6 us
    ppermute x2, starting transfers between devices, extend_rows(): after = lax.ppermute(head, 'tile', [(i + 1, i) for i in range(count - 1)])  7.99 us
    broadcast_in_dim x2, other arithmetic, per_device(): return (analysis[None, None], grad_base[None, None])  5.92 us
    dot_general x1, matrix products, per_device(): gridded = jnp.dot(onehot, got_values, preferred_element_type=jnp.float32)  5.35 us
    ppermute x2, starting transfers between devices, extend_rows(): before = lax.ppermute(tail, 'tile', [(i, i + 1) for i in range(count - 1)])  4.06 us
  transfers between devices with their start and end apart: 5, of which 2 were waited for; matrix products, arithmetic and copies ran while one was open for 15% of the time, Pallas kernels for 16%

commit v1 on v0

--- a/solution.py
+++ b/solution.py
@@ -53,7 +53,7 @@
         z_left = product(lhs, stacks[0])
         z_mid = product(lhs, stacks[1])
         z_right = product(lhs, stacks[2])
-        if backward:
+        if backward or side_ref is None:
             left_full = jnp.zeros((pixels, cout), jnp.float32)
             right_full = left_full
         else:
@@ -92,36 +92,8 @@
     return out, margins
 
 
-def extend_rows(source, last_tile):
-    count = lax.axis_size("tile")
-    band_rows = source.shape[1]
-    head = source[:, 0:1]
-    tail = source[:, band_rows - 1 : band_rows]
-    before = lax.ppermute(tail, "tile", [(i, i + 1) for i in range(count - 1)])
-    after = lax.ppermute(head, "tile", [(i + 1, i) for i in range(count - 1)])
-    after = jnp.where(last_tile, tail[::-1], after)
-    return source, before, after
-
-
-def edge_cols(pieces, first, width):
-    extended = jnp.concatenate([piece[..., first : first + width] for piece in (pieces[1], pieces[0], pieces[2])], axis=1)
-    return jnp.stack([extended[:, :, 0], extended[:, :, -1]], axis=2)
-
-
-def pick_partner(gathered, matching_row):
-    picked_sides = []
-    for side_number in range(2):
-        partner = matching_row[side_number, 0]
-        their_side = matching_row[side_number, 1]
-        flipped = matching_row[side_number, 2]
-        chosen = lax.dynamic_index_in_dim(gathered, partner, 0, keepdims=False)
-        column = jnp.where(their_side == 0, chosen[:, :, 0], chosen[:, :, 1])
-        column = jnp.where(flipped == 1, column[::-1], column)
-        picked_sides.append(column)
-    return picked_sides
-
-
-def face_gather_kernel(count, block_ref, out_ref, landed, send_sems, recv_sems):
+def conv_gather_kernel(count, first, width, block_ref, src_ref, before_ref, after_ref, k_ref,
+                       out_ref, gathered_ref, landed, send_sems, recv_sems):
     face = lax.axis_index("face")
     tile = lax.axis_index("tile")
     barrier = pltpu.get_barrier_semaphore()
@@ -142,34 +114,102 @@
         )
         copy.start()
         copies.append(copy)
-    out_ref[0] = block_ref[...]
+    gathered_ref[0] = block_ref[...]
+    conv_kernel(False, first, width, src_ref, before_ref, after_ref, None, k_ref, out_ref, None)
     for copy in copies:
         copy.wait()
     for step in range(1, count):
-        out_ref[step] = landed[step]
-
-
-def face_gather(block, count, gather_id):
-    rows, lanes = block.shape
+        gathered_ref[step] = landed[step]
+
+
+def conv_gather(pieces, first, width, block, kernel, gather_id):
+    source, before, after = pieces
+    bands, rows, cols, _ = source.shape
+    cout = kernel.shape[2]
+    count = lax.axis_size("face")
+    block_rows, lanes = block.shape
+    vmem = pl.BlockSpec(memory_space=pltpu.VMEM)
     return pl.pallas_call(
-        functools.partial(face_gather_kernel, count),
-        out_shape=jax.ShapeDtypeStruct((count, rows, lanes), block.dtype),
-        in_specs=[pl.BlockSpec(memory_space=pltpu.VMEM)],
-        out_specs=pl.BlockSpec(memory_space=pltpu.VMEM),
+        functools.partial(conv_gather_kernel, count, first, width),
+        in_specs=[vmem] * 5,
+        out_specs=[vmem, vmem],
+        out_shape=[
+            jax.ShapeDtypeStruct((bands, rows, cols, cout), jnp.float32),
+            jax.ShapeDtypeStruct((count, block_rows, lanes), block.dtype),
+        ],
         scratch_shapes=[
-            pltpu.VMEM((count, rows, lanes), block.dtype),
+            pltpu.VMEM((count, block_rows, lanes), block.dtype),
             pltpu.SemaphoreType.DMA((count,)),
             pltpu.SemaphoreType.DMA((count,)),
         ],
-        compiler_params=pltpu.CompilerParams(collective_id=gather_id, has_side_effects=True),
-    )(block)
-
-
-def gather_faces(parts, gather_id):
+        compiler_params=pltpu.CompilerParams(
+            collective_id=gather_id, has_side_effects=True, vmem_limit_bytes=60 * 1024 * 1024
+        ),
+    )(block, source, before, after, kernel)
+
+
+def side_terms(sides, kernel):
+    bands, _, ext_rows, width = sides.shape
+    rows = ext_rows - 2
+    terms = []
+    for band in range(bands):
+        per_side = []
+        for side, col_tap in ((0, 0), (1, 2)):
+            stacked = jnp.concatenate([sides[band, side, dy : dy + rows] for dy in range(3)], axis=1)
+            weights = jnp.concatenate(
+                [kernel[tap_index(band, dy, col_tap, False)] for dy in range(3)], axis=0
+            )
+            per_side.append(jnp.dot(stacked, weights, preferred_element_type=jnp.float32))
+        terms.append(jnp.stack(per_side))
+    return jnp.stack(terms)
+
+
+def at_edges(field, left_add, right_add):
+    cols = field.shape[2]
+    col = lax.broadcasted_iota(jnp.int32, field.shape, 2)
+    return field + jnp.where(col == 0, left_add[:, :, None], 0.0) + jnp.where(
+        col == cols - 1, right_add[:, :, None], 0.0
+    )
+
+
+def extend_rows(source, last_tile):
+    count = lax.axis_size("tile")
+    band_rows = source.shape[1]
+    head = source[:, 0:1]
+    tail = source[:, band_rows - 1 : band_rows]
+    before = lax.ppermute(tail, "tile", [(i, i + 1) for i in range(count - 1)])
+    after = lax.ppermute(head, "tile", [(i + 1, i) for i in range(count - 1)])
+    after = jnp.where(last_tile, tail[::-1], after)
+    return source, before, after
+
+
+def edge_cols(pieces, first, width):
+    extended = jnp.concatenate([piece[..., first : first + width] for piece in (pieces[1], pieces[0], pieces[2])], axis=1)
+    return jnp.stack([extended[:, :, 0], extended[:, :, -1]], axis=2)
+
+
+def pick_partner(gathered, matching_row):
+    picked_sides = []
+    for side_number in range(2):
+        partner = matching_row[side_number, 0]
+        their_side = matching_row[side_number, 1]
+        flipped = matching_row[side_number, 2]
+        chosen = lax.dynamic_index_in_dim(gathered, partner, 0, keepdims=False)
+        column = jnp.where(their_side == 0, chosen[:, :, 0], chosen[:, :, 1])
+        column = jnp.where(flipped == 1, column[::-1], column)
+        picked_sides.append(column)
+    return picked_sides
+
+
+def pack_parts(parts):
     flat = jnp.concatenate([part.astype(jnp.float32).reshape(-1) for part in parts])
+    return flat.reshape(-1, 128)
+
+
+def unpack_parts(landed, parts):
     face_count = lax.axis_size("face")
     face_at = lax.axis_index("face")
-    landed = face_gather(flat.reshape(-1, 128), face_count, gather_id).reshape(face_count, -1)
+    landed = landed.reshape(face_count, -1)
     slot_of_face = lax.rem(face_at - lax.iota(jnp.int32, face_count) + face_count, face_count)
     gathered = jnp.take(landed, slot_of_face, axis=0)
     pieces = []
@@ -197,8 +237,7 @@
 
 def return_sides(inside, gathered_margins, matching_row):
     left_back, right_back = pick_partner(gathered_margins, matching_row)
-    inside = inside.at[:, :, 0].add(left_back)
-    return inside.at[:, :, inside.shape[2] - 1].add(right_back)
+    return at_edges(inside, left_back, right_back)
 
 
 def route_observations(obs_values, obs_dest, obs_pixel, device_count):
@@ -269,23 +308,24 @@
     lifted = kernel_one.shape[2]
     both = extend_rows(jnp.concatenate([base_field, cot_field], axis=3), last_tile)
     cot_back, cot_margins = conv_pallas(both, channels, channels, None, kernel_two, True)
-    base_edges, cot_gathered = gather_faces(
-        [edge_cols(both, 0, channels), jnp.swapaxes(cot_margins, 1, 2)], 0
-    )
-
-    first_out = conv_pallas(both, 0, channels, side_columns(base_edges, matching_row), kernel_one, False)[0]
-    pre_act = first_out + bias_one + gridded
+    parts = [edge_cols(both, 0, channels), jnp.swapaxes(cot_margins, 1, 2)]
+    first_out, landed = conv_gather(both, 0, channels, pack_parts(parts), kernel_one, 0)
+    base_edges, cot_gathered = unpack_parts(landed, parts)
+    first_sides = side_terms(side_columns(base_edges, matching_row), kernel_one)
+
+    pre_act = at_edges(first_out, first_sides[:, 0], first_sides[:, 1]) + bias_one + gridded
     inner = activation(pre_act).astype(jnp.bfloat16)
     grad_inner = return_sides(cot_back, cot_gathered, matching_row)
     grad_pre = jax.vjp(activation, pre_act)[1](grad_inner)[0].astype(jnp.bfloat16)
 
     pair = extend_rows(jnp.concatenate([inner, grad_pre], axis=3), last_tile)
     pre_back, pre_margins = conv_pallas(pair, lifted, lifted, None, kernel_one, True)
-    inner_edges, pre_gathered = gather_faces(
-        [edge_cols(pair, 0, lifted), jnp.swapaxes(pre_margins, 1, 2)], 1
-    )
-
-    second_out = conv_pallas(pair, 0, lifted, side_columns(inner_edges, matching_row), kernel_two, False)[0]
+    parts = [edge_cols(pair, 0, lifted), jnp.swapaxes(pre_margins, 1, 2)]
+    second_out, landed = conv_gather(pair, 0, lifted, pack_parts(parts), kernel_two, 1)
+    inner_edges, pre_gathered = unpack_parts(landed, parts)
+    second_sides = side_terms(side_columns(inner_edges, matching_row), kernel_two)
+
+    second_out = at_edges(second_out, second_sides[:, 0], second_sides[:, 1])
     analysis = (base_field.astype(jnp.float32) + second_out + bias_two).astype(jnp.bfloat16)
     grad_base = cot_field.astype(jnp.float32) + return_sides(pre_back, pre_gathered, matching_row)
     return (analysis[None, None], grad_base[None, None])

time: 160 us -> 141 us (0.88)
  Pallas kernels: 52.8 us -> 42.1 us
  local copies, waits for them, and re-layouts: 16.9 us -> 11.5 us
  other arithmetic: 29.9 us -> 26.4 us
    pallas_call x4 -> x2, Pallas kernels: 33.9 us -> 16.8 us  [conv_pallas(): pl.pallas_call(functools.partial(conv_kernel, backward, first, width), in...]
    pallas_call x2, Pallas kernels: 18.9 us -> 25.3 us  [conv_gather(): pl.pallas_call(functools.partial(conv_gather_kernel, count, first, width)...]
    scatter-add x4 -> x0, local copies, waits for them, and re-layouts: 5.79 us -> none  [the longest x2 2.9 us: return_sides(): return inside.at[:, :, inside.shape[2] - 1].add(right_back)]
    add x4 -> x0, other arithmetic: 3.24 us -> none  [the longest x2 1.62 us: return_sides(): inside = inside.at[:, :, 0].add(left_back)]
    broadcast_in_dim x2 -> x1, other arithmetic: 5.92 us -> 5.17 us  [per_device(): return (analysis[None, None], grad_base[None, None])]
    unnamed x34 -> x54, local copies, waits for them, and re-layouts: 3.32 us -> 3.31 us
  transfers between devices with their start and end apart: 5 -> 5, of which waited for: 2 -> 2; matrix products, arithmetic and copies ran while one was open for 15% -> 14% of each run, Pallas kernels for 16% -> 15%
where the time goes in v1:
time: 141 us; the launch traced here: 140 us
  Pallas kernels  42.1 us (30%)
  other arithmetic  26.4 us (19%)
  starting transfers between devices  23.7 us (17%)
  waiting for transfers between devices  20.5 us (15%)
  local copies, waits for them, and re-layouts  11.5 us (8%)
  matrix products  8.13 us (6%)
  between operations  7.66 us (5%)
    pallas_call x2, Pallas kernels, conv_gather(): pl.pallas_call(functools.partial(conv_gather_kernel, count, first, width)...  25.3 us
    pallas_call x2, Pallas kernels, conv_pallas(): pl.pallas_call(functools.partial(conv_kernel, backward, first, width), in...  16.8 us
    ppermute x2, waiting for transfers between devices, extend_rows(): after = lax.ppermute(head, 'tile', [(i + 1, i) for i in range(count - 1)])  16.5 us
    all_to_all x1, starting transfers between devices, route_observations(): lax.all_to_all(payload, ('face', 'tile'), split_axis=0, concat_axis=0, ti...  11.6 us
    ppermute x2, starting transfers between devices, extend_rows(): after = lax.ppermute(head, 'tile', [(i + 1, i) for i in range(count - 1)])  8.01 us
    dot_general x1, matrix products, per_device(): gridded = jnp.dot(onehot, got_values, preferred_element_type=jnp.float32)  5.33 us
    broadcast_in_dim x1, other arithmetic, per_device(): return (analysis[None, None], grad_base[None, None])  5.17 us
    convert_element_type x1, other arithmetic, per_device(): inner = activation(pre_act).astype(jnp.bfloat16)  5.04 us
  transfers between devices with their start and end apart: 5, of which 2 were waited for; matrix products, arithmetic and copies ran while one was open for 14% of the time, Pallas kernels for 15%

profile of v1, /device:TPU:24, one launch (start us, length us, event | category | flops | bytes accessed | tf_op | source)
XLA Modules:
  0.0 139.9 jit_solution(16085898801033813950)
XLA Ops:
  0.6 0.0 copy-start
  0.6 2.3 %fusion.19 = (bf16[2,1,512,256]{3,2,1,0:T(8,128)(2,1)}, bf16[2,1,512,256]{3,2,1,0:T(8,128)(2,1)}) fusion(bf16[2,4,512,128]{3,2,1,0:T(8,128)(2,1)} %bitcast.235, bf16[2,4,512,128]{3,2,1,0:T(8,128)(2,1)} %bitcast.238), kind=kLoop, calls=%fused_computation.51 | loop fusion | flops 2097152 | bytes 3145728 | tf_op jit(solution)/shard_map/concatenate | solution.py:309
  3.0 4.5 %collective-permute-start.1 = (bf16[2,1,512,256]{3,2,1,0:T(8,128)(2,1)}, bf16[2,1,512,256]{3,2,1,0:T(8,128)(2,1)}, u32[]{:S(2)}, u32[]{:S(2)}) collective-permute-start(bf16[2,1,512,256]{3,2,1,0:T(8,128)(2,1)} %get-tuple-element.22), channel_id=1, source_target_pairs={{1,0},{2,1},{3,2},{4,3},{5,4},{6,5},{7,6},{8,7},{9,8},{10,9},{11,1... | collective-permute-start | bytes 1572872 | tf_op jit(solution)/shard_map/ppermute | solution.py:181
  7.5 1.9 %collective-permute-start = (bf16[2,1,512,256]{3,2,1,0:T(8,128)(2,1)}, bf16[2,1,512,256]{3,2,1,0:T(8,128)(2,1)}, u32[]{:S(2)}, u32[]{:S(2)}) collective-permute-start(bf16[2,1,512,256]{3,2,1,0:T(8,128)(2,1)} %get-tuple-element.23), channel_id=1, source_target_pairs={{0,1},{1,2},{2,3},{3,4},{4,5},{5,6},{6,7},{7,8},{8,9},{9,10},{10,1... | collective-permute-start | bytes 1572872 | tf_op jit(solution)/shard_map/ppermute | solution.py:180
  9.4 1.3 convert_reduce_fusion
  10.7 0.7 multiply_add_fusion.1
  11.4 1.6 %select_reduce_fusion = s32[2048]{0:T(1024)S(1)} fusion(s32[1024]{0:T(1024)} %param.13, s32[1024]{0:T(1024)S(1)} %multiply_add_fusion.1), kind=kLoop, calls=%fused_computation.6 | loop fusion | flops 6289408 | bytes 16384 | tf_op jit(solution)/shard_map/reduce_sum | solution.py:257
  13.0 0.1 reduce_sum.22
  13.1 0.1 fusion.52
  13.2 0.1 pad.43.clone
  13.3 0.1 maximum_bitcast_fusion
  13.4 0.1 copy.117
  13.5 1.6 %fusion.14 = bf16[2048,256]{1,0:T(8,128)(2,1)S(1)} fusion(bf16[1024,256]{1,0:T(8,128)(2,1)S(1)} %copy-done, s32[1024]{0:T(1024)S(1)} %multiply_add_fusion.1), kind=kOutput, calls=%fused_computation.34 | convolution fusion | flops 1076363264 | bytes 1576960 | tf_op jit(solution)/shard_map/dot_general | solution.py:254
  15.1 0.0 copy-start.11
  15.2 1.3 pad_maximum_fusion.2
  16.5 11.6 %all-to-all-start = ((bf16[128,17,256]{2,1,0:T(8,128)(2,1)}), bf16[128,17,256]{2,1,0:T(8,128)(2,1)}, u32[]{:S(2)}, u32[]{:S(2)}) async-start(bf16[128,17,256]{2,1,0:T(8,128)(2,1)} %pad_maximum_fusion.2), calls=%async_computation | async-start | bytes 3145728 | tf_op jit(solution)/shard_map/all_to_all | solution.py:266
  28.2 0.1 constant_dynamic-slice_fusion.8
  28.3 0.1 copy.114
  28.4 0.7 fusion.153
  29.1 1.5 %pad_maximum_fusion.1.src_ref = bf16[2,4,512,256]{3,2,1,0:T(8,128)(2,1)} fusion(bf16[2,4,512,128]{3,2,1,0:T(8,128)(2,1)S(1)} %bitcast.239, bf16[2,4,512,128]{3,2,1,0:T(8,128)(2,1)S(1)} %bitcast.236), kind=kLoop, calls=%fused_computation.31 | loop fusion | flops 4194304 | bytes 4194304 | tf_op jit(solution)/shard_map/concatenate | solution.py:309
  36.8 1.3 reverse_select_fusion.1.after_ref
  38.2 0.7 broadcast_in_dim.130.side_ref
  38.9 0.1 copy-done.6
  38.9 7.5 %shard_map.113 = (f32[2,4,512,256]{3,2,1,0:T(8,128)}, f32[2,2,4,256]{3,2,1,0:T(4,128)}) custom-call(bf16[2,4,512,256]{3,2,1,0:T(8,128)(2,1)} %pad_maximum_fusion.1.src_ref, bf16[2,1,512,256]{3,2,1,0:T(8,128)(2,1)} %collective-permute-done.before_ref, bf16[2,1,512,256]{3,2,1,0:T(8,128)(2,1)} %copy-done.6, bf16[2,2,6,128]{3,2,1,0:T(8,128)(2,1)} %broadcast_in_dim.130.side_ref, ...), custom_call_target="tpu_custom_call" | custom-call | tf_op jit(solution)/shard_map/pallas_call | solution.py:82
  46.4 0.7 copy.113
  47.1 1.0 slice.384
  48.1 0.6 maximum_bitcast_fusion.2.block_ref
  48.7 12.9 %shard_map.114 = (f32[2,4,512,256]{3,2,1,0:T(8,128)}, f32[8,56,128]{2,1,0:T(8,128)}) custom-call(f32[56,128]{1,0:T(8,128)} %maximum_bitcast_fusion.2.block_ref, bf16[2,4,512,256]{3,2,1,0:T(8,128)(2,1)} %pad_maximum_fusion.1.src_ref, bf16[2,1,512,256]{3,2,1,0:T(8,128)(2,1)} %collective-permute-done.before_ref, bf16[2,1,512,256]{3,2,1,0:T(8,128)(2,1)} %copy-done.6, ...), custom_call_target="tpu_custom_call" | custom-call | tf_op jit(solution)/shard_map/pallas_call | solution.py:132
  61.7 1.0 copy.189
  62.7 0.6 gather_fusion
  63.3 0.1 broadcast_select_fusion.1
  63.8 0.1 convolution_bitcast_fusion.1
  64.0 0.1 convolution_bitcast_fusion
  64.1 0.2 convolution_bitcast_fusion.3
  64.3 0.1 convolution_bitcast_fusion.2
  64.5 1.4 fusion.55
  65.9 0.1 add.158
  66.0 1.3 slice.409
  67.4 5.3 %fusion = f32[2,4,512,256]{3,2,1,0:T(8,128)S(1)} fusion(bf16[2048,256,1,1]{1,0,3,2:T(8,128)(2,1)S(1)} %bitcast.240, s32[2048]{0:T(1024)S(1)} %add.158, s32[2,4,512]{2,1,0:T(4,128)S(1)} %multiply_add_fusion), kind=kOutput, calls=%fused_computation.2 | convolution fusion | flops 4303355904 | bytes 5267456 | tf_op jit(solution)/shard_map/dot_general | solution.py:302
  72.7 5.0 %multiply_convert_fusion = (bf16[2,4,512,256]{3,2,1,0:T(8,128)(2,1)S(1)}, bf16[2,4,512,256]{3,2,1,0:T(8,128)(2,1)S(1)}) fusion(f32[2,4,512,256]{3,2,1,0:T(8,128)S(1)} %fusion, f32[256]{0:T(256)S(1)} %copy-done.12, f32[2,4,256]{2,1,0:T(4,128)S(1)} %get-tuple-element.47, pred[512]{0:T(512)(128)(4,1)S(1)} %get-tuple-element.86, ...), kind=kLoop, calls=%fused_computation.23 | loop fusion | flops 33554432 | bytes 16812032 | tf_op jit(solution)/shard_map/convert_element_type | solution.py:317
  77.8 0.2 fusion.17
  78.0 3.5 %collective-permute-start.3 = (bf16[2,1,512,512]{3,2,1,0:T(8,128)(2,1)S(1)}, bf16[2,1,512,512]{3,2,1,0:T(8,128)(2,1)S(1)}, u32[]{:S(2)}, u32[]{:S(2)}) collective-permute-start(bf16[2,1,512,512]{3,2,1,0:T(8,128)(2,1)S(1)} %get-tuple-element.20), channel_id=1, source_target_pairs={{1,0},{2,1},{3,2},{4,3},{5,4},{6,5},{7,6},{8,7},{9,8},{10,9},{11,1... | collective-permute-start | bytes 3145736 | tf_op jit(solution)/shard_map/ppermute | solution.py:181
  81.5 2.1 %collective-permute-start.2 = (bf16[2,1,512,512]{3,2,1,0:T(8,128)(2,1)S(1)}, bf16[2,1,512,512]{3,2,1,0:T(8,128)(2,1)S(1)}, u32[]{:S(2)}, u32[]{:S(2)}) collective-permute-start(bf16[2,1,512,512]{3,2,1,0:T(8,128)(2,1)S(1)} %get-tuple-element.21), channel_id=1, source_target_pairs={{0,1},{1,2},{2,3},{3,4},{4,5},{5,6},{6,7},{7,8},{8,9},{9,10},{10,1... | collective-permute-start | bytes 3145736 | tf_op jit(solution)/shard_map/ppermute | solution.py:180
  83.7 2.3 %pad_maximum_fusion.src_ref = bf16[2,4,512,512]{3,2,1,0:T(8,128)(2,1)} fusion(bf16[2,4,512,256]{3,2,1,0:T(8,128)(2,1)S(1)} %get-tuple-element.19, bf16[2,4,512,256]{3,2,1,0:T(8,128)(2,1)S(1)} %get-tuple-element.18), kind=kLoop, calls=%fused_computation.13 | loop fusion | flops 8388608 | bytes 8388608 | tf_op jit(solution)/shard_map/concatenate | solution.py:321
  86.0 16.5 %collective-permute-done.3 = bf16[2,1,512,512]{3,2,1,0:T(8,128)(2,1)S(1)} collective-permute-done((bf16[2,1,512,512]{3,2,1,0:T(8,128)(2,1)S(1)}, bf16[2,1,512,512]{3,2,1,0:T(8,128)(2,1)S(1)}, u32[]{:S(2)}, u32[]{:S(2)}) %collective-permute-start.3) | collective-permute-done | bytes 1048608 | tf_op jit(solution)/shard_map/ppermute | solution.py:181
  102.5 0.3 reverse_select_fusion.after_ref
  102.9 4.0 %collective-permute-done.2.before_ref = bf16[2,1,512,512]{3,2,1,0:T(8,128)(2,1)S(1)} collective-permute-done((bf16[2,1,512,512]{3,2,1,0:T(8,128)(2,1)S(1)}, bf16[2,1,512,512]{3,2,1,0:T(8,128)(2,1)S(1)}, u32[]{:S(2)}, u32[]{:S(2)}) %collective-permute-start.2) | collective-permute-done | bytes 1048608 | tf_op jit(solution)/shard_map/ppermute | solution.py:180
  106.9 0.9 copy-done.5
  107.8 0.6 broadcast_in_dim.144.side_ref
  108.4 9.3 %shard_map.115 = (f32[2,4,512,128]{3,2,1,0:T(8,128)}, f32[2,2,4,128]{3,2,1,0:T(4,128)}) custom-call(bf16[2,4,512,512]{3,2,1,0:T(8,128)(2,1)} %pad_maximum_fusion.src_ref, bf16[2,1,512,512]{3,2,1,0:T(8,128)(2,1)} %copy-done.5, bf16[2,1,512,512]{3,2,1,0:T(8,128)(2,1)} %copy-done.2, bf16[2,2,6,256]{3,2,1,0:T(8,128)(2,1)} %broadcast_in_dim.144.side_ref, ...), custom_call_target="tpu_custom_call" | custom-call | tf_op jit(solution)/shard_map/pallas_call | solution.py:82
  117.8 0.7 copy.120
  118.5 0.6 maximum_bitcast_fusion.1.block_ref
  119.1 12.3 %shard_map.116 = (f32[2,4,512,128]{3,2,1,0:T(8,128)}, f32[8,64,128]{2,1,0:T(8,128)}) custom-call(f32[64,128]{1,0:T(8,128)} %maximum_bitcast_fusion.1.block_ref, bf16[2,4,512,512]{3,2,1,0:T(8,128)(2,1)} %pad_maximum_fusion.src_ref, bf16[2,1,512,512]{3,2,1,0:T(8,128)(2,1)} %copy-done.5, bf16[2,1,512,512]{3,2,1,0:T(8,128)(2,1)} %copy-done.2, ...), custom_call_target="tpu_custom_call" | custom-call | tf_op jit(solution)/shard_map/pallas_call | solution.py:132
  131.4 1.2 copy.188
  132.6 0.6 gather_fusion.1
  133.3 0.1 broadcast_select_fusion
  133.4 0.1 constant_dynamic-slice_fusion.3
  133.5 0.1 rev.36
  133.7 0.1 rev.37
  134.1 0.1 convolution_bitcast_fusion.5
  134.3 0.2 convolution_bitcast_fusion.4
  134.4 0.2 convolution_bitcast_fusion.7
  134.6 0.2 convolution_bitcast_fusion.6
  134.8 5.2 %add_bitcast_fusion = (f32[1,1,2,4,512,128]{5,4,3,2,1,0:T(8,128)}, bf16[1,1,2,4,512,128]{5,4,3,2,1,0:T(8,128)(2,1)}) fusion(f32[2,4,512,128]{3,2,1,0:T(8,128)} %get-tuple-element.17, f32[2,4,128]{2,1,0:T(4,128)S(1)} %reverse_select_fusion.4, f32[2,4,128]{2,1,0:T(4,128)S(1)} %reverse_select_fusion.5, pred[512]{0:T(512)(128)(4,1)S(1)} %get-tuple-element.86, ...), kind=kLoop, calls=%fused_computation.35 | loop fusion | flops 7340032 | bytes 9455104 | tf_op jit(solution)/shard_map/broadcast_in_dim | solution.py:331
  (106 shorter events, 0.9 us)
Async XLA Ops:
  0.6 12.9 %copy-start = (bf16[1024,256]{1,0:T(8,128)(2,1)S(1)}, bf16[1024,256]{1,0:T(8,128)(2,1)}, u32[]{:S(2)}) copy-start(bf16[1024,256]{1,0:T(8,128)(2,1)} %param.11) | copy-start | bytes 1572868
  3.0 33.8 %collective-permute-start.1 = (bf16[2,1,512,256]{3,2,1,0:T(8,128)(2,1)}, bf16[2,1,512,256]{3,2,1,0:T(8,128)(2,1)}, u32[]{:S(2)}, u32[]{:S(2)}) collective-permute-start(bf16[2,1,512,256]{3,2,1,0:T(8,128)(2,1)} %get-tuple-element.22), channel_id=1, source_target_pairs={{1,0},{2,1},{3,2},{4,3},{5,4},{6,5},{7,6},{8,7},{9,8},{10,9},{11,1... | collective-permute-start | bytes 1572872 | tf_op jit(solution)/shard_map/ppermute | solution.py:181
  7.5 30.6 %collective-permute-start = (bf16[2,1,512,256]{3,2,1,0:T(8,128)(2,1)}, bf16[2,1,512,256]{3,2,1,0:T(8,128)(2,1)}, u32[]{:S(2)}, u32[]{:S(2)}) collective-permute-start(bf16[2,1,512,256]{3,2,1,0:T(8,128)(2,1)} %get-tuple-element.23), channel_id=1, source_target_pairs={{0,1},{1,2},{2,3},{3,4},{4,5},{5,6},{6,7},{7,8},{8,9},{9,10},{10,1... | collective-permute-start | bytes 1572872 | tf_op jit(solution)/shard_map/ppermute | solution.py:180
  15.1 13.1 %copy-start.11 = (s32[8,2,3]{0,1,2:T(2,128)S(1)}, s32[8,2,3]{0,1,2:T(2,128)}, u32[]{:S(2)}) copy-start(s32[8,2,3]{0,1,2:T(2,128)} %param.14) | copy-start | bytes 580
  15.1 13.9 %copy-start.1 = (bf16[1,1,2,4,512,128]{5,4,3,2,1,0:T(8,128)(2,1)S(1)}, bf16[1,1,2,4,512,128]{5,4,3,2,1,0:T(8,128)(2,1)}, u32[]{:S(2)}) copy-start(bf16[1,1,2,4,512,128]{5,4,3,2,1,0:T(8,128)(2,1)} %param.10) | copy-start | bytes 3145732
  15.2 13.9 %copy-start.3 = (bf16[1,1,2,4,512,128]{5,4,3,2,1,0:T(8,128)(2,1)S(1)}, bf16[1,1,2,4,512,128]{5,4,3,2,1,0:T(8,128)(2,1)}, u32[]{:S(2)}) copy-start(bf16[1,1,2,4,512,128]{5,4,3,2,1,0:T(8,128)(2,1)} %param.19) | copy-start | bytes 3145732
  16.5 20.2 %copy-start.10 = (bf16[9,128,256]{2,1,0:T(8,128)(2,1)S(1)}, bf16[9,128,256]{2,1,0:T(8,128)(2,1)}, u32[]{:S(2)}) copy-start(bf16[9,128,256]{2,1,0:T(8,128)(2,1)} %k_ref.6) | copy-start | bytes 1769476
  16.5 48.0 %all-to-all-start = ((bf16[128,17,256]{2,1,0:T(8,128)(2,1)}), bf16[128,17,256]{2,1,0:T(8,128)(2,1)}, u32[]{:S(2)}, u32[]{:S(2)}) async-start(bf16[128,17,256]{2,1,0:T(8,128)(2,1)} %pad_maximum_fusion.2), calls=%async_computation | async-start | bytes 3145728 | tf_op jit(solution)/shard_map/all_to_all | solution.py:266
  38.1 0.8 copy-start.6
  67.3 5.4 %copy-start.7 = (f32[2,4,512,256]{3,2,1,0:T(8,128)S(1)}, f32[2,4,512,256]{3,2,1,0:T(8,128)}, u32[]{:S(2)}) copy-start(f32[2,4,512,256]{3,2,1,0:T(8,128)} %get-tuple-element.13) | copy-start | bytes 12582916
  67.3 5.4 %copy-start.8 = (f32[2,4,512,256]{3,2,1,0:T(8,128)S(1)}, f32[2,4,512,256]{3,2,1,0:T(8,128)}, u32[]{:S(2)}) copy-start(f32[2,4,512,256]{3,2,1,0:T(8,128)} %get-tuple-element.11) | copy-start | bytes 12582916
  67.3 5.4 %copy-start.12 = (f32[256]{0:T(256)S(1)}, f32[256]{0:T(256)}, u32[]{:S(2)}) copy-start(f32[256]{0:T(256)} %param.16) | copy-start | bytes 3076
  77.8 5.8 %copy-start.9 = (bf16[9,256,128]{2,1,0:T(8,128)(2,1)S(1)}, bf16[9,256,128]{2,1,0:T(8,128)(2,1)}, u32[]{:S(2)}) copy-start(bf16[9,256,128]{2,1,0:T(8,128)(2,1)} %k_ref.7) | copy-start | bytes 1769476
  78.0 24.5 %collective-permute-start.3 = (bf16[2,1,512,512]{3,2,1,0:T(8,128)(2,1)S(1)}, bf16[2,1,512,512]{3,2,1,0:T(8,128)(2,1)S(1)}, u32[]{:S(2)}, u32[]{:S(2)}) collective-permute-start(bf16[2,1,512,512]{3,2,1,0:T(8,128)(2,1)S(1)} %get-tuple-element.20), channel_id=1, source_target_pairs={{1,0},{2,1},{3,2},{4,3},{5,4},{6,5},{7,6},{8,7},{9,8},{10,9},{11,1... | collective-permute-start | bytes 3145736 | tf_op jit(solution)/shard_map/ppermute | solution.py:181
  81.5 25.4 %collective-permute-start.2 = (bf16[2,1,512,512]{3,2,1,0:T(8,128)(2,1)S(1)}, bf16[2,1,512,512]{3,2,1,0:T(8,128)(2,1)S(1)}, u32[]{:S(2)}, u32[]{:S(2)}) collective-permute-start(bf16[2,1,512,512]{3,2,1,0:T(8,128)(2,1)S(1)} %get-tuple-element.21), channel_id=1, source_target_pairs={{0,1},{1,2},{2,3},{3,4},{4,5},{5,6},{6,7},{7,8},{8,9},{9,10},{10,1... | collective-permute-start | bytes 3145736 | tf_op jit(solution)/shard_map/ppermute | solution.py:180
  102.8 5.6 %copy-start.2 = (bf16[2,1,512,512]{3,2,1,0:T(8,128)(2,1)}, bf16[2,1,512,512]{3,2,1,0:T(8,128)(2,1)S(1)}, u32[]{:S(2)}) copy-start(bf16[2,1,512,512]{3,2,1,0:T(8,128)(2,1)S(1)} %reverse_select_fusion.after_ref) | copy-start | bytes 3145732
  106.8 1.0 copy-start.5
  131.4 3.3 %copy-start.4 = (bf16[1,1,2,4,512,128]{5,4,3,2,1,0:T(8,128)(2,1)S(1)}, bf16[1,1,2,4,512,128]{5,4,3,2,1,0:T(8,128)(2,1)}, u32[]{:S(2)}) copy-start(bf16[1,1,2,4,512,128]{5,4,3,2,1,0:T(8,128)(2,1)} %param.19) | copy-start | bytes 3145732

commit v2 on v1

--- a/solution.py
+++ b/solution.py
@@ -306,10 +306,12 @@
     matching_row = lax.dynamic_index_in_dim(matching, face_at, 0, keepdims=False)
 
     lifted = kernel_one.shape[2]
-    both = extend_rows(jnp.concatenate([base_field, cot_field], axis=3), last_tile)
-    cot_back, cot_margins = conv_pallas(both, channels, channels, None, kernel_two, True)
-    parts = [edge_cols(both, 0, channels), jnp.swapaxes(cot_margins, 1, 2)]
-    first_out, landed = conv_gather(both, 0, channels, pack_parts(parts), kernel_one, 0)
+    cot_rows = extend_rows(cot_field, last_tile)
+    base_src = lax.optimization_barrier((base_field, cot_rows[1], cot_rows[2]))[0]
+    base_rows = extend_rows(base_src, last_tile)
+    cot_back, cot_margins = conv_pallas(cot_rows, 0, channels, None, kernel_two, True)
+    parts = [edge_cols(base_rows, 0, channels), jnp.swapaxes(cot_margins, 1, 2)]
+    first_out, landed = conv_gather(base_rows, 0, channels, pack_parts(parts), kernel_one, 0)
     base_edges, cot_gathered = unpack_parts(landed, parts)
     first_sides = side_terms(side_columns(base_edges, matching_row), kernel_one)
 
@@ -318,10 +320,12 @@
     grad_inner = return_sides(cot_back, cot_gathered, matching_row)
     grad_pre = jax.vjp(activation, pre_act)[1](grad_inner)[0].astype(jnp.bfloat16)
 
-    pair = extend_rows(jnp.concatenate([inner, grad_pre], axis=3), last_tile)
-    pre_back, pre_margins = conv_pallas(pair, lifted, lifted, None, kernel_one, True)
-    parts = [edge_cols(pair, 0, lifted), jnp.swapaxes(pre_margins, 1, 2)]
-    second_out, landed = conv_gather(pair, 0, lifted, pack_parts(parts), kernel_two, 1)
+    grad_pre_rows = extend_rows(grad_pre, last_tile)
+    inner_src = lax.optimization_barrier((inner, grad_pre_rows[1], grad_pre_rows[2]))[0]
+    inner_rows = extend_rows(inner_src, last_tile)
+    pre_back, pre_margins = conv_pallas(grad_pre_rows, 0, lifted, None, kernel_one, True)
+    parts = [edge_cols(inner_rows, 0, lifted), jnp.swapaxes(pre_margins, 1, 2)]
+    second_out, landed = conv_gather(inner_rows, 0, lifted, pack_parts(parts), kernel_two, 1)
     inner_edges, pre_gathered = unpack_parts(landed, parts)
     second_sides = side_terms(side_columns(inner_edges, matching_row), kernel_two)
 

time: 141 us -> 151 us (1.071); the launches traced: 140 us -> 148 us
  starting transfers between devices: 23.7 us -> 39.1 us
  waiting for transfers between devices: 20.5 us -> 10.1 us
  local copies, waits for them, and re-layouts: 11.5 us -> 16.1 us
  Pallas kernels: 42.1 us -> 38.5 us
  matrix products: 8.13 us -> 11.6 us
  other arithmetic: 26.4 us -> 24.8 us
    ppermute x2 -> x4, starting transfers between devices: 8.01 us -> 19.8 us  [extend_rows(): after = lax.ppermute(head, 'tile', [(i + 1, i) for i in range(count - 1)])]
    ppermute x2 -> x4, waiting for transfers between devices: 16.5 us -> 9.01 us  [extend_rows(): after = lax.ppermute(head, 'tile', [(i + 1, i) for i in range(count - 1)])]
    concatenate x4 -> x0, other arithmetic: 6.38 us -> none  [the longest x2 3.87 us: per_device(): jnp.concatenate([base_field, cot_field], axis=3)]
    ppermute x2 -> x4, starting transfers between devices: 4.06 us -> 8.07 us  [extend_rows(): before = lax.ppermute(tail, 'tile', [(i, i + 1) for i in range(count - 1)])]
    dot_general x8, matrix products: 1.17 us -> 4.65 us  [side_terms(): jnp.dot(stacked, weights, preferred_element_type=jnp.float32)]
    select_n x2 -> x4, other arithmetic: 1.62 us -> 5.08 us  [extend_rows(): after = jnp.where(last_tile, tail[::-1], after)]
    ppermute x2 -> x4, waiting for transfers between devices: 3.97 us -> 1.09 us  [extend_rows(): before = lax.ppermute(tail, 'tile', [(i, i + 1) for i in range(count - 1)])]
    slice x4, local copies, waits for them, and re-layouts: 1.06 us -> 3.92 us  [the longest x2 2.03 us: extend_rows(): tail = source[:, band_rows - 1:band_rows]]
  transfers between devices with their start and end apart: 5 -> 9, of which waited for: 2 -> 2; matrix products, arithmetic and copies ran while one was open for 14% -> 19% of each run, Pallas kernels for 15% -> 18%
where the time goes in v2:
time: 151 us; the launch traced here: 148 us
  starting transfers between devices  39.1 us (26%)
  Pallas kernels  38.5 us (25%)
  other arithmetic  24.8 us (16%)
  local copies, waits for them, and re-layouts  16.1 us (11%)
  matrix products  11.6 us (8%)
  waiting for transfers between devices  10.1 us (7%)
  between operations  8.02 us (5%)
    pallas_call x2, Pallas kernels, conv_gather(): pl.pallas_call(functools.partial(conv_gather_kernel, count, first, width)...  23 us
    ppermute x4, starting transfers between devices, extend_rows(): after = lax.ppermute(head, 'tile', [(i + 1, i) for i in range(count - 1)])  19.8 us
    pallas_call x2, Pallas kernels, conv_pallas(): pl.pallas_call(functools.partial(conv_kernel, backward, first, width), in...  15.4 us
    all_to_all x1, starting transfers between devices, route_observations(): lax.all_to_all(payload, ('face', 'tile'), split_axis=0, concat_axis=0, ti...  11.2 us
    ppermute x4, waiting for transfers between devices, extend_rows(): after = lax.ppermute(head, 'tile', [(i + 1, i) for i in range(count - 1)])  9.01 us
    ppermute x4, starting transfers between devices, extend_rows(): before = lax.ppermute(tail, 'tile', [(i, i + 1) for i in range(count - 1)])  8.07 us
    dot_general x1, matrix products, per_device(): gridded = jnp.dot(onehot, got_values, preferred_element_type=jnp.float32)  5.35 us
    broadcast_in_dim x1, other arithmetic, per_device(): return (analysis[None, None], grad_base[None, None])  5.14 us
  transfers between devices with their start and end apart: 9, of which 2 were waited for; matrix products, arithmetic and copies ran while one was open for 19% of the time, Pallas kernels for 18%

profile of v2, /device:TPU:24, one launch (start us, length us, event | category | flops | bytes accessed | tf_op | source)
XLA Modules:
  0.0 148.2 jit_solution(6151591190263273899)
XLA Ops:
  0.6 1.8 %fusion.148 = (bf16[2,1,512,128]{3,2,1,0:T(8,128)(2,1)}, bf16[2,1,512,128]{3,2,1,0:T(8,128)(2,1)S(1)}) fusion(bf16[2,4,512,128]{3,2,1,0:T(8,128)(2,1)} %bitcast.238), kind=kLoop, calls=%fused_computation.284 | loop fusion | bytes 1048576 | tf_op jit(solution)/shard_map/slice | solution.py:178
  2.5 4.5 %collective-permute-start.1 = (bf16[2,1,512,128]{3,2,1,0:T(8,128)(2,1)}, bf16[2,1,512,128]{3,2,1,0:T(8,128)(2,1)}, u32[]{:S(2)}, u32[]{:S(2)}) collective-permute-start(bf16[2,1,512,128]{3,2,1,0:T(8,128)(2,1)} %get-tuple-element.30), channel_id=1, source_target_pairs={{1,0},{2,1},{3,2},{4,3},{5,4},{6,5},{7,6},{8,7},{9,8},{10,9},{11,1... | collective-permute-start | bytes 786440 | tf_op jit(solution)/shard_map/ppermute | solution.py:181
  7.0 1.9 %collective-permute-start = (bf16[2,1,512,128]{3,2,1,0:T(8,128)(2,1)S(1)}, bf16[2,1,512,128]{3,2,1,0:T(8,128)(2,1)}, u32[]{:S(2)}, u32[]{:S(2)}) collective-permute-start(bf16[2,1,512,128]{3,2,1,0:T(8,128)(2,1)S(1)} %get-tuple-element.31), channel_id=1, source_target_pairs={{0,1},{1,2},{2,3},{3,4},{4,5},{5,6},{6,7},{7,8},{8,9},{9,10},{10,1... | collective-permute-start | bytes 786440 | tf_op jit(solution)/shard_map/ppermute | solution.py:180
  9.0 1.3 convert_reduce_fusion
  10.2 0.7 multiply_add_fusion.1
  10.9 1.6 %select_reduce_fusion = s32[2048]{0:T(1024)S(1)} fusion(s32[1024]{0:T(1024)} %param.13, s32[1024]{0:T(1024)S(1)} %multiply_add_fusion.1), kind=kLoop, calls=%fused_computation.6 | loop fusion | flops 6289408 | bytes 16384 | tf_op jit(solution)/shard_map/reduce_sum | solution.py:257
  12.8 0.1 maximum_bitcast_fusion
  12.9 0.1 copy.117
  13.0 1.6 %fusion.14 = bf16[2048,256]{1,0:T(8,128)(2,1)S(1)} fusion(bf16[1024,256]{1,0:T(8,128)(2,1)S(1)} %copy-done, s32[1024]{0:T(1024)S(1)} %multiply_add_fusion.1), kind=kOutput, calls=%fused_computation.24 | convolution fusion | flops 1076363264 | bytes 1576960 | tf_op jit(solution)/shard_map/dot_general | solution.py:254
  14.7 1.3 pad_maximum_fusion
  16.0 11.2 %all-to-all-start = ((bf16[128,17,256]{2,1,0:T(8,128)(2,1)}), bf16[128,17,256]{2,1,0:T(8,128)(2,1)S(1)}, u32[]{:S(2)}, u32[]{:S(2)}) async-start(bf16[128,17,256]{2,1,0:T(8,128)(2,1)} %pad_maximum_fusion), calls=%async_computation | async-start | bytes 3145728 | tf_op jit(solution)/shard_map/all_to_all | solution.py:266
  27.2 1.7 %slice_bitcast_fusion.9 = (bf16[128,256]{1,0:T(8,128)(2,1)}, bf16[128,256]{1,0:T(8,128)(2,1)S(1)}, bf16[128,256]{1,0:T(8,128)(2,1)S(1)}, bf16[128,256]{1,0:T(8,1...) fusion(bf16[9,128,256]{2,1,0:T(8,128)(2,1)} %k_ref.6), kind=kLoop, calls=%fused_computation.100 | loop fusion | bytes 786432 | tf_op jit(solution)/shard_map/squeeze | solution.py:160
  29.0 0.1 copy.114
  29.1 0.7 fusion.153
  29.8 0.6 pad_clamp_fusion
  30.4 1.7 %reverse_select_fusion.3.after_ref = bf16[2,1,512,128]{3,2,1,0:T(8,128)(2,1)} fusion(bf16[2,1,512,128]{3,2,1,0:T(8,128)(2,1)} %collective-permute-done.1, bf16[2,1,512,128]{3,2,1,0:T(8,128)(2,1)S(1)} %get-tuple-element.31, pred[]{:T(512)S(6)} %eq.125), kind=kLoop, calls=%fused_computation.41 | loop fusion | flops 131072 | bytes 786433 | tf_op jit(solution)/shard_map/jit(_where)/select_n | solution.py:182
  32.1 0.9 fusion.147
  33.0 4.9 %collective-permute-start.3 = (bf16[2,1,512,128]{3,2,1,0:T(8,128)(2,1)}, bf16[2,1,512,128]{3,2,1,0:T(8,128)(2,1)}, u32[]{:S(2)}, u32[]{:S(2)}) collective-permute-start(bf16[2,1,512,128]{3,2,1,0:T(8,128)(2,1)} %get-tuple-element.29), channel_id=1, source_target_pairs={{1,0},{2,1},{3,2},{4,3},{5,4},{6,5},{7,6},{8,7},{9,8},{10,9},{11,1... | collective-permute-start | bytes 786440 | tf_op jit(solution)/shard_map/ppermute | solution.py:181
  37.9 0.6 iota_compare_fusion.9
  38.5 2.1 %collective-permute-start.2 = (bf16[2,1,512,128]{3,2,1,0:T(8,128)(2,1)}, bf16[2,1,512,128]{3,2,1,0:T(8,128)(2,1)S(1)}, u32[]{:S(2)}, u32[]{:S(2)}) collective-permute-start(bf16[2,1,512,128]{3,2,1,0:T(8,128)(2,1)} %get-tuple-element.28), channel_id=1, source_target_pairs={{0,1},{1,2},{2,3},{3,4},{4,5},{5,6},{6,7},{7,8},{8,9},{9,10},{10,1... | collective-permute-start | bytes 786440 | tf_op jit(solution)/shard_map/ppermute | solution.py:180
  40.6 0.5 compare_and_fusion
  47.5 0.6 broadcast_in_dim.130.side_ref
  48.1 7.0 %shard_map.113 = (f32[2,4,512,256]{3,2,1,0:T(8,128)}, f32[2,2,4,256]{3,2,1,0:T(4,128)}) custom-call(bf16[2,4,512,128]{3,2,1,0:T(8,128)(2,1)} %bitcast.239, bf16[2,1,512,128]{3,2,1,0:T(8,128)(2,1)} %collective-permute-done.before_ref, bf16[2,1,512,128]{3,2,1,0:T(8,128)(2,1)} %reverse_select_fusion.3.after_ref, ...), custom_call_target="tpu_custom_call" | custom-call | tf_op jit(solution)/shard_map/pallas_call | solution.py:82
  55.0 0.7 copy.113
  55.8 1.1 reverse_select_fusion.2.after_ref
  57.0 0.7 maximum_bitcast_fusion.2.block_ref
  57.7 11.8 %shard_map.114 = (f32[2,4,512,256]{3,2,1,0:T(8,128)}, f32[8,56,128]{2,1,0:T(8,128)}) custom-call(f32[56,128]{1,0:T(8,128)} %maximum_bitcast_fusion.2.block_ref, bf16[2,4,512,128]{3,2,1,0:T(8,128)(2,1)} %bitcast.235, bf16[2,1,512,128]{3,2,1,0:T(8,128)(2,1)} %copy-done.12, bf16[2,1,512,128]{3,2,1,0:T(8,128)(2,1)} %copy-done.10, bf16[9,128,256]{2,1,0:T(8,128)(2,1)} %k_ref.6), custom_call_target="tpu_custom_call" | custom-call | tf_op jit(solution)/shard_map/pallas_call | solution.py:132
  69.6 1.0 copy.189
  70.6 0.7 gather_fusion
  71.3 0.7 broadcast_select_fusion.1
  72.5 1.0 convolution_bitcast_fusion.1
  73.5 1.0 convolution_bitcast_fusion
  74.5 1.1 convolution_bitcast_fusion.3
  75.5 1.0 convolution_bitcast_fusion.2
  76.6 0.3 fusion.51
  77.0 0.1 add.158
  77.2 5.3 %fusion = f32[2,4,512,256]{3,2,1,0:T(8,128)S(1)} fusion(bf16[2048,256,1,1]{1,0,3,2:T(8,128)(2,1)S(1)} %bitcast.240, s32[2048]{0:T(1024)S(1)} %add.158, s32[2,4,512]{2,1,0:T(4,128)S(1)} %multiply_add_fusion), kind=kOutput, calls=%fused_computation.2 | convolution fusion | flops 4303355904 | bytes 5267456 | tf_op jit(solution)/shard_map/dot_general | solution.py:302
  82.6 5.1 %multiply_convert_fusion = (bf16[2,4,512,256]{3,2,1,0:T(8,128)(2,1)S(1)}, bf16[2,4,512,256]{3,2,1,0:T(8,128)(2,1)S(1)}) fusion(f32[2,4,512,256]{3,2,1,0:T(8,128)S(1)} %fusion, f32[256]{0:T(256)S(1)} %copy-done.20, f32[2,4,256]{2,1,0:T(4,128)S(1)} %get-tuple-element.55, pred[512]{0:T(512)(128)(4,1)S(1)} %copy-done.15, f32[2,4,512,256]{3,2,1,0:T(8,128)S(1)} %copy-done.8, ...), kind=kLoop, calls=%fused_computation.18 | loop fusion | flops 33554432 | bytes 16812032 | tf_op jit(solution)/shard_map/convert_element_type | solution.py:319
  87.7 1.3 copy-done.2
  89.1 5.3 %collective-permute-start.5 = (bf16[2,1,512,256]{3,2,1,0:T(8,128)(2,1)S(1)}, bf16[2,1,512,256]{3,2,1,0:T(8,128)(2,1)S(1)}, u32[]{:S(2)}, u32[]{:S(2)}) collective-permute-start(bf16[2,1,512,256]{3,2,1,0:T(8,128)(2,1)S(1)} %get-tuple-element.26), channel_id=1, source_target_pairs={{1,0},{2,1},{3,2},{4,3},{5,4},{6,5},{7,6},{8,7},{9,8},{10,9},{11,1... | collective-permute-start | bytes 1572872 | tf_op jit(solution)/shard_map/ppermute | solution.py:181
  94.4 1.9 %collective-permute-start.4 = (bf16[2,1,512,256]{3,2,1,0:T(8,128)(2,1)S(1)}, bf16[2,1,512,256]{3,2,1,0:T(8,128)(2,1)S(1)}, u32[]{:S(2)}, u32[]{:S(2)}) collective-permute-start(bf16[2,1,512,256]{3,2,1,0:T(8,128)(2,1)S(1)} %get-tuple-element.27), channel_id=1, source_target_pairs={{0,1},{1,2},{2,3},{3,4},{4,5},{5,6},{6,7},{7,8},{8,9},{9,10},{10,1... | collective-permute-start | bytes 1572872 | tf_op jit(solution)/shard_map/ppermute | solution.py:180
  96.3 9.0 %collective-permute-done.5 = bf16[2,1,512,256]{3,2,1,0:T(8,128)(2,1)S(1)} collective-permute-done((bf16[2,1,512,256]{3,2,1,0:T(8,128)(2,1)S(1)}, bf16[2,1,512,256]{3,2,1,0:T(8,128)(2,1)S(1)}, u32[]{:S(2)}, u32[]{:S(2)}) %collective-permute-start.5) | collective-permute-done | bytes 524320 | tf_op jit(solution)/shard_map/ppermute | solution.py:181
  105.3 0.9 reverse_select_fusion.1.after_ref
  106.2 1.1 collective-permute-done.4.before_ref
  107.3 1.2 fusion.145
  108.5 5.1 %collective-permute-start.7 = (bf16[2,1,512,256]{3,2,1,0:T(8,128)(2,1)}, bf16[2,1,512,256]{3,2,1,0:T(8,128)(2,1)}, u32[]{:S(2)}, u32[]{:S(2)}) collective-permute-start(bf16[2,1,512,256]{3,2,1,0:T(8,128)(2,1)} %get-tuple-element.25), channel_id=1, source_target_pairs={{1,0},{2,1},{3,2},{4,3},{5,4},{6,5},{7,6},{8,7},{9,8},{10,9},{11,1... | collective-permute-start | bytes 1572872 | tf_op jit(solution)/shard_map/ppermute | solution.py:181
  113.6 2.1 %collective-permute-start.6 = (bf16[2,1,512,256]{3,2,1,0:T(8,128)(2,1)}, bf16[2,1,512,256]{3,2,1,0:T(8,128)(2,1)S(1)}, u32[]{:S(2)}, u32[]{:S(2)}) collective-permute-start(bf16[2,1,512,256]{3,2,1,0:T(8,128)(2,1)} %get-tuple-element.24), channel_id=1, source_target_pairs={{0,1},{1,2},{2,3},{3,4},{4,5},{5,6},{6,7},{7,8},{8,9},{9,10},{10,1... | collective-permute-start | bytes 1572872 | tf_op jit(solution)/shard_map/ppermute | solution.py:180
  115.8 0.6 broadcast_in_dim.144.side_ref
  116.4 8.5 %shard_map.115 = (f32[2,4,512,128]{3,2,1,0:T(8,128)}, f32[2,2,4,128]{3,2,1,0:T(4,128)}) custom-call(bf16[2,4,512,256]{3,2,1,0:T(8,128)(2,1)} %copy-done.2, bf16[2,1,512,256]{3,2,1,0:T(8,128)(2,1)} %copy-done.13, bf16[2,1,512,256]{3,2,1,0:T(8,128)(2,1)} %reverse_select_fusion.1.after_ref, bf16[2,2,6,256]{3,2,1,0:T(8,128)(2,1)} %broadcast_in_dim.144.side_ref, ...), custom_call_target="tpu_custom_call" | custom-call | tf_op jit(solution)/shard_map/pallas_call | solution.py:82
  124.9 0.7 copy.120
  125.6 1.3 reverse_select_fusion.after_ref
  127.0 0.8 copy-done.11
  127.8 0.6 maximum_bitcast_fusion.1.block_ref
  128.5 11.2 %shard_map.116 = (f32[2,4,512,128]{3,2,1,0:T(8,128)}, f32[8,64,128]{2,1,0:T(8,128)}) custom-call(f32[64,128]{1,0:T(8,128)} %maximum_bitcast_fusion.1.block_ref, bf16[2,4,512,256]{3,2,1,0:T(8,128)(2,1)} %copy-done.1, bf16[2,1,512,256]{3,2,1,0:T(8,128)(2,1)} %copy-done.11, bf16[2,1,512,256]{3,2,1,0:T(8,128)(2,1)} %copy-done.6, bf16[9,256,128]{2,1,0:T(8,128)(2,1)} %k_ref.7), custom_call_target="tpu_custom_call" | custom-call | tf_op jit(solution)/shard_map/pallas_call | solution.py:132
  139.7 1.1 copy.188
  140.8 0.8 gather_fusion.1
  141.6 0.1 broadcast_select_fusion
  141.8 0.1 rev.44
  142.0 0.1 rev.45
  142.4 0.1 convolution_bitcast_fusion.5
  142.6 0.1 convolution_bitcast_fusion.4
  142.7 0.2 convolution_bitcast_fusion.7
  142.9 0.2 convolution_bitcast_fusion.6
  143.1 5.1 %add_bitcast_fusion = (f32[1,1,2,4,512,128]{5,4,3,2,1,0:T(8,128)}, bf16[1,1,2,4,512,128]{5,4,3,2,1,0:T(8,128)(2,1)}) fusion(f32[2,4,512,128]{3,2,1,0:T(8,128)} %get-tuple-element.21, f32[2,4,128]{2,1,0:T(4,128)S(1)} %reverse_select_fusion.6, f32[2,4,128]{2,1,0:T(4,128)S(1)} %reverse_select_fusion.7, pred[512]{0:T(512)(128)(4,1)S(1)} %copy-done.16, ...), kind=kLoop, calls=%fused_computation.25 | loop fusion | flops 7340032 | bytes 9455104 | tf_op jit(solution)/shard_map/broadcast_in_dim | solution.py:335
  (130 shorter events, 1.4 us)
Async XLA Ops:
  0.6 12.4 %copy-start = (bf16[1024,256]{1,0:T(8,128)(2,1)S(1)}, bf16[1024,256]{1,0:T(8,128)(2,1)}, u32[]{:S(2)}) copy-start(bf16[1024,256]{1,0:T(8,128)(2,1)} %param.11) | copy-start | bytes 1572868
  2.5 27.9 %collective-permute-start.1 = (bf16[2,1,512,128]{3,2,1,0:T(8,128)(2,1)}, bf16[2,1,512,128]{3,2,1,0:T(8,128)(2,1)}, u32[]{:S(2)}, u32[]{:S(2)}) collective-permute-start(bf16[2,1,512,128]{3,2,1,0:T(8,128)(2,1)} %get-tuple-element.30), channel_id=1, source_target_pairs={{1,0},{2,1},{3,2},{4,3},{5,4},{6,5},{7,6},{8,7},{9,8},{10,9},{11,1... | collective-permute-start | bytes 786440 | tf_op jit(solution)/shard_map/ppermute | solution.py:181
  7.0 25.1 %collective-permute-start = (bf16[2,1,512,128]{3,2,1,0:T(8,128)(2,1)S(1)}, bf16[2,1,512,128]{3,2,1,0:T(8,128)(2,1)}, u32[]{:S(2)}, u32[]{:S(2)}) collective-permute-start(bf16[2,1,512,128]{3,2,1,0:T(8,128)(2,1)S(1)} %get-tuple-element.31), channel_id=1, source_target_pairs={{0,1},{1,2},{2,3},{3,4},{4,5},{5,6},{6,7},{7,8},{8,9},{9,10},{10,1... | collective-permute-start | bytes 786440 | tf_op jit(solution)/shard_map/ppermute | solution.py:180
  14.6 14.3 %copy-start.14 = (s32[8,2,3]{0,1,2:T(2,128)S(1)}, s32[8,2,3]{0,1,2:T(2,128)}, u32[]{:S(2)}) copy-start(s32[8,2,3]{0,1,2:T(2,128)} %param.14) | copy-start | bytes 580
  14.6 17.5 %copy-start.3 = (bf16[1,1,2,4,512,128]{5,4,3,2,1,0:T(8,128)(2,1)S(1)}, bf16[1,1,2,4,512,128]{5,4,3,2,1,0:T(8,128)(2,1)}, u32[]{:S(2)}) copy-start(bf16[1,1,2,4,512,128]{5,4,3,2,1,0:T(8,128)(2,1)} %param.10) | copy-start | bytes 3145732
  16.0 60.6 %all-to-all-start = ((bf16[128,17,256]{2,1,0:T(8,128)(2,1)}), bf16[128,17,256]{2,1,0:T(8,128)(2,1)S(1)}, u32[]{:S(2)}, u32[]{:S(2)}) async-start(bf16[128,17,256]{2,1,0:T(8,128)(2,1)} %pad_maximum_fusion), calls=%async_computation | async-start | bytes 3145728 | tf_op jit(solution)/shard_map/all_to_all | solution.py:266
  33.0 22.8 %collective-permute-start.3 = (bf16[2,1,512,128]{3,2,1,0:T(8,128)(2,1)}, bf16[2,1,512,128]{3,2,1,0:T(8,128)(2,1)}, u32[]{:S(2)}, u32[]{:S(2)}) collective-permute-start(bf16[2,1,512,128]{3,2,1,0:T(8,128)(2,1)} %get-tuple-element.29), channel_id=1, source_target_pairs={{1,0},{2,1},{3,2},{4,3},{5,4},{6,5},{7,6},{8,7},{9,8},{10,9},{11,1... | collective-permute-start | bytes 786440 | tf_op jit(solution)/shard_map/ppermute | solution.py:181
  38.5 18.4 %collective-permute-start.2 = (bf16[2,1,512,128]{3,2,1,0:T(8,128)(2,1)}, bf16[2,1,512,128]{3,2,1,0:T(8,128)(2,1)S(1)}, u32[]{:S(2)}, u32[]{:S(2)}) collective-permute-start(bf16[2,1,512,128]{3,2,1,0:T(8,128)(2,1)} %get-tuple-element.28), channel_id=1, source_target_pairs={{0,1},{1,2},{2,3},{3,4},{4,5},{5,6},{6,7},{7,8},{8,9},{9,10},{10,1... | collective-permute-start | bytes 786440 | tf_op jit(solution)/shard_map/ppermute | solution.py:180
  56.9 0.8 copy-start.10
  56.9 0.8 copy-start.12
  77.2 5.4 %copy-start.7 = (f32[2,4,512,256]{3,2,1,0:T(8,128)S(1)}, f32[2,4,512,256]{3,2,1,0:T(8,128)}, u32[]{:S(2)}) copy-start(f32[2,4,512,256]{3,2,1,0:T(8,128)} %get-tuple-element.16) | copy-start | bytes 12582916
  77.2 5.4 %copy-start.8 = (f32[2,4,512,256]{3,2,1,0:T(8,128)S(1)}, f32[2,4,512,256]{3,2,1,0:T(8,128)}, u32[]{:S(2)}) copy-start(f32[2,4,512,256]{3,2,1,0:T(8,128)} %get-tuple-element.14) | copy-start | bytes 12582916
  77.2 5.4 %copy-start.15 = (pred[512]{0:T(512)(128)(4,1)S(1)}, pred[512]{0:T(512)(128)(4,1)}, u32[]{:S(2)}) copy-start(pred[512]{0:T(512)(128)(4,1)} %get-tuple-element.94) | copy-start | bytes 1540
  77.2 5.4 %copy-start.17 = (pred[512]{0:T(512)(128)(4,1)S(1)}, pred[512]{0:T(512)(128)(4,1)}, u32[]{:S(2)}) copy-start(pred[512]{0:T(512)(128)(4,1)} %get-tuple-element.95) | copy-start | bytes 1540
  77.2 5.4 %copy-start.20 = (f32[256]{0:T(256)S(1)}, f32[256]{0:T(256)}, u32[]{:S(2)}) copy-start(f32[256]{0:T(256)} %param.16) | copy-start | bytes 3076
  87.7 1.3 copy-start.2
  87.7 39.2 %copy-start.1 = (bf16[2,4,512,256]{3,2,1,0:T(8,128)(2,1)}, bf16[2,4,512,256]{3,2,1,0:T(8,128)(2,1)S(1)}, u32[]{:S(2)}) copy-start(bf16[2,4,512,256]{3,2,1,0:T(8,128)(2,1)S(1)} %get-tuple-element.17.src_ref) | copy-start | bytes 6291460
  87.7 28.1 %copy-start.9 = (bf16[9,256,128]{2,1,0:T(8,128)(2,1)S(1)}, bf16[9,256,128]{2,1,0:T(8,128)(2,1)}, u32[]{:S(2)}) copy-start(bf16[9,256,128]{2,1,0:T(8,128)(2,1)} %k_ref.7) | copy-start | bytes 1769476
  89.1 16.2 %collective-permute-start.5 = (bf16[2,1,512,256]{3,2,1,0:T(8,128)(2,1)S(1)}, bf16[2,1,512,256]{3,2,1,0:T(8,128)(2,1)S(1)}, u32[]{:S(2)}, u32[]{:S(2)}) collective-permute-start(bf16[2,1,512,256]{3,2,1,0:T(8,128)(2,1)S(1)} %get-tuple-element.26), channel_id=1, source_target_pairs={{1,0},{2,1},{3,2},{4,3},{5,4},{6,5},{7,6},{8,7},{9,8},{10,9},{11,1... | collective-permute-start | bytes 1572872 | tf_op jit(solution)/shard_map/ppermute | solution.py:181
  94.4 12.9 %collective-permute-start.4 = (bf16[2,1,512,256]{3,2,1,0:T(8,128)(2,1)S(1)}, bf16[2,1,512,256]{3,2,1,0:T(8,128)(2,1)S(1)}, u32[]{:S(2)}, u32[]{:S(2)}) collective-permute-start(bf16[2,1,512,256]{3,2,1,0:T(8,128)(2,1)S(1)} %get-tuple-element.27), channel_id=1, source_target_pairs={{0,1},{1,2},{2,3},{3,4},{4,5},{5,6},{6,7},{7,8},{8,9},{9,10},{10,1... | collective-permute-start | bytes 1572872 | tf_op jit(solution)/shard_map/ppermute | solution.py:180
  107.3 9.1 %copy-start.13 = (bf16[2,1,512,256]{3,2,1,0:T(8,128)(2,1)}, bf16[2,1,512,256]{3,2,1,0:T(8,128)(2,1)S(1)}, u32[]{:S(2)}) copy-start(bf16[2,1,512,256]{3,2,1,0:T(8,128)(2,1)S(1)} %collective-permute-done.4.before_ref) | copy-start | bytes 1572868
  108.5 17.1 %collective-permute-start.7 = (bf16[2,1,512,256]{3,2,1,0:T(8,128)(2,1)}, bf16[2,1,512,256]{3,2,1,0:T(8,128)(2,1)}, u32[]{:S(2)}, u32[]{:S(2)}) collective-permute-start(bf16[2,1,512,256]{3,2,1,0:T(8,128)(2,1)} %get-tuple-element.25), channel_id=1, source_target_pairs={{1,0},{2,1},{3,2},{4,3},{5,4},{6,5},{7,6},{8,7},{9,8},{10,9},{11,1... | collective-permute-start | bytes 1572872 | tf_op jit(solution)/shard_map/ppermute | solution.py:181
  113.6 13.3 %collective-permute-start.6 = (bf16[2,1,512,256]{3,2,1,0:T(8,128)(2,1)}, bf16[2,1,512,256]{3,2,1,0:T(8,128)(2,1)S(1)}, u32[]{:S(2)}, u32[]{:S(2)}) collective-permute-start(bf16[2,1,512,256]{3,2,1,0:T(8,128)(2,1)} %get-tuple-element.24), channel_id=1, source_target_pairs={{0,1},{1,2},{2,3},{3,4},{4,5},{5,6},{6,7},{7,8},{8,9},{9,10},{10,1... | collective-permute-start | bytes 1572872 | tf_op jit(solution)/shard_map/ppermute | solution.py:180
  126.9 1.5 %copy-start.6 = (bf16[2,1,512,256]{3,2,1,0:T(8,128)(2,1)}, bf16[2,1,512,256]{3,2,1,0:T(8,128)(2,1)S(1)}, u32[]{:S(2)}) copy-start(bf16[2,1,512,256]{3,2,1,0:T(8,128)(2,1)S(1)} %reverse_select_fusion.after_ref) | copy-start | bytes 1572868
  126.9 14.6 %copy-start.19 = (pred[8]{0:T(512)(128)(4,1)S(1)}, pred[8]{0:T(512)(128)(4,1)}, u32[]{:S(2)}) copy-start(pred[8]{0:T(512)(128)(4,1)} %compare_and_fusion) | copy-start | bytes 28
  127.0 0.9 copy-start.11
  128.4 14.6 %copy-start.4 = (bf16[1,1,2,4,512,128]{5,4,3,2,1,0:T(8,128)(2,1)S(1)}, bf16[1,1,2,4,512,128]{5,4,3,2,1,0:T(8,128)(2,1)}, u32[]{:S(2)}) copy-start(bf16[1,1,2,4,512,128]{5,4,3,2,1,0:T(8,128)(2,1)} %param.10) | copy-start | bytes 3145732
  128.4 14.6 %copy-start.5 = (bf16[1,1,2,4,512,128]{5,4,3,2,1,0:T(8,128)(2,1)S(1)}, bf16[1,1,2,4,512,128]{5,4,3,2,1,0:T(8,128)(2,1)}, u32[]{:S(2)}) copy-start(bf16[1,1,2,4,512,128]{5,4,3,2,1,0:T(8,128)(2,1)} %param.19) | copy-start | bytes 3145732
  128.4 14.6 %copy-start.16 = (pred[512]{0:T(512)(128)(4,1)S(1)}, pred[512]{0:T(512)(128)(4,1)}, u32[]{:S(2)}) copy-start(pred[512]{0:T(512)(128)(4,1)} %get-tuple-element.94) | copy-start | bytes 1540
  128.4 14.6 %copy-start.18 = (pred[512]{0:T(512)(128)(4,1)S(1)}, pred[512]{0:T(512)(128)(4,1)}, u32[]{:S(2)}) copy-start(pred[512]{0:T(512)(128)(4,1)} %get-tuple-element.95) | copy-start | bytes 1540
  128.5 14.6 %copy-start.21 = (f32[128]{0:T(128)S(1)}, f32[128]{0:T(128)}, u32[]{:S(2)}) copy-start(f32[128]{0:T(128)} %param.18) | copy-start | bytes 1540

commit v3 on v1

--- a/solution.py
+++ b/solution.py
@@ -173,10 +173,12 @@
 
 
 def extend_rows(source, last_tile):
+    band_rows = source.shape[1]
+    return exchange_rows(source, source[:, 0:1], source[:, band_rows - 1 : band_rows], last_tile)
+
+
+def exchange_rows(source, head, tail, last_tile):
     count = lax.axis_size("tile")
-    band_rows = source.shape[1]
-    head = source[:, 0:1]
-    tail = source[:, band_rows - 1 : band_rows]
     before = lax.ppermute(tail, "tile", [(i, i + 1) for i in range(count - 1)])
     after = lax.ppermute(head, "tile", [(i + 1, i) for i in range(count - 1)])
     after = jnp.where(last_tile, tail[::-1], after)
@@ -307,18 +309,27 @@
 
     lifted = kernel_one.shape[2]
     both = extend_rows(jnp.concatenate([base_field, cot_field], axis=3), last_tile)
+    gridded, cot_before = lax.optimization_barrier((gridded, both[1]))
+    both = (both[0], cot_before, both[2])
     cot_back, cot_margins = conv_pallas(both, channels, channels, None, kernel_two, True)
     parts = [edge_cols(both, 0, channels), jnp.swapaxes(cot_margins, 1, 2)]
     first_out, landed = conv_gather(both, 0, channels, pack_parts(parts), kernel_one, 0)
     base_edges, cot_gathered = unpack_parts(landed, parts)
     first_sides = side_terms(side_columns(base_edges, matching_row), kernel_one)
-
-    pre_act = at_edges(first_out, first_sides[:, 0], first_sides[:, 1]) + bias_one + gridded
-    inner = activation(pre_act).astype(jnp.bfloat16)
-    grad_inner = return_sides(cot_back, cot_gathered, matching_row)
-    grad_pre = jax.vjp(activation, pre_act)[1](grad_inner)[0].astype(jnp.bfloat16)
-
-    pair = extend_rows(jnp.concatenate([inner, grad_pre], axis=3), last_tile)
+    cot_left, cot_right = pick_partner(cot_gathered, matching_row)
+
+    def epilogue(rows):
+        pre_act = at_edges(first_out[:, rows], first_sides[:, 0, rows], first_sides[:, 1, rows])
+        pre_act = pre_act + bias_one + gridded[:, rows]
+        inner = activation(pre_act).astype(jnp.bfloat16)
+        grad_inner = at_edges(cot_back[:, rows], cot_left[:, rows], cot_right[:, rows])
+        grad_pre = jax.vjp(activation, pre_act)[1](grad_inner)[0].astype(jnp.bfloat16)
+        return jnp.concatenate([inner, grad_pre], axis=3)
+
+    edge_pair = epilogue(slice(0, band_rows, band_rows - 1))
+    middle_pair = epilogue(slice(1, band_rows - 1))
+    whole_pair = jnp.concatenate([edge_pair[:, 0:1], middle_pair, edge_pair[:, 1:2]], axis=1)
+    pair = exchange_rows(whole_pair, edge_pair[:, 0:1], edge_pair[:, 1:2], last_tile)
     pre_back, pre_margins = conv_pallas(pair, lifted, lifted, None, kernel_one, True)
     parts = [edge_cols(pair, 0, lifted), jnp.swapaxes(pre_margins, 1, 2)]
     second_out, landed = conv_gather(pair, 0, lifted, pack_parts(parts), kernel_two, 1)

time: 141 us -> 156 us (1.11)
  waiting for transfers between devices: 20.5 us -> 27.9 us
  starting transfers between devices: 23.7 us -> 27.3 us
  local copies, waits for them, and re-layouts: 11.5 us -> 13.5 us
    ppermute x4, waiting for transfers between devices: 20.5 us -> 27.9 us  [the longest x2 24.5 us: exchange_rows(): after = lax.ppermute(head, 'tile', [(i + 1, i) for i in range(count - 1)])]
    ppermute x4, starting transfers between devices: 12.1 us -> 16.6 us  [the longest x2 12.5 us: exchange_rows(): after = lax.ppermute(head, 'tile', [(i + 1, i) for i in range(count - 1)])]
    convert_element_type x1 -> x2, other arithmetic: 5.04 us -> 9.24 us  [the longest x1 7.76 us: epilogue(): jax.vjp(activation, pre_act)[1](grad_inner)[0].astype(jnp.bfloat16)]
    concatenate x2, other arithmetic: 2.5 us -> 0.56 us  [the longest x1 0.39 us: per_device(): jnp.concatenate([edge_pair[:, 0:1], middle_pair, edge_pair[:, 1:2]], axis=1)]
    unnamed x54 -> x60, local copies, waits for them, and re-layouts: 3.31 us -> 5.21 us
  transfers between devices with their start and end apart: 5 -> 5, of which waited for: 2 -> 3; matrix products, arithmetic and copies ran while one was open for 14% -> 10% of each run, Pallas kernels for 15% -> 0%
where the time goes in v3:
time: 156 us
  Pallas kernels  42.2 us (27%)
  waiting for transfers between devices  27.9 us (18%)
  other arithmetic  27.6 us (18%)
  starting transfers between devices  27.3 us (18%)
  local copies, waits for them, and re-layouts  13.5 us (9%)
  matrix products  9.13 us (6%)
  between operations  8.04 us (5%)
    pallas_call x2, Pallas kernels, conv_gather(): pl.pallas_call(functools.partial(conv_gather_kernel, count, first, width)...  25.2 us
    ppermute x2, waiting for transfers between devices, exchange_rows(): after = lax.ppermute(head, 'tile', [(i + 1, i) for i in range(count - 1)])  24.5 us
    pallas_call x2, Pallas kernels, conv_pallas(): pl.pallas_call(functools.partial(conv_kernel, backward, first, width), in...  17 us
    ppermute x2, starting transfers between devices, exchange_rows(): after = lax.ppermute(head, 'tile', [(i + 1, i) for i in range(count - 1)])  12.5 us
    all_to_all x1, starting transfers between devices, route_observations(): lax.all_to_all(payload, ('face', 'tile'), split_axis=0, concat_axis=0, ti...  10.7 us
    convert_element_type x1, other arithmetic, epilogue(): jax.vjp(activation, pre_act)[1](grad_inner)[0].astype(jnp.bfloat16)  7.76 us
    dot_general x1, matrix products, per_device(): gridded = jnp.dot(onehot, got_values, preferred_element_type=jnp.float32)  6.32 us
    unnamed x60, local copies, waits for them, and re-layouts  5.21 us
  transfers between devices with their start and end apart: 5, of which 3 were waited for; matrix products, arithmetic and copies ran while one was open for 10% of the time, Pallas kernels for 0%

profile of v3, /device:TPU:24, one launch (start us, length us, event | category | flops | bytes accessed | tf_op | source)
XLA Modules:
  0.0 155.7 jit_solution(12741218235021671937)
XLA Ops:
  0.6 1.3 convert_reduce_fusion
  1.9 0.7 multiply_add_fusion.1
  2.6 1.6 %select_reduce_fusion = s32[2048]{0:T(1024)S(1)} fusion(s32[1024]{0:T(1024)} %param.13, s32[1024]{0:T(1024)S(1)} %multiply_add_fusion.1), kind=kLoop, calls=%fused_computation.6 | loop fusion | flops 6289408 | bytes 16384 | tf_op jit(solution)/shard_map/reduce_sum | solution.py:259
  4.2 0.1 reduce_sum.22
  4.4 0.1 pad.86.clone
  4.5 0.1 maximum_bitcast_fusion
  4.6 0.1 copy.113
  4.7 1.6 %fusion.7 = bf16[2048,256]{1,0:T(8,128)(2,1)S(1)} fusion(bf16[1024,256]{1,0:T(8,128)(2,1)S(1)} %copy-done, s32[1024]{0:T(1024)S(1)} %multiply_add_fusion.1), kind=kOutput, calls=%fused_computation.23 | convolution fusion | flops 1076363264 | bytes 1576960 | tf_op jit(solution)/shard_map/dot_general | solution.py:256
  6.3 1.4 pad_maximum_fusion.2
  7.7 10.7 %all-to-all-start = ((bf16[128,17,256]{2,1,0:T(8,128)(2,1)}), bf16[128,17,256]{2,1,0:T(8,128)(2,1)}, u32[]{:S(2)}, u32[]{:S(2)}) async-start(bf16[128,17,256]{2,1,0:T(8,128)(2,1)} %pad_maximum_fusion.2), calls=%async_computation | async-start | bytes 3145728 | tf_op jit(solution)/shard_map/all_to_all | solution.py:268
  18.4 1.1 fusion.25
  19.5 2.0 %collective-permute-start = (bf16[2,1,512,256]{3,2,1,0:T(8,128)(2,1)}, bf16[2,1,512,256]{3,2,1,0:T(8,128)(2,1)}, u32[]{:S(2)}, u32[]{:S(2)}) collective-permute-start(bf16[2,1,512,256]{3,2,1,0:T(8,128)(2,1)} %get-tuple-element.28), channel_id=1, source_target_pairs={{0,1},{1,2},{2,3},{3,4},{4,5},{5,6},{6,7},{7,8},{8,9},{9,10},{10,1... | collective-permute-start | bytes 1572872 | tf_op jit(solution)/shard_map/ppermute | solution.py:182
  21.6 6.1 %collective-permute-start.1 = (bf16[2,1,512,256]{3,2,1,0:T(8,128)(2,1)}, bf16[2,1,512,256]{3,2,1,0:T(8,128)(2,1)}, u32[]{:S(2)}, u32[]{:S(2)}) collective-permute-start(bf16[2,1,512,256]{3,2,1,0:T(8,128)(2,1)} %get-tuple-element.27), channel_id=1, source_target_pairs={{1,0},{2,1},{3,2},{4,3},{5,4},{6,5},{7,6},{8,7},{9,8},{10,9},{11,1... | collective-permute-start | bytes 1572872 | tf_op jit(solution)/shard_map/ppermute | solution.py:183
  27.7 0.1 constant_dynamic-slice_fusion.8
  27.8 0.1 copy.115
  27.9 0.7 fusion.160
  35.0 1.6 pad_maximum_fusion.1.src_ref
  36.6 9.4 %collective-permute-done.1 = bf16[2,1,512,256]{3,2,1,0:T(8,128)(2,1)} collective-permute-done((bf16[2,1,512,256]{3,2,1,0:T(8,128)(2,1)}, bf16[2,1,512,256]{3,2,1,0:T(8,128)(2,1)}, u32[]{:S(2)}, u32[]{:S(2)}) %collective-permute-start.1) | collective-permute-done | bytes 524320 | tf_op jit(solution)/shard_map/ppermute | solution.py:183
  46.0 1.3 reverse_select_fusion.1.after_ref
  47.4 1.6 %fusion.61 = s32[128,16]{1,0:T(8,128)S(1)} fusion(bf16[128,17,256]{2,1,0:T(8,128)(2,1)} %all-to-all-done), kind=kLoop, calls=%fused_computation.107 | loop fusion | flops 8192 | bytes 16384 | tf_op jit(solution)/shard_map/add | solution.py:272
  49.0 0.1 add.177
  49.0 1.3 slice.438
  50.4 6.3 %fusion = f32[2,4,512,256]{3,2,1,0:T(8,128)} fusion(bf16[2048,256,1,1]{1,0,3,2:T(8,128)(2,1)S(1)} %bitcast.242, s32[2048]{0:T(1024)S(1)} %add.177, s32[2,4,512]{2,1,0:T(4,128)S(1)} %multiply_add_fusion), kind=kOutput, calls=%fused_computation.2 | convolution fusion | flops 4303355904 | bytes 5267456 | tf_op jit(solution)/shard_map/dot_general | solution.py:304
  56.7 1.0 slice.342
  57.7 0.6 broadcast_in_dim.165.side_ref
  58.3 7.5 %shard_map.113 = (f32[2,4,512,256]{3,2,1,0:T(8,128)}, f32[2,2,4,256]{3,2,1,0:T(4,128)}) custom-call(bf16[2,4,512,256]{3,2,1,0:T(8,128)(2,1)} %pad_maximum_fusion.1.src_ref, bf16[2,1,512,256]{3,2,1,0:T(8,128)(2,1)} %collective-permute-done.before_ref, bf16[2,1,512,256]{3,2,1,0:T(8,128)(2,1)} %copy-done.10, bf16[2,2,6,128]{3,2,1,0:T(8,128)(2,1)} %broadcast_in_dim.165.side_ref, ...), custom_call_target="tpu_custom_call" | custom-call | tf_op jit(solution)/shard_map/pallas_call | solution.py:82
  65.8 0.7 copy.114
  66.6 0.6 maximum_bitcast_fusion.2.block_ref
  67.2 12.6 %shard_map.114 = (f32[2,4,512,256]{3,2,1,0:T(8,128)}, f32[8,56,128]{2,1,0:T(8,128)}) custom-call(f32[56,128]{1,0:T(8,128)} %maximum_bitcast_fusion.2.block_ref, bf16[2,4,512,256]{3,2,1,0:T(8,128)(2,1)} %pad_maximum_fusion.1.src_ref, bf16[2,1,512,256]{3,2,1,0:T(8,128)(2,1)} %collective-permute-done.before_ref, bf16[2,1,512,256]{3,2,1,0:T(8,128)(2,1)} %copy-done.10, ...), custom_call_target="tpu_custom_call" | custom-call | tf_op jit(solution)/shard_map/pallas_call | solution.py:132
  79.8 1.0 copy.189
  80.8 0.6 gather_fusion
  81.5 0.1 broadcast_select_fusion.1
  82.0 0.1 convolution_bitcast_fusion.2
  82.1 0.1 convolution_bitcast_fusion.3
  82.3 0.1 convolution_bitcast_fusion
  82.4 0.1 convolution_bitcast_fusion.1
  82.6 0.1 slice.378
  82.7 0.1 slice.377
  83.0 7.8 %fusion.21 = (bf16[2,2,512,256]{3,2,1,0:T(8,128)(2,1)S(1)}, bf16[2,2,512,256]{3,2,1,0:T(8,128)(2,1)S(1)}, bf16[2,2,512,256]{3,2,1,0:T(8,128)(2,1)S(1)}) fusion(f32[2,4,512,256]{3,2,1,0:T(8,128)} %get-tuple-element.17, f32[2,2,256]{2,1,0:T(2,128)S(1)} %slice.474, f32[2,2,256]{2,1,0:T(2,128)S(1)} %slice.473, pred[512]{0:T(512)(128)(4,1)S(1)} %get-tuple-element.91, ...), kind=kLoop, calls=%fused_computation.37 | loop fusion | flops 32505856 | bytes 15763456 | tf_op jit(solution)/shard_map/convert_element_type | solution.py:326
  90.8 0.2 pad_maximum_fusion.3
  90.9 6.4 %collective-permute-start.3 = (bf16[2,1,512,512]{3,2,1,0:T(8,128)(2,1)S(1)}, bf16[2,1,512,512]{3,2,1,0:T(8,128)(2,1)S(1)}, u32[]{:S(2)}, u32[]{:S(2)}) collective-permute-start(bf16[2,1,512,512]{3,2,1,0:T(8,128)(2,1)S(1)} %get-tuple-element.25), channel_id=1, source_target_pairs={{1,0},{2,1},{3,2},{4,3},{5,4},{6,5},{7,6},{8,7},{9,8},{10,9},{11,1... | collective-permute-start | bytes 3145736 | tf_op jit(solution)/shard_map/ppermute | solution.py:183
  97.4 2.1 %collective-permute-start.2 = (bf16[2,1,512,512]{3,2,1,0:T(8,128)(2,1)S(1)}, bf16[2,1,512,512]{3,2,1,0:T(8,128)(2,1)S(1)}, u32[]{:S(2)}, u32[]{:S(2)}) collective-permute-start(bf16[2,1,512,512]{3,2,1,0:T(8,128)(2,1)S(1)} %get-tuple-element.26), channel_id=1, source_target_pairs={{0,1},{1,2},{2,3},{3,4},{4,5},{5,6},{6,7},{7,8},{8,9},{9,10},{10,1... | collective-permute-start | bytes 3145736 | tf_op jit(solution)/shard_map/ppermute | solution.py:182
  99.5 1.5 multiply_convert_fusion
  101.0 0.4 pad_maximum_fusion.src_ref
  101.4 1.9 %copy-done.1 = bf16[2,4,512,512]{3,2,1,0:T(8,128)(2,1)} copy-done((bf16[2,4,512,512]{3,2,1,0:T(8,128)(2,1)}, bf16[2,4,512,512]{3,2,1,0:T(8,128)(2,1)S(1)}, u32[]{:S(2)}) %copy-start.1) | copy-done | bytes 4194328
  103.4 15.1 %collective-permute-done.3 = bf16[2,1,512,512]{3,2,1,0:T(8,128)(2,1)S(1)} collective-permute-done((bf16[2,1,512,512]{3,2,1,0:T(8,128)(2,1)S(1)}, bf16[2,1,512,512]{3,2,1,0:T(8,128)(2,1)S(1)}, u32[]{:S(2)}, u32[]{:S(2)}) %collective-permute-start.3) | collective-permute-done | bytes 1048608 | tf_op jit(solution)/shard_map/ppermute | solution.py:183
  118.5 0.3 reverse_select_fusion.after_ref
  118.7 3.4 %collective-permute-done.2.before_ref = bf16[2,1,512,512]{3,2,1,0:T(8,128)(2,1)S(1)} collective-permute-done((bf16[2,1,512,512]{3,2,1,0:T(8,128)(2,1)S(1)}, bf16[2,1,512,512]{3,2,1,0:T(8,128)(2,1)S(1)}, u32[]{:S(2)}, u32[]{:S(2)}) %collective-permute-start.2) | collective-permute-done | bytes 1048608 | tf_op jit(solution)/shard_map/ppermute | solution.py:182
  122.1 1.0 copy-done.9
  123.1 0.6 broadcast_in_dim.181.side_ref
  123.7 9.5 %shard_map.115 = (f32[2,4,512,128]{3,2,1,0:T(8,128)}, f32[2,2,4,128]{3,2,1,0:T(4,128)}) custom-call(bf16[2,4,512,512]{3,2,1,0:T(8,128)(2,1)} %copy-done.1, bf16[2,1,512,512]{3,2,1,0:T(8,128)(2,1)} %copy-done.9, bf16[2,1,512,512]{3,2,1,0:T(8,128)(2,1)} %copy-done.4, bf16[2,2,6,256]{3,2,1,0:T(8,128)(2,1)} %broadcast_in_dim.181.side_ref, bf16[9,128,256]{2,1,0:T(8,128)(2,1)} %k_ref.6), custom_call_target="tpu_custom_call" | custom-call | tf_op jit(solution)/shard_map/pallas_call | solution.py:82
  133.2 0.7 copy.120
  134.0 0.6 maximum_bitcast_fusion.1.block_ref
  134.6 12.6 %shard_map.116 = (f32[2,4,512,128]{3,2,1,0:T(8,128)}, f32[8,64,128]{2,1,0:T(8,128)}) custom-call(f32[64,128]{1,0:T(8,128)} %maximum_bitcast_fusion.1.block_ref, bf16[2,4,512,512]{3,2,1,0:T(8,128)(2,1)} %copy-done.1, bf16[2,1,512,512]{3,2,1,0:T(8,128)(2,1)} %copy-done.9, bf16[2,1,512,512]{3,2,1,0:T(8,128)(2,1)} %copy-done.4, bf16[9,256,128]{2,1,0:T(8,128)(2,1)} %k_ref.7), custom_call_target="tpu_custom_call" | custom-call | tf_op jit(solution)/shard_map/pallas_call | solution.py:132
  147.2 1.1 copy.188
  148.3 0.6 gather_fusion.1
  149.0 0.1 broadcast_select_fusion
  149.3 0.1 rev.37
  149.6 0.1 rev.36
  149.9 0.1 convolution_bitcast_fusion.6
  150.0 0.2 convolution_bitcast_fusion.7
  150.2 0.2 convolution_bitcast_fusion.4
  150.3 0.2 convolution_bitcast_fusion.5
  150.5 5.1 %add_bitcast_fusion = (f32[1,1,2,4,512,128]{5,4,3,2,1,0:T(8,128)}, bf16[1,1,2,4,512,128]{5,4,3,2,1,0:T(8,128)(2,1)}) fusion(f32[2,4,512,128]{3,2,1,0:T(8,128)} %get-tuple-element.21, f32[2,4,128]{2,1,0:T(4,128)S(1)} %reverse_select_fusion.4, f32[2,4,128]{2,1,0:T(4,128)S(1)} %reverse_select_fusion.5, pred[512]{0:T(512)(128)(4,1)S(1)} %get-tuple-element.91, ...), kind=kLoop, calls=%fused_computation.40 | loop fusion | flops 7340032 | bytes 9455104 | tf_op jit(solution)/shard_map/broadcast_in_dim | solution.py:342
  (125 shorter events, 1.1 us)
Async XLA Ops:
  0.6 4.1 %copy-start = (bf16[1024,256]{1,0:T(8,128)(2,1)S(1)}, bf16[1024,256]{1,0:T(8,128)(2,1)}, u32[]{:S(2)}) copy-start(bf16[1024,256]{1,0:T(8,128)(2,1)} %param.11) | copy-start | bytes 1572868
  7.7 10.7 %copy-start.2 = (bf16[1,1,2,4,512,128]{5,4,3,2,1,0:T(8,128)(2,1)S(1)}, bf16[1,1,2,4,512,128]{5,4,3,2,1,0:T(8,128)(2,1)}, u32[]{:S(2)}) copy-start(bf16[1,1,2,4,512,128]{5,4,3,2,1,0:T(8,128)(2,1)} %param.10) | copy-start | bytes 3145732
  7.7 10.7 %copy-start.5 = (bf16[1,1,2,4,512,128]{5,4,3,2,1,0:T(8,128)(2,1)S(1)}, bf16[1,1,2,4,512,128]{5,4,3,2,1,0:T(8,128)(2,1)}, u32[]{:S(2)}) copy-start(bf16[1,1,2,4,512,128]{5,4,3,2,1,0:T(8,128)(2,1)} %param.19) | copy-start | bytes 3145732
  7.7 39.7 %all-to-all-start = ((bf16[128,17,256]{2,1,0:T(8,128)(2,1)}), bf16[128,17,256]{2,1,0:T(8,128)(2,1)}, u32[]{:S(2)}, u32[]{:S(2)}) async-start(bf16[128,17,256]{2,1,0:T(8,128)(2,1)} %pad_maximum_fusion.2), calls=%async_computation | async-start | bytes 3145728 | tf_op jit(solution)/shard_map/all_to_all | solution.py:268
  18.4 9.3 %copy-start.14 = (s32[8,2,3]{0,1,2:T(2,128)S(1)}, s32[8,2,3]{0,1,2:T(2,128)}, u32[]{:S(2)}) copy-start(s32[8,2,3]{0,1,2:T(2,128)} %param.14) | copy-start | bytes 580
  19.5 37.2 %collective-permute-start = (bf16[2,1,512,256]{3,2,1,0:T(8,128)(2,1)}, bf16[2,1,512,256]{3,2,1,0:T(8,128)(2,1)}, u32[]{:S(2)}, u32[]{:S(2)}) collective-permute-start(bf16[2,1,512,256]{3,2,1,0:T(8,128)(2,1)} %get-tuple-element.28), channel_id=1, source_target_pairs={{0,1},{1,2},{2,3},{3,4},{4,5},{5,6},{6,7},{7,8},{8,9},{9,10},{10,1... | collective-permute-start | bytes 1572872 | tf_op jit(solution)/shard_map/ppermute | solution.py:182
  21.6 24.5 %collective-permute-start.1 = (bf16[2,1,512,256]{3,2,1,0:T(8,128)(2,1)}, bf16[2,1,512,256]{3,2,1,0:T(8,128)(2,1)}, u32[]{:S(2)}, u32[]{:S(2)}) collective-permute-start(bf16[2,1,512,256]{3,2,1,0:T(8,128)(2,1)} %get-tuple-element.27), channel_id=1, source_target_pairs={{1,0},{2,1},{3,2},{4,3},{5,4},{6,5},{7,6},{8,7},{9,8},{10,9},{11,1... | collective-permute-start | bytes 1572872 | tf_op jit(solution)/shard_map/ppermute | solution.py:183
  35.0 1.6 %copy-start.12 = (bf16[9,128,256]{2,1,0:T(8,128)(2,1)S(1)}, bf16[9,128,256]{2,1,0:T(8,128)(2,1)}, u32[]{:S(2)}) copy-start(bf16[9,128,256]{2,1,0:T(8,128)(2,1)} %k_ref.6) | copy-start | bytes 1769476
  47.4 9.3 %copy-start.10 = (bf16[2,1,512,256]{3,2,1,0:T(8,128)(2,1)}, bf16[2,1,512,256]{3,2,1,0:T(8,128)(2,1)S(1)}, u32[]{:S(2)}) copy-start(bf16[2,1,512,256]{3,2,1,0:T(8,128)(2,1)S(1)} %reverse_select_fusion.1.after_ref) | copy-start | bytes 1572868
  56.7 9.9 %slice-start.3 = ((bf16[2,1,512,256]{3,2,1,0:T(8,128)(2,1)}), bf16[2,1,512,128]{3,2,1,0:T(8,128)(2,1)S(1)}, s32[]{:S(2)}) async-start(bf16[2,1,512,256]{3,2,1,0:T(8,128)(2,1)} %copy-done.10), calls=%async_computation.4 | async-start | bytes 524288 | tf_op jit(solution)/shard_map/slice | solution.py:189
  81.5 1.5 copy-start.13
  83.0 14.4 %copy-start.11 = (bf16[9,256,128]{2,1,0:T(8,128)(2,1)S(1)}, bf16[9,256,128]{2,1,0:T(8,128)(2,1)}, u32[]{:S(2)}) copy-start(bf16[9,256,128]{2,1,0:T(8,128)(2,1)} %k_ref.7) | copy-start | bytes 1769476
  83.0 16.5 %copy-start.8 = (f32[2,4,512,256]{3,2,1,0:T(8,128)S(1)}, f32[2,4,512,256]{3,2,1,0:T(8,128)}, u32[]{:S(2)}) copy-start(f32[2,4,512,256]{3,2,1,0:T(8,128)} %get-tuple-element.14) | copy-start | bytes 12582916
  90.8 8.8 %copy-start.7 = (f32[2,4,512,256]{3,2,1,0:T(8,128)S(1)}, f32[2,4,512,256]{3,2,1,0:T(8,128)}, u32[]{:S(2)}) copy-start(f32[2,4,512,256]{3,2,1,0:T(8,128)} %fusion) | copy-start | bytes 12582916
  90.9 27.5 %collective-permute-start.3 = (bf16[2,1,512,512]{3,2,1,0:T(8,128)(2,1)S(1)}, bf16[2,1,512,512]{3,2,1,0:T(8,128)(2,1)S(1)}, u32[]{:S(2)}, u32[]{:S(2)}) collective-permute-start(bf16[2,1,512,512]{3,2,1,0:T(8,128)(2,1)S(1)} %get-tuple-element.25), channel_id=1, source_target_pairs={{1,0},{2,1},{3,2},{4,3},{5,4},{6,5},{7,6},{8,7},{9,8},{10,9},{11,1... | collective-permute-start | bytes 3145736 | tf_op jit(solution)/shard_map/ppermute | solution.py:183
  97.4 24.8 %collective-permute-start.2 = (bf16[2,1,512,512]{3,2,1,0:T(8,128)(2,1)S(1)}, bf16[2,1,512,512]{3,2,1,0:T(8,128)(2,1)S(1)}, u32[]{:S(2)}, u32[]{:S(2)}) collective-permute-start(bf16[2,1,512,512]{3,2,1,0:T(8,128)(2,1)S(1)} %get-tuple-element.26), channel_id=1, source_target_pairs={{0,1},{1,2},{2,3},{3,4},{4,5},{5,6},{6,7},{7,8},{8,9},{9,10},{10,1... | collective-permute-start | bytes 3145736 | tf_op jit(solution)/shard_map/ppermute | solution.py:182
  101.4 2.0 %copy-start.1 = (bf16[2,4,512,512]{3,2,1,0:T(8,128)(2,1)}, bf16[2,4,512,512]{3,2,1,0:T(8,128)(2,1)S(1)}, u32[]{:S(2)}) copy-start(bf16[2,4,512,512]{3,2,1,0:T(8,128)(2,1)S(1)} %pad_maximum_fusion.src_ref) | copy-start | bytes 12582916
  118.7 3.4 %copy-start.4 = (bf16[2,1,512,512]{3,2,1,0:T(8,128)(2,1)}, bf16[2,1,512,512]{3,2,1,0:T(8,128)(2,1)S(1)}, u32[]{:S(2)}) copy-start(bf16[2,1,512,512]{3,2,1,0:T(8,128)(2,1)S(1)} %reverse_select_fusion.after_ref) | copy-start | bytes 3145732
  122.1 1.0 copy-start.9
  123.7 10.2 %slice-start = ((bf16[2,4,512,512]{3,2,1,0:T(8,128)(2,1)}), bf16[2,4,512,256]{3,2,1,0:T(8,128)(2,1)S(1)}, s32[]{:S(2)}) async-start(bf16[2,4,512,512]{3,2,1,0:T(8,128)(2,1)} %copy-done.1), calls=%async_computation.1 | async-start | bytes 4194304 | tf_op jit(solution)/shard_map/slice | solution.py:189
  123.7 10.2 %slice-start.1 = ((bf16[2,1,512,512]{3,2,1,0:T(8,128)(2,1)}), bf16[2,1,512,256]{3,2,1,0:T(8,128)(2,1)S(1)}, s32[]{:S(2)}) async-start(bf16[2,1,512,512]{3,2,1,0:T(8,128)(2,1)} %copy-done.4), calls=%async_computation.2 | async-start | bytes 1048576 | tf_op jit(solution)/shard_map/slice | solution.py:189
  123.7 10.2 %slice-start.2 = ((bf16[2,1,512,512]{3,2,1,0:T(8,128)(2,1)}), bf16[2,1,512,256]{3,2,1,0:T(8,128)(2,1)S(1)}, s32[]{:S(2)}) async-start(bf16[2,1,512,512]{3,2,1,0:T(8,128)(2,1)} %copy-done.9), calls=%async_computation.3 | async-start | bytes 1048576 | tf_op jit(solution)/shard_map/slice | solution.py:189
  149.0 1.5 copy-start.3
  149.0 1.5 copy-start.6
  149.0 1.5 copy-start.15

commit v4 on v1

--- a/solution.py
+++ b/solution.py
@@ -90,6 +90,55 @@
         compiler_params=pltpu.CompilerParams(vmem_limit_bytes=60 * 1024 * 1024),
     )(source, before, after, sides, kernel)
     return out, margins
+
+
+def back_kernel(src_ref, before_ref, after_ref, k_ref, out_ref, margin_ref):
+    band = pl.program_id(0)
+    _, rows, cols, cout = out_ref.shape
+    width = src_ref.shape[3]
+    pixels = rows * cols
+    col = lax.broadcasted_iota(jnp.int32, (rows, cols, cout), 1).reshape(pixels, cout)
+    ext = jnp.concatenate([before_ref[0], src_ref[0], after_ref[0]], axis=0)
+    lhs = jnp.concatenate([ext[dy : dy + rows].reshape(pixels, width) for dy in range(3)], axis=1)
+    products = []
+    for col_tap in range(3):
+        taps = [k_ref[3 * (2 - dy + band * (2 * dy - 2)) + 2 - col_tap] for dy in range(3)]
+        stack = jnp.concatenate(taps, axis=1)
+        products.append(
+            lax.dot_general(lhs, stack, (((1,), (1,)), ((), ())), preferred_element_type=jnp.float32)
+        )
+    z_left, z_mid, z_right = products
+    from_left = jnp.where(col == 0, 0.0, pltpu.roll(z_left, 1, 0))
+    from_right = jnp.where(col == cols - 1, 0.0, pltpu.roll(z_right, pixels - 1, 0))
+    out_ref[0] = (z_mid + from_left + from_right).reshape(rows, cols, cout)
+    margin_ref[0, 0] = z_right.reshape(rows, cols, cout)[:, 0, :]
+    margin_ref[0, 1] = z_left.reshape(rows, cols, cout)[:, cols - 1, :]
+
+
+def conv_back(pieces, first, width, kernel):
+    source, before, after = pieces
+    bands, rows, cols, _ = source.shape
+    cout = kernel.shape[1]
+    block = first // width
+    return pl.pallas_call(
+        back_kernel,
+        grid=(bands,),
+        in_specs=[
+            pl.BlockSpec((1, rows, cols, width), lambda b: (b, 0, 0, block)),
+            pl.BlockSpec((1, 1, cols, width), lambda b: (b, 0, 0, block)),
+            pl.BlockSpec((1, 1, cols, width), lambda b: (b, 0, 0, block)),
+            pl.BlockSpec(kernel.shape, lambda b: (0, 0, 0)),
+        ],
+        out_specs=[
+            pl.BlockSpec((1, rows, cols, cout), lambda b: (b, 0, 0, 0)),
+            pl.BlockSpec((1, 2, rows, cout), lambda b: (b, 0, 0, 0)),
+        ],
+        out_shape=[
+            jax.ShapeDtypeStruct((bands, rows, cols, cout), jnp.float32),
+            jax.ShapeDtypeStruct((bands, 2, rows, cout), jnp.float32),
+        ],
+        compiler_params=pltpu.CompilerParams(vmem_limit_bytes=60 * 1024 * 1024),
+    )(source, before, after, kernel)
 
 
 def conv_gather_kernel(count, first, width, block_ref, src_ref, before_ref, after_ref, k_ref,
@@ -307,7 +356,7 @@
 
     lifted = kernel_one.shape[2]
     both = extend_rows(jnp.concatenate([base_field, cot_field], axis=3), last_tile)
-    cot_back, cot_margins = conv_pallas(both, channels, channels, None, kernel_two, True)
+    cot_back, cot_margins = conv_back(both, channels, channels, kernel_two)
     parts = [edge_cols(both, 0, channels), jnp.swapaxes(cot_margins, 1, 2)]
     first_out, landed = conv_gather(both, 0, channels, pack_parts(parts), kernel_one, 0)
     base_edges, cot_gathered = unpack_parts(landed, parts)
@@ -319,7 +368,7 @@
     grad_pre = jax.vjp(activation, pre_act)[1](grad_inner)[0].astype(jnp.bfloat16)
 
     pair = extend_rows(jnp.concatenate([inner, grad_pre], axis=3), last_tile)
-    pre_back, pre_margins = conv_pallas(pair, lifted, lifted, None, kernel_one, True)
+    pre_back, pre_margins = conv_back(pair, lifted, lifted, kernel_one)
     parts = [edge_cols(pair, 0, lifted), jnp.swapaxes(pre_margins, 1, 2)]
     second_out, landed = conv_gather(pair, 0, lifted, pack_parts(parts), kernel_two, 1)
     inner_edges, pre_gathered = unpack_parts(landed, parts)

time: 141 us -> 138 us (0.979)
  Pallas kernels: 42.1 us -> 39.6 us
    pallas_call x2, Pallas kernels: 16.8 us -> 14.3 us  [conv_back(): pl.pallas_call(back_kernel, grid=(bands,), in_specs=[pl.BlockSpec((1, row...]
  transfers between devices with their start and end apart: 5 -> 5, of which waited for: 2 -> 2; matrix products, arithmetic and copies ran while one was open for 14% -> 13% of each run, Pallas kernels for 15% -> 14%
where the time goes in v4:
time: 138 us; the launch traced here: 137 us
  Pallas kernels  39.6 us (29%)
  other arithmetic  26.4 us (19%)
  starting transfers between devices  23.7 us (17%)
  waiting for transfers between devices  20.5 us (15%)
  local copies, waits for them, and re-layouts  10.9 us (8%)
  matrix products  8.13 us (6%)
  between operations  7.66 us (6%)
    pallas_call x2, Pallas kernels, conv_gather(): pl.pallas_call(functools.partial(conv_gather_kernel, count, first, width)...  25.3 us
    ppermute x2, waiting for transfers between devices, extend_rows(): after = lax.ppermute(head, 'tile', [(i + 1, i) for i in range(count - 1)])  16.5 us
    pallas_call x2, Pallas kernels, conv_back(): pl.pallas_call(back_kernel, grid=(bands,), in_specs=[pl.BlockSpec((1, row...  14.3 us
    all_to_all x1, starting transfers between devices, route_observations(): lax.all_to_all(payload, ('face', 'tile'), split_axis=0, concat_axis=0, ti...  11.6 us
    ppermute x2, starting transfers between devices, extend_rows(): after = lax.ppermute(head, 'tile', [(i + 1, i) for i in range(count - 1)])  8.01 us
    dot_general x1, matrix products, per_device(): gridded = jnp.dot(onehot, got_values, preferred_element_type=jnp.float32)  5.33 us
    broadcast_in_dim x1, other arithmetic, per_device(): return (analysis[None, None], grad_base[None, None])  5.17 us
    convert_element_type x1, other arithmetic, per_device(): inner = activation(pre_act).astype(jnp.bfloat16)  5.04 us
  transfers between devices with their start and end apart: 5, of which 2 were waited for; matrix products, arithmetic and copies ran while one was open for 13% of the time, Pallas kernels for 14%

profile of v4, /device:TPU:24, one launch (start us, length us, event | category | flops | bytes accessed | tf_op | source)
XLA Modules:
  0.0 136.8 jit_solution(2164792495283462545)
XLA Ops:
  0.6 0.0 copy-start
  0.6 2.3 %fusion.19 = (bf16[2,1,512,256]{3,2,1,0:T(8,128)(2,1)}, bf16[2,1,512,256]{3,2,1,0:T(8,128)(2,1)}) fusion(bf16[2,4,512,128]{3,2,1,0:T(8,128)(2,1)} %bitcast.235, bf16[2,4,512,128]{3,2,1,0:T(8,128)(2,1)} %bitcast.238), kind=kLoop, calls=%fused_computation.51 | loop fusion | flops 2097152 | bytes 3145728 | tf_op jit(solution)/shard_map/concatenate | solution.py:358
  3.0 4.5 %collective-permute-start.1 = (bf16[2,1,512,256]{3,2,1,0:T(8,128)(2,1)}, bf16[2,1,512,256]{3,2,1,0:T(8,128)(2,1)}, u32[]{:S(2)}, u32[]{:S(2)}) collective-permute-start(bf16[2,1,512,256]{3,2,1,0:T(8,128)(2,1)} %get-tuple-element.22), channel_id=1, source_target_pairs={{1,0},{2,1},{3,2},{4,3},{5,4},{6,5},{7,6},{8,7},{9,8},{10,9},{11,1... | collective-permute-start | bytes 1572872 | tf_op jit(solution)/shard_map/ppermute | solution.py:230
  7.5 1.9 %collective-permute-start = (bf16[2,1,512,256]{3,2,1,0:T(8,128)(2,1)}, bf16[2,1,512,256]{3,2,1,0:T(8,128)(2,1)}, u32[]{:S(2)}, u32[]{:S(2)}) collective-permute-start(bf16[2,1,512,256]{3,2,1,0:T(8,128)(2,1)} %get-tuple-element.23), channel_id=1, source_target_pairs={{0,1},{1,2},{2,3},{3,4},{4,5},{5,6},{6,7},{7,8},{8,9},{9,10},{10,1... | collective-permute-start | bytes 1572872 | tf_op jit(solution)/shard_map/ppermute | solution.py:229
  9.4 1.3 convert_reduce_fusion
  10.7 0.7 multiply_add_fusion.1
  11.4 1.6 %select_reduce_fusion = s32[2048]{0:T(1024)S(1)} fusion(s32[1024]{0:T(1024)} %param.13, s32[1024]{0:T(1024)S(1)} %multiply_add_fusion.1), kind=kLoop, calls=%fused_computation.6 | loop fusion | flops 6289408 | bytes 16384 | tf_op jit(solution)/shard_map/reduce_sum | solution.py:306
  13.0 0.1 reduce_sum.22
  13.1 0.1 fusion.52
  13.2 0.1 pad.43.clone
  13.3 0.1 maximum_bitcast_fusion
  13.4 0.1 copy.117
  13.5 1.6 %fusion.14 = bf16[2048,256]{1,0:T(8,128)(2,1)S(1)} fusion(bf16[1024,256]{1,0:T(8,128)(2,1)S(1)} %copy-done, s32[1024]{0:T(1024)S(1)} %multiply_add_fusion.1), kind=kOutput, calls=%fused_computation.34 | convolution fusion | flops 1076363264 | bytes 1576960 | tf_op jit(solution)/shard_map/dot_general | solution.py:303
  15.1 0.0 copy-start.11
  15.2 1.3 pad_maximum_fusion.2
  16.5 11.6 %all-to-all-start = ((bf16[128,17,256]{2,1,0:T(8,128)(2,1)}), bf16[128,17,256]{2,1,0:T(8,128)(2,1)}, u32[]{:S(2)}, u32[]{:S(2)}) async-start(bf16[128,17,256]{2,1,0:T(8,128)(2,1)} %pad_maximum_fusion.2), calls=%async_computation | async-start | bytes 3145728 | tf_op jit(solution)/shard_map/all_to_all | solution.py:315
  28.2 0.1 constant_dynamic-slice_fusion.8
  28.3 0.1 copy.114
  28.4 0.7 fusion.153
  29.1 1.5 %pad_maximum_fusion.1.src_ref = bf16[2,4,512,256]{3,2,1,0:T(8,128)(2,1)} fusion(bf16[2,4,512,128]{3,2,1,0:T(8,128)(2,1)S(1)} %bitcast.239, bf16[2,4,512,128]{3,2,1,0:T(8,128)(2,1)S(1)} %bitcast.236), kind=kLoop, calls=%fused_computation.31 | loop fusion | flops 4194304 | bytes 4194304 | tf_op jit(solution)/shard_map/concatenate | solution.py:358
  36.8 1.3 reverse_select_fusion.1.after_ref
  38.1 0.0 copy-start.6
  38.2 0.7 copy-done.6
  38.9 6.4 %shard_map.113 = (f32[2,4,512,256]{3,2,1,0:T(8,128)}, f32[2,2,4,256]{3,2,1,0:T(4,128)}) custom-call(bf16[2,4,512,256]{3,2,1,0:T(8,128)(2,1)} %pad_maximum_fusion.1.src_ref, bf16[2,1,512,256]{3,2,1,0:T(8,128)(2,1)} %collective-permute-done.before_ref, bf16[2,1,512,256]{3,2,1,0:T(8,128)(2,1)} %copy-done.6, bf16[9,256,128]{2,1,0:T(8,128)(2,1)} %k_ref.7), custom_call_target="tpu_custom_call" | custom-call | tf_op jit(solution)/shard_map/pallas_call | solution.py:123
  45.3 0.7 copy.113
  46.0 1.0 slice.384
  47.1 0.6 maximum_bitcast_fusion.2.block_ref
  47.7 12.9 %shard_map.114 = (f32[2,4,512,256]{3,2,1,0:T(8,128)}, f32[8,56,128]{2,1,0:T(8,128)}) custom-call(f32[56,128]{1,0:T(8,128)} %maximum_bitcast_fusion.2.block_ref, bf16[2,4,512,256]{3,2,1,0:T(8,128)(2,1)} %pad_maximum_fusion.1.src_ref, bf16[2,1,512,256]{3,2,1,0:T(8,128)(2,1)} %collective-permute-done.before_ref, bf16[2,1,512,256]{3,2,1,0:T(8,128)(2,1)} %copy-done.6, ...), custom_call_target="tpu_custom_call" | custom-call | tf_op jit(solution)/shard_map/pallas_call | solution.py:181
  60.6 1.0 copy.189
  61.6 0.6 gather_fusion
  62.2 0.1 broadcast_select_fusion.1
  62.8 0.1 convolution_bitcast_fusion.1
  62.9 0.1 convolution_bitcast_fusion
  63.0 0.2 convolution_bitcast_fusion.3
  63.2 0.1 convolution_bitcast_fusion.2
  63.5 1.4 %fusion.55 = s32[128,16]{1,0:T(8,128)S(1)} fusion(bf16[128,17,256]{2,1,0:T(8,128)(2,1)} %all-to-all-done), kind=kLoop, calls=%fused_computation.98 | loop fusion | flops 8192 | bytes 16384 | tf_op jit(solution)/shard_map/add | solution.py:319
  64.8 0.1 add.158
  64.9 1.3 slice.409
  66.3 0.0 copy-start.12
  66.3 5.3 %fusion = f32[2,4,512,256]{3,2,1,0:T(8,128)S(1)} fusion(bf16[2048,256,1,1]{1,0,3,2:T(8,128)(2,1)S(1)} %bitcast.240, s32[2048]{0:T(1024)S(1)} %add.158, s32[2,4,512]{2,1,0:T(4,128)S(1)} %multiply_add_fusion), kind=kOutput, calls=%fused_computation.2 | convolution fusion | flops 4303355904 | bytes 5267456 | tf_op jit(solution)/shard_map/dot_general | solution.py:351
  71.7 5.0 %multiply_convert_fusion = (bf16[2,4,512,256]{3,2,1,0:T(8,128)(2,1)S(1)}, bf16[2,4,512,256]{3,2,1,0:T(8,128)(2,1)S(1)}) fusion(f32[2,4,512,256]{3,2,1,0:T(8,128)S(1)} %fusion, f32[256]{0:T(256)S(1)} %copy-done.12, f32[2,4,256]{2,1,0:T(4,128)S(1)} %get-tuple-element.47, pred[512]{0:T(512)(128)(4,1)S(1)} %get-tuple-element.86, ...), kind=kLoop, calls=%fused_computation.23 | loop fusion | flops 33554432 | bytes 16812032 | tf_op jit(solution)/shard_map/convert_element_type | solution.py:366
  76.7 0.2 fusion.17
  76.9 3.5 %collective-permute-start.3 = (bf16[2,1,512,512]{3,2,1,0:T(8,128)(2,1)S(1)}, bf16[2,1,512,512]{3,2,1,0:T(8,128)(2,1)S(1)}, u32[]{:S(2)}, u32[]{:S(2)}) collective-permute-start(bf16[2,1,512,512]{3,2,1,0:T(8,128)(2,1)S(1)} %get-tuple-element.20), channel_id=1, source_target_pairs={{1,0},{2,1},{3,2},{4,3},{5,4},{6,5},{7,6},{8,7},{9,8},{10,9},{11,1... | collective-permute-start | bytes 3145736 | tf_op jit(solution)/shard_map/ppermute | solution.py:230
  80.4 2.1 %collective-permute-start.2 = (bf16[2,1,512,512]{3,2,1,0:T(8,128)(2,1)S(1)}, bf16[2,1,512,512]{3,2,1,0:T(8,128)(2,1)S(1)}, u32[]{:S(2)}, u32[]{:S(2)}) collective-permute-start(bf16[2,1,512,512]{3,2,1,0:T(8,128)(2,1)S(1)} %get-tuple-element.21), channel_id=1, source_target_pairs={{0,1},{1,2},{2,3},{3,4},{4,5},{5,6},{6,7},{7,8},{8,9},{9,10},{10,1... | collective-permute-start | bytes 3145736 | tf_op jit(solution)/shard_map/ppermute | solution.py:229
  82.6 2.3 %pad_maximum_fusion.src_ref = bf16[2,4,512,512]{3,2,1,0:T(8,128)(2,1)} fusion(bf16[2,4,512,256]{3,2,1,0:T(8,128)(2,1)S(1)} %get-tuple-element.19, bf16[2,4,512,256]{3,2,1,0:T(8,128)(2,1)S(1)} %get-tuple-element.18), kind=kLoop, calls=%fused_computation.13 | loop fusion | flops 8388608 | bytes 8388608 | tf_op jit(solution)/shard_map/concatenate | solution.py:370
  84.9 16.5 %collective-permute-done.3 = bf16[2,1,512,512]{3,2,1,0:T(8,128)(2,1)S(1)} collective-permute-done((bf16[2,1,512,512]{3,2,1,0:T(8,128)(2,1)S(1)}, bf16[2,1,512,512]{3,2,1,0:T(8,128)(2,1)S(1)}, u32[]{:S(2)}, u32[]{:S(2)}) %collective-permute-start.3) | collective-permute-done | bytes 1048608 | tf_op jit(solution)/shard_map/ppermute | solution.py:230
  101.4 0.3 reverse_select_fusion.after_ref
  101.8 4.0 %collective-permute-done.2.before_ref = bf16[2,1,512,512]{3,2,1,0:T(8,128)(2,1)S(1)} collective-permute-done((bf16[2,1,512,512]{3,2,1,0:T(8,128)(2,1)S(1)}, bf16[2,1,512,512]{3,2,1,0:T(8,128)(2,1)S(1)}, u32[]{:S(2)}, u32[]{:S(2)}) %collective-permute-start.2) | collective-permute-done | bytes 1048608 | tf_op jit(solution)/shard_map/ppermute | solution.py:229
  105.8 0.9 copy-done.5
  106.8 7.9 %shard_map.115 = (f32[2,4,512,128]{3,2,1,0:T(8,128)}, f32[2,2,4,128]{3,2,1,0:T(4,128)}) custom-call(bf16[2,4,512,512]{3,2,1,0:T(8,128)(2,1)} %pad_maximum_fusion.src_ref, bf16[2,1,512,512]{3,2,1,0:T(8,128)(2,1)} %copy-done.5, bf16[2,1,512,512]{3,2,1,0:T(8,128)(2,1)} %copy-done.2, bf16[9,128,256]{2,1,0:T(8,128)(2,1)} %k_ref.6), custom_call_target="tpu_custom_call" | custom-call | tf_op jit(solution)/shard_map/pallas_call | solution.py:123
  114.6 0.7 copy.120
  115.3 0.6 maximum_bitcast_fusion.1.block_ref
  116.0 12.3 %shard_map.116 = (f32[2,4,512,128]{3,2,1,0:T(8,128)}, f32[8,64,128]{2,1,0:T(8,128)}) custom-call(f32[64,128]{1,0:T(8,128)} %maximum_bitcast_fusion.1.block_ref, bf16[2,4,512,512]{3,2,1,0:T(8,128)(2,1)} %pad_maximum_fusion.src_ref, bf16[2,1,512,512]{3,2,1,0:T(8,128)(2,1)} %copy-done.5, bf16[2,1,512,512]{3,2,1,0:T(8,128)(2,1)} %copy-done.2, ...), custom_call_target="tpu_custom_call" | custom-call | tf_op jit(solution)/shard_map/pallas_call | solution.py:181
  128.3 1.2 copy.188
  129.5 0.6 gather_fusion.1
  130.2 0.1 broadcast_select_fusion
  130.3 0.1 constant_dynamic-slice_fusion.3
  130.4 0.1 rev.36
  130.6 0.1 rev.37
  131.0 0.1 convolution_bitcast_fusion.5
  131.1 0.2 convolution_bitcast_fusion.4
  131.3 0.2 convolution_bitcast_fusion.7
  131.5 0.2 convolution_bitcast_fusion.6
  131.7 5.2 %add_bitcast_fusion = (f32[1,1,2,4,512,128]{5,4,3,2,1,0:T(8,128)}, bf16[1,1,2,4,512,128]{5,4,3,2,1,0:T(8,128)(2,1)}) fusion(f32[2,4,512,128]{3,2,1,0:T(8,128)} %get-tuple-element.17, f32[2,4,128]{2,1,0:T(4,128)S(1)} %reverse_select_fusion.4, f32[2,4,128]{2,1,0:T(4,128)S(1)} %reverse_select_fusion.5, pred[512]{0:T(512)(128)(4,1)S(1)} %get-tuple-element.86, ...), kind=kLoop, calls=%fused_computation.35 | loop fusion | flops 7340032 | bytes 9455104 | tf_op jit(solution)/shard_map/broadcast_in_dim | solution.py:380
  (104 shorter events, 0.9 us)
Async XLA Ops:
  0.6 12.9 %copy-start = (bf16[1024,256]{1,0:T(8,128)(2,1)S(1)}, bf16[1024,256]{1,0:T(8,128)(2,1)}, u32[]{:S(2)}) copy-start(bf16[1024,256]{1,0:T(8,128)(2,1)} %param.11) | copy-start | bytes 1572868
  3.0 33.8 %collective-permute-start.1 = (bf16[2,1,512,256]{3,2,1,0:T(8,128)(2,1)}, bf16[2,1,512,256]{3,2,1,0:T(8,128)(2,1)}, u32[]{:S(2)}, u32[]{:S(2)}) collective-permute-start(bf16[2,1,512,256]{3,2,1,0:T(8,128)(2,1)} %get-tuple-element.22), channel_id=1, source_target_pairs={{1,0},{2,1},{3,2},{4,3},{5,4},{6,5},{7,6},{8,7},{9,8},{10,9},{11,1... | collective-permute-start | bytes 1572872 | tf_op jit(solution)/shard_map/ppermute | solution.py:230
  7.5 30.6 %collective-permute-start = (bf16[2,1,512,256]{3,2,1,0:T(8,128)(2,1)}, bf16[2,1,512,256]{3,2,1,0:T(8,128)(2,1)}, u32[]{:S(2)}, u32[]{:S(2)}) collective-permute-start(bf16[2,1,512,256]{3,2,1,0:T(8,128)(2,1)} %get-tuple-element.23), channel_id=1, source_target_pairs={{0,1},{1,2},{2,3},{3,4},{4,5},{5,6},{6,7},{7,8},{8,9},{9,10},{10,1... | collective-permute-start | bytes 1572872 | tf_op jit(solution)/shard_map/ppermute | solution.py:229
  15.1 13.1 %copy-start.11 = (s32[8,2,3]{0,1,2:T(2,128)S(1)}, s32[8,2,3]{0,1,2:T(2,128)}, u32[]{:S(2)}) copy-start(s32[8,2,3]{0,1,2:T(2,128)} %param.14) | copy-start | bytes 580
  15.1 13.9 %copy-start.1 = (bf16[1,1,2,4,512,128]{5,4,3,2,1,0:T(8,128)(2,1)S(1)}, bf16[1,1,2,4,512,128]{5,4,3,2,1,0:T(8,128)(2,1)}, u32[]{:S(2)}) copy-start(bf16[1,1,2,4,512,128]{5,4,3,2,1,0:T(8,128)(2,1)} %param.10) | copy-start | bytes 3145732
  15.2 13.9 %copy-start.3 = (bf16[1,1,2,4,512,128]{5,4,3,2,1,0:T(8,128)(2,1)S(1)}, bf16[1,1,2,4,512,128]{5,4,3,2,1,0:T(8,128)(2,1)}, u32[]{:S(2)}) copy-start(bf16[1,1,2,4,512,128]{5,4,3,2,1,0:T(8,128)(2,1)} %param.19) | copy-start | bytes 3145732
  16.5 20.2 %copy-start.10 = (bf16[9,128,256]{2,1,0:T(8,128)(2,1)S(1)}, bf16[9,128,256]{2,1,0:T(8,128)(2,1)}, u32[]{:S(2)}) copy-start(bf16[9,128,256]{2,1,0:T(8,128)(2,1)} %k_ref.6) | copy-start | bytes 1769476
  16.5 46.9 %all-to-all-start = ((bf16[128,17,256]{2,1,0:T(8,128)(2,1)}), bf16[128,17,256]{2,1,0:T(8,128)(2,1)}, u32[]{:S(2)}, u32[]{:S(2)}) async-start(bf16[128,17,256]{2,1,0:T(8,128)(2,1)} %pad_maximum_fusion.2), calls=%async_computation | async-start | bytes 3145728 | tf_op jit(solution)/shard_map/all_to_all | solution.py:315
  38.1 0.8 copy-start.6
  66.2 5.4 %copy-start.7 = (f32[2,4,512,256]{3,2,1,0:T(8,128)S(1)}, f32[2,4,512,256]{3,2,1,0:T(8,128)}, u32[]{:S(2)}) copy-start(f32[2,4,512,256]{3,2,1,0:T(8,128)} %get-tuple-element.13) | copy-start | bytes 12582916
  66.3 5.4 %copy-start.8 = (f32[2,4,512,256]{3,2,1,0:T(8,128)S(1)}, f32[2,4,512,256]{3,2,1,0:T(8,128)}, u32[]{:S(2)}) copy-start(f32[2,4,512,256]{3,2,1,0:T(8,128)} %get-tuple-element.11) | copy-start | bytes 12582916
  66.3 5.4 %copy-start.12 = (f32[256]{0:T(256)S(1)}, f32[256]{0:T(256)}, u32[]{:S(2)}) copy-start(f32[256]{0:T(256)} %param.16) | copy-start | bytes 3076
  76.7 5.8 %copy-start.9 = (bf16[9,256,128]{2,1,0:T(8,128)(2,1)S(1)}, bf16[9,256,128]{2,1,0:T(8,128)(2,1)}, u32[]{:S(2)}) copy-start(bf16[9,256,128]{2,1,0:T(8,128)(2,1)} %k_ref.7) | copy-start | bytes 1769476
  76.9 24.5 %collective-permute-start.3 = (bf16[2,1,512,512]{3,2,1,0:T(8,128)(2,1)S(1)}, bf16[2,1,512,512]{3,2,1,0:T(8,128)(2,1)S(1)}, u32[]{:S(2)}, u32[]{:S(2)}) collective-permute-start(bf16[2,1,512,512]{3,2,1,0:T(8,128)(2,1)S(1)} %get-tuple-element.20), channel_id=1, source_target_pairs={{1,0},{2,1},{3,2},{4,3},{5,4},{6,5},{7,6},{8,7},{9,8},{10,9},{11,1... | collective-permute-start | bytes 3145736 | tf_op jit(solution)/shard_map/ppermute | solution.py:230
  80.4 25.4 %collective-permute-start.2 = (bf16[2,1,512,512]{3,2,1,0:T(8,128)(2,1)S(1)}, bf16[2,1,512,512]{3,2,1,0:T(8,128)(2,1)S(1)}, u32[]{:S(2)}, u32[]{:S(2)}) collective-permute-start(bf16[2,1,512,512]{3,2,1,0:T(8,128)(2,1)S(1)} %get-tuple-element.21), channel_id=1, source_target_pairs={{0,1},{1,2},{2,3},{3,4},{4,5},{5,6},{6,7},{7,8},{8,9},{9,10},{10,1... | collective-permute-start | bytes 3145736 | tf_op jit(solution)/shard_map/ppermute | solution.py:229
  101.7 5.0 %copy-start.2 = (bf16[2,1,512,512]{3,2,1,0:T(8,128)(2,1)}, bf16[2,1,512,512]{3,2,1,0:T(8,128)(2,1)S(1)}, u32[]{:S(2)}) copy-start(bf16[2,1,512,512]{3,2,1,0:T(8,128)(2,1)S(1)} %reverse_select_fusion.after_ref) | copy-start | bytes 3145732
  105.8 1.0 copy-start.5
  128.3 3.3 %copy-start.4 = (bf16[1,1,2,4,512,128]{5,4,3,2,1,0:T(8,128)(2,1)S(1)}, bf16[1,1,2,4,512,128]{5,4,3,2,1,0:T(8,128)(2,1)}, u32[]{:S(2)}) copy-start(bf16[1,1,2,4,512,128]{5,4,3,2,1,0:T(8,128)(2,1)} %param.19) | copy-start | bytes 3145732

commit v5 on v4

--- a/solution.py
+++ b/solution.py
@@ -92,7 +92,12 @@
     return out, margins
 
 
-def back_kernel(src_ref, before_ref, after_ref, k_ref, out_ref, margin_ref):
+def back_kernel(src_ref, before_ref, after_ref, k_ref, *rest):
+    if len(rest) == 3:
+        residual_ref, out_ref, margin_ref = rest
+    else:
+        residual_ref = None
+        out_ref, margin_ref = rest
     band = pl.program_id(0)
     _, rows, cols, cout = out_ref.shape
     width = src_ref.shape[3]
@@ -110,16 +115,24 @@
     z_left, z_mid, z_right = products
     from_left = jnp.where(col == 0, 0.0, pltpu.roll(z_left, 1, 0))
     from_right = jnp.where(col == cols - 1, 0.0, pltpu.roll(z_right, pixels - 1, 0))
-    out_ref[0] = (z_mid + from_left + from_right).reshape(rows, cols, cout)
+    total = (z_mid + from_left + from_right).reshape(rows, cols, cout)
+    if residual_ref is not None:
+        total = total + residual_ref[0].astype(jnp.float32)
+    out_ref[0] = total
     margin_ref[0, 0] = z_right.reshape(rows, cols, cout)[:, 0, :]
     margin_ref[0, 1] = z_left.reshape(rows, cols, cout)[:, cols - 1, :]
 
 
-def conv_back(pieces, first, width, kernel):
+def conv_back(pieces, first, width, kernel, residual=None):
     source, before, after = pieces
     bands, rows, cols, _ = source.shape
     cout = kernel.shape[1]
     block = first // width
+    extra_specs = []
+    extra_args = ()
+    if residual is not None:
+        extra_specs = [pl.BlockSpec((1, rows, cols, cout), lambda b: (b, 0, 0, 0))]
+        extra_args = (residual,)
     return pl.pallas_call(
         back_kernel,
         grid=(bands,),
@@ -128,7 +141,8 @@
             pl.BlockSpec((1, 1, cols, width), lambda b: (b, 0, 0, block)),
             pl.BlockSpec((1, 1, cols, width), lambda b: (b, 0, 0, block)),
             pl.BlockSpec(kernel.shape, lambda b: (0, 0, 0)),
-        ],
+        ]
+        + extra_specs,
         out_specs=[
             pl.BlockSpec((1, rows, cols, cout), lambda b: (b, 0, 0, 0)),
             pl.BlockSpec((1, 2, rows, cout), lambda b: (b, 0, 0, 0)),
@@ -138,7 +152,7 @@
             jax.ShapeDtypeStruct((bands, 2, rows, cout), jnp.float32),
         ],
         compiler_params=pltpu.CompilerParams(vmem_limit_bytes=60 * 1024 * 1024),
-    )(source, before, after, kernel)
+    )(source, before, after, kernel, *extra_args)
 
 
 def conv_gather_kernel(count, first, width, block_ref, src_ref, before_ref, after_ref, k_ref,
@@ -368,7 +382,7 @@
     grad_pre = jax.vjp(activation, pre_act)[1](grad_inner)[0].astype(jnp.bfloat16)
 
     pair = extend_rows(jnp.concatenate([inner, grad_pre], axis=3), last_tile)
-    pre_back, pre_margins = conv_back(pair, lifted, lifted, kernel_one)
+    pre_back, pre_margins = conv_back(pair, lifted, lifted, kernel_one, cot_field)
     parts = [edge_cols(pair, 0, lifted), jnp.swapaxes(pre_margins, 1, 2)]
     second_out, landed = conv_gather(pair, 0, lifted, pack_parts(parts), kernel_two, 1)
     inner_edges, pre_gathered = unpack_parts(landed, parts)
@@ -376,7 +390,14 @@
 
     second_out = at_edges(second_out, second_sides[:, 0], second_sides[:, 1])
     analysis = (base_field.astype(jnp.float32) + second_out + bias_two).astype(jnp.bfloat16)
-    grad_base = cot_field.astype(jnp.float32) + return_sides(pre_back, pre_gathered, matching_row)
+    left_back, right_back = pick_partner(pre_gathered, matching_row)
+    last_col = column_count - 1
+    grad_base = lax.dynamic_update_slice(
+        pre_back, pre_back[:, :, 0:1] + left_back[:, :, None], (0, 0, 0, 0)
+    )
+    grad_base = lax.dynamic_update_slice(
+        grad_base, pre_back[:, :, last_col:] + right_back[:, :, None], (0, 0, last_col, 0)
+    )
     return (analysis[None, None], grad_base[None, None])
 
 

time: 138 us -> 140 us (1.014)
  local copies, waits for them, and re-layouts: 10.9 us -> 13.6 us
    dynamic_update_slice x0 -> x2, local copies, waits for them, and re-layouts: none -> 2.8 us  [the longest x1 1.4 us: per_device(): lax.dynamic_update_slice(pre_back, pre_back[:, :, 0:1] + left_back[:, :,...]
    broadcast_in_dim x1 -> x2, other arithmetic: 5.17 us -> 4.02 us  [per_device(): return (analysis[None, None], grad_base[None, None])]
    unnamed x54 -> x56, local copies, waits for them, and re-layouts: 4 us -> 3.93 us
where the time goes in v5:
time: 140 us; the launch traced here: 139 us
  Pallas kernels  39.7 us (28%)
  other arithmetic  25.2 us (18%)
  starting transfers between devices  23.7 us (17%)
  waiting for transfers between devices  20.5 us (15%)
  local copies, waits for them, and re-layouts  13.6 us (10%)
  matrix products  8.13 us (6%)
  between operations  7.66 us (5%)
    pallas_call x2, Pallas kernels, conv_gather(): pl.pallas_call(functools.partial(conv_gather_kernel, count, first, width)...  25.3 us
    ppermute x2, waiting for transfers between devices, extend_rows(): after = lax.ppermute(head, 'tile', [(i + 1, i) for i in range(count - 1)])  16.5 us
    pallas_call x2, Pallas kernels, conv_back(): pl.pallas_call(back_kernel, grid=(bands,), in_specs=[pl.BlockSpec((1, row...  14.4 us
    all_to_all x1, starting transfers between devices, route_observations(): lax.all_to_all(payload, ('face', 'tile'), split_axis=0, concat_axis=0, ti...  11.6 us
    ppermute x2, starting transfers between devices, extend_rows(): after = lax.ppermute(head, 'tile', [(i + 1, i) for i in range(count - 1)])  8.01 us
    dot_general x1, matrix products, per_device(): gridded = jnp.dot(onehot, got_values, preferred_element_type=jnp.float32)  5.34 us
    convert_element_type x1, other arithmetic, per_device(): inner = activation(pre_act).astype(jnp.bfloat16)  5.04 us
    ppermute x2, starting transfers between devices, extend_rows(): before = lax.ppermute(tail, 'tile', [(i, i + 1) for i in range(count - 1)])  4.06 us
  transfers between devices with their start and end apart: 5, of which 2 were waited for; matrix products, arithmetic and copies ran while one was open for 13% of the time, Pallas kernels for 14%

profile of v5, /device:TPU:24, one launch (start us, length us, event | category | flops | bytes accessed | tf_op | source)
XLA Modules:
  0.0 138.5 jit_solution(999342987121640300)
XLA Ops:
  0.6 0.0 copy-start
  0.6 2.3 %fusion.19 = (bf16[2,1,512,256]{3,2,1,0:T(8,128)(2,1)}, bf16[2,1,512,256]{3,2,1,0:T(8,128)(2,1)}) fusion(bf16[2,4,512,128]{3,2,1,0:T(8,128)(2,1)} %bitcast.243, bf16[2,4,512,128]{3,2,1,0:T(8,128)(2,1)} %bitcast.246), kind=kLoop, calls=%fused_computation.50 | loop fusion | flops 2097152 | bytes 3145728 | tf_op jit(solution)/shard_map/concatenate | solution.py:372
  3.0 4.5 %collective-permute-start.1 = (bf16[2,1,512,256]{3,2,1,0:T(8,128)(2,1)}, bf16[2,1,512,256]{3,2,1,0:T(8,128)(2,1)}, u32[]{:S(2)}, u32[]{:S(2)}) collective-permute-start(bf16[2,1,512,256]{3,2,1,0:T(8,128)(2,1)} %get-tuple-element.24), channel_id=1, source_target_pairs={{1,0},{2,1},{3,2},{4,3},{5,4},{6,5},{7,6},{8,7},{9,8},{10,9},{11,1... | collective-permute-start | bytes 1572872 | tf_op jit(solution)/shard_map/ppermute | solution.py:244
  7.5 1.9 %collective-permute-start = (bf16[2,1,512,256]{3,2,1,0:T(8,128)(2,1)}, bf16[2,1,512,256]{3,2,1,0:T(8,128)(2,1)}, u32[]{:S(2)}, u32[]{:S(2)}) collective-permute-start(bf16[2,1,512,256]{3,2,1,0:T(8,128)(2,1)} %get-tuple-element.25), channel_id=1, source_target_pairs={{0,1},{1,2},{2,3},{3,4},{4,5},{5,6},{6,7},{7,8},{8,9},{9,10},{10,1... | collective-permute-start | bytes 1572872 | tf_op jit(solution)/shard_map/ppermute | solution.py:243
  9.4 1.3 convert_reduce_fusion
  10.7 0.7 multiply_add_fusion.1
  11.4 1.6 %select_reduce_fusion = s32[2048]{0:T(1024)S(1)} fusion(s32[1024]{0:T(1024)} %param.13, s32[1024]{0:T(1024)S(1)} %multiply_add_fusion.1), kind=kLoop, calls=%fused_computation.6 | loop fusion | flops 6289408 | bytes 16384 | tf_op jit(solution)/shard_map/reduce_sum | solution.py:320
  13.0 0.1 reduce_sum.22
  13.1 0.1 fusion.52
  13.2 0.1 pad.43.clone
  13.3 0.1 maximum_bitcast_fusion
  13.4 0.1 copy.129
  13.5 1.6 %fusion.14 = bf16[2048,256]{1,0:T(8,128)(2,1)S(1)} fusion(bf16[1024,256]{1,0:T(8,128)(2,1)S(1)} %copy-done, s32[1024]{0:T(1024)S(1)} %multiply_add_fusion.1), kind=kOutput, calls=%fused_computation.34 | convolution fusion | flops 1076363264 | bytes 1576960 | tf_op jit(solution)/shard_map/dot_general | solution.py:317
  15.2 1.3 pad_maximum_fusion.2
  16.5 11.6 %all-to-all-start = ((bf16[128,17,256]{2,1,0:T(8,128)(2,1)}), bf16[128,17,256]{2,1,0:T(8,128)(2,1)}, u32[]{:S(2)}, u32[]{:S(2)}) async-start(bf16[128,17,256]{2,1,0:T(8,128)(2,1)} %pad_maximum_fusion.2), calls=%async_computation | async-start | bytes 3145728 | tf_op jit(solution)/shard_map/all_to_all | solution.py:329
  28.2 0.1 constant_dynamic-slice_fusion.8
  28.3 0.1 copy.126
  28.4 0.7 fusion.153
  29.1 1.5 %pad_maximum_fusion.1.src_ref = bf16[2,4,512,256]{3,2,1,0:T(8,128)(2,1)} fusion(bf16[2,4,512,128]{3,2,1,0:T(8,128)(2,1)S(1)} %bitcast.248, bf16[2,4,512,128]{3,2,1,0:T(8,128)(2,1)S(1)} %bitcast.244), kind=kLoop, calls=%fused_computation.31 | loop fusion | flops 4194304 | bytes 4194304 | tf_op jit(solution)/shard_map/concatenate | solution.py:372
  36.8 1.3 reverse_select_fusion.1.after_ref
  38.2 0.7 copy-done.5
  38.9 6.4 %shard_map.113 = (f32[2,4,512,256]{3,2,1,0:T(8,128)}, f32[2,2,4,256]{3,2,1,0:T(4,128)}) custom-call(bf16[2,4,512,256]{3,2,1,0:T(8,128)(2,1)} %pad_maximum_fusion.1.src_ref, bf16[2,1,512,256]{3,2,1,0:T(8,128)(2,1)} %collective-permute-done.before_ref, bf16[2,1,512,256]{3,2,1,0:T(8,128)(2,1)} %copy-done.5, bf16[9,256,128]{2,1,0:T(8,128)(2,1)} %k_ref.7), custom_call_target="tpu_custom_call" | custom-call | tf_op jit(solution)/shard_map/pallas_call | solution.py:136
  45.3 0.7 copy.125
  46.0 1.0 slice.392
  47.1 0.6 maximum_bitcast_fusion.2.block_ref
  47.7 12.9 %shard_map.114 = (f32[2,4,512,256]{3,2,1,0:T(8,128)}, f32[8,56,128]{2,1,0:T(8,128)}) custom-call(f32[56,128]{1,0:T(8,128)} %maximum_bitcast_fusion.2.block_ref, bf16[2,4,512,256]{3,2,1,0:T(8,128)(2,1)} %pad_maximum_fusion.1.src_ref, bf16[2,1,512,256]{3,2,1,0:T(8,128)(2,1)} %collective-permute-done.before_ref, bf16[2,1,512,256]{3,2,1,0:T(8,128)(2,1)} %copy-done.5, ...), custom_call_target="tpu_custom_call" | custom-call | tf_op jit(solution)/shard_map/pallas_call | solution.py:195
  60.6 1.0 copy.205
  61.6 0.6 gather_fusion
  62.2 0.1 broadcast_select_fusion.1
  62.8 0.1 convolution_bitcast_fusion.1
  62.9 0.1 convolution_bitcast_fusion
  63.0 0.1 convolution_bitcast_fusion.3
  63.2 0.1 convolution_bitcast_fusion.2
  63.5 1.4 fusion.55
  64.8 0.1 add.155
  64.9 1.3 slice.417
  66.3 5.3 %fusion = f32[2,4,512,256]{3,2,1,0:T(8,128)S(1)} fusion(bf16[2048,256,1,1]{1,0,3,2:T(8,128)(2,1)S(1)} %bitcast.249, s32[2048]{0:T(1024)S(1)} %add.155, s32[2,4,512]{2,1,0:T(4,128)S(1)} %multiply_add_fusion), kind=kOutput, calls=%fused_computation.2 | convolution fusion | flops 4303355904 | bytes 5267456 | tf_op jit(solution)/shard_map/dot_general | solution.py:365
  71.7 5.0 %multiply_convert_fusion = (bf16[2,4,512,256]{3,2,1,0:T(8,128)(2,1)S(1)}, bf16[2,4,512,256]{3,2,1,0:T(8,128)(2,1)S(1)}) fusion(f32[2,4,512,256]{3,2,1,0:T(8,128)S(1)} %fusion, f32[256]{0:T(256)S(1)} %copy-done.11, f32[2,4,256]{2,1,0:T(4,128)S(1)} %get-tuple-element.49, pred[512]{0:T(512)(128)(4,1)S(1)} %get-tuple-element.86, ...), kind=kLoop, calls=%fused_computation.23 | loop fusion | flops 33554432 | bytes 16812032 | tf_op jit(solution)/shard_map/convert_element_type | solution.py:380
  76.7 0.2 fusion.17
  76.9 3.5 %collective-permute-start.3 = (bf16[2,1,512,512]{3,2,1,0:T(8,128)(2,1)S(1)}, bf16[2,1,512,512]{3,2,1,0:T(8,128)(2,1)S(1)}, u32[]{:S(2)}, u32[]{:S(2)}) collective-permute-start(bf16[2,1,512,512]{3,2,1,0:T(8,128)(2,1)S(1)} %get-tuple-element.20), channel_id=1, source_target_pairs={{1,0},{2,1},{3,2},{4,3},{5,4},{6,5},{7,6},{8,7},{9,8},{10,9},{11,1... | collective-permute-start | bytes 3145736 | tf_op jit(solution)/shard_map/ppermute | solution.py:244
  80.4 2.1 %collective-permute-start.2 = (bf16[2,1,512,512]{3,2,1,0:T(8,128)(2,1)S(1)}, bf16[2,1,512,512]{3,2,1,0:T(8,128)(2,1)S(1)}, u32[]{:S(2)}, u32[]{:S(2)}) collective-permute-start(bf16[2,1,512,512]{3,2,1,0:T(8,128)(2,1)S(1)} %get-tuple-element.21), channel_id=1, source_target_pairs={{0,1},{1,2},{2,3},{3,4},{4,5},{5,6},{6,7},{7,8},{8,9},{9,10},{10,1... | collective-permute-start | bytes 3145736 | tf_op jit(solution)/shard_map/ppermute | solution.py:243
  82.6 2.3 %pad_maximum_fusion.src_ref = bf16[2,4,512,512]{3,2,1,0:T(8,128)(2,1)} fusion(bf16[2,4,512,256]{3,2,1,0:T(8,128)(2,1)S(1)} %get-tuple-element.19, bf16[2,4,512,256]{3,2,1,0:T(8,128)(2,1)S(1)} %get-tuple-element.18), kind=kLoop, calls=%fused_computation.13 | loop fusion | flops 8388608 | bytes 8388608 | tf_op jit(solution)/shard_map/concatenate | solution.py:384
  84.9 16.5 %collective-permute-done.3 = bf16[2,1,512,512]{3,2,1,0:T(8,128)(2,1)S(1)} collective-permute-done((bf16[2,1,512,512]{3,2,1,0:T(8,128)(2,1)S(1)}, bf16[2,1,512,512]{3,2,1,0:T(8,128)(2,1)S(1)}, u32[]{:S(2)}, u32[]{:S(2)}) %collective-permute-start.3) | collective-permute-done | bytes 1048608 | tf_op jit(solution)/shard_map/ppermute | solution.py:244
  101.4 0.3 reverse_select_fusion.after_ref
  101.8 4.0 %collective-permute-done.2.before_ref = bf16[2,1,512,512]{3,2,1,0:T(8,128)(2,1)S(1)} collective-permute-done((bf16[2,1,512,512]{3,2,1,0:T(8,128)(2,1)S(1)}, bf16[2,1,512,512]{3,2,1,0:T(8,128)(2,1)S(1)}, u32[]{:S(2)}, u32[]{:S(2)}) %collective-permute-start.2) | collective-permute-done | bytes 1048608 | tf_op jit(solution)/shard_map/ppermute | solution.py:243
  105.8 0.9 copy-done.4
  106.7 8.1 %shard_map.115 = (f32[2,4,512,128]{3,2,1,0:T(8,128)}, f32[2,2,4,128]{3,2,1,0:T(4,128)}) custom-call(bf16[2,4,512,512]{3,2,1,0:T(8,128)(2,1)} %pad_maximum_fusion.src_ref, bf16[2,1,512,512]{3,2,1,0:T(8,128)(2,1)} %copy-done.4, bf16[2,1,512,512]{3,2,1,0:T(8,128)(2,1)} %copy-done.2, bf16[9,128,256]{2,1,0:T(8,128)(2,1)} %k_ref.6, bf16[2,4,512,128]{3,2,1,0:T(8,128)(2,1)} %bitcast.247), custom_call_target="tpu_custom_call" | custom-call | tf_op jit(solution)/shard_map/pallas_call | solution.py:136
  114.8 0.7 copy.132
  115.5 0.6 maximum_bitcast_fusion.1.block_ref
  116.1 12.4 %shard_map.116 = (f32[2,4,512,128]{3,2,1,0:T(8,128)}, f32[8,64,128]{2,1,0:T(8,128)}) custom-call(f32[64,128]{1,0:T(8,128)} %maximum_bitcast_fusion.1.block_ref, bf16[2,4,512,512]{3,2,1,0:T(8,128)(2,1)} %pad_maximum_fusion.src_ref, bf16[2,1,512,512]{3,2,1,0:T(8,128)(2,1)} %copy-done.4, bf16[2,1,512,512]{3,2,1,0:T(8,128)(2,1)} %copy-done.2, ...), custom_call_target="tpu_custom_call" | custom-call | tf_op jit(solution)/shard_map/pallas_call | solution.py:195
  128.5 1.1 copy.204
  129.6 0.6 gather_fusion.1
  130.2 0.1 broadcast_select_fusion
  130.5 0.1 constant_dynamic-slice_fusion.3
  130.6 0.1 rev.36
  130.8 0.1 rev.37
  131.1 0.8 add_bitcast_fusion
  131.9 1.4 %dynamic_update_slice.8 = f32[1,1,2,4,512,128]{5,4,3,2,1,0:T(8,128)} dynamic-update-slice(f32[1,1,2,4,512,128]{5,4,3,2,1,0:T(8,128)} %bitcast.300, f32[1,1,2,4,1,128]{5,4,3,2,1,0:T(1,128)S(1)} %get-tuple-element.23, s32[]{:T(128)} %constant.111.clone.1, s32[]{:T(128)} %constant.111.clone.1, s32[]{:T(128)} %constant.111.clone.1, s32[]{:T(128)} %constant.111.clone.1, s32[]{:T(128)} %constant.111.clone.1, ...) | dynamic-update-slice | bytes 8196 | tf_op jit(solution)/shard_map/dynamic_update_slice | solution.py:395
  133.3 0.1 convolution_bitcast_fusion.5
  133.4 0.1 convolution_bitcast_fusion.4
  133.6 0.2 convolution_bitcast_fusion.7
  133.7 0.2 convolution_bitcast_fusion.6
  133.9 1.4 %dynamic_update_slice.9 = f32[1,1,2,4,512,128]{5,4,3,2,1,0:T(8,128)} dynamic-update-slice(f32[1,1,2,4,512,128]{5,4,3,2,1,0:T(8,128)} %dynamic_update_slice.8, f32[1,1,2,4,1,128]{5,4,3,2,1,0:T(1,128)S(1)} %get-tuple-element.22, s32[]{:T(128)} %constant.111.clone.1, s32[]{:T(128)} %constant.111.clone.1, s32[]{:T(128)} %constant.111.clone.1, s32[]{:T(128)} %constant.111.clone.1, ...) | dynamic-update-slice | bytes 8196 | tf_op jit(solution)/shard_map/dynamic_update_slice | solution.py:398
  135.3 3.2 %fusion.15 = bf16[1,1,2,4,512,128]{5,4,3,2,1,0:T(8,128)(2,1)} fusion(f32[2,4,512,128]{3,2,1,0:T(8,128)} %get-tuple-element.15, f32[128]{0:T(128)S(1)} %copy-done.12, f32[2,4,128]{2,1,0:T(4,128)S(1)} %get-tuple-element.51, f32[2,4,128]{2,1,0:T(4,128)S(1)} %get-tuple-element.50, pred[512]{0:T(512)(128)(4,1)S(1)} %get-tuple-element.86, ...), kind=kLoop, calls=%fused_computation.45 | loop fusion | flops 4194304 | bytes 4204032 | tf_op jit(solution)/shard_map/broadcast_in_dim | solution.py:401
  (107 shorter events, 1.0 us)
Async XLA Ops:
  0.6 12.9 %copy-start = (bf16[1024,256]{1,0:T(8,128)(2,1)S(1)}, bf16[1024,256]{1,0:T(8,128)(2,1)}, u32[]{:S(2)}) copy-start(bf16[1024,256]{1,0:T(8,128)(2,1)} %param.11) | copy-start | bytes 1572868
  3.0 33.8 %collective-permute-start.1 = (bf16[2,1,512,256]{3,2,1,0:T(8,128)(2,1)}, bf16[2,1,512,256]{3,2,1,0:T(8,128)(2,1)}, u32[]{:S(2)}, u32[]{:S(2)}) collective-permute-start(bf16[2,1,512,256]{3,2,1,0:T(8,128)(2,1)} %get-tuple-element.24), channel_id=1, source_target_pairs={{1,0},{2,1},{3,2},{4,3},{5,4},{6,5},{7,6},{8,7},{9,8},{10,9},{11,1... | collective-permute-start | bytes 1572872 | tf_op jit(solution)/shard_map/ppermute | solution.py:244
  7.5 30.6 %collective-permute-start = (bf16[2,1,512,256]{3,2,1,0:T(8,128)(2,1)}, bf16[2,1,512,256]{3,2,1,0:T(8,128)(2,1)}, u32[]{:S(2)}, u32[]{:S(2)}) collective-permute-start(bf16[2,1,512,256]{3,2,1,0:T(8,128)(2,1)} %get-tuple-element.25), channel_id=1, source_target_pairs={{0,1},{1,2},{2,3},{3,4},{4,5},{5,6},{6,7},{7,8},{8,9},{9,10},{10,1... | collective-permute-start | bytes 1572872 | tf_op jit(solution)/shard_map/ppermute | solution.py:243
  15.1 13.1 %copy-start.10 = (s32[8,2,3]{0,1,2:T(2,128)S(1)}, s32[8,2,3]{0,1,2:T(2,128)}, u32[]{:S(2)}) copy-start(s32[8,2,3]{0,1,2:T(2,128)} %param.14) | copy-start | bytes 580
  15.1 13.9 %copy-start.1 = (bf16[1,1,2,4,512,128]{5,4,3,2,1,0:T(8,128)(2,1)S(1)}, bf16[1,1,2,4,512,128]{5,4,3,2,1,0:T(8,128)(2,1)}, u32[]{:S(2)}) copy-start(bf16[1,1,2,4,512,128]{5,4,3,2,1,0:T(8,128)(2,1)} %param.10) | copy-start | bytes 3145732
  15.2 13.9 %copy-start.3 = (bf16[1,1,2,4,512,128]{5,4,3,2,1,0:T(8,128)(2,1)S(1)}, bf16[1,1,2,4,512,128]{5,4,3,2,1,0:T(8,128)(2,1)}, u32[]{:S(2)}) copy-start(bf16[1,1,2,4,512,128]{5,4,3,2,1,0:T(8,128)(2,1)} %param.19) | copy-start | bytes 3145732
  16.5 20.2 %copy-start.9 = (bf16[9,128,256]{2,1,0:T(8,128)(2,1)S(1)}, bf16[9,128,256]{2,1,0:T(8,128)(2,1)}, u32[]{:S(2)}) copy-start(bf16[9,128,256]{2,1,0:T(8,128)(2,1)} %k_ref.6) | copy-start | bytes 1769476
  16.5 46.9 %all-to-all-start = ((bf16[128,17,256]{2,1,0:T(8,128)(2,1)}), bf16[128,17,256]{2,1,0:T(8,128)(2,1)}, u32[]{:S(2)}, u32[]{:S(2)}) async-start(bf16[128,17,256]{2,1,0:T(8,128)(2,1)} %pad_maximum_fusion.2), calls=%async_computation | async-start | bytes 3145728 | tf_op jit(solution)/shard_map/all_to_all | solution.py:329
  38.1 0.8 copy-start.5
  66.2 5.4 %copy-start.6 = (f32[2,4,512,256]{3,2,1,0:T(8,128)S(1)}, f32[2,4,512,256]{3,2,1,0:T(8,128)}, u32[]{:S(2)}) copy-start(f32[2,4,512,256]{3,2,1,0:T(8,128)} %get-tuple-element.13) | copy-start | bytes 12582916
  66.3 5.4 %copy-start.7 = (f32[2,4,512,256]{3,2,1,0:T(8,128)S(1)}, f32[2,4,512,256]{3,2,1,0:T(8,128)}, u32[]{:S(2)}) copy-start(f32[2,4,512,256]{3,2,1,0:T(8,128)} %get-tuple-element.11) | copy-start | bytes 12582916
  66.3 5.4 %copy-start.11 = (f32[256]{0:T(256)S(1)}, f32[256]{0:T(256)}, u32[]{:S(2)}) copy-start(f32[256]{0:T(256)} %param.16) | copy-start | bytes 3076
  76.7 5.8 %copy-start.8 = (bf16[9,256,128]{2,1,0:T(8,128)(2,1)S(1)}, bf16[9,256,128]{2,1,0:T(8,128)(2,1)}, u32[]{:S(2)}) copy-start(bf16[9,256,128]{2,1,0:T(8,128)(2,1)} %k_ref.7) | copy-start | bytes 1769476
  76.9 24.5 %collective-permute-start.3 = (bf16[2,1,512,512]{3,2,1,0:T(8,128)(2,1)S(1)}, bf16[2,1,512,512]{3,2,1,0:T(8,128)(2,1)S(1)}, u32[]{:S(2)}, u32[]{:S(2)}) collective-permute-start(bf16[2,1,512,512]{3,2,1,0:T(8,128)(2,1)S(1)} %get-tuple-element.20), channel_id=1, source_target_pairs={{1,0},{2,1},{3,2},{4,3},{5,4},{6,5},{7,6},{8,7},{9,8},{10,9},{11,1... | collective-permute-start | bytes 3145736 | tf_op jit(solution)/shard_map/ppermute | solution.py:244
  80.4 25.4 %collective-permute-start.2 = (bf16[2,1,512,512]{3,2,1,0:T(8,128)(2,1)S(1)}, bf16[2,1,512,512]{3,2,1,0:T(8,128)(2,1)S(1)}, u32[]{:S(2)}, u32[]{:S(2)}) collective-permute-start(bf16[2,1,512,512]{3,2,1,0:T(8,128)(2,1)S(1)} %get-tuple-element.21), channel_id=1, source_target_pairs={{0,1},{1,2},{2,3},{3,4},{4,5},{5,6},{6,7},{7,8},{8,9},{9,10},{10,1... | collective-permute-start | bytes 3145736 | tf_op jit(solution)/shard_map/ppermute | solution.py:243
  101.7 5.0 %copy-start.2 = (bf16[2,1,512,512]{3,2,1,0:T(8,128)(2,1)}, bf16[2,1,512,512]{3,2,1,0:T(8,128)(2,1)S(1)}, u32[]{:S(2)}) copy-start(bf16[2,1,512,512]{3,2,1,0:T(8,128)(2,1)S(1)} %reverse_select_fusion.after_ref) | copy-start | bytes 3145732
  105.8 1.0 copy-start.4
  128.5 6.8 %copy-start.12 = (f32[128]{0:T(128)S(1)}, f32[128]{0:T(128)}, u32[]{:S(2)}) copy-start(f32[128]{0:T(128)} %param.18) | copy-start | bytes 1540

commit v6 on v4

--- a/solution.py
+++ b/solution.py
@@ -141,34 +141,58 @@
     )(source, before, after, kernel)
 
 
-def conv_gather_kernel(count, first, width, block_ref, src_ref, before_ref, after_ref, k_ref,
+def conv_gather_kernel(count, block_ref, src_ref, before_ref, after_ref, k_ref,
                        out_ref, gathered_ref, landed, send_sems, recv_sems):
+    step_at = pl.program_id(0)
     face = lax.axis_index("face")
     tile = lax.axis_index("tile")
-    barrier = pltpu.get_barrier_semaphore()
-    for step in range(1, count):
-        peer = lax.rem(face + step, count)
-        pl.semaphore_signal(barrier, inc=1, device_id=(peer, tile), device_id_type=MESH_IDS)
-    pl.semaphore_wait(barrier, count - 1)
     copies = []
     for step in range(1, count):
         peer = lax.rem(face + step, count)
-        copy = pltpu.make_async_remote_copy(
-            src_ref=block_ref,
-            dst_ref=landed.at[step],
-            send_sem=send_sems.at[step],
-            recv_sem=recv_sems.at[step],
-            device_id=(peer, tile),
-            device_id_type=MESH_IDS,
+        copies.append(
+            pltpu.make_async_remote_copy(
+                src_ref=block_ref,
+                dst_ref=landed.at[step],
+                send_sem=send_sems.at[step],
+                recv_sem=recv_sems.at[step],
+                device_id=(peer, tile),
+                device_id_type=MESH_IDS,
+            )
         )
-        copy.start()
-        copies.append(copy)
-    gathered_ref[0] = block_ref[...]
-    conv_kernel(False, first, width, src_ref, before_ref, after_ref, None, k_ref, out_ref, None)
-    for copy in copies:
-        copy.wait()
-    for step in range(1, count):
-        gathered_ref[step] = landed[step]
+
+    @pl.when(step_at == 0)
+    def _():
+        barrier = pltpu.get_barrier_semaphore()
+        for step in range(1, count):
+            peer = lax.rem(face + step, count)
+            pl.semaphore_signal(barrier, inc=1, device_id=(peer, tile), device_id_type=MESH_IDS)
+        pl.semaphore_wait(barrier, count - 1)
+        for copy in copies:
+            copy.start()
+        gathered_ref[0] = block_ref[...]
+
+    _, rows, cols, cout = out_ref.shape
+    width = src_ref.shape[3]
+    pixels = rows * cols
+    col = lax.broadcasted_iota(jnp.int32, (rows, cols, cout), 1).reshape(pixels, cout)
+    ext = jnp.concatenate([before_ref[0], src_ref[0], after_ref[0]], axis=0)
+    lhs = jnp.concatenate([ext[dy : dy + rows].reshape(pixels, width) for dy in range(3)], axis=1)
+    products = []
+    for col_tap in range(3):
+        taps = [k_ref[3 * (dy + step_at * (2 - 2 * dy)) + col_tap] for dy in range(3)]
+        stack = jnp.concatenate(taps, axis=0)
+        products.append(jnp.dot(lhs, stack, preferred_element_type=jnp.float32))
+    z_left, z_mid, z_right = products
+    from_left = jnp.where(col == 0, 0.0, pltpu.roll(z_left, 1, 0))
+    from_right = jnp.where(col == cols - 1, 0.0, pltpu.roll(z_right, pixels - 1, 0))
+    out_ref[0] = (z_mid + from_left + from_right).reshape(rows, cols, cout)
+
+    @pl.when(step_at == pl.num_programs(0) - 1)
+    def _():
+        for copy in copies:
+            copy.wait()
+        for step in range(1, count):
+            gathered_ref[step] = landed[step]
 
 
 def conv_gather(pieces, first, width, block, kernel, gather_id):
@@ -177,11 +201,21 @@
     cout = kernel.shape[2]
     count = lax.axis_size("face")
     block_rows, lanes = block.shape
-    vmem = pl.BlockSpec(memory_space=pltpu.VMEM)
+    lane_block = first // width
     return pl.pallas_call(
-        functools.partial(conv_gather_kernel, count, first, width),
-        in_specs=[vmem] * 5,
-        out_specs=[vmem, vmem],
+        functools.partial(conv_gather_kernel, count),
+        grid=(bands,),
+        in_specs=[
+            pl.BlockSpec((block_rows, lanes), lambda b: (0, 0)),
+            pl.BlockSpec((1, rows, cols, width), lambda b: (b, 0, 0, lane_block)),
+            pl.BlockSpec((1, 1, cols, width), lambda b: (b, 0, 0, lane_block)),
+            pl.BlockSpec((1, 1, cols, width), lambda b: (b, 0, 0, lane_block)),
+            pl.BlockSpec(kernel.shape, lambda b: (0, 0, 0)),
+        ],
+        out_specs=[
+            pl.BlockSpec((1, rows, cols, cout), lambda b: (b, 0, 0, 0)),
+            pl.BlockSpec((count, block_rows, lanes), lambda b: (0, 0, 0)),
+        ],
         out_shape=[
             jax.ShapeDtypeStruct((bands, rows, cols, cout), jnp.float32),
             jax.ShapeDtypeStruct((count, block_rows, lanes), block.dtype),

time: 138 us -> 135 us (0.978)
  Pallas kernels: 39.6 us -> 37 us
    pallas_call x2, Pallas kernels: 25.3 us -> 22.7 us  [conv_gather(): pl.pallas_call(functools.partial(conv_gather_kernel, count), grid=(bands,...]
  transfers between devices with their start and end apart: 5 -> 5, of which waited for: 2 -> 2; matrix products, arithmetic and copies ran while one was open for 13% -> 14% of each run, Pallas kernels for 14% -> 13%
where the time goes in v6:
time: 135 us; the launch traced here: 134 us
  Pallas kernels  37 us (27%)
  other arithmetic  26.4 us (20%)
  starting transfers between devices  23.9 us (18%)
  waiting for transfers between devices  20.3 us (15%)
  local copies, waits for them, and re-layouts  10.9 us (8%)
  matrix products  8.13 us (6%)
  between operations  7.66 us (6%)
    pallas_call x2, Pallas kernels, conv_gather(): pl.pallas_call(functools.partial(conv_gather_kernel, count), grid=(bands,...  22.7 us
    ppermute x2, waiting for transfers between devices, extend_rows(): after = lax.ppermute(head, 'tile', [(i + 1, i) for i in range(count - 1)])  16.8 us
    pallas_call x2, Pallas kernels, conv_back(): pl.pallas_call(back_kernel, grid=(bands,), in_specs=[pl.BlockSpec((1, row...  14.3 us
    all_to_all x1, starting transfers between devices, route_observations(): lax.all_to_all(payload, ('face', 'tile'), split_axis=0, concat_axis=0, ti...  11.6 us
    ppermute x2, starting transfers between devices, extend_rows(): after = lax.ppermute(head, 'tile', [(i + 1, i) for i in range(count - 1)])  8.23 us
    dot_general x1, matrix products, per_device(): gridded = jnp.dot(onehot, got_values, preferred_element_type=jnp.float32)  5.34 us
    broadcast_in_dim x1, other arithmetic, per_device(): return (analysis[None, None], grad_base[None, None])  5.17 us
    convert_element_type x1, other arithmetic, per_device(): inner = activation(pre_act).astype(jnp.bfloat16)  5.04 us
  transfers between devices with their start and end apart: 5, of which 2 were waited for; matrix products, arithmetic and copies ran while one was open for 14% of the time, Pallas kernels for 13%

profile of v6, /device:TPU:24, one launch (start us, length us, event | category | flops | bytes accessed | tf_op | source)
XLA Modules:
  0.0 134.3 jit_solution(15211132913912958226)
XLA Ops:
  0.6 0.0 copy-start
  0.6 2.3 %fusion.19 = (bf16[2,1,512,256]{3,2,1,0:T(8,128)(2,1)}, bf16[2,1,512,256]{3,2,1,0:T(8,128)(2,1)}) fusion(bf16[2,4,512,128]{3,2,1,0:T(8,128)(2,1)} %bitcast.235, bf16[2,4,512,128]{3,2,1,0:T(8,128)(2,1)} %bitcast.238), kind=kLoop, calls=%fused_computation.51 | loop fusion | flops 2097152 | bytes 3145728 | tf_op jit(solution)/shard_map/concatenate | solution.py:392
  3.0 4.5 %collective-permute-start.1 = (bf16[2,1,512,256]{3,2,1,0:T(8,128)(2,1)}, bf16[2,1,512,256]{3,2,1,0:T(8,128)(2,1)}, u32[]{:S(2)}, u32[]{:S(2)}) collective-permute-start(bf16[2,1,512,256]{3,2,1,0:T(8,128)(2,1)} %get-tuple-element.22), channel_id=1, source_target_pairs={{1,0},{2,1},{3,2},{4,3},{5,4},{6,5},{7,6},{8,7},{9,8},{10,9},{11,1... | collective-permute-start | bytes 1572872 | tf_op jit(solution)/shard_map/ppermute | solution.py:264
  7.5 1.9 %collective-permute-start = (bf16[2,1,512,256]{3,2,1,0:T(8,128)(2,1)}, bf16[2,1,512,256]{3,2,1,0:T(8,128)(2,1)}, u32[]{:S(2)}, u32[]{:S(2)}) collective-permute-start(bf16[2,1,512,256]{3,2,1,0:T(8,128)(2,1)} %get-tuple-element.23), channel_id=1, source_target_pairs={{0,1},{1,2},{2,3},{3,4},{4,5},{5,6},{6,7},{7,8},{8,9},{9,10},{10,1... | collective-permute-start | bytes 1572872 | tf_op jit(solution)/shard_map/ppermute | solution.py:263
  9.4 1.3 convert_reduce_fusion
  10.7 0.7 multiply_add_fusion.1
  11.4 1.6 %select_reduce_fusion = s32[2048]{0:T(1024)S(1)} fusion(s32[1024]{0:T(1024)} %param.13, s32[1024]{0:T(1024)S(1)} %multiply_add_fusion.1), kind=kLoop, calls=%fused_computation.6 | loop fusion | flops 6289408 | bytes 16384 | tf_op jit(solution)/shard_map/reduce_sum | solution.py:340
  13.0 0.1 reduce_sum.22
  13.1 0.1 fusion.52
  13.2 0.1 pad.43.clone
  13.3 0.1 maximum_bitcast_fusion
  13.4 0.1 copy.117
  13.5 1.6 %fusion.14 = bf16[2048,256]{1,0:T(8,128)(2,1)S(1)} fusion(bf16[1024,256]{1,0:T(8,128)(2,1)S(1)} %copy-done, s32[1024]{0:T(1024)S(1)} %multiply_add_fusion.1), kind=kOutput, calls=%fused_computation.34 | convolution fusion | flops 1076363264 | bytes 1576960 | tf_op jit(solution)/shard_map/dot_general | solution.py:337
  15.1 0.0 copy-start.11
  15.2 1.3 %pad_maximum_fusion.2 = bf16[128,17,256]{2,1,0:T(8,128)(2,1)} fusion(bf16[128,1,256]{2,1,0:T(2,128)(2,1)S(1)} %copy.117, bf16[128,16,256]{2,1,0:T(8,128)(2,1)S(1)} %bitcast.241), kind=kLoop, calls=%fused_computation.37 | loop fusion | flops 2228224 | bytes 2228224 | tf_op jit(solution)/shard_map/concatenate | solution.py:346
  16.5 11.6 %all-to-all-start = ((bf16[128,17,256]{2,1,0:T(8,128)(2,1)}), bf16[128,17,256]{2,1,0:T(8,128)(2,1)}, u32[]{:S(2)}, u32[]{:S(2)}) async-start(bf16[128,17,256]{2,1,0:T(8,128)(2,1)} %pad_maximum_fusion.2), calls=%async_computation | async-start | bytes 3145728 | tf_op jit(solution)/shard_map/all_to_all | solution.py:349
  28.2 0.1 constant_dynamic-slice_fusion.8
  28.3 0.1 copy.114
  28.4 0.7 fusion.153
  29.1 1.5 %pad_maximum_fusion.1.src_ref = bf16[2,4,512,256]{3,2,1,0:T(8,128)(2,1)} fusion(bf16[2,4,512,128]{3,2,1,0:T(8,128)(2,1)S(1)} %bitcast.239, bf16[2,4,512,128]{3,2,1,0:T(8,128)(2,1)S(1)} %bitcast.236), kind=kLoop, calls=%fused_computation.31 | loop fusion | flops 4194304 | bytes 4194304 | tf_op jit(solution)/shard_map/concatenate | solution.py:392
  36.8 1.3 reverse_select_fusion.1.after_ref
  38.1 0.0 copy-start.6
  38.2 0.7 copy-done.6
  38.9 6.4 %shard_map.113 = (f32[2,4,512,256]{3,2,1,0:T(8,128)}, f32[2,2,4,256]{3,2,1,0:T(4,128)}) custom-call(bf16[2,4,512,256]{3,2,1,0:T(8,128)(2,1)} %pad_maximum_fusion.1.src_ref, bf16[2,1,512,256]{3,2,1,0:T(8,128)(2,1)} %collective-permute-done.before_ref, bf16[2,1,512,256]{3,2,1,0:T(8,128)(2,1)} %copy-done.6, bf16[9,256,128]{2,1,0:T(8,128)(2,1)} %k_ref.7), custom_call_target="tpu_custom_call" | custom-call | tf_op jit(solution)/shard_map/pallas_call | solution.py:123
  45.3 0.7 copy.113
  46.0 1.0 slice.384
  47.1 0.6 maximum_bitcast_fusion.2.block_ref
  47.7 11.7 %shard_map.114 = (f32[2,4,512,256]{3,2,1,0:T(8,128)}, f32[8,56,128]{2,1,0:T(8,128)}) custom-call(f32[56,128]{1,0:T(8,128)} %maximum_bitcast_fusion.2.block_ref, bf16[2,4,512,256]{3,2,1,0:T(8,128)(2,1)} %pad_maximum_fusion.1.src_ref, bf16[2,1,512,256]{3,2,1,0:T(8,128)(2,1)} %collective-permute-done.before_ref, bf16[2,1,512,256]{3,2,1,0:T(8,128)(2,1)} %copy-done.6, ...), custom_call_target="tpu_custom_call" | custom-call | tf_op jit(solution)/shard_map/pallas_call | solution.py:205
  59.4 1.0 copy.189
  60.4 0.6 gather_fusion
  61.0 0.1 broadcast_select_fusion.1
  61.6 0.1 convolution_bitcast_fusion.1
  61.7 0.1 convolution_bitcast_fusion
  61.8 0.2 convolution_bitcast_fusion.3
  62.0 0.1 convolution_bitcast_fusion.2
  62.3 1.4 %fusion.55 = s32[128,16]{1,0:T(8,128)S(1)} fusion(bf16[128,17,256]{2,1,0:T(8,128)(2,1)} %all-to-all-done), kind=kLoop, calls=%fused_computation.98 | loop fusion | flops 8192 | bytes 16384 | tf_op jit(solution)/shard_map/add | solution.py:353
  63.7 0.1 add.158
  63.7 1.3 slice.409
  65.1 0.0 copy-start.12
  65.1 5.3 %fusion = f32[2,4,512,256]{3,2,1,0:T(8,128)S(1)} fusion(bf16[2048,256,1,1]{1,0,3,2:T(8,128)(2,1)S(1)} %bitcast.240, s32[2048]{0:T(1024)S(1)} %add.158, s32[2,4,512]{2,1,0:T(4,128)S(1)} %multiply_add_fusion), kind=kOutput, calls=%fused_computation.2 | convolution fusion | flops 4303355904 | bytes 5267456 | tf_op jit(solution)/shard_map/dot_general | solution.py:385
  70.5 5.0 %multiply_convert_fusion = (bf16[2,4,512,256]{3,2,1,0:T(8,128)(2,1)S(1)}, bf16[2,4,512,256]{3,2,1,0:T(8,128)(2,1)S(1)}) fusion(f32[2,4,512,256]{3,2,1,0:T(8,128)S(1)} %fusion, f32[256]{0:T(256)S(1)} %copy-done.12, f32[2,4,256]{2,1,0:T(4,128)S(1)} %get-tuple-element.47, pred[512]{0:T(512)(128)(4,1)S(1)} %get-tuple-element.86, ...), kind=kLoop, calls=%fused_computation.23 | loop fusion | flops 33554432 | bytes 16812032 | tf_op jit(solution)/shard_map/convert_element_type | solution.py:400
  75.5 0.2 fusion.17
  75.7 3.7 %collective-permute-start.3 = (bf16[2,1,512,512]{3,2,1,0:T(8,128)(2,1)S(1)}, bf16[2,1,512,512]{3,2,1,0:T(8,128)(2,1)S(1)}, u32[]{:S(2)}, u32[]{:S(2)}) collective-permute-start(bf16[2,1,512,512]{3,2,1,0:T(8,128)(2,1)S(1)} %get-tuple-element.20), channel_id=1, source_target_pairs={{1,0},{2,1},{3,2},{4,3},{5,4},{6,5},{7,6},{8,7},{9,8},{10,9},{11,1... | collective-permute-start | bytes 3145736 | tf_op jit(solution)/shard_map/ppermute | solution.py:264
  79.4 2.1 %collective-permute-start.2 = (bf16[2,1,512,512]{3,2,1,0:T(8,128)(2,1)S(1)}, bf16[2,1,512,512]{3,2,1,0:T(8,128)(2,1)S(1)}, u32[]{:S(2)}, u32[]{:S(2)}) collective-permute-start(bf16[2,1,512,512]{3,2,1,0:T(8,128)(2,1)S(1)} %get-tuple-element.21), channel_id=1, source_target_pairs={{0,1},{1,2},{2,3},{3,4},{4,5},{5,6},{6,7},{7,8},{8,9},{9,10},{10,1... | collective-permute-start | bytes 3145736 | tf_op jit(solution)/shard_map/ppermute | solution.py:263
  81.6 2.3 %pad_maximum_fusion.src_ref = bf16[2,4,512,512]{3,2,1,0:T(8,128)(2,1)} fusion(bf16[2,4,512,256]{3,2,1,0:T(8,128)(2,1)S(1)} %get-tuple-element.19, bf16[2,4,512,256]{3,2,1,0:T(8,128)(2,1)S(1)} %get-tuple-element.18), kind=kLoop, calls=%fused_computation.13 | loop fusion | flops 8388608 | bytes 8388608 | tf_op jit(solution)/shard_map/concatenate | solution.py:404
  83.9 16.8 %collective-permute-done.3 = bf16[2,1,512,512]{3,2,1,0:T(8,128)(2,1)S(1)} collective-permute-done((bf16[2,1,512,512]{3,2,1,0:T(8,128)(2,1)S(1)}, bf16[2,1,512,512]{3,2,1,0:T(8,128)(2,1)S(1)}, u32[]{:S(2)}, u32[]{:S(2)}) %collective-permute-start.3) | collective-permute-done | bytes 1048608 | tf_op jit(solution)/shard_map/ppermute | solution.py:264
  100.7 0.3 reverse_select_fusion.after_ref
  101.0 3.5 %collective-permute-done.2.before_ref = bf16[2,1,512,512]{3,2,1,0:T(8,128)(2,1)S(1)} collective-permute-done((bf16[2,1,512,512]{3,2,1,0:T(8,128)(2,1)S(1)}, bf16[2,1,512,512]{3,2,1,0:T(8,128)(2,1)S(1)}, u32[]{:S(2)}, u32[]{:S(2)}) %collective-permute-start.2) | collective-permute-done | bytes 1048608 | tf_op jit(solution)/shard_map/ppermute | solution.py:263
  104.6 0.9 copy-done.5
  105.6 7.9 %shard_map.115 = (f32[2,4,512,128]{3,2,1,0:T(8,128)}, f32[2,2,4,128]{3,2,1,0:T(4,128)}) custom-call(bf16[2,4,512,512]{3,2,1,0:T(8,128)(2,1)} %pad_maximum_fusion.src_ref, bf16[2,1,512,512]{3,2,1,0:T(8,128)(2,1)} %copy-done.5, bf16[2,1,512,512]{3,2,1,0:T(8,128)(2,1)} %copy-done.2, bf16[9,128,256]{2,1,0:T(8,128)(2,1)} %k_ref.6), custom_call_target="tpu_custom_call" | custom-call | tf_op jit(solution)/shard_map/pallas_call | solution.py:123
  113.4 0.7 copy.120
  114.1 0.6 maximum_bitcast_fusion.1.block_ref
  114.7 11.0 %shard_map.116 = (f32[2,4,512,128]{3,2,1,0:T(8,128)}, f32[8,64,128]{2,1,0:T(8,128)}) custom-call(f32[64,128]{1,0:T(8,128)} %maximum_bitcast_fusion.1.block_ref, bf16[2,4,512,512]{3,2,1,0:T(8,128)(2,1)} %pad_maximum_fusion.src_ref, bf16[2,1,512,512]{3,2,1,0:T(8,128)(2,1)} %copy-done.5, bf16[2,1,512,512]{3,2,1,0:T(8,128)(2,1)} %copy-done.2, ...), custom_call_target="tpu_custom_call" | custom-call | tf_op jit(solution)/shard_map/pallas_call | solution.py:205
  125.8 1.2 copy.188
  127.0 0.6 gather_fusion.1
  127.6 0.1 broadcast_select_fusion
  127.7 0.1 constant_dynamic-slice_fusion.3
  127.8 0.1 rev.36
  128.1 0.1 rev.37
  128.5 0.1 convolution_bitcast_fusion.5
  128.6 0.2 convolution_bitcast_fusion.4
  128.8 0.2 convolution_bitcast_fusion.7
  128.9 0.2 convolution_bitcast_fusion.6
  129.1 5.2 %add_bitcast_fusion = (f32[1,1,2,4,512,128]{5,4,3,2,1,0:T(8,128)}, bf16[1,1,2,4,512,128]{5,4,3,2,1,0:T(8,128)(2,1)}) fusion(f32[2,4,512,128]{3,2,1,0:T(8,128)} %get-tuple-element.17, f32[2,4,128]{2,1,0:T(4,128)S(1)} %reverse_select_fusion.4, f32[2,4,128]{2,1,0:T(4,128)S(1)} %reverse_select_fusion.5, pred[512]{0:T(512)(128)(4,1)S(1)} %get-tuple-element.86, ...), kind=kLoop, calls=%fused_computation.35 | loop fusion | flops 7340032 | bytes 9455104 | tf_op jit(solution)/shard_map/broadcast_in_dim | solution.py:414
  (104 shorter events, 0.9 us)
Async XLA Ops:
  0.6 12.9 %copy-start = (bf16[1024,256]{1,0:T(8,128)(2,1)S(1)}, bf16[1024,256]{1,0:T(8,128)(2,1)}, u32[]{:S(2)}) copy-start(bf16[1024,256]{1,0:T(8,128)(2,1)} %param.11) | copy-start | bytes 1572868
  3.0 33.8 %collective-permute-start.1 = (bf16[2,1,512,256]{3,2,1,0:T(8,128)(2,1)}, bf16[2,1,512,256]{3,2,1,0:T(8,128)(2,1)}, u32[]{:S(2)}, u32[]{:S(2)}) collective-permute-start(bf16[2,1,512,256]{3,2,1,0:T(8,128)(2,1)} %get-tuple-element.22), channel_id=1, source_target_pairs={{1,0},{2,1},{3,2},{4,3},{5,4},{6,5},{7,6},{8,7},{9,8},{10,9},{11,1... | collective-permute-start | bytes 1572872 | tf_op jit(solution)/shard_map/ppermute | solution.py:264
  7.5 30.6 %collective-permute-start = (bf16[2,1,512,256]{3,2,1,0:T(8,128)(2,1)}, bf16[2,1,512,256]{3,2,1,0:T(8,128)(2,1)}, u32[]{:S(2)}, u32[]{:S(2)}) collective-permute-start(bf16[2,1,512,256]{3,2,1,0:T(8,128)(2,1)} %get-tuple-element.23), channel_id=1, source_target_pairs={{0,1},{1,2},{2,3},{3,4},{4,5},{5,6},{6,7},{7,8},{8,9},{9,10},{10,1... | collective-permute-start | bytes 1572872 | tf_op jit(solution)/shard_map/ppermute | solution.py:263
  15.1 13.1 %copy-start.11 = (s32[8,2,3]{0,1,2:T(2,128)S(1)}, s32[8,2,3]{0,1,2:T(2,128)}, u32[]{:S(2)}) copy-start(s32[8,2,3]{0,1,2:T(2,128)} %param.14) | copy-start | bytes 580
  15.1 13.9 %copy-start.1 = (bf16[1,1,2,4,512,128]{5,4,3,2,1,0:T(8,128)(2,1)S(1)}, bf16[1,1,2,4,512,128]{5,4,3,2,1,0:T(8,128)(2,1)}, u32[]{:S(2)}) copy-start(bf16[1,1,2,4,512,128]{5,4,3,2,1,0:T(8,128)(2,1)} %param.10) | copy-start | bytes 3145732
  15.2 13.9 %copy-start.3 = (bf16[1,1,2,4,512,128]{5,4,3,2,1,0:T(8,128)(2,1)S(1)}, bf16[1,1,2,4,512,128]{5,4,3,2,1,0:T(8,128)(2,1)}, u32[]{:S(2)}) copy-start(bf16[1,1,2,4,512,128]{5,4,3,2,1,0:T(8,128)(2,1)} %param.19) | copy-start | bytes 3145732
  16.5 20.2 %copy-start.10 = (bf16[9,128,256]{2,1,0:T(8,128)(2,1)S(1)}, bf16[9,128,256]{2,1,0:T(8,128)(2,1)}, u32[]{:S(2)}) copy-start(bf16[9,128,256]{2,1,0:T(8,128)(2,1)} %k_ref.6) | copy-start | bytes 1769476
  16.5 45.7 %all-to-all-start = ((bf16[128,17,256]{2,1,0:T(8,128)(2,1)}), bf16[128,17,256]{2,1,0:T(8,128)(2,1)}, u32[]{:S(2)}, u32[]{:S(2)}) async-start(bf16[128,17,256]{2,1,0:T(8,128)(2,1)} %pad_maximum_fusion.2), calls=%async_computation | async-start | bytes 3145728 | tf_op jit(solution)/shard_map/all_to_all | solution.py:349
  38.1 0.8 copy-start.6
  65.1 5.4 %copy-start.7 = (f32[2,4,512,256]{3,2,1,0:T(8,128)S(1)}, f32[2,4,512,256]{3,2,1,0:T(8,128)}, u32[]{:S(2)}) copy-start(f32[2,4,512,256]{3,2,1,0:T(8,128)} %get-tuple-element.13) | copy-start | bytes 12582916
  65.1 5.4 %copy-start.8 = (f32[2,4,512,256]{3,2,1,0:T(8,128)S(1)}, f32[2,4,512,256]{3,2,1,0:T(8,128)}, u32[]{:S(2)}) copy-start(f32[2,4,512,256]{3,2,1,0:T(8,128)} %get-tuple-element.11) | copy-start | bytes 12582916
  65.1 5.4 %copy-start.12 = (f32[256]{0:T(256)S(1)}, f32[256]{0:T(256)}, u32[]{:S(2)}) copy-start(f32[256]{0:T(256)} %param.16) | copy-start | bytes 3076
  75.5 6.0 %copy-start.9 = (bf16[9,256,128]{2,1,0:T(8,128)(2,1)S(1)}, bf16[9,256,128]{2,1,0:T(8,128)(2,1)}, u32[]{:S(2)}) copy-start(bf16[9,256,128]{2,1,0:T(8,128)(2,1)} %k_ref.7) | copy-start | bytes 1769476
  75.7 25.0 %collective-permute-start.3 = (bf16[2,1,512,512]{3,2,1,0:T(8,128)(2,1)S(1)}, bf16[2,1,512,512]{3,2,1,0:T(8,128)(2,1)S(1)}, u32[]{:S(2)}, u32[]{:S(2)}) collective-permute-start(bf16[2,1,512,512]{3,2,1,0:T(8,128)(2,1)S(1)} %get-tuple-element.20), channel_id=1, source_target_pairs={{1,0},{2,1},{3,2},{4,3},{5,4},{6,5},{7,6},{8,7},{9,8},{10,9},{11,1... | collective-permute-start | bytes 3145736 | tf_op jit(solution)/shard_map/ppermute | solution.py:264
  79.4 25.2 %collective-permute-start.2 = (bf16[2,1,512,512]{3,2,1,0:T(8,128)(2,1)S(1)}, bf16[2,1,512,512]{3,2,1,0:T(8,128)(2,1)S(1)}, u32[]{:S(2)}, u32[]{:S(2)}) collective-permute-start(bf16[2,1,512,512]{3,2,1,0:T(8,128)(2,1)S(1)} %get-tuple-element.21), channel_id=1, source_target_pairs={{0,1},{1,2},{2,3},{3,4},{4,5},{5,6},{6,7},{7,8},{8,9},{9,10},{10,1... | collective-permute-start | bytes 3145736 | tf_op jit(solution)/shard_map/ppermute | solution.py:263
  101.0 4.6 %copy-start.2 = (bf16[2,1,512,512]{3,2,1,0:T(8,128)(2,1)}, bf16[2,1,512,512]{3,2,1,0:T(8,128)(2,1)S(1)}, u32[]{:S(2)}) copy-start(bf16[2,1,512,512]{3,2,1,0:T(8,128)(2,1)S(1)} %reverse_select_fusion.after_ref) | copy-start | bytes 3145732
  104.6 1.0 copy-start.5
  125.7 3.3 %copy-start.4 = (bf16[1,1,2,4,512,128]{5,4,3,2,1,0:T(8,128)(2,1)S(1)}, bf16[1,1,2,4,512,128]{5,4,3,2,1,0:T(8,128)(2,1)}, u32[]{:S(2)}) copy-start(bf16[1,1,2,4,512,128]{5,4,3,2,1,0:T(8,128)(2,1)} %param.19) | copy-start | bytes 3145732

commit v7 on v6

--- a/solution.py
+++ b/solution.py
@@ -378,19 +378,20 @@
     device_count = tile_count * face_count
     obs_width = obs_values.shape[1]
 
+
+    last_tile = tile_at == tile_count - 1
+    matching_row = lax.dynamic_index_in_dim(matching, face_at, 0, keepdims=False)
+
+    lifted = kernel_one.shape[2]
+    both = extend_rows(jnp.concatenate([base_field, cot_field], axis=3), last_tile)
+    cot_back, cot_margins = conv_back(both, channels, channels, kernel_two)
+    obs_values, cot_back = lax.optimization_barrier((obs_values, cot_back))
     got_values, got_pixels = route_observations(obs_values, obs_dest, obs_pixel, device_count)
     pixel_count = 2 * band_rows * column_count
     pixel_ids = lax.iota(jnp.int32, pixel_count)
     onehot = (pixel_ids[:, None] == got_pixels[None, :]).astype(jnp.bfloat16)
     gridded = jnp.dot(onehot, got_values, preferred_element_type=jnp.float32)
     gridded = gridded.reshape(2, band_rows, column_count, obs_width)
-
-    last_tile = tile_at == tile_count - 1
-    matching_row = lax.dynamic_index_in_dim(matching, face_at, 0, keepdims=False)
-
-    lifted = kernel_one.shape[2]
-    both = extend_rows(jnp.concatenate([base_field, cot_field], axis=3), last_tile)
-    cot_back, cot_margins = conv_back(both, channels, channels, kernel_two)
     parts = [edge_cols(both, 0, channels), jnp.swapaxes(cot_margins, 1, 2)]
     first_out, landed = conv_gather(both, 0, channels, pack_parts(parts), kernel_one, 0)
     base_edges, cot_gathered = unpack_parts(landed, parts)

time: 135 us -> 163 us (1.21)
  waiting for transfers between devices: 20.3 us -> 38.8 us
  local copies, waits for them, and re-layouts: 10.9 us -> 19 us
  matrix products: 8.13 us -> 11.7 us
  starting transfers between devices: 23.9 us -> 20.8 us
    all_to_all x1, waiting for transfers between devices: 0.01 us -> 18.5 us  [route_observations(): lax.all_to_all(payload, ('face', 'tile'), split_axis=0, concat_axis=0, ti...]
    unnamed x54 -> x68, local copies, waits for them, and re-layouts: 4 us -> 11.2 us
    all_to_all x1, starting transfers between devices: 11.6 us -> 8.63 us  [route_observations(): lax.all_to_all(payload, ('face', 'tile'), split_axis=0, concat_axis=0, ti...]
    dot_general x8, matrix products: 1.17 us -> 3.86 us  [side_terms(): jnp.dot(stacked, weights, preferred_element_type=jnp.float32)]
  transfers between devices with their start and end apart: 5 -> 5, of which waited for: 2 -> 3; matrix products, arithmetic and copies ran while one was open for 14% -> 10% of each run, Pallas kernels for 13% -> 0%
where the time goes in v7:
time: 163 us; the launch traced here: 161 us
  waiting for transfers between devices  38.8 us (24%)
  Pallas kernels  36.5 us (22%)
  other arithmetic  26.6 us (16%)
  starting transfers between devices  20.8 us (13%)
  local copies, waits for them, and re-layouts  19 us (12%)
  matrix products  11.7 us (7%)
  between operations  7.63 us (5%)
    pallas_call x2, Pallas kernels, conv_gather(): pl.pallas_call(functools.partial(conv_gather_kernel, count), grid=(bands,...  22.2 us
    all_to_all x1, waiting for transfers between devices, route_observations(): lax.all_to_all(payload, ('face', 'tile'), split_axis=0, concat_axis=0, ti...  18.5 us
    ppermute x2, waiting for transfers between devices, extend_rows(): after = lax.ppermute(head, 'tile', [(i + 1, i) for i in range(count - 1)])  16.9 us
    pallas_call x2, Pallas kernels, conv_back(): pl.pallas_call(back_kernel, grid=(bands,), in_specs=[pl.BlockSpec((1, row...  14.3 us
    unnamed x68, local copies, waits for them, and re-layouts  11.2 us
    all_to_all x1, starting transfers between devices, route_observations(): lax.all_to_all(payload, ('face', 'tile'), split_axis=0, concat_axis=0, ti...  8.63 us
    ppermute x2, starting transfers between devices, extend_rows(): after = lax.ppermute(head, 'tile', [(i + 1, i) for i in range(count - 1)])  8.35 us
    dot_general x1, matrix products, per_device(): gridded = jnp.dot(onehot, got_values, preferred_element_type=jnp.float32)  6.17 us
  transfers between devices with their start and end apart: 5, of which 3 were waited for; matrix products, arithmetic and copies ran while one was open for 10% of the time, Pallas kernels for 0%

profile of v7, /device:TPU:24, one launch (start us, length us, event | category | flops | bytes accessed | tf_op | source)
XLA Modules:
  0.0 161.1 jit_solution(8629150104254169641)
XLA Ops:
  0.7 2.4 %fusion.19 = (bf16[2,1,512,256]{3,2,1,0:T(8,128)(2,1)}, bf16[2,1,512,256]{3,2,1,0:T(8,128)(2,1)}) fusion(bf16[2,4,512,128]{3,2,1,0:T(8,128)(2,1)} %bitcast.235, bf16[2,4,512,128]{3,2,1,0:T(8,128)(2,1)} %bitcast.238), kind=kLoop, calls=%fused_computation.51 | loop fusion | flops 2097152 | bytes 3145728 | tf_op jit(solution)/shard_map/concatenate | solution.py:386
  3.1 4.5 %collective-permute-start.1 = (bf16[2,1,512,256]{3,2,1,0:T(8,128)(2,1)}, bf16[2,1,512,256]{3,2,1,0:T(8,128)(2,1)}, u32[]{:S(2)}, u32[]{:S(2)}) collective-permute-start(bf16[2,1,512,256]{3,2,1,0:T(8,128)(2,1)} %get-tuple-element.26), channel_id=1, source_target_pairs={{1,0},{2,1},{3,2},{4,3},{5,4},{6,5},{7,6},{8,7},{9,8},{10,9},{11,1... | collective-permute-start | bytes 1572872 | tf_op jit(solution)/shard_map/ppermute | solution.py:264
  7.6 1.9 %collective-permute-start = (bf16[2,1,512,256]{3,2,1,0:T(8,128)(2,1)}, bf16[2,1,512,256]{3,2,1,0:T(8,128)(2,1)}, u32[]{:S(2)}, u32[]{:S(2)}) collective-permute-start(bf16[2,1,512,256]{3,2,1,0:T(8,128)(2,1)} %get-tuple-element.27), channel_id=1, source_target_pairs={{0,1},{1,2},{2,3},{3,4},{4,5},{5,6},{6,7},{7,8},{8,9},{9,10},{10,1... | collective-permute-start | bytes 1572872 | tf_op jit(solution)/shard_map/ppermute | solution.py:263
  9.6 0.6 multiply_add_fusion
  10.2 0.8 constant_dynamic-slice_fusion.8
  11.1 0.7 fusion.153
  11.7 1.3 convert_reduce_fusion
  13.0 0.7 multiply_add_fusion.1
  13.7 0.6 copy-done.12
  14.3 1.6 select_reduce_fusion
  16.3 0.6 iota_compare_fusion.9
  16.9 1.5 pad_maximum_fusion.1.src_ref
  24.7 1.3 reverse_select_fusion.1.after_ref
  26.1 0.7 copy-done.6
  26.8 6.4 %shard_map.113 = (f32[2,4,512,256]{3,2,1,0:T(8,128)}, f32[2,2,4,256]{3,2,1,0:T(4,128)}) custom-call(bf16[2,4,512,256]{3,2,1,0:T(8,128)(2,1)} %pad_maximum_fusion.1.src_ref, bf16[2,1,512,256]{3,2,1,0:T(8,128)(2,1)} %collective-permute-done.before_ref, bf16[2,1,512,256]{3,2,1,0:T(8,128)(2,1)} %copy-done.6, bf16[9,256,128]{2,1,0:T(8,128)(2,1)} %k_ref.7), custom_call_target="tpu_custom_call" | custom-call | tf_op jit(solution)/shard_map/pallas_call | solution.py:123
  33.2 0.7 copy.113
  34.0 1.0 slice.384
  35.0 0.6 maximum_bitcast_fusion.2.block_ref
  35.6 11.7 %shard_map.114 = (f32[2,4,512,256]{3,2,1,0:T(8,128)}, f32[8,56,128]{2,1,0:T(8,128)}) custom-call(f32[56,128]{1,0:T(8,128)} %maximum_bitcast_fusion.2.block_ref, bf16[2,4,512,256]{3,2,1,0:T(8,128)(2,1)} %pad_maximum_fusion.1.src_ref, bf16[2,1,512,256]{3,2,1,0:T(8,128)(2,1)} %collective-permute-done.before_ref, bf16[2,1,512,256]{3,2,1,0:T(8,128)(2,1)} %copy-done.6, ...), custom_call_target="tpu_custom_call" | custom-call | tf_op jit(solution)/shard_map/pallas_call | solution.py:205
  47.4 1.0 copy.189
  48.4 0.6 gather_fusion
  49.1 0.6 constant_dynamic-slice_fusion.5
  49.9 0.5 copy.209
  50.4 0.5 copy.210
  51.0 0.6 copy.211
  51.6 0.5 copy.206
  52.2 0.6 copy.207
  52.8 0.5 copy.208
  53.3 0.5 copy.215
  53.8 0.5 copy.216
  54.3 0.6 copy.217
  54.9 0.6 copy.212
  55.5 0.6 copy.213
  56.1 0.6 copy.214
  56.6 1.6 %fusion.14 = bf16[2048,256]{1,0:T(8,128)(2,1)S(1)} fusion(bf16[1024,256]{1,0:T(8,128)(2,1)S(1)} %copy-done, s32[1024]{0:T(1024)S(1)} %copy-done.13), kind=kOutput, calls=%fused_computation.34 | convolution fusion | flops 1076363264 | bytes 1576960 | tf_op jit(solution)/shard_map/dot_general | solution.py:337
  58.3 1.4 pad_maximum_fusion.2
  59.6 8.6 %all-to-all-start = ((bf16[128,17,256]{2,1,0:T(8,128)(2,1)}), bf16[128,17,256]{2,1,0:T(8,128)(2,1)S(1)}, u32[]{:S(2)}, u32[]{:S(2)}) async-start(bf16[128,17,256]{2,1,0:T(8,128)(2,1)} %pad_maximum_fusion.2), calls=%async_computation | async-start | bytes 3145728 | tf_op jit(solution)/shard_map/all_to_all | solution.py:349
  68.3 0.8 convolution_bitcast_fusion.1
  69.1 0.8 convolution_bitcast_fusion
  69.9 0.8 convolution_bitcast_fusion.3
  70.7 0.8 convolution_bitcast_fusion.2
  71.6 0.7 copy_bitcast_fusion.4
  72.4 18.5 %all-to-all-done = bf16[128,17,256]{2,1,0:T(8,128)(2,1)S(1)} async-done(((bf16[128,17,256]{2,1,0:T(8,128)(2,1)}), bf16[128,17,256]{2,1,0:T(8,128)(2,1)S(1)}, u32[]{:S(2)}, u32[]{:S(2)}) %all-to-all-start) | async-done | bytes 1114144 | tf_op jit(solution)/shard_map/all_to_all | solution.py:349
  90.8 0.3 fusion.55
  91.4 6.2 %fusion = f32[2,4,512,256]{3,2,1,0:T(8,128)S(1)} fusion(bf16[2048,256,1,1]{1,0,3,2:T(8,128)(2,1)S(1)} %bitcast.240, s32[2048]{0:T(1024)S(1)} %add.158, s32[2,4,512]{2,1,0:T(4,128)} %multiply_add_fusion), kind=kOutput, calls=%fused_computation.2 | convolution fusion | flops 4303355904 | bytes 5267456 | tf_op jit(solution)/shard_map/dot_general | solution.py:393
  97.6 5.0 %multiply_convert_fusion = (bf16[2,4,512,256]{3,2,1,0:T(8,128)(2,1)S(1)}, bf16[2,4,512,256]{3,2,1,0:T(8,128)(2,1)S(1)}) fusion(f32[2,4,512,256]{3,2,1,0:T(8,128)S(1)} %fusion, f32[256]{0:T(256)S(1)} %copy-done.18, f32[2,4,256]{2,1,0:T(4,128)S(1)} %get-tuple-element.51, pred[512]{0:T(512)(128)(4,1)S(1)} %copy-done.14, f32[2,4,512,256]{3,2,1,0:T(8,128)S(1)} %copy-done.8, ...), kind=kLoop, calls=%fused_computation.23 | loop fusion | flops 33554432 | bytes 16812032 | tf_op jit(solution)/shard_map/convert_element_type | solution.py:401
  102.7 0.2 fusion.17
  102.9 3.8 %collective-permute-start.3 = (bf16[2,1,512,512]{3,2,1,0:T(8,128)(2,1)S(1)}, bf16[2,1,512,512]{3,2,1,0:T(8,128)(2,1)S(1)}, u32[]{:S(2)}, u32[]{:S(2)}) collective-permute-start(bf16[2,1,512,512]{3,2,1,0:T(8,128)(2,1)S(1)} %get-tuple-element.24), channel_id=1, source_target_pairs={{1,0},{2,1},{3,2},{4,3},{5,4},{6,5},{7,6},{8,7},{9,8},{10,9},{11,1... | collective-permute-start | bytes 3145736 | tf_op jit(solution)/shard_map/ppermute | solution.py:264
  106.7 1.9 %collective-permute-start.2 = (bf16[2,1,512,512]{3,2,1,0:T(8,128)(2,1)S(1)}, bf16[2,1,512,512]{3,2,1,0:T(8,128)(2,1)S(1)}, u32[]{:S(2)}, u32[]{:S(2)}) collective-permute-start(bf16[2,1,512,512]{3,2,1,0:T(8,128)(2,1)S(1)} %get-tuple-element.25), channel_id=1, source_target_pairs={{0,1},{1,2},{2,3},{3,4},{4,5},{5,6},{6,7},{7,8},{8,9},{9,10},{10,1... | collective-permute-start | bytes 3145736 | tf_op jit(solution)/shard_map/ppermute | solution.py:263
  108.7 2.4 %pad_maximum_fusion.src_ref = bf16[2,4,512,512]{3,2,1,0:T(8,128)(2,1)} fusion(bf16[2,4,512,256]{3,2,1,0:T(8,128)(2,1)S(1)} %get-tuple-element.23, bf16[2,4,512,256]{3,2,1,0:T(8,128)(2,1)S(1)} %get-tuple-element.22), kind=kLoop, calls=%fused_computation.13 | loop fusion | flops 8388608 | bytes 8388608 | tf_op jit(solution)/shard_map/concatenate | solution.py:405
  111.0 16.9 %collective-permute-done.3 = bf16[2,1,512,512]{3,2,1,0:T(8,128)(2,1)S(1)} collective-permute-done((bf16[2,1,512,512]{3,2,1,0:T(8,128)(2,1)S(1)}, bf16[2,1,512,512]{3,2,1,0:T(8,128)(2,1)S(1)}, u32[]{:S(2)}, u32[]{:S(2)}) %collective-permute-start.3) | collective-permute-done | bytes 1048608 | tf_op jit(solution)/shard_map/ppermute | solution.py:264
  127.9 0.3 reverse_select_fusion.after_ref
  128.2 3.5 %collective-permute-done.2.before_ref = bf16[2,1,512,512]{3,2,1,0:T(8,128)(2,1)S(1)} collective-permute-done((bf16[2,1,512,512]{3,2,1,0:T(8,128)(2,1)S(1)}, bf16[2,1,512,512]{3,2,1,0:T(8,128)(2,1)S(1)}, u32[]{:S(2)}, u32[]{:S(2)}) %collective-permute-start.2) | collective-permute-done | bytes 1048608 | tf_op jit(solution)/shard_map/ppermute | solution.py:263
  131.8 0.9 copy-done.5
  132.7 7.9 %shard_map.115 = (f32[2,4,512,128]{3,2,1,0:T(8,128)}, f32[2,2,4,128]{3,2,1,0:T(4,128)}) custom-call(bf16[2,4,512,512]{3,2,1,0:T(8,128)(2,1)} %pad_maximum_fusion.src_ref, bf16[2,1,512,512]{3,2,1,0:T(8,128)(2,1)} %copy-done.5, bf16[2,1,512,512]{3,2,1,0:T(8,128)(2,1)} %copy-done.2, bf16[9,128,256]{2,1,0:T(8,128)(2,1)} %k_ref.6), custom_call_target="tpu_custom_call" | custom-call | tf_op jit(solution)/shard_map/pallas_call | solution.py:123
  140.6 0.7 copy.120
  141.3 0.6 maximum_bitcast_fusion.1.block_ref
  141.9 10.5 %shard_map.116 = (f32[2,4,512,128]{3,2,1,0:T(8,128)}, f32[8,64,128]{2,1,0:T(8,128)}) custom-call(f32[64,128]{1,0:T(8,128)} %maximum_bitcast_fusion.1.block_ref, bf16[2,4,512,512]{3,2,1,0:T(8,128)(2,1)} %pad_maximum_fusion.src_ref, bf16[2,1,512,512]{3,2,1,0:T(8,128)(2,1)} %copy-done.5, bf16[2,1,512,512]{3,2,1,0:T(8,128)(2,1)} %copy-done.2, ...), custom_call_target="tpu_custom_call" | custom-call | tf_op jit(solution)/shard_map/pallas_call | solution.py:205
  152.4 1.2 copy.188
  153.6 0.8 gather_fusion.1
  155.4 0.1 convolution_bitcast_fusion.4
  155.6 0.2 convolution_bitcast_fusion.7
  155.7 0.2 convolution_bitcast_fusion.6
  155.9 5.1 %add_bitcast_fusion = (f32[1,1,2,4,512,128]{5,4,3,2,1,0:T(8,128)}, bf16[1,1,2,4,512,128]{5,4,3,2,1,0:T(8,128)(2,1)}) fusion(f32[2,4,512,128]{3,2,1,0:T(8,128)} %get-tuple-element.21, f32[2,4,128]{2,1,0:T(4,128)S(1)} %reverse_select_fusion.4, f32[2,4,128]{2,1,0:T(4,128)S(1)} %reverse_select_fusion.5, pred[512]{0:T(512)(128)(4,1)S(1)} %copy-done.14, ...), kind=kLoop, calls=%fused_computation.35 | loop fusion | flops 7340032 | bytes 9455104 | tf_op jit(solution)/shard_map/broadcast_in_dim | solution.py:415
  (118 shorter events, 2.1 us)
Async XLA Ops:
  0.6 56.0 %copy-start = (bf16[1024,256]{1,0:T(8,128)(2,1)S(1)}, bf16[1024,256]{1,0:T(8,128)(2,1)}, u32[]{:S(2)}) copy-start(bf16[1024,256]{1,0:T(8,128)(2,1)} %param.11) | copy-start | bytes 1572868
  0.6 16.2 %copy-start.1 = (bf16[1,1,2,4,512,128]{5,4,3,2,1,0:T(8,128)(2,1)S(1)}, bf16[1,1,2,4,512,128]{5,4,3,2,1,0:T(8,128)(2,1)}, u32[]{:S(2)}) copy-start(bf16[1,1,2,4,512,128]{5,4,3,2,1,0:T(8,128)(2,1)} %param.10) | copy-start | bytes 3145732
  0.7 16.2 %copy-start.3 = (bf16[1,1,2,4,512,128]{5,4,3,2,1,0:T(8,128)(2,1)S(1)}, bf16[1,1,2,4,512,128]{5,4,3,2,1,0:T(8,128)(2,1)}, u32[]{:S(2)}) copy-start(bf16[1,1,2,4,512,128]{5,4,3,2,1,0:T(8,128)(2,1)} %param.19) | copy-start | bytes 3145732
  0.7 24.0 %copy-start.10 = (bf16[9,128,256]{2,1,0:T(8,128)(2,1)S(1)}, bf16[9,128,256]{2,1,0:T(8,128)(2,1)}, u32[]{:S(2)}) copy-start(bf16[9,128,256]{2,1,0:T(8,128)(2,1)} %k_ref.6) | copy-start | bytes 1769476
  3.1 21.6 %collective-permute-start.1 = (bf16[2,1,512,256]{3,2,1,0:T(8,128)(2,1)}, bf16[2,1,512,256]{3,2,1,0:T(8,128)(2,1)}, u32[]{:S(2)}, u32[]{:S(2)}) collective-permute-start(bf16[2,1,512,256]{3,2,1,0:T(8,128)(2,1)} %get-tuple-element.26), channel_id=1, source_target_pairs={{1,0},{2,1},{3,2},{4,3},{5,4},{6,5},{7,6},{8,7},{9,8},{10,9},{11,1... | collective-permute-start | bytes 1572872 | tf_op jit(solution)/shard_map/ppermute | solution.py:264
  7.6 18.4 %collective-permute-start = (bf16[2,1,512,256]{3,2,1,0:T(8,128)(2,1)}, bf16[2,1,512,256]{3,2,1,0:T(8,128)(2,1)}, u32[]{:S(2)}, u32[]{:S(2)}) collective-permute-start(bf16[2,1,512,256]{3,2,1,0:T(8,128)(2,1)} %get-tuple-element.27), channel_id=1, source_target_pairs={{0,1},{1,2},{2,3},{3,4},{4,5},{5,6},{6,7},{7,8},{8,9},{9,10},{10,1... | collective-permute-start | bytes 1572872 | tf_op jit(solution)/shard_map/ppermute | solution.py:263
  10.2 38.1 %copy-start.11 = (s32[1024]{0:T(1024)}, s32[1024]{0:T(1024)S(1)}, u32[]{:S(2)}) copy-start(s32[1024]{0:T(1024)S(1)} %pad_clamp_fusion) | copy-start | bytes 12292
  13.7 0.6 copy-start.12
  18.4 30.6 %copy-start.16 = (pred[8]{0:T(512)(128)(4,1)}, pred[8]{0:T(512)(128)(4,1)S(1)}, u32[]{:S(2)}) copy-start(pred[8]{0:T(512)(128)(4,1)S(1)} %compare_and_fusion) | copy-start | bytes 28
  26.0 0.8 copy-start.6
  34.9 21.7 %copy-start.13 = (s32[1024]{0:T(1024)S(1)}, s32[1024]{0:T(1024)}, u32[]{:S(2)}) copy-start(s32[1024]{0:T(1024)} %copy-done.12) | copy-start | bytes 12292
  59.6 31.2 %all-to-all-start = ((bf16[128,17,256]{2,1,0:T(8,128)(2,1)}), bf16[128,17,256]{2,1,0:T(8,128)(2,1)S(1)}, u32[]{:S(2)}, u32[]{:S(2)}) async-start(bf16[128,17,256]{2,1,0:T(8,128)(2,1)} %pad_maximum_fusion.2), calls=%async_computation | async-start | bytes 3145728 | tf_op jit(solution)/shard_map/all_to_all | solution.py:349
  91.3 6.2 %copy-start.7 = (f32[2,4,512,256]{3,2,1,0:T(8,128)S(1)}, f32[2,4,512,256]{3,2,1,0:T(8,128)}, u32[]{:S(2)}) copy-start(f32[2,4,512,256]{3,2,1,0:T(8,128)} %get-tuple-element.17) | copy-start | bytes 12582916
  91.4 6.2 %copy-start.8 = (f32[2,4,512,256]{3,2,1,0:T(8,128)S(1)}, f32[2,4,512,256]{3,2,1,0:T(8,128)}, u32[]{:S(2)}) copy-start(f32[2,4,512,256]{3,2,1,0:T(8,128)} %get-tuple-element.13) | copy-start | bytes 12582916
  91.4 6.2 %copy-start.14 = (pred[512]{0:T(512)(128)(4,1)S(1)}, pred[512]{0:T(512)(128)(4,1)}, u32[]{:S(2)}) copy-start(pred[512]{0:T(512)(128)(4,1)} %get-tuple-element.90) | copy-start | bytes 1540
  91.4 6.2 %copy-start.15 = (pred[512]{0:T(512)(128)(4,1)S(1)}, pred[512]{0:T(512)(128)(4,1)}, u32[]{:S(2)}) copy-start(pred[512]{0:T(512)(128)(4,1)} %get-tuple-element.91) | copy-start | bytes 1540
  91.4 6.2 %copy-start.18 = (f32[256]{0:T(256)S(1)}, f32[256]{0:T(256)}, u32[]{:S(2)}) copy-start(f32[256]{0:T(256)} %param.16) | copy-start | bytes 3076
  102.7 5.9 %copy-start.9 = (bf16[9,256,128]{2,1,0:T(8,128)(2,1)S(1)}, bf16[9,256,128]{2,1,0:T(8,128)(2,1)}, u32[]{:S(2)}) copy-start(bf16[9,256,128]{2,1,0:T(8,128)(2,1)} %k_ref.7) | copy-start | bytes 1769476
  102.9 25.0 %collective-permute-start.3 = (bf16[2,1,512,512]{3,2,1,0:T(8,128)(2,1)S(1)}, bf16[2,1,512,512]{3,2,1,0:T(8,128)(2,1)S(1)}, u32[]{:S(2)}, u32[]{:S(2)}) collective-permute-start(bf16[2,1,512,512]{3,2,1,0:T(8,128)(2,1)S(1)} %get-tuple-element.24), channel_id=1, source_target_pairs={{1,0},{2,1},{3,2},{4,3},{5,4},{6,5},{7,6},{8,7},{9,8},{10,9},{11,1... | collective-permute-start | bytes 3145736 | tf_op jit(solution)/shard_map/ppermute | solution.py:264
  106.7 25.0 %collective-permute-start.2 = (bf16[2,1,512,512]{3,2,1,0:T(8,128)(2,1)S(1)}, bf16[2,1,512,512]{3,2,1,0:T(8,128)(2,1)S(1)}, u32[]{:S(2)}, u32[]{:S(2)}) collective-permute-start(bf16[2,1,512,512]{3,2,1,0:T(8,128)(2,1)S(1)} %get-tuple-element.25), channel_id=1, source_target_pairs={{0,1},{1,2},{2,3},{3,4},{4,5},{5,6},{6,7},{7,8},{8,9},{9,10},{10,1... | collective-permute-start | bytes 3145736 | tf_op jit(solution)/shard_map/ppermute | solution.py:263
  128.2 4.5 %copy-start.2 = (bf16[2,1,512,512]{3,2,1,0:T(8,128)(2,1)}, bf16[2,1,512,512]{3,2,1,0:T(8,128)(2,1)S(1)}, u32[]{:S(2)}) copy-start(bf16[2,1,512,512]{3,2,1,0:T(8,128)(2,1)S(1)} %reverse_select_fusion.after_ref) | copy-start | bytes 3145732
  131.7 1.0 copy-start.5
  141.9 12.5 %copy-start.17 = (pred[8]{0:T(512)(128)(4,1)S(1)}, pred[8]{0:T(512)(128)(4,1)}, u32[]{:S(2)}) copy-start(pred[8]{0:T(512)(128)(4,1)} %copy-done.16) | copy-start | bytes 28
  152.4 3.5 %copy-start.4 = (bf16[1,1,2,4,512,128]{5,4,3,2,1,0:T(8,128)(2,1)S(1)}, bf16[1,1,2,4,512,128]{5,4,3,2,1,0:T(8,128)(2,1)}, u32[]{:S(2)}) copy-start(bf16[1,1,2,4,512,128]{5,4,3,2,1,0:T(8,128)(2,1)} %param.19) | copy-start | bytes 3145732
  152.4 3.5 %copy-start.19 = (f32[128]{0:T(128)S(1)}, f32[128]{0:T(128)}, u32[]{:S(2)}) copy-start(f32[128]{0:T(128)} %param.18) | copy-start | bytes 1540

commit v8 on v6

--- a/solution.py
+++ b/solution.py
@@ -389,7 +389,10 @@
     matching_row = lax.dynamic_index_in_dim(matching, face_at, 0, keepdims=False)
 
     lifted = kernel_one.shape[2]
-    both = extend_rows(jnp.concatenate([base_field, cot_field], axis=3), last_tile)
+    fields, got_values = lax.optimization_barrier(
+        (jnp.concatenate([base_field, cot_field], axis=3), got_values)
+    )
+    both = extend_rows(fields, last_tile)
     cot_back, cot_margins = conv_back(both, channels, channels, kernel_two)
     parts = [edge_cols(both, 0, channels), jnp.swapaxes(cot_margins, 1, 2)]
     first_out, landed = conv_gather(both, 0, channels, pack_parts(parts), kernel_one, 0)

time: 135 us -> 132 us (0.978)
  other arithmetic: 26.4 us -> 22.4 us
  local copies, waits for them, and re-layouts: 10.9 us -> 12.7 us
    concatenate x2 -> x1, other arithmetic: 3.87 us -> 1.84 us  [per_device(): jnp.concatenate([base_field, cot_field], axis=3)]
    unnamed x54 -> x60, local copies, waits for them, and re-layouts: 4 us -> 4.04 us
  transfers between devices with their start and end apart: 5 -> 5, of which waited for: 2 -> 2; matrix products, arithmetic and copies ran while one was open for 14% -> 12% of each run, Pallas kernels for 13% -> 14%
where the time goes in v8:
time: 132 us; the launch traced here: 131 us
  Pallas kernels  37 us (28%)
  starting transfers between devices  23.9 us (18%)
  other arithmetic  22.4 us (17%)
  waiting for transfers between devices  19.6 us (15%)
  local copies, waits for them, and re-layouts  12.7 us (10%)
  matrix products  8.13 us (6%)
  between operations  7.53 us (6%)
    pallas_call x2, Pallas kernels, conv_gather(): pl.pallas_call(functools.partial(conv_gather_kernel, count), grid=(bands,...  22.8 us
    ppermute x2, waiting for transfers between devices, extend_rows(): after = lax.ppermute(head, 'tile', [(i + 1, i) for i in range(count - 1)])  16.1 us
    pallas_call x2, Pallas kernels, conv_back(): pl.pallas_call(back_kernel, grid=(bands,), in_specs=[pl.BlockSpec((1, row...  14.3 us
    all_to_all x1, starting transfers between devices, route_observations(): lax.all_to_all(payload, ('face', 'tile'), split_axis=0, concat_axis=0, ti...  11.6 us
    ppermute x2, starting transfers between devices, extend_rows(): after = lax.ppermute(head, 'tile', [(i + 1, i) for i in range(count - 1)])  8.24 us
    dot_general x1, matrix products, per_device(): gridded = jnp.dot(onehot, got_values, preferred_element_type=jnp.float32)  5.33 us
    broadcast_in_dim x1, other arithmetic, per_device(): return (analysis[None, None], grad_base[None, None])  5.17 us
    convert_element_type x1, other arithmetic, per_device(): inner = activation(pre_act).astype(jnp.bfloat16)  5.04 us
  transfers between devices with their start and end apart: 5, of which 2 were waited for; matrix products, arithmetic and copies ran while one was open for 12% of the time, Pallas kernels for 14%

profile of v8, /device:TPU:24, one launch (start us, length us, event | category | flops | bytes accessed | tf_op | source)
XLA Modules:
  0.0 131.4 jit_solution(8851664863141891732)
XLA Ops:
  0.6 0.0 copy-start
  0.7 1.8 %pad_maximum_fusion.1.src_ref = bf16[2,4,512,256]{3,2,1,0:T(8,128)(2,1)S(1)} fusion(bf16[2,4,512,128]{3,2,1,0:T(8,128)(2,1)} %bitcast.235, bf16[2,4,512,128]{3,2,1,0:T(8,128)(2,1)} %bitcast.236), kind=kLoop, calls=%fused_computation.30 | loop fusion | flops 4194304 | bytes 4194304 | tf_op jit(solution)/shard_map/concatenate | solution.py:393
  2.5 0.0 copy-start.1
  2.5 1.1 fusion.147
  3.7 4.5 %collective-permute-start.1 = (bf16[2,1,512,256]{3,2,1,0:T(8,128)(2,1)}, bf16[2,1,512,256]{3,2,1,0:T(8,128)(2,1)}, u32[]{:S(2)}, u32[]{:S(2)}) collective-permute-start(bf16[2,1,512,256]{3,2,1,0:T(8,128)(2,1)} %get-tuple-element.24), channel_id=1, source_target_pairs={{1,0},{2,1},{3,2},{4,3},{5,4},{6,5},{7,6},{8,7},{9,8},{10,9},{11,1... | collective-permute-start | bytes 1572872 | tf_op jit(solution)/shard_map/ppermute | solution.py:264
  8.2 1.9 %collective-permute-start = (bf16[2,1,512,256]{3,2,1,0:T(8,128)(2,1)}, bf16[2,1,512,256]{3,2,1,0:T(8,128)(2,1)}, u32[]{:S(2)}, u32[]{:S(2)}) collective-permute-start(bf16[2,1,512,256]{3,2,1,0:T(8,128)(2,1)} %get-tuple-element.25), channel_id=1, source_target_pairs={{0,1},{1,2},{2,3},{3,4},{4,5},{5,6},{6,7},{7,8},{8,9},{9,10},{10,1... | collective-permute-start | bytes 1572872 | tf_op jit(solution)/shard_map/ppermute | solution.py:263
  10.2 0.5 convert_reduce_fusion
  10.7 0.9 select_reduce_fusion
  11.6 0.1 reduce_sum.22
  11.7 0.1 fusion.50
  11.8 0.1 pad.43.clone
  11.9 0.1 maximum_bitcast_fusion
  12.0 0.1 copy.113
  12.1 1.6 %fusion.14 = bf16[2048,256]{1,0:T(8,128)(2,1)S(1)} fusion(bf16[1024,256]{1,0:T(8,128)(2,1)S(1)} %copy-done, s32[1024]{0:T(1024)S(1)} %multiply_add_fusion.1), kind=kOutput, calls=%fused_computation.29 | convolution fusion | flops 1076363264 | bytes 1576960 | tf_op jit(solution)/shard_map/dot_general | solution.py:337
  13.8 1.4 %pad_maximum_fusion.2 = bf16[128,17,256]{2,1,0:T(8,128)(2,1)} fusion(bf16[128,1,256]{2,1,0:T(2,128)(2,1)S(1)} %copy.113, bf16[128,16,256]{2,1,0:T(8,128)(2,1)S(1)} %bitcast.238), kind=kLoop, calls=%fused_computation.33 | loop fusion | flops 2228224 | bytes 2228224 | tf_op jit(solution)/shard_map/concatenate | solution.py:346
  15.1 11.6 %all-to-all-start = ((bf16[128,17,256]{2,1,0:T(8,128)(2,1)}), bf16[128,17,256]{2,1,0:T(8,128)(2,1)}, u32[]{:S(2)}, u32[]{:S(2)}) async-start(bf16[128,17,256]{2,1,0:T(8,128)(2,1)} %pad_maximum_fusion.2), calls=%async_computation | async-start | bytes 3145728 | tf_op jit(solution)/shard_map/all_to_all | solution.py:349
  26.8 0.1 constant_dynamic-slice_fusion.8
  26.9 0.1 copy.115
  27.0 0.6 fusion.152
  33.6 1.3 %reverse_select_fusion.1.after_ref = bf16[2,1,512,256]{3,2,1,0:T(8,128)(2,1)S(1)} fusion(bf16[2,1,512,256]{3,2,1,0:T(8,128)(2,1)} %collective-permute-done.1, bf16[2,1,512,256]{3,2,1,0:T(8,128)(2,1)} %get-tuple-element.25, pred[]{:T(512)S(6)} %eq.131), kind=kLoop, calls=%fused_computation.46 | loop fusion | flops 262144 | bytes 1572865 | tf_op jit(solution)/shard_map/jit(_where)/select_n | solution.py:265
  35.0 0.7 copy-done.4
  35.7 6.4 %shard_map.113 = (f32[2,4,512,256]{3,2,1,0:T(8,128)}, f32[2,2,4,256]{3,2,1,0:T(4,128)}) custom-call(bf16[2,4,512,256]{3,2,1,0:T(8,128)(2,1)} %copy-done.1, bf16[2,1,512,256]{3,2,1,0:T(8,128)(2,1)} %collective-permute-done.before_ref, bf16[2,1,512,256]{3,2,1,0:T(8,128)(2,1)} %copy-done.4, bf16[9,256,128]{2,1,0:T(8,128)(2,1)} %k_ref.7), custom_call_target="tpu_custom_call" | custom-call | tf_op jit(solution)/shard_map/pallas_call | solution.py:123
  42.1 0.7 copy.114
  42.9 1.0 slice.386
  43.9 0.6 maximum_bitcast_fusion.2.block_ref
  44.5 11.7 %shard_map.114 = (f32[2,4,512,256]{3,2,1,0:T(8,128)}, f32[8,56,128]{2,1,0:T(8,128)}) custom-call(f32[56,128]{1,0:T(8,128)} %maximum_bitcast_fusion.2.block_ref, bf16[2,4,512,256]{3,2,1,0:T(8,128)(2,1)} %copy-done.1, bf16[2,1,512,256]{3,2,1,0:T(8,128)(2,1)} %collective-permute-done.before_ref, bf16[2,1,512,256]{3,2,1,0:T(8,128)(2,1)} %copy-done.4, ...), custom_call_target="tpu_custom_call" | custom-call | tf_op jit(solution)/shard_map/pallas_call | solution.py:205
  56.3 1.0 copy.189
  57.3 0.6 gather_fusion
  57.9 0.1 broadcast_select_fusion.1
  58.4 0.1 convolution_bitcast_fusion.1
  58.6 0.1 convolution_bitcast_fusion
  58.7 0.1 convolution_bitcast_fusion.3
  58.9 0.1 convolution_bitcast_fusion.2
  59.1 1.5 %fusion.53 = s32[128,16]{1,0:T(8,128)S(1)} fusion(bf16[128,17,256]{2,1,0:T(8,128)(2,1)} %all-to-all-done), kind=kLoop, calls=%fused_computation.92 | loop fusion | flops 8192 | bytes 16384 | tf_op jit(solution)/shard_map/add | solution.py:353
  60.6 0.1 add.158
  60.7 1.3 slice.409
  62.1 5.3 %fusion = f32[2,4,512,256]{3,2,1,0:T(8,128)S(1)} fusion(bf16[2048,256,1,1]{1,0,3,2:T(8,128)(2,1)S(1)} %bitcast.237, s32[2048]{0:T(1024)S(1)} %add.158, s32[2,4,512]{2,1,0:T(4,128)S(1)} %multiply_add_fusion), kind=kOutput, calls=%fused_computation.2 | convolution fusion | flops 4303355904 | bytes 5267456 | tf_op jit(solution)/shard_map/dot_general | solution.py:385
  67.4 5.0 %multiply_convert_fusion = (bf16[2,4,512,256]{3,2,1,0:T(8,128)(2,1)S(1)}, bf16[2,4,512,256]{3,2,1,0:T(8,128)(2,1)S(1)}) fusion(f32[2,4,512,256]{3,2,1,0:T(8,128)S(1)} %fusion, f32[256]{0:T(256)S(1)} %copy-done.14, f32[2,4,256]{2,1,0:T(4,128)S(1)} %get-tuple-element.49, pred[512]{0:T(512)(128)(4,1)S(1)} %get-tuple-element.88, ...), kind=kLoop, calls=%fused_computation.23 | loop fusion | flops 33554432 | bytes 16812032 | tf_op jit(solution)/shard_map/convert_element_type | solution.py:403
  72.5 0.2 fusion.17
  72.7 3.7 %collective-permute-start.3 = (bf16[2,1,512,512]{3,2,1,0:T(8,128)(2,1)S(1)}, bf16[2,1,512,512]{3,2,1,0:T(8,128)(2,1)S(1)}, u32[]{:S(2)}, u32[]{:S(2)}) collective-permute-start(bf16[2,1,512,512]{3,2,1,0:T(8,128)(2,1)S(1)} %get-tuple-element.22), channel_id=1, source_target_pairs={{1,0},{2,1},{3,2},{4,3},{5,4},{6,5},{7,6},{8,7},{9,8},{10,9},{11,1... | collective-permute-start | bytes 3145736 | tf_op jit(solution)/shard_map/ppermute | solution.py:264
  76.4 2.1 %collective-permute-start.2 = (bf16[2,1,512,512]{3,2,1,0:T(8,128)(2,1)S(1)}, bf16[2,1,512,512]{3,2,1,0:T(8,128)(2,1)S(1)}, u32[]{:S(2)}, u32[]{:S(2)}) collective-permute-start(bf16[2,1,512,512]{3,2,1,0:T(8,128)(2,1)S(1)} %get-tuple-element.23), channel_id=1, source_target_pairs={{0,1},{1,2},{2,3},{3,4},{4,5},{5,6},{6,7},{7,8},{8,9},{9,10},{10,1... | collective-permute-start | bytes 3145736 | tf_op jit(solution)/shard_map/ppermute | solution.py:263
  78.5 0.7 slice_bitcast_fusion.3
  79.2 2.3 %pad_maximum_fusion.src_ref = bf16[2,4,512,512]{3,2,1,0:T(8,128)(2,1)} fusion(bf16[2,4,512,256]{3,2,1,0:T(8,128)(2,1)S(1)} %get-tuple-element.21, bf16[2,4,512,256]{3,2,1,0:T(8,128)(2,1)S(1)} %get-tuple-element.20), kind=kLoop, calls=%fused_computation.13 | loop fusion | flops 8388608 | bytes 8388608 | tf_op jit(solution)/shard_map/concatenate | solution.py:407
  81.6 16.1 %collective-permute-done.3 = bf16[2,1,512,512]{3,2,1,0:T(8,128)(2,1)S(1)} collective-permute-done((bf16[2,1,512,512]{3,2,1,0:T(8,128)(2,1)S(1)}, bf16[2,1,512,512]{3,2,1,0:T(8,128)(2,1)S(1)}, u32[]{:S(2)}, u32[]{:S(2)}) %collective-permute-start.3) | collective-permute-done | bytes 1048608 | tf_op jit(solution)/shard_map/ppermute | solution.py:264
  97.7 0.3 reverse_select_fusion.after_ref
  98.0 3.5 %collective-permute-done.2.before_ref = bf16[2,1,512,512]{3,2,1,0:T(8,128)(2,1)S(1)} collective-permute-done((bf16[2,1,512,512]{3,2,1,0:T(8,128)(2,1)S(1)}, bf16[2,1,512,512]{3,2,1,0:T(8,128)(2,1)S(1)}, u32[]{:S(2)}, u32[]{:S(2)}) %collective-permute-start.2) | collective-permute-done | bytes 1048608 | tf_op jit(solution)/shard_map/ppermute | solution.py:263
  101.7 0.9 copy-done.3
  102.5 7.9 %shard_map.115 = (f32[2,4,512,128]{3,2,1,0:T(8,128)}, f32[2,2,4,128]{3,2,1,0:T(4,128)}) custom-call(bf16[2,4,512,512]{3,2,1,0:T(8,128)(2,1)} %pad_maximum_fusion.src_ref, bf16[2,1,512,512]{3,2,1,0:T(8,128)(2,1)} %copy-done.3, bf16[2,1,512,512]{3,2,1,0:T(8,128)(2,1)} %copy-done.2, bf16[9,128,256]{2,1,0:T(8,128)(2,1)} %k_ref.6), custom_call_target="tpu_custom_call" | custom-call | tf_op jit(solution)/shard_map/pallas_call | solution.py:123
  110.4 0.7 copy.120
  111.1 0.6 maximum_bitcast_fusion.1.block_ref
  111.7 11.0 %shard_map.116 = (f32[2,4,512,128]{3,2,1,0:T(8,128)}, f32[8,64,128]{2,1,0:T(8,128)}) custom-call(f32[64,128]{1,0:T(8,128)} %maximum_bitcast_fusion.1.block_ref, bf16[2,4,512,512]{3,2,1,0:T(8,128)(2,1)} %pad_maximum_fusion.src_ref, bf16[2,1,512,512]{3,2,1,0:T(8,128)(2,1)} %copy-done.3, bf16[2,1,512,512]{3,2,1,0:T(8,128)(2,1)} %copy-done.2, ...), custom_call_target="tpu_custom_call" | custom-call | tf_op jit(solution)/shard_map/pallas_call | solution.py:205
  122.8 0.0 copy-start.8
  122.8 0.0 copy-start.9
  122.8 1.3 copy.188
  124.0 0.6 gather_fusion.1
  124.7 0.1 broadcast_select_fusion
  124.8 0.1 constant_dynamic-slice_fusion.3
  124.9 0.1 rev.36
  125.2 0.1 rev.37
  125.5 0.1 convolution_bitcast_fusion.5
  125.7 0.1 convolution_bitcast_fusion.4
  125.8 0.2 convolution_bitcast_fusion.7
  126.0 0.2 convolution_bitcast_fusion.6
  126.2 5.2 %add_bitcast_fusion = (f32[1,1,2,4,512,128]{5,4,3,2,1,0:T(8,128)}, bf16[1,1,2,4,512,128]{5,4,3,2,1,0:T(8,128)(2,1)}) fusion(f32[2,4,512,128]{3,2,1,0:T(8,128)} %get-tuple-element.19, f32[2,4,128]{2,1,0:T(4,128)S(1)} %reverse_select_fusion.4, f32[2,4,128]{2,1,0:T(4,128)S(1)} %reverse_select_fusion.5, pred[512]{0:T(512)(128)(4,1)S(1)} %get-tuple-element.88, ...), kind=kLoop, calls=%fused_computation.31 | loop fusion | flops 7340032 | bytes 9455104 | tf_op jit(solution)/shard_map/broadcast_in_dim | solution.py:417
  (112 shorter events, 0.9 us)
Async XLA Ops:
  0.6 11.5 %copy-start = (bf16[1024,256]{1,0:T(8,128)(2,1)S(1)}, bf16[1024,256]{1,0:T(8,128)(2,1)}, u32[]{:S(2)}) copy-start(bf16[1024,256]{1,0:T(8,128)(2,1)} %param.11) | copy-start | bytes 1572868
  0.6 9.5 %copy-start.12 = (s32[1024,1]{0,1:T(1,128)S(1)}, s32[1024,1]{0,1:T(1,128)}, u32[]{:S(2)}) copy-start(s32[1024,1]{0,1:T(1,128)} %param.12) | copy-start | bytes 12292
  0.7 10.0 %copy-start.15 = (s32[1024]{0:T(1024)S(1)}, s32[1024]{0:T(1024)}, u32[]{:S(2)}) copy-start(s32[1024]{0:T(1024)} %param.13) | copy-start | bytes 12292
  2.5 25.1 %copy-start.1 = (bf16[2,4,512,256]{3,2,1,0:T(8,128)(2,1)}, bf16[2,4,512,256]{3,2,1,0:T(8,128)(2,1)S(1)}, u32[]{:S(2)}) copy-start(bf16[2,4,512,256]{3,2,1,0:T(8,128)(2,1)S(1)} %pad_maximum_fusion.1.src_ref) | copy-start | bytes 6291460
  3.7 29.9 %collective-permute-start.1 = (bf16[2,1,512,256]{3,2,1,0:T(8,128)(2,1)}, bf16[2,1,512,256]{3,2,1,0:T(8,128)(2,1)}, u32[]{:S(2)}, u32[]{:S(2)}) collective-permute-start(bf16[2,1,512,256]{3,2,1,0:T(8,128)(2,1)} %get-tuple-element.24), channel_id=1, source_target_pairs={{1,0},{2,1},{3,2},{4,3},{5,4},{6,5},{7,6},{8,7},{9,8},{10,9},{11,1... | collective-permute-start | bytes 1572872 | tf_op jit(solution)/shard_map/ppermute | solution.py:264
  8.2 26.7 %collective-permute-start = (bf16[2,1,512,256]{3,2,1,0:T(8,128)(2,1)}, bf16[2,1,512,256]{3,2,1,0:T(8,128)(2,1)}, u32[]{:S(2)}, u32[]{:S(2)}) collective-permute-start(bf16[2,1,512,256]{3,2,1,0:T(8,128)(2,1)} %get-tuple-element.25), channel_id=1, source_target_pairs={{0,1},{1,2},{2,3},{3,4},{4,5},{5,6},{6,7},{7,8},{8,9},{9,10},{10,1... | collective-permute-start | bytes 1572872 | tf_op jit(solution)/shard_map/ppermute | solution.py:263
  13.7 13.0 %copy-start.13 = (s32[8,2,3]{0,1,2:T(2,128)S(1)}, s32[8,2,3]{0,1,2:T(2,128)}, u32[]{:S(2)}) copy-start(s32[8,2,3]{0,1,2:T(2,128)} %param.14) | copy-start | bytes 580
  13.7 19.8 %copy-start.10 = (bf16[9,128,256]{2,1,0:T(8,128)(2,1)S(1)}, bf16[9,128,256]{2,1,0:T(8,128)(2,1)}, u32[]{:S(2)}) copy-start(bf16[9,128,256]{2,1,0:T(8,128)(2,1)} %k_ref.6) | copy-start | bytes 1769476
  15.1 44.0 %all-to-all-start = ((bf16[128,17,256]{2,1,0:T(8,128)(2,1)}), bf16[128,17,256]{2,1,0:T(8,128)(2,1)}, u32[]{:S(2)}, u32[]{:S(2)}) async-start(bf16[128,17,256]{2,1,0:T(8,128)(2,1)} %pad_maximum_fusion.2), calls=%async_computation | async-start | bytes 3145728 | tf_op jit(solution)/shard_map/all_to_all | solution.py:349
  27.6 16.2 %slice-start = ((bf16[2,4,512,256]{3,2,1,0:T(8,128)(2,1)}), bf16[2,4,512,128]{3,2,1,0:T(8,128)(2,1)S(1)}, s32[]{:S(2)}) async-start(bf16[2,4,512,256]{3,2,1,0:T(8,128)(2,1)} %copy-done.1), calls=%async_computation.1 | async-start | bytes 2097152 | tf_op jit(solution)/shard_map/slice | solution.py:270
  34.9 0.8 copy-start.4
  62.0 5.4 %copy-start.5 = (f32[2,4,512,256]{3,2,1,0:T(8,128)S(1)}, f32[2,4,512,256]{3,2,1,0:T(8,128)}, u32[]{:S(2)}) copy-start(f32[2,4,512,256]{3,2,1,0:T(8,128)} %get-tuple-element.15) | copy-start | bytes 12582916
  62.1 5.4 %copy-start.6 = (f32[2,4,512,256]{3,2,1,0:T(8,128)S(1)}, f32[2,4,512,256]{3,2,1,0:T(8,128)}, u32[]{:S(2)}) copy-start(f32[2,4,512,256]{3,2,1,0:T(8,128)} %get-tuple-element.13) | copy-start | bytes 12582916
  62.1 5.4 %copy-start.14 = (f32[256]{0:T(256)S(1)}, f32[256]{0:T(256)}, u32[]{:S(2)}) copy-start(f32[256]{0:T(256)} %param.16) | copy-start | bytes 3076
  72.5 6.0 %copy-start.7 = (bf16[9,256,128]{2,1,0:T(8,128)(2,1)S(1)}, bf16[9,256,128]{2,1,0:T(8,128)(2,1)}, u32[]{:S(2)}) copy-start(bf16[9,256,128]{2,1,0:T(8,128)(2,1)} %k_ref.7) | copy-start | bytes 1769476
  72.7 25.0 %collective-permute-start.3 = (bf16[2,1,512,512]{3,2,1,0:T(8,128)(2,1)S(1)}, bf16[2,1,512,512]{3,2,1,0:T(8,128)(2,1)S(1)}, u32[]{:S(2)}, u32[]{:S(2)}) collective-permute-start(bf16[2,1,512,512]{3,2,1,0:T(8,128)(2,1)S(1)} %get-tuple-element.22), channel_id=1, source_target_pairs={{1,0},{2,1},{3,2},{4,3},{5,4},{6,5},{7,6},{8,7},{9,8},{10,9},{11,1... | collective-permute-start | bytes 3145736 | tf_op jit(solution)/shard_map/ppermute | solution.py:264
  76.4 25.2 %collective-permute-start.2 = (bf16[2,1,512,512]{3,2,1,0:T(8,128)(2,1)S(1)}, bf16[2,1,512,512]{3,2,1,0:T(8,128)(2,1)S(1)}, u32[]{:S(2)}, u32[]{:S(2)}) collective-permute-start(bf16[2,1,512,512]{3,2,1,0:T(8,128)(2,1)S(1)} %get-tuple-element.23), channel_id=1, source_target_pairs={{0,1},{1,2},{2,3},{3,4},{4,5},{5,6},{6,7},{7,8},{8,9},{9,10},{10,1... | collective-permute-start | bytes 3145736 | tf_op jit(solution)/shard_map/ppermute | solution.py:263
  98.0 3.7 %copy-start.2 = (bf16[2,1,512,512]{3,2,1,0:T(8,128)(2,1)}, bf16[2,1,512,512]{3,2,1,0:T(8,128)(2,1)S(1)}, u32[]{:S(2)}) copy-start(bf16[2,1,512,512]{3,2,1,0:T(8,128)(2,1)S(1)} %reverse_select_fusion.after_ref) | copy-start | bytes 3145732
  101.5 1.0 copy-start.3
  111.7 13.8 %copy-start.11 = (bf16[256,128]{1,0:T(8,128)(2,1)S(1)}, bf16[256,128]{1,0:T(8,128)(2,1)}, u32[]{:S(2)}) copy-start(bf16[256,128]{1,0:T(8,128)(2,1)} %get-tuple-element.29) | copy-start | bytes 196612
  122.8 3.4 %copy-start.8 = (bf16[1,1,2,4,512,128]{5,4,3,2,1,0:T(8,128)(2,1)S(1)}, bf16[1,1,2,4,512,128]{5,4,3,2,1,0:T(8,128)(2,1)}, u32[]{:S(2)}) copy-start(bf16[1,1,2,4,512,128]{5,4,3,2,1,0:T(8,128)(2,1)} %param.19) | copy-start | bytes 3145732
  122.8 3.4 %copy-start.9 = (bf16[1,1,2,4,512,128]{5,4,3,2,1,0:T(8,128)(2,1)S(1)}, bf16[1,1,2,4,512,128]{5,4,3,2,1,0:T(8,128)(2,1)}, u32[]{:S(2)}) copy-start(bf16[1,1,2,4,512,128]{5,4,3,2,1,0:T(8,128)(2,1)} %param.10) | copy-start | bytes 3145732

commit v9 on v8

--- a/solution.py
+++ b/solution.py
@@ -100,14 +100,14 @@
     col = lax.broadcasted_iota(jnp.int32, (rows, cols, cout), 1).reshape(pixels, cout)
     ext = jnp.concatenate([before_ref[0], src_ref[0], after_ref[0]], axis=0)
     lhs = jnp.concatenate([ext[dy : dy + rows].reshape(pixels, width) for dy in range(3)], axis=1)
-    products = []
+    stacks = []
     for col_tap in range(3):
         taps = [k_ref[3 * (2 - dy + band * (2 * dy - 2)) + 2 - col_tap] for dy in range(3)]
-        stack = jnp.concatenate(taps, axis=1)
-        products.append(
-            lax.dot_general(lhs, stack, (((1,), (1,)), ((), ())), preferred_element_type=jnp.float32)
-        )
-    z_left, z_mid, z_right = products
+        stacks.append(jnp.concatenate(taps, axis=1))
+    joined = lax.dot_general(
+        lhs, jnp.concatenate(stacks, axis=0), (((1,), (1,)), ((), ())), preferred_element_type=jnp.float32
+    )
+    z_left, z_mid, z_right = [joined[:, i * cout : (i + 1) * cout] for i in range(3)]
     from_left = jnp.where(col == 0, 0.0, pltpu.roll(z_left, 1, 0))
     from_right = jnp.where(col == cols - 1, 0.0, pltpu.roll(z_right, pixels - 1, 0))
     out_ref[0] = (z_mid + from_left + from_right).reshape(rows, cols, cout)
@@ -177,12 +177,12 @@
     col = lax.broadcasted_iota(jnp.int32, (rows, cols, cout), 1).reshape(pixels, cout)
     ext = jnp.concatenate([before_ref[0], src_ref[0], after_ref[0]], axis=0)
     lhs = jnp.concatenate([ext[dy : dy + rows].reshape(pixels, width) for dy in range(3)], axis=1)
-    products = []
+    stacks = []
     for col_tap in range(3):
         taps = [k_ref[3 * (dy + step_at * (2 - 2 * dy)) + col_tap] for dy in range(3)]
-        stack = jnp.concatenate(taps, axis=0)
-        products.append(jnp.dot(lhs, stack, preferred_element_type=jnp.float32))
-    z_left, z_mid, z_right = products
+        stacks.append(jnp.concatenate(taps, axis=0))
+    joined = jnp.dot(lhs, jnp.concatenate(stacks, axis=1), preferred_element_type=jnp.float32)
+    z_left, z_mid, z_right = [joined[:, i * cout : (i + 1) * cout] for i in range(3)]
     from_left = jnp.where(col == 0, 0.0, pltpu.roll(z_left, 1, 0))
     from_right = jnp.where(col == cols - 1, 0.0, pltpu.roll(z_right, pixels - 1, 0))
     out_ref[0] = (z_mid + from_left + from_right).reshape(rows, cols, cout)

time: 132 us -> 129 us (0.977)
  Pallas kernels: 37 us -> 34.4 us
    pallas_call x2, Pallas kernels: 14.3 us -> 12.7 us  [conv_back(): pl.pallas_call(back_kernel, grid=(bands,), in_specs=[pl.BlockSpec((1, row...]
where the time goes in v9:
time: 129 us
  Pallas kernels  34.4 us (27%)
  starting transfers between devices  23.9 us (19%)
  other arithmetic  22.4 us (17%)
  waiting for transfers between devices  19.6 us (15%)
  local copies, waits for them, and re-layouts  12.7 us (10%)
  matrix products  8.13 us (6%)
  between operations  7.53 us (6%)
    pallas_call x2, Pallas kernels, conv_gather(): pl.pallas_call(functools.partial(conv_gather_kernel, count), grid=(bands,...  21.7 us
    ppermute x2, waiting for transfers between devices, extend_rows(): after = lax.ppermute(head, 'tile', [(i + 1, i) for i in range(count - 1)])  16.1 us
    pallas_call x2, Pallas kernels, conv_back(): pl.pallas_call(back_kernel, grid=(bands,), in_specs=[pl.BlockSpec((1, row...  12.7 us
    all_to_all x1, starting transfers between devices, route_observations(): lax.all_to_all(payload, ('face', 'tile'), split_axis=0, concat_axis=0, ti...  11.6 us
    ppermute x2, starting transfers between devices, extend_rows(): after = lax.ppermute(head, 'tile', [(i + 1, i) for i in range(count - 1)])  8.23 us
    dot_general x1, matrix products, per_device(): gridded = jnp.dot(onehot, got_values, preferred_element_type=jnp.float32)  5.34 us
    broadcast_in_dim x1, other arithmetic, per_device(): return (analysis[None, None], grad_base[None, None])  5.17 us
    convert_element_type x1, other arithmetic, per_device(): inner = activation(pre_act).astype(jnp.bfloat16)  5.04 us
  transfers between devices with their start and end apart: 5, of which 2 were waited for; matrix products, arithmetic and copies ran while one was open for 12% of the time, Pallas kernels for 14%

profile of v9, /device:TPU:24, one launch (start us, length us, event | category | flops | bytes accessed | tf_op | source)
XLA Modules:
  0.0 128.7 jit_solution(3191541128216456570)
XLA Ops:
  0.6 0.0 copy-start
  0.7 1.8 %pad_maximum_fusion.1.src_ref = bf16[2,4,512,256]{3,2,1,0:T(8,128)(2,1)S(1)} fusion(bf16[2,4,512,128]{3,2,1,0:T(8,128)(2,1)} %bitcast.235, bf16[2,4,512,128]{3,2,1,0:T(8,128)(2,1)} %bitcast.236), kind=kLoop, calls=%fused_computation.30 | loop fusion | flops 4194304 | bytes 4194304 | tf_op jit(solution)/shard_map/concatenate | solution.py:393
  2.5 1.1 fusion.147
  3.7 4.5 %collective-permute-start.1 = (bf16[2,1,512,256]{3,2,1,0:T(8,128)(2,1)}, bf16[2,1,512,256]{3,2,1,0:T(8,128)(2,1)}, u32[]{:S(2)}, u32[]{:S(2)}) collective-permute-start(bf16[2,1,512,256]{3,2,1,0:T(8,128)(2,1)} %get-tuple-element.24), channel_id=1, source_target_pairs={{1,0},{2,1},{3,2},{4,3},{5,4},{6,5},{7,6},{8,7},{9,8},{10,9},{11,1... | collective-permute-start | bytes 1572872 | tf_op jit(solution)/shard_map/ppermute | solution.py:264
  8.2 1.9 %collective-permute-start = (bf16[2,1,512,256]{3,2,1,0:T(8,128)(2,1)}, bf16[2,1,512,256]{3,2,1,0:T(8,128)(2,1)}, u32[]{:S(2)}, u32[]{:S(2)}) collective-permute-start(bf16[2,1,512,256]{3,2,1,0:T(8,128)(2,1)} %get-tuple-element.25), channel_id=1, source_target_pairs={{0,1},{1,2},{2,3},{3,4},{4,5},{5,6},{6,7},{7,8},{8,9},{9,10},{10,1... | collective-permute-start | bytes 1572872 | tf_op jit(solution)/shard_map/ppermute | solution.py:263
  10.2 0.5 convert_reduce_fusion
  10.7 0.9 select_reduce_fusion
  11.6 0.1 reduce_sum.22
  11.7 0.1 fusion.50
  11.8 0.1 pad.43.clone
  11.9 0.1 maximum_bitcast_fusion
  12.0 0.1 copy.113
  12.1 1.6 %fusion.14 = bf16[2048,256]{1,0:T(8,128)(2,1)S(1)} fusion(bf16[1024,256]{1,0:T(8,128)(2,1)S(1)} %copy-done, s32[1024]{0:T(1024)S(1)} %multiply_add_fusion.1), kind=kOutput, calls=%fused_computation.29 | convolution fusion | flops 1076363264 | bytes 1576960 | tf_op jit(solution)/shard_map/dot_general | solution.py:337
  13.8 1.4 %pad_maximum_fusion.2 = bf16[128,17,256]{2,1,0:T(8,128)(2,1)} fusion(bf16[128,1,256]{2,1,0:T(2,128)(2,1)S(1)} %copy.113, bf16[128,16,256]{2,1,0:T(8,128)(2,1)S(1)} %bitcast.238), kind=kLoop, calls=%fused_computation.33 | loop fusion | flops 2228224 | bytes 2228224 | tf_op jit(solution)/shard_map/concatenate | solution.py:346
  15.1 11.6 %all-to-all-start = ((bf16[128,17,256]{2,1,0:T(8,128)(2,1)}), bf16[128,17,256]{2,1,0:T(8,128)(2,1)}, u32[]{:S(2)}, u32[]{:S(2)}) async-start(bf16[128,17,256]{2,1,0:T(8,128)(2,1)} %pad_maximum_fusion.2), calls=%async_computation | async-start | bytes 3145728 | tf_op jit(solution)/shard_map/all_to_all | solution.py:349
  26.8 0.1 constant_dynamic-slice_fusion.8
  26.9 0.1 copy.115
  27.0 0.6 fusion.152
  33.6 1.3 %reverse_select_fusion.1.after_ref = bf16[2,1,512,256]{3,2,1,0:T(8,128)(2,1)S(1)} fusion(bf16[2,1,512,256]{3,2,1,0:T(8,128)(2,1)} %collective-permute-done.1, bf16[2,1,512,256]{3,2,1,0:T(8,128)(2,1)} %get-tuple-element.25, pred[]{:T(512)S(6)} %eq.131), kind=kLoop, calls=%fused_computation.46 | loop fusion | flops 262144 | bytes 1572865 | tf_op jit(solution)/shard_map/jit(_where)/select_n | solution.py:265
  35.0 0.7 copy-done.4
  35.7 6.4 %shard_map.113 = (f32[2,4,512,256]{3,2,1,0:T(8,128)}, f32[2,2,4,256]{3,2,1,0:T(4,128)}) custom-call(bf16[2,4,512,256]{3,2,1,0:T(8,128)(2,1)} %copy-done.1, bf16[2,1,512,256]{3,2,1,0:T(8,128)(2,1)} %collective-permute-done.before_ref, bf16[2,1,512,256]{3,2,1,0:T(8,128)(2,1)} %copy-done.4, bf16[9,256,128]{2,1,0:T(8,128)(2,1)} %k_ref.7), custom_call_target="tpu_custom_call" | custom-call | tf_op jit(solution)/shard_map/pallas_call | solution.py:123
  42.1 0.7 copy.114
  42.9 1.0 slice.386
  43.9 0.6 maximum_bitcast_fusion.2.block_ref
  44.5 11.7 %shard_map.114 = (f32[2,4,512,256]{3,2,1,0:T(8,128)}, f32[8,56,128]{2,1,0:T(8,128)}) custom-call(f32[56,128]{1,0:T(8,128)} %maximum_bitcast_fusion.2.block_ref, bf16[2,4,512,256]{3,2,1,0:T(8,128)(2,1)} %copy-done.1, bf16[2,1,512,256]{3,2,1,0:T(8,128)(2,1)} %collective-permute-done.before_ref, bf16[2,1,512,256]{3,2,1,0:T(8,128)(2,1)} %copy-done.4, ...), custom_call_target="tpu_custom_call" | custom-call | tf_op jit(solution)/shard_map/pallas_call | solution.py:205
  56.3 1.0 copy.189
  57.3 0.6 gather_fusion
  57.9 0.1 broadcast_select_fusion.1
  58.4 0.1 convolution_bitcast_fusion.1
  58.5 0.1 convolution_bitcast_fusion
  58.7 0.1 convolution_bitcast_fusion.3
  58.9 0.1 convolution_bitcast_fusion.2
  59.1 1.5 %fusion.53 = s32[128,16]{1,0:T(8,128)S(1)} fusion(bf16[128,17,256]{2,1,0:T(8,128)(2,1)} %all-to-all-done), kind=kLoop, calls=%fused_computation.92 | loop fusion | flops 8192 | bytes 16384 | tf_op jit(solution)/shard_map/add | solution.py:353
  60.6 0.1 add.158
  60.7 1.3 %slice.409 = bf16[128,16,256]{2,1,0:T(8,128)(2,1)S(1)} slice(bf16[128,17,256]{2,1,0:T(8,128)(2,1)} %all-to-all-done), slice={[0:128], [0:16], [0:256]} | slice | bytes 2097152 | tf_op jit(solution)/shard_map/slice | solution.py:350
  62.1 0.0 copy-start.14
  62.1 5.3 %fusion = f32[2,4,512,256]{3,2,1,0:T(8,128)S(1)} fusion(bf16[2048,256,1,1]{1,0,3,2:T(8,128)(2,1)S(1)} %bitcast.237, s32[2048]{0:T(1024)S(1)} %add.158, s32[2,4,512]{2,1,0:T(4,128)S(1)} %multiply_add_fusion), kind=kOutput, calls=%fused_computation.2 | convolution fusion | flops 4303355904 | bytes 5267456 | tf_op jit(solution)/shard_map/dot_general | solution.py:385
  67.4 5.0 %multiply_convert_fusion = (bf16[2,4,512,256]{3,2,1,0:T(8,128)(2,1)S(1)}, bf16[2,4,512,256]{3,2,1,0:T(8,128)(2,1)S(1)}) fusion(f32[2,4,512,256]{3,2,1,0:T(8,128)S(1)} %fusion, f32[256]{0:T(256)S(1)} %copy-done.14, f32[2,4,256]{2,1,0:T(4,128)S(1)} %get-tuple-element.49, pred[512]{0:T(512)(128)(4,1)S(1)} %get-tuple-element.88, ...), kind=kLoop, calls=%fused_computation.23 | loop fusion | flops 33554432 | bytes 16812032 | tf_op jit(solution)/shard_map/convert_element_type | solution.py:403
  72.5 0.0 copy-start.7
  72.5 0.2 fusion.17
  72.7 3.7 %collective-permute-start.3 = (bf16[2,1,512,512]{3,2,1,0:T(8,128)(2,1)S(1)}, bf16[2,1,512,512]{3,2,1,0:T(8,128)(2,1)S(1)}, u32[]{:S(2)}, u32[]{:S(2)}) collective-permute-start(bf16[2,1,512,512]{3,2,1,0:T(8,128)(2,1)S(1)} %get-tuple-element.22), channel_id=1, source_target_pairs={{1,0},{2,1},{3,2},{4,3},{5,4},{6,5},{7,6},{8,7},{9,8},{10,9},{11,1... | collective-permute-start | bytes 3145736 | tf_op jit(solution)/shard_map/ppermute | solution.py:264
  76.4 2.1 %collective-permute-start.2 = (bf16[2,1,512,512]{3,2,1,0:T(8,128)(2,1)S(1)}, bf16[2,1,512,512]{3,2,1,0:T(8,128)(2,1)S(1)}, u32[]{:S(2)}, u32[]{:S(2)}) collective-permute-start(bf16[2,1,512,512]{3,2,1,0:T(8,128)(2,1)S(1)} %get-tuple-element.23), channel_id=1, source_target_pairs={{0,1},{1,2},{2,3},{3,4},{4,5},{5,6},{6,7},{7,8},{8,9},{9,10},{10,1... | collective-permute-start | bytes 3145736 | tf_op jit(solution)/shard_map/ppermute | solution.py:263
  78.5 0.7 slice_bitcast_fusion.3
  79.2 2.3 %pad_maximum_fusion.src_ref = bf16[2,4,512,512]{3,2,1,0:T(8,128)(2,1)} fusion(bf16[2,4,512,256]{3,2,1,0:T(8,128)(2,1)S(1)} %get-tuple-element.21, bf16[2,4,512,256]{3,2,1,0:T(8,128)(2,1)S(1)} %get-tuple-element.20), kind=kLoop, calls=%fused_computation.13 | loop fusion | flops 8388608 | bytes 8388608 | tf_op jit(solution)/shard_map/concatenate | solution.py:407
  81.6 16.1 %collective-permute-done.3 = bf16[2,1,512,512]{3,2,1,0:T(8,128)(2,1)S(1)} collective-permute-done((bf16[2,1,512,512]{3,2,1,0:T(8,128)(2,1)S(1)}, bf16[2,1,512,512]{3,2,1,0:T(8,128)(2,1)S(1)}, u32[]{:S(2)}, u32[]{:S(2)}) %collective-permute-start.3) | collective-permute-done | bytes 1048608 | tf_op jit(solution)/shard_map/ppermute | solution.py:264
  97.7 0.3 reverse_select_fusion.after_ref
  98.0 3.5 %collective-permute-done.2.before_ref = bf16[2,1,512,512]{3,2,1,0:T(8,128)(2,1)S(1)} collective-permute-done((bf16[2,1,512,512]{3,2,1,0:T(8,128)(2,1)S(1)}, bf16[2,1,512,512]{3,2,1,0:T(8,128)(2,1)S(1)}, u32[]{:S(2)}, u32[]{:S(2)}) %collective-permute-start.2) | collective-permute-done | bytes 1048608 | tf_op jit(solution)/shard_map/ppermute | solution.py:263
  101.6 0.9 copy-done.3
  102.5 6.3 %shard_map.115 = (f32[2,4,512,128]{3,2,1,0:T(8,128)}, f32[2,2,4,128]{3,2,1,0:T(4,128)}) custom-call(bf16[2,4,512,512]{3,2,1,0:T(8,128)(2,1)} %pad_maximum_fusion.src_ref, bf16[2,1,512,512]{3,2,1,0:T(8,128)(2,1)} %copy-done.3, bf16[2,1,512,512]{3,2,1,0:T(8,128)(2,1)} %copy-done.2, bf16[9,128,256]{2,1,0:T(8,128)(2,1)} %k_ref.6), custom_call_target="tpu_custom_call" | custom-call | tf_op jit(solution)/shard_map/pallas_call | solution.py:123
  108.8 0.7 copy.120
  109.5 0.6 maximum_bitcast_fusion.1.block_ref
  110.1 10.0 %shard_map.116 = (f32[2,4,512,128]{3,2,1,0:T(8,128)}, f32[8,64,128]{2,1,0:T(8,128)}) custom-call(f32[64,128]{1,0:T(8,128)} %maximum_bitcast_fusion.1.block_ref, bf16[2,4,512,512]{3,2,1,0:T(8,128)(2,1)} %pad_maximum_fusion.src_ref, bf16[2,1,512,512]{3,2,1,0:T(8,128)(2,1)} %copy-done.3, bf16[2,1,512,512]{3,2,1,0:T(8,128)(2,1)} %copy-done.2, ...), custom_call_target="tpu_custom_call" | custom-call | tf_op jit(solution)/shard_map/pallas_call | solution.py:205
  120.1 0.0 copy-start.8
  120.1 1.3 copy.188
  121.4 0.6 gather_fusion.1
  122.0 0.1 broadcast_select_fusion
  122.1 0.1 constant_dynamic-slice_fusion.3
  122.2 0.1 rev.36
  122.5 0.1 rev.37
  122.9 0.1 convolution_bitcast_fusion.5
  123.0 0.1 convolution_bitcast_fusion.4
  123.2 0.2 convolution_bitcast_fusion.7
  123.3 0.2 convolution_bitcast_fusion.6
  123.5 5.2 %add_bitcast_fusion = (f32[1,1,2,4,512,128]{5,4,3,2,1,0:T(8,128)}, bf16[1,1,2,4,512,128]{5,4,3,2,1,0:T(8,128)(2,1)}) fusion(f32[2,4,512,128]{3,2,1,0:T(8,128)} %get-tuple-element.19, f32[2,4,128]{2,1,0:T(4,128)S(1)} %reverse_select_fusion.4, f32[2,4,128]{2,1,0:T(4,128)S(1)} %reverse_select_fusion.5, pred[512]{0:T(512)(128)(4,1)S(1)} %get-tuple-element.88, ...), kind=kLoop, calls=%fused_computation.31 | loop fusion | flops 7340032 | bytes 9455104 | tf_op jit(solution)/shard_map/broadcast_in_dim | solution.py:417
  (112 shorter events, 0.9 us)
Async XLA Ops:
  0.6 11.5 %copy-start = (bf16[1024,256]{1,0:T(8,128)(2,1)S(1)}, bf16[1024,256]{1,0:T(8,128)(2,1)}, u32[]{:S(2)}) copy-start(bf16[1024,256]{1,0:T(8,128)(2,1)} %param.11) | copy-start | bytes 1572868
  0.6 9.5 %copy-start.12 = (s32[1024,1]{0,1:T(1,128)S(1)}, s32[1024,1]{0,1:T(1,128)}, u32[]{:S(2)}) copy-start(s32[1024,1]{0,1:T(1,128)} %param.12) | copy-start | bytes 12292
  0.7 10.0 %copy-start.15 = (s32[1024]{0:T(1024)S(1)}, s32[1024]{0:T(1024)}, u32[]{:S(2)}) copy-start(s32[1024]{0:T(1024)} %param.13) | copy-start | bytes 12292
  2.5 25.1 %copy-start.1 = (bf16[2,4,512,256]{3,2,1,0:T(8,128)(2,1)}, bf16[2,4,512,256]{3,2,1,0:T(8,128)(2,1)S(1)}, u32[]{:S(2)}) copy-start(bf16[2,4,512,256]{3,2,1,0:T(8,128)(2,1)S(1)} %pad_maximum_fusion.1.src_ref) | copy-start | bytes 6291460
  3.7 29.9 %collective-permute-start.1 = (bf16[2,1,512,256]{3,2,1,0:T(8,128)(2,1)}, bf16[2,1,512,256]{3,2,1,0:T(8,128)(2,1)}, u32[]{:S(2)}, u32[]{:S(2)}) collective-permute-start(bf16[2,1,512,256]{3,2,1,0:T(8,128)(2,1)} %get-tuple-element.24), channel_id=1, source_target_pairs={{1,0},{2,1},{3,2},{4,3},{5,4},{6,5},{7,6},{8,7},{9,8},{10,9},{11,1... | collective-permute-start | bytes 1572872 | tf_op jit(solution)/shard_map/ppermute | solution.py:264
  8.2 26.7 %collective-permute-start = (bf16[2,1,512,256]{3,2,1,0:T(8,128)(2,1)}, bf16[2,1,512,256]{3,2,1,0:T(8,128)(2,1)}, u32[]{:S(2)}, u32[]{:S(2)}) collective-permute-start(bf16[2,1,512,256]{3,2,1,0:T(8,128)(2,1)} %get-tuple-element.25), channel_id=1, source_target_pairs={{0,1},{1,2},{2,3},{3,4},{4,5},{5,6},{6,7},{7,8},{8,9},{9,10},{10,1... | collective-permute-start | bytes 1572872 | tf_op jit(solution)/shard_map/ppermute | solution.py:263
  13.7 13.0 %copy-start.13 = (s32[8,2,3]{0,1,2:T(2,128)S(1)}, s32[8,2,3]{0,1,2:T(2,128)}, u32[]{:S(2)}) copy-start(s32[8,2,3]{0,1,2:T(2,128)} %param.14) | copy-start | bytes 580
  13.7 19.8 %copy-start.10 = (bf16[9,128,256]{2,1,0:T(8,128)(2,1)S(1)}, bf16[9,128,256]{2,1,0:T(8,128)(2,1)}, u32[]{:S(2)}) copy-start(bf16[9,128,256]{2,1,0:T(8,128)(2,1)} %k_ref.6) | copy-start | bytes 1769476
  15.1 44.0 %all-to-all-start = ((bf16[128,17,256]{2,1,0:T(8,128)(2,1)}), bf16[128,17,256]{2,1,0:T(8,128)(2,1)}, u32[]{:S(2)}, u32[]{:S(2)}) async-start(bf16[128,17,256]{2,1,0:T(8,128)(2,1)} %pad_maximum_fusion.2), calls=%async_computation | async-start | bytes 3145728 | tf_op jit(solution)/shard_map/all_to_all | solution.py:349
  27.6 16.2 %slice-start = ((bf16[2,4,512,256]{3,2,1,0:T(8,128)(2,1)}), bf16[2,4,512,128]{3,2,1,0:T(8,128)(2,1)S(1)}, s32[]{:S(2)}) async-start(bf16[2,4,512,256]{3,2,1,0:T(8,128)(2,1)} %copy-done.1), calls=%async_computation.1 | async-start | bytes 2097152 | tf_op jit(solution)/shard_map/slice | solution.py:270
  34.9 0.8 copy-start.4
  62.0 5.4 %copy-start.5 = (f32[2,4,512,256]{3,2,1,0:T(8,128)S(1)}, f32[2,4,512,256]{3,2,1,0:T(8,128)}, u32[]{:S(2)}) copy-start(f32[2,4,512,256]{3,2,1,0:T(8,128)} %get-tuple-element.15) | copy-start | bytes 12582916
  62.1 5.4 %copy-start.6 = (f32[2,4,512,256]{3,2,1,0:T(8,128)S(1)}, f32[2,4,512,256]{3,2,1,0:T(8,128)}, u32[]{:S(2)}) copy-start(f32[2,4,512,256]{3,2,1,0:T(8,128)} %get-tuple-element.13) | copy-start | bytes 12582916
  62.1 5.4 %copy-start.14 = (f32[256]{0:T(256)S(1)}, f32[256]{0:T(256)}, u32[]{:S(2)}) copy-start(f32[256]{0:T(256)} %param.16) | copy-start | bytes 3076
  72.5 6.0 %copy-start.7 = (bf16[9,256,128]{2,1,0:T(8,128)(2,1)S(1)}, bf16[9,256,128]{2,1,0:T(8,128)(2,1)}, u32[]{:S(2)}) copy-start(bf16[9,256,128]{2,1,0:T(8,128)(2,1)} %k_ref.7) | copy-start | bytes 1769476
  72.7 25.0 %collective-permute-start.3 = (bf16[2,1,512,512]{3,2,1,0:T(8,128)(2,1)S(1)}, bf16[2,1,512,512]{3,2,1,0:T(8,128)(2,1)S(1)}, u32[]{:S(2)}, u32[]{:S(2)}) collective-permute-start(bf16[2,1,512,512]{3,2,1,0:T(8,128)(2,1)S(1)} %get-tuple-element.22), channel_id=1, source_target_pairs={{1,0},{2,1},{3,2},{4,3},{5,4},{6,5},{7,6},{8,7},{9,8},{10,9},{11,1... | collective-permute-start | bytes 3145736 | tf_op jit(solution)/shard_map/ppermute | solution.py:264
  76.4 25.1 %collective-permute-start.2 = (bf16[2,1,512,512]{3,2,1,0:T(8,128)(2,1)S(1)}, bf16[2,1,512,512]{3,2,1,0:T(8,128)(2,1)S(1)}, u32[]{:S(2)}, u32[]{:S(2)}) collective-permute-start(bf16[2,1,512,512]{3,2,1,0:T(8,128)(2,1)S(1)} %get-tuple-element.23), channel_id=1, source_target_pairs={{0,1},{1,2},{2,3},{3,4},{4,5},{5,6},{6,7},{7,8},{8,9},{9,10},{10,1... | collective-permute-start | bytes 3145736 | tf_op jit(solution)/shard_map/ppermute | solution.py:263
  98.0 3.7 %copy-start.2 = (bf16[2,1,512,512]{3,2,1,0:T(8,128)(2,1)}, bf16[2,1,512,512]{3,2,1,0:T(8,128)(2,1)S(1)}, u32[]{:S(2)}) copy-start(bf16[2,1,512,512]{3,2,1,0:T(8,128)(2,1)S(1)} %reverse_select_fusion.after_ref) | copy-start | bytes 3145732
  101.5 1.0 copy-start.3
  110.1 12.7 %copy-start.11 = (bf16[256,128]{1,0:T(8,128)(2,1)S(1)}, bf16[256,128]{1,0:T(8,128)(2,1)}, u32[]{:S(2)}) copy-start(bf16[256,128]{1,0:T(8,128)(2,1)} %get-tuple-element.29) | copy-start | bytes 196612
  120.1 3.4 %copy-start.8 = (bf16[1,1,2,4,512,128]{5,4,3,2,1,0:T(8,128)(2,1)S(1)}, bf16[1,1,2,4,512,128]{5,4,3,2,1,0:T(8,128)(2,1)}, u32[]{:S(2)}) copy-start(bf16[1,1,2,4,512,128]{5,4,3,2,1,0:T(8,128)(2,1)} %param.19) | copy-start | bytes 3145732
  120.1 3.4 %copy-start.9 = (bf16[1,1,2,4,512,128]{5,4,3,2,1,0:T(8,128)(2,1)S(1)}, bf16[1,1,2,4,512,128]{5,4,3,2,1,0:T(8,128)(2,1)}, u32[]{:S(2)}) copy-start(bf16[1,1,2,4,512,128]{5,4,3,2,1,0:T(8,128)(2,1)} %param.10) | copy-start | bytes 3145732

commit v10 on v9

--- a/solution.py
+++ b/solution.py
@@ -141,8 +141,13 @@
     )(source, before, after, kernel)
 
 
-def conv_gather_kernel(count, block_ref, src_ref, before_ref, after_ref, k_ref,
-                       out_ref, gathered_ref, landed, send_sems, recv_sems):
+def conv_gather_kernel(count, block_ref, src_ref, before_ref, after_ref, k_ref, *rest):
+    if len(rest) == 7:
+        values_ref, pixels_ref = rest[:2]
+        rest = rest[2:]
+    else:
+        values_ref = None
+    out_ref, gathered_ref, landed, send_sems, recv_sems = rest
     step_at = pl.program_id(0)
     face = lax.axis_index("face")
     tile = lax.axis_index("tile")
@@ -185,7 +190,18 @@
     z_left, z_mid, z_right = [joined[:, i * cout : (i + 1) * cout] for i in range(3)]
     from_left = jnp.where(col == 0, 0.0, pltpu.roll(z_left, 1, 0))
     from_right = jnp.where(col == cols - 1, 0.0, pltpu.roll(z_right, pixels - 1, 0))
-    out_ref[0] = (z_mid + from_left + from_right).reshape(rows, cols, cout)
+    total = z_mid + from_left + from_right
+    if values_ref is not None:
+        slots = values_ref.shape[0]
+        chunk = 512
+        pixel_ids = step_at * pixels + lax.broadcasted_iota(jnp.int32, (pixels, chunk), 0)
+        for start in range(0, slots, chunk):
+            hits = pixel_ids == pixels_ref[:, start : start + chunk]
+            onehot = jnp.where(hits, 1.0, 0.0).astype(jnp.bfloat16)
+            total = total + jnp.dot(
+                onehot, values_ref[start : start + chunk], preferred_element_type=jnp.float32
+            )
+    out_ref[0] = total.reshape(rows, cols, cout)
 
     @pl.when(step_at == pl.num_programs(0) - 1)
     def _():
@@ -195,8 +211,16 @@
             gathered_ref[step] = landed[step]
 
 
-def conv_gather(pieces, first, width, block, kernel, gather_id):
+def conv_gather(pieces, first, width, block, kernel, gather_id, observed=None):
     source, before, after = pieces
+    extra_specs = []
+    extra_args = ()
+    if observed is not None:
+        extra_specs = [
+            pl.BlockSpec(observed[0].shape, lambda b: (0, 0)),
+            pl.BlockSpec(observed[1].shape, lambda b: (0, 0)),
+        ]
+        extra_args = observed
     bands, rows, cols, _ = source.shape
     cout = kernel.shape[2]
     count = lax.axis_size("face")
@@ -211,7 +235,8 @@
             pl.BlockSpec((1, 1, cols, width), lambda b: (b, 0, 0, lane_block)),
             pl.BlockSpec((1, 1, cols, width), lambda b: (b, 0, 0, lane_block)),
             pl.BlockSpec(kernel.shape, lambda b: (0, 0, 0)),
-        ],
+        ]
+        + extra_specs,
         out_specs=[
             pl.BlockSpec((1, rows, cols, cout), lambda b: (b, 0, 0, 0)),
             pl.BlockSpec((count, block_rows, lanes), lambda b: (0, 0, 0)),
@@ -228,7 +253,7 @@
         compiler_params=pltpu.CompilerParams(
             collective_id=gather_id, has_side_effects=True, vmem_limit_bytes=60 * 1024 * 1024
         ),
-    )(block, source, before, after, kernel)
+    )(block, source, before, after, kernel, *extra_args)
 
 
 def side_terms(sides, kernel):
@@ -379,11 +404,6 @@
     obs_width = obs_values.shape[1]
 
     got_values, got_pixels = route_observations(obs_values, obs_dest, obs_pixel, device_count)
-    pixel_count = 2 * band_rows * column_count
-    pixel_ids = lax.iota(jnp.int32, pixel_count)
-    onehot = (pixel_ids[:, None] == got_pixels[None, :]).astype(jnp.bfloat16)
-    gridded = jnp.dot(onehot, got_values, preferred_element_type=jnp.float32)
-    gridded = gridded.reshape(2, band_rows, column_count, obs_width)
 
     last_tile = tile_at == tile_count - 1
     matching_row = lax.dynamic_index_in_dim(matching, face_at, 0, keepdims=False)
@@ -395,11 +415,13 @@
     both = extend_rows(fields, last_tile)
     cot_back, cot_margins = conv_back(both, channels, channels, kernel_two)
     parts = [edge_cols(both, 0, channels), jnp.swapaxes(cot_margins, 1, 2)]
-    first_out, landed = conv_gather(both, 0, channels, pack_parts(parts), kernel_one, 0)
+    first_out, landed = conv_gather(
+        both, 0, channels, pack_parts(parts), kernel_one, 0, (got_values, got_pixels.reshape(1, -1))
+    )
     base_edges, cot_gathered = unpack_parts(landed, parts)
     first_sides = side_terms(side_columns(base_edges, matching_row), kernel_one)
 
-    pre_act = at_edges(first_out, first_sides[:, 0], first_sides[:, 1]) + bias_one + gridded
+    pre_act = at_edges(first_out, first_sides[:, 0], first_sides[:, 1]) + bias_one
     inner = activation(pre_act).astype(jnp.bfloat16)
     grad_inner = return_sides(cot_back, cot_gathered, matching_row)
     grad_pre = jax.vjp(activation, pre_act)[1](grad_inner)[0].astype(jnp.bfloat16)

time: 129 us -> 154 us (1.19); the launches traced: 129 us -> 152 us
  waiting for transfers between devices: 19.6 us -> 40.1 us
  matrix products: 8.13 us -> 2.81 us
  other arithmetic: 22.4 us -> 26.2 us
  local copies, waits for them, and re-layouts: 12.7 us -> 15 us
  Pallas kernels: 34.4 us -> 36.5 us
    all_to_all x1, waiting for transfers between devices: 0.01 us -> 19.6 us  [route_observations(): lax.all_to_all(payload, ('face', 'tile'), split_axis=0, concat_axis=0, ti...]
    dot_general x1 -> x0, matrix products: 5.34 us -> none  [per_device(): gridded = jnp.dot(onehot, got_values, preferred_element_type=jnp.float32)]
    pallas_call x2, Pallas kernels: 21.7 us -> 23.8 us  [conv_gather(): pl.pallas_call(functools.partial(conv_gather_kernel, count), grid=(bands,...]
    convert_element_type x1, other arithmetic: 5.04 us -> 6.82 us  [per_device(): inner = activation(pre_act).astype(jnp.bfloat16)]
    unnamed x60 -> x62, local copies, waits for them, and re-layouts: 4.04 us -> 4.09 us
  transfers between devices with their start and end apart: 5 -> 5, of which waited for: 2 -> 4; matrix products, arithmetic and copies ran while one was open for 12% -> 7% of each run, Pallas kernels for 14% -> 0%
where the time goes in v10:
time: 154 us; the launch traced here: 152 us
  waiting for transfers between devices  40.1 us (26%)
  Pallas kernels  36.5 us (24%)
  other arithmetic  26.2 us (17%)
  starting transfers between devices  23.4 us (15%)
  local copies, waits for them, and re-layouts  15 us (10%)
  between operations  7.9 us (5%)
  matrix products  2.81 us (2%)
    pallas_call x2, Pallas kernels, conv_gather(): pl.pallas_call(functools.partial(conv_gather_kernel, count), grid=(bands,...  23.8 us
    all_to_all x1, waiting for transfers between devices, route_observations(): lax.all_to_all(payload, ('face', 'tile'), split_axis=0, concat_axis=0, ti...  19.6 us
    ppermute x2, waiting for transfers between devices, extend_rows(): after = lax.ppermute(head, 'tile', [(i + 1, i) for i in range(count - 1)])  16 us
    pallas_call x2, Pallas kernels, conv_back(): pl.pallas_call(back_kernel, grid=(bands,), in_specs=[pl.BlockSpec((1, row...  12.7 us
    all_to_all x1, starting transfers between devices, route_observations(): lax.all_to_all(payload, ('face', 'tile'), split_axis=0, concat_axis=0, ti...  10.7 us
    ppermute x2, starting transfers between devices, extend_rows(): after = lax.ppermute(head, 'tile', [(i + 1, i) for i in range(count - 1)])  8.5 us
    convert_element_type x1, other arithmetic, per_device(): inner = activation(pre_act).astype(jnp.bfloat16)  6.82 us
    broadcast_in_dim x1, other arithmetic, per_device(): return (analysis[None, None], grad_base[None, None])  5.17 us
  transfers between devices with their start and end apart: 5, of which 4 were waited for; matrix products, arithmetic and copies ran while one was open for 7% of the time, Pallas kernels for 0%

profile of v10, /device:TPU:24, one launch (start us, length us, event | category | flops | bytes accessed | tf_op | source)
XLA Modules:
  0.0 151.8 jit_solution(6134857522306769916)
XLA Ops:
  0.6 0.0 copy-start
  0.6 1.3 convert_reduce_fusion
  1.9 0.7 multiply_add_fusion
  2.6 1.6 %select_reduce_fusion = s32[2048]{0:T(1024)S(1)} fusion(s32[1024]{0:T(1024)} %param.13, s32[1024]{0:T(1024)S(1)} %multiply_add_fusion), kind=kLoop, calls=%fused_computation.2 | loop fusion | flops 6289408 | bytes 16384 | tf_op jit(solution)/shard_map/reduce_sum | solution.py:365
  4.2 0.1 reduce_sum.22
  4.3 0.1 fusion.46
  4.4 0.1 pad.80.clone
  4.5 0.1 maximum_bitcast_fusion
  4.6 0.1 copy.126
  4.7 1.6 %fusion.10 = bf16[2048,256]{1,0:T(8,128)(2,1)S(1)} fusion(bf16[1024,256]{1,0:T(8,128)(2,1)S(1)} %copy-done, s32[1024]{0:T(1024)S(1)} %multiply_add_fusion), kind=kOutput, calls=%fused_computation.25 | convolution fusion | flops 1076363264 | bytes 1576960 | tf_op jit(solution)/shard_map/dot_general | solution.py:362
  6.3 1.4 pad_maximum_fusion.2
  7.7 10.7 %all-to-all-start = ((bf16[128,17,256]{2,1,0:T(8,128)(2,1)}), bf16[128,17,256]{2,1,0:T(8,128)(2,1)}, u32[]{:S(2)}, u32[]{:S(2)}) async-start(bf16[128,17,256]{2,1,0:T(8,128)(2,1)} %pad_maximum_fusion.2), calls=%async_computation | async-start | bytes 3145728 | tf_op jit(solution)/shard_map/all_to_all | solution.py:374
  18.4 0.1 constant_dynamic-slice_fusion.8
  18.5 1.8 %pad_maximum_fusion.1.src_ref = bf16[2,4,512,256]{3,2,1,0:T(8,128)(2,1)S(1)} fusion(bf16[2,4,512,128]{3,2,1,0:T(8,128)(2,1)} %bitcast.230, bf16[2,4,512,128]{3,2,1,0:T(8,128)(2,1)} %bitcast.231), kind=kLoop, calls=%fused_computation.26 | loop fusion | flops 4194304 | bytes 4194304 | tf_op jit(solution)/shard_map/concatenate | solution.py:413
  20.3 0.8 slice_bitcast_fusion.9
  21.1 19.6 %all-to-all-done = bf16[128,17,256]{2,1,0:T(8,128)(2,1)} async-done(((bf16[128,17,256]{2,1,0:T(8,128)(2,1)}), bf16[128,17,256]{2,1,0:T(8,128)(2,1)}, u32[]{:S(2)}, u32[]{:S(2)}) %all-to-all-start) | async-done | bytes 1114144 | tf_op jit(solution)/shard_map/all_to_all | solution.py:374
  40.7 2.3 %slice.386 = bf16[128,16,256]{2,1,0:T(8,128)(2,1)} slice(bf16[128,17,256]{2,1,0:T(8,128)(2,1)} %all-to-all-done), slice={[0:128], [0:16], [0:256]} | slice | bytes 2097152 | tf_op jit(solution)/shard_map/slice | solution.py:375
  42.9 1.1 fusion.143
  44.0 3.8 %collective-permute-start.1 = (bf16[2,1,512,256]{3,2,1,0:T(8,128)(2,1)}, bf16[2,1,512,256]{3,2,1,0:T(8,128)(2,1)}, u32[]{:S(2)}, u32[]{:S(2)}) collective-permute-start(bf16[2,1,512,256]{3,2,1,0:T(8,128)(2,1)} %get-tuple-element.26), channel_id=1, source_target_pairs={{1,0},{2,1},{3,2},{4,3},{5,4},{6,5},{7,6},{8,7},{9,8},{10,9},{11,1... | collective-permute-start | bytes 1572872 | tf_op jit(solution)/shard_map/ppermute | solution.py:289
  47.8 0.1 copy.128
  47.9 0.7 fusion.148
  48.6 2.1 %collective-permute-start = (bf16[2,1,512,256]{3,2,1,0:T(8,128)(2,1)}, bf16[2,1,512,256]{3,2,1,0:T(8,128)(2,1)S(1)}, u32[]{:S(2)}, u32[]{:S(2)}) collective-permute-start(bf16[2,1,512,256]{3,2,1,0:T(8,128)(2,1)} %get-tuple-element.27), channel_id=1, source_target_pairs={{0,1},{1,2},{2,3},{3,4},{4,5},{5,6},{6,7},{7,8},{8,9},{9,10},{10,1... | collective-permute-start | bytes 1572872 | tf_op jit(solution)/shard_map/ppermute | solution.py:288
  57.1 1.5 fusion.49
  58.6 0.7 add.139.rest_1_
  59.3 1.3 reverse_select_fusion.1.after_ref
  60.7 1.2 collective-permute-done.before_ref
  61.8 0.8 copy-done.9
  62.6 6.4 %shard_map.113 = (f32[2,4,512,256]{3,2,1,0:T(8,128)}, f32[2,2,4,256]{3,2,1,0:T(4,128)}) custom-call(bf16[2,4,512,256]{3,2,1,0:T(8,128)(2,1)} %copy-done.1, bf16[2,1,512,256]{3,2,1,0:T(8,128)(2,1)} %copy-done.9, bf16[2,1,512,256]{3,2,1,0:T(8,128)(2,1)} %copy-done.4, bf16[9,256,128]{2,1,0:T(8,128)(2,1)} %k_ref.7), custom_call_target="tpu_custom_call" | custom-call | tf_op jit(solution)/shard_map/pallas_call | solution.py:123
  69.0 0.7 copy.127
  69.8 1.0 slice.387
  70.8 0.6 maximum_bitcast_fusion.2.block_ref
  71.4 13.7 %shard_map.114 = (f32[2,4,512,256]{3,2,1,0:T(8,128)}, f32[8,56,128]{2,1,0:T(8,128)}) custom-call(f32[56,128]{1,0:T(8,128)} %maximum_bitcast_fusion.2.block_ref, bf16[2,4,512,256]{3,2,1,0:T(8,128)(2,1)} %copy-done.1, bf16[2,1,512,256]{3,2,1,0:T(8,128)(2,1)} %copy-done.9, bf16[2,1,512,256]{3,2,1,0:T(8,128)(2,1)} %copy-done.4, bf16[9,128,256]{2,1,0:T(8,128)(2,1)} %k_ref.6, ...), custom_call_target="tpu_custom_call" | custom-call | tf_op jit(solution)/shard_map/pallas_call | solution.py:229
  85.1 1.0 copy.201
  86.1 0.6 gather_fusion
  86.8 0.1 broadcast_select_fusion.1
  87.4 0.1 convolution_bitcast_fusion.1
  87.5 0.1 convolution_bitcast_fusion
  87.7 0.1 convolution_bitcast_fusion.3
  87.8 0.1 convolution_bitcast_fusion.2
  88.0 6.8 %multiply_convert_fusion = (bf16[2,4,512,256]{3,2,1,0:T(8,128)(2,1)S(1)}, bf16[2,4,512,256]{3,2,1,0:T(8,128)(2,1)S(1)}) fusion(f32[2,4,512,256]{3,2,1,0:T(8,128)} %get-tuple-element.15, f32[256]{0:T(256)S(1)} %copy-done.16, f32[2,4,256]{2,1,0:T(4,128)S(1)} %get-tuple-element.51, f32[2,4,256]{2,1,0:T(4,128)S(1)} %get-tuple-element.50, ...), kind=kLoop, calls=%fused_computation.19 | loop fusion | flops 32505856 | bytes 12617728 | tf_op jit(solution)/shard_map/convert_element_type | solution.py:425
  94.9 0.2 fusion.13
  95.1 4.7 %collective-permute-start.3 = (bf16[2,1,512,512]{3,2,1,0:T(8,128)(2,1)S(1)}, bf16[2,1,512,512]{3,2,1,0:T(8,128)(2,1)S(1)}, u32[]{:S(2)}, u32[]{:S(2)}) collective-permute-start(bf16[2,1,512,512]{3,2,1,0:T(8,128)(2,1)S(1)} %get-tuple-element.24), channel_id=1, source_target_pairs={{1,0},{2,1},{3,2},{4,3},{5,4},{6,5},{7,6},{8,7},{9,8},{10,9},{11,1... | collective-permute-start | bytes 3145736 | tf_op jit(solution)/shard_map/ppermute | solution.py:289
  99.8 2.1 %collective-permute-start.2 = (bf16[2,1,512,512]{3,2,1,0:T(8,128)(2,1)S(1)}, bf16[2,1,512,512]{3,2,1,0:T(8,128)(2,1)S(1)}, u32[]{:S(2)}, u32[]{:S(2)}) collective-permute-start(bf16[2,1,512,512]{3,2,1,0:T(8,128)(2,1)S(1)} %get-tuple-element.25), channel_id=1, source_target_pairs={{0,1},{1,2},{2,3},{3,4},{4,5},{5,6},{6,7},{7,8},{8,9},{9,10},{10,1... | collective-permute-start | bytes 3145736 | tf_op jit(solution)/shard_map/ppermute | solution.py:288
  101.9 0.7 slice_bitcast_fusion.3
  102.6 2.3 %pad_maximum_fusion.src_ref = bf16[2,4,512,512]{3,2,1,0:T(8,128)(2,1)} fusion(bf16[2,4,512,256]{3,2,1,0:T(8,128)(2,1)S(1)} %get-tuple-element.23, bf16[2,4,512,256]{3,2,1,0:T(8,128)(2,1)S(1)} %get-tuple-element.22), kind=kLoop, calls=%fused_computation.9 | loop fusion | flops 8388608 | bytes 8388608 | tf_op jit(solution)/shard_map/concatenate | solution.py:429
  104.9 16.0 %collective-permute-done.3 = bf16[2,1,512,512]{3,2,1,0:T(8,128)(2,1)S(1)} collective-permute-done((bf16[2,1,512,512]{3,2,1,0:T(8,128)(2,1)S(1)}, bf16[2,1,512,512]{3,2,1,0:T(8,128)(2,1)S(1)}, u32[]{:S(2)}, u32[]{:S(2)}) %collective-permute-start.3) | collective-permute-done | bytes 1048608 | tf_op jit(solution)/shard_map/ppermute | solution.py:289
  120.9 0.3 reverse_select_fusion.after_ref
  121.3 3.3 %collective-permute-done.2.before_ref = bf16[2,1,512,512]{3,2,1,0:T(8,128)(2,1)S(1)} collective-permute-done((bf16[2,1,512,512]{3,2,1,0:T(8,128)(2,1)S(1)}, bf16[2,1,512,512]{3,2,1,0:T(8,128)(2,1)S(1)}, u32[]{:S(2)}, u32[]{:S(2)}) %collective-permute-start.2) | collective-permute-done | bytes 1048608 | tf_op jit(solution)/shard_map/ppermute | solution.py:288
  124.7 0.9 copy-done.3
  125.5 6.3 %shard_map.115 = (f32[2,4,512,128]{3,2,1,0:T(8,128)}, f32[2,2,4,128]{3,2,1,0:T(4,128)}) custom-call(bf16[2,4,512,512]{3,2,1,0:T(8,128)(2,1)} %pad_maximum_fusion.src_ref, bf16[2,1,512,512]{3,2,1,0:T(8,128)(2,1)} %copy-done.3, bf16[2,1,512,512]{3,2,1,0:T(8,128)(2,1)} %copy-done.2, bf16[9,128,256]{2,1,0:T(8,128)(2,1)} %k_ref.6), custom_call_target="tpu_custom_call" | custom-call | tf_op jit(solution)/shard_map/pallas_call | solution.py:123
  131.8 0.7 copy.133
  132.5 0.6 maximum_bitcast_fusion.1.block_ref
  133.1 10.1 %shard_map.116 = (f32[2,4,512,128]{3,2,1,0:T(8,128)}, f32[8,64,128]{2,1,0:T(8,128)}) custom-call(f32[64,128]{1,0:T(8,128)} %maximum_bitcast_fusion.1.block_ref, bf16[2,4,512,512]{3,2,1,0:T(8,128)(2,1)} %pad_maximum_fusion.src_ref, bf16[2,1,512,512]{3,2,1,0:T(8,128)(2,1)} %copy-done.3, bf16[2,1,512,512]{3,2,1,0:T(8,128)(2,1)} %copy-done.2, ...), custom_call_target="tpu_custom_call" | custom-call | tf_op jit(solution)/shard_map/pallas_call | solution.py:229
  143.2 1.3 copy.200
  144.5 0.6 gather_fusion.1
  145.1 0.1 broadcast_select_fusion
  145.3 0.1 constant_dynamic-slice_fusion.3
  145.4 0.1 rev.36
  145.6 0.1 rev.37
  146.0 0.1 convolution_bitcast_fusion.5
  146.2 0.2 convolution_bitcast_fusion.4
  146.3 0.2 convolution_bitcast_fusion.7
  146.5 0.2 convolution_bitcast_fusion.6
  146.7 5.2 %add_bitcast_fusion = (f32[1,1,2,4,512,128]{5,4,3,2,1,0:T(8,128)}, bf16[1,1,2,4,512,128]{5,4,3,2,1,0:T(8,128)(2,1)}) fusion(f32[2,4,512,128]{3,2,1,0:T(8,128)} %get-tuple-element.21, f32[2,4,128]{2,1,0:T(4,128)S(1)} %reverse_select_fusion.4, f32[2,4,128]{2,1,0:T(4,128)S(1)} %reverse_select_fusion.5, pred[512]{0:T(512)(128)(4,1)S(1)} %get-tuple-element.90, ...), kind=kLoop, calls=%fused_computation.27 | loop fusion | flops 7340032 | bytes 9455104 | tf_op jit(solution)/shard_map/broadcast_in_dim | solution.py:439
  (112 shorter events, 0.9 us)
Async XLA Ops:
  0.6 4.1 %copy-start = (bf16[1024,256]{1,0:T(8,128)(2,1)S(1)}, bf16[1024,256]{1,0:T(8,128)(2,1)}, u32[]{:S(2)}) copy-start(bf16[1024,256]{1,0:T(8,128)(2,1)} %param.11) | copy-start | bytes 1572868
  6.3 12.1 %copy-start.15 = (s32[8,2,3]{0,1,2:T(2,128)S(1)}, s32[8,2,3]{0,1,2:T(2,128)}, u32[]{:S(2)}) copy-start(s32[8,2,3]{0,1,2:T(2,128)} %param.14) | copy-start | bytes 580
  7.7 12.6 %copy-start.8 = (bf16[9,128,256]{2,1,0:T(8,128)(2,1)S(1)}, bf16[9,128,256]{2,1,0:T(8,128)(2,1)}, u32[]{:S(2)}) copy-start(bf16[9,128,256]{2,1,0:T(8,128)(2,1)} %k_ref.6) | copy-start | bytes 1769476
  7.7 33.0 %all-to-all-start = ((bf16[128,17,256]{2,1,0:T(8,128)(2,1)}), bf16[128,17,256]{2,1,0:T(8,128)(2,1)}, u32[]{:S(2)}, u32[]{:S(2)}) async-start(bf16[128,17,256]{2,1,0:T(8,128)(2,1)} %pad_maximum_fusion.2), calls=%async_computation | async-start | bytes 3145728 | tf_op jit(solution)/shard_map/all_to_all | solution.py:374
  20.3 40.3 %copy-start.1 = (bf16[2,4,512,256]{3,2,1,0:T(8,128)(2,1)}, bf16[2,4,512,256]{3,2,1,0:T(8,128)(2,1)S(1)}, u32[]{:S(2)}) copy-start(bf16[2,4,512,256]{3,2,1,0:T(8,128)(2,1)S(1)} %pad_maximum_fusion.1.src_ref) | copy-start | bytes 6291460
  44.0 15.3 %collective-permute-start.1 = (bf16[2,1,512,256]{3,2,1,0:T(8,128)(2,1)}, bf16[2,1,512,256]{3,2,1,0:T(8,128)(2,1)}, u32[]{:S(2)}, u32[]{:S(2)}) collective-permute-start(bf16[2,1,512,256]{3,2,1,0:T(8,128)(2,1)} %get-tuple-element.26), channel_id=1, source_target_pairs={{1,0},{2,1},{3,2},{4,3},{5,4},{6,5},{7,6},{8,7},{9,8},{10,9},{11,1... | collective-permute-start | bytes 1572872 | tf_op jit(solution)/shard_map/ppermute | solution.py:289
  48.6 13.2 %collective-permute-start = (bf16[2,1,512,256]{3,2,1,0:T(8,128)(2,1)}, bf16[2,1,512,256]{3,2,1,0:T(8,128)(2,1)S(1)}, u32[]{:S(2)}, u32[]{:S(2)}) collective-permute-start(bf16[2,1,512,256]{3,2,1,0:T(8,128)(2,1)} %get-tuple-element.27), channel_id=1, source_target_pairs={{0,1},{1,2},{2,3},{3,4},{4,5},{5,6},{6,7},{7,8},{8,9},{9,10},{10,1... | collective-permute-start | bytes 1572872 | tf_op jit(solution)/shard_map/ppermute | solution.py:288
  60.6 1.2 copy-start.4
  60.6 10.1 %slice-start = ((bf16[2,4,512,256]{3,2,1,0:T(8,128)(2,1)}), bf16[2,4,512,128]{3,2,1,0:T(8,128)(2,1)S(1)}, s32[]{:S(2)}) async-start(bf16[2,4,512,256]{3,2,1,0:T(8,128)(2,1)} %copy-done.1), calls=%async_computation.1 | async-start | bytes 2097152 | tf_op jit(solution)/shard_map/slice | solution.py:295
  61.8 0.8 copy-start.9
  71.4 16.0 %copy-start.11 = (bf16[128,256]{1,0:T(8,128)(2,1)S(1)}, bf16[128,256]{1,0:T(8,128)(2,1)}, u32[]{:S(2)}) copy-start(bf16[128,256]{1,0:T(8,128)(2,1)} %get-tuple-element.34) | copy-start | bytes 196612
  71.4 16.0 %copy-start.12 = (bf16[128,256]{1,0:T(8,128)(2,1)S(1)}, bf16[128,256]{1,0:T(8,128)(2,1)}, u32[]{:S(2)}) copy-start(bf16[128,256]{1,0:T(8,128)(2,1)} %get-tuple-element.37) | copy-start | bytes 196612
  71.4 16.0 %copy-start.13 = (bf16[128,256]{1,0:T(8,128)(2,1)S(1)}, bf16[128,256]{1,0:T(8,128)(2,1)}, u32[]{:S(2)}) copy-start(bf16[128,256]{1,0:T(8,128)(2,1)} %get-tuple-element.38) | copy-start | bytes 196612
  71.4 16.1 %copy-start.10 = (bf16[128,256]{1,0:T(8,128)(2,1)S(1)}, bf16[128,256]{1,0:T(8,128)(2,1)}, u32[]{:S(2)}) copy-start(bf16[128,256]{1,0:T(8,128)(2,1)} %get-tuple-element.39) | copy-start | bytes 196612
  71.4 16.6 %copy-start.16 = (f32[256]{0:T(256)S(1)}, f32[256]{0:T(256)}, u32[]{:S(2)}) copy-start(f32[256]{0:T(256)} %param.16) | copy-start | bytes 3076
  94.9 7.1 %copy-start.5 = (bf16[9,256,128]{2,1,0:T(8,128)(2,1)S(1)}, bf16[9,256,128]{2,1,0:T(8,128)(2,1)}, u32[]{:S(2)}) copy-start(bf16[9,256,128]{2,1,0:T(8,128)(2,1)} %k_ref.7) | copy-start | bytes 1769476
  95.1 25.9 %collective-permute-start.3 = (bf16[2,1,512,512]{3,2,1,0:T(8,128)(2,1)S(1)}, bf16[2,1,512,512]{3,2,1,0:T(8,128)(2,1)S(1)}, u32[]{:S(2)}, u32[]{:S(2)}) collective-permute-start(bf16[2,1,512,512]{3,2,1,0:T(8,128)(2,1)S(1)} %get-tuple-element.24), channel_id=1, source_target_pairs={{1,0},{2,1},{3,2},{4,3},{5,4},{6,5},{7,6},{8,7},{9,8},{10,9},{11,1... | collective-permute-start | bytes 3145736 | tf_op jit(solution)/shard_map/ppermute | solution.py:289
  99.8 24.8 %collective-permute-start.2 = (bf16[2,1,512,512]{3,2,1,0:T(8,128)(2,1)S(1)}, bf16[2,1,512,512]{3,2,1,0:T(8,128)(2,1)S(1)}, u32[]{:S(2)}, u32[]{:S(2)}) collective-permute-start(bf16[2,1,512,512]{3,2,1,0:T(8,128)(2,1)S(1)} %get-tuple-element.25), channel_id=1, source_target_pairs={{0,1},{1,2},{2,3},{3,4},{4,5},{5,6},{6,7},{7,8},{8,9},{9,10},{10,1... | collective-permute-start | bytes 3145736 | tf_op jit(solution)/shard_map/ppermute | solution.py:288
  121.2 3.5 %copy-start.2 = (bf16[2,1,512,512]{3,2,1,0:T(8,128)(2,1)}, bf16[2,1,512,512]{3,2,1,0:T(8,128)(2,1)S(1)}, u32[]{:S(2)}) copy-start(bf16[2,1,512,512]{3,2,1,0:T(8,128)(2,1)S(1)} %reverse_select_fusion.after_ref) | copy-start | bytes 3145732
  124.6 1.0 copy-start.3
  133.1 12.9 %copy-start.14 = (bf16[256,128]{1,0:T(8,128)(2,1)S(1)}, bf16[256,128]{1,0:T(8,128)(2,1)}, u32[]{:S(2)}) copy-start(bf16[256,128]{1,0:T(8,128)(2,1)} %get-tuple-element.31) | copy-start | bytes 196612
  143.2 3.4 %copy-start.6 = (bf16[1,1,2,4,512,128]{5,4,3,2,1,0:T(8,128)(2,1)S(1)}, bf16[1,1,2,4,512,128]{5,4,3,2,1,0:T(8,128)(2,1)}, u32[]{:S(2)}) copy-start(bf16[1,1,2,4,512,128]{5,4,3,2,1,0:T(8,128)(2,1)} %param.19) | copy-start | bytes 3145732
  143.2 3.4 %copy-start.7 = (bf16[1,1,2,4,512,128]{5,4,3,2,1,0:T(8,128)(2,1)S(1)}, bf16[1,1,2,4,512,128]{5,4,3,2,1,0:T(8,128)(2,1)}, u32[]{:S(2)}) copy-start(bf16[1,1,2,4,512,128]{5,4,3,2,1,0:T(8,128)(2,1)} %param.10) | copy-start | bytes 3145732

commit v11 on v10

--- a/solution.py
+++ b/solution.py
@@ -409,10 +409,7 @@
     matching_row = lax.dynamic_index_in_dim(matching, face_at, 0, keepdims=False)
 
     lifted = kernel_one.shape[2]
-    fields, got_values = lax.optimization_barrier(
-        (jnp.concatenate([base_field, cot_field], axis=3), got_values)
-    )
-    both = extend_rows(fields, last_tile)
+    both = extend_rows(jnp.concatenate([base_field, cot_field], axis=3), last_tile)
     cot_back, cot_margins = conv_back(both, channels, channels, kernel_two)
     parts = [edge_cols(both, 0, channels), jnp.swapaxes(cot_margins, 1, 2)]
     first_out, landed = conv_gather(

time: 154 us -> 137 us (0.89)
  waiting for transfers between devices: 40.1 us -> 22.6 us
  local copies, waits for them, and re-layouts: 15 us -> 12.5 us
  other arithmetic: 26.2 us -> 28.2 us
    all_to_all x1, waiting for transfers between devices: 19.6 us -> 2.62 us  [route_observations(): lax.all_to_all(payload, ('face', 'tile'), split_axis=0, concat_axis=0, ti...]
    concatenate x1 -> x2, other arithmetic: 1.79 us -> 3.91 us  [per_device(): jnp.concatenate([base_field, cot_field], axis=3)]
    unnamed x62 -> x50, local copies, waits for them, and re-layouts: 4.09 us -> 3.99 us
  transfers between devices with their start and end apart: 5 -> 5, of which waited for: 4 -> 3; matrix products, arithmetic and copies ran while one was open for 7% -> 12% of each run, Pallas kernels for 0% -> 5%
where the time goes in v11:
time: 137 us; the launch traced here: 134 us
  Pallas kernels  36.8 us (27%)
  other arithmetic  28.2 us (21%)
  starting transfers between devices  23.6 us (17%)
  waiting for transfers between devices  22.6 us (16%)
  local copies, waits for them, and re-layouts  12.5 us (9%)
  between operations  7.77 us (6%)
  matrix products  2.8 us (2%)
    pallas_call x2, Pallas kernels, conv_gather(): pl.pallas_call(functools.partial(conv_gather_kernel, count), grid=(bands,...  24.2 us
    ppermute x2, waiting for transfers between devices, extend_rows(): after = lax.ppermute(head, 'tile', [(i + 1, i) for i in range(count - 1)])  16.9 us
    pallas_call x2, Pallas kernels, conv_back(): pl.pallas_call(back_kernel, grid=(bands,), in_specs=[pl.BlockSpec((1, row...  12.7 us
    all_to_all x1, starting transfers between devices, route_observations(): lax.all_to_all(payload, ('face', 'tile'), split_axis=0, concat_axis=0, ti...  11.6 us
    ppermute x2, starting transfers between devices, extend_rows(): after = lax.ppermute(head, 'tile', [(i + 1, i) for i in range(count - 1)])  7.9 us
    convert_element_type x1, other arithmetic, per_device(): inner = activation(pre_act).astype(jnp.bfloat16)  6.82 us
    broadcast_in_dim x1, other arithmetic, per_device(): return (analysis[None, None], grad_base[None, None])  5.17 us
    ppermute x2, starting transfers between devices, extend_rows(): before = lax.ppermute(tail, 'tile', [(i, i + 1) for i in range(count - 1)])  4.06 us
  transfers between devices with their start and end apart: 5, of which 3 were waited for; matrix products, arithmetic and copies ran while one was open for 12% of the time, Pallas kernels for 5%

profile of v11, /device:TPU:24, one launch (start us, length us, event | category | flops | bytes accessed | tf_op | source)
XLA Modules:
  0.0 134.2 jit_solution(4441739692828132032)
XLA Ops:
  0.6 0.0 copy-start
  0.6 2.4 %fusion.15 = (bf16[2,1,512,256]{3,2,1,0:T(8,128)(2,1)}, bf16[2,1,512,256]{3,2,1,0:T(8,128)(2,1)}) fusion(bf16[2,4,512,128]{3,2,1,0:T(8,128)(2,1)} %bitcast.230, bf16[2,4,512,128]{3,2,1,0:T(8,128)(2,1)} %bitcast.233), kind=kLoop, calls=%fused_computation.47 | loop fusion | flops 2097152 | bytes 3145728 | tf_op jit(solution)/shard_map/concatenate | solution.py:412
  3.0 4.5 %collective-permute-start.1 = (bf16[2,1,512,256]{3,2,1,0:T(8,128)(2,1)}, bf16[2,1,512,256]{3,2,1,0:T(8,128)(2,1)}, u32[]{:S(2)}, u32[]{:S(2)}) collective-permute-start(bf16[2,1,512,256]{3,2,1,0:T(8,128)(2,1)} %get-tuple-element.22), channel_id=1, source_target_pairs={{1,0},{2,1},{3,2},{4,3},{5,4},{6,5},{7,6},{8,7},{9,8},{10,9},{11,1... | collective-permute-start | bytes 1572872 | tf_op jit(solution)/shard_map/ppermute | solution.py:289
  7.6 1.9 %collective-permute-start = (bf16[2,1,512,256]{3,2,1,0:T(8,128)(2,1)}, bf16[2,1,512,256]{3,2,1,0:T(8,128)(2,1)}, u32[]{:S(2)}, u32[]{:S(2)}) collective-permute-start(bf16[2,1,512,256]{3,2,1,0:T(8,128)(2,1)} %get-tuple-element.23), channel_id=1, source_target_pairs={{0,1},{1,2},{2,3},{3,4},{4,5},{5,6},{6,7},{7,8},{8,9},{9,10},{10,1... | collective-permute-start | bytes 1572872 | tf_op jit(solution)/shard_map/ppermute | solution.py:288
  9.5 1.3 convert_reduce_fusion
  10.8 0.7 multiply_add_fusion
  11.5 1.6 %select_reduce_fusion = s32[2048]{0:T(1024)S(1)} fusion(s32[1024]{0:T(1024)} %param.13, s32[1024]{0:T(1024)S(1)} %multiply_add_fusion), kind=kLoop, calls=%fused_computation.2 | loop fusion | flops 6289408 | bytes 16384 | tf_op jit(solution)/shard_map/reduce_sum | solution.py:365
  13.1 0.1 reduce_sum.22
  13.2 0.1 fusion.48
  13.2 0.1 pad.73.clone
  13.3 0.1 maximum_bitcast_fusion
  13.4 0.1 copy.127
  13.5 1.6 %fusion.10 = bf16[2048,256]{1,0:T(8,128)(2,1)S(1)} fusion(bf16[1024,256]{1,0:T(8,128)(2,1)S(1)} %copy-done, s32[1024]{0:T(1024)S(1)} %multiply_add_fusion), kind=kOutput, calls=%fused_computation.30 | convolution fusion | flops 1076363264 | bytes 1576960 | tf_op jit(solution)/shard_map/dot_general | solution.py:362
  15.2 0.0 copy-start.1
  15.2 0.0 copy-start.3
  15.2 1.3 %pad_maximum_fusion.2 = bf16[128,17,256]{2,1,0:T(8,128)(2,1)} fusion(bf16[128,1,256]{2,1,0:T(2,128)(2,1)S(1)} %copy.127, bf16[128,16,256]{2,1,0:T(8,128)(2,1)S(1)} %bitcast.236), kind=kLoop, calls=%fused_computation.33 | loop fusion | flops 2228224 | bytes 2228224 | tf_op jit(solution)/shard_map/concatenate | solution.py:371
  16.6 11.6 %all-to-all-start = ((bf16[128,17,256]{2,1,0:T(8,128)(2,1)}), bf16[128,17,256]{2,1,0:T(8,128)(2,1)}, u32[]{:S(2)}, u32[]{:S(2)}) async-start(bf16[128,17,256]{2,1,0:T(8,128)(2,1)} %pad_maximum_fusion.2), calls=%async_computation | async-start | bytes 3145728 | tf_op jit(solution)/shard_map/all_to_all | solution.py:374
  28.2 0.1 constant_dynamic-slice_fusion.8
  28.3 0.1 copy.128
  28.4 0.7 fusion.149
  29.1 1.5 %pad_maximum_fusion.1.src_ref = bf16[2,4,512,256]{3,2,1,0:T(8,128)(2,1)} fusion(bf16[2,4,512,128]{3,2,1,0:T(8,128)(2,1)S(1)} %bitcast.234, bf16[2,4,512,128]{3,2,1,0:T(8,128)(2,1)S(1)} %bitcast.231), kind=kLoop, calls=%fused_computation.27 | loop fusion | flops 4194304 | bytes 4194304 | tf_op jit(solution)/shard_map/concatenate | solution.py:412
  37.0 1.3 reverse_select_fusion.1.after_ref
  38.3 0.8 copy-done.6
  39.1 6.4 %shard_map.113 = (f32[2,4,512,256]{3,2,1,0:T(8,128)}, f32[2,2,4,256]{3,2,1,0:T(4,128)}) custom-call(bf16[2,4,512,256]{3,2,1,0:T(8,128)(2,1)} %pad_maximum_fusion.1.src_ref, bf16[2,1,512,256]{3,2,1,0:T(8,128)(2,1)} %collective-permute-done.before_ref, bf16[2,1,512,256]{3,2,1,0:T(8,128)(2,1)} %copy-done.6, bf16[9,256,128]{2,1,0:T(8,128)(2,1)} %k_ref.7), custom_call_target="tpu_custom_call" | custom-call | tf_op jit(solution)/shard_map/pallas_call | solution.py:123
  45.5 0.7 copy.126
  46.2 1.0 slice.384
  47.2 0.6 maximum_bitcast_fusion.2.block_ref
  47.8 2.6 %all-to-all-done = bf16[128,17,256]{2,1,0:T(8,128)(2,1)} async-done(((bf16[128,17,256]{2,1,0:T(8,128)(2,1)}), bf16[128,17,256]{2,1,0:T(8,128)(2,1)}, u32[]{:S(2)}, u32[]{:S(2)}) %all-to-all-start) | async-done | bytes 1114144 | tf_op jit(solution)/shard_map/all_to_all | solution.py:374
  50.5 1.4 %fusion.51 = s32[128,16]{1,0:T(8,128)S(1)} fusion(bf16[128,17,256]{2,1,0:T(8,128)(2,1)} %all-to-all-done), kind=kLoop, calls=%fused_computation.94 | loop fusion | flops 8192 | bytes 16384 | tf_op jit(solution)/shard_map/add | solution.py:378
  51.9 0.7 add.139.rest_1_
  52.6 2.3 %slice.388 = bf16[128,16,256]{2,1,0:T(8,128)(2,1)} slice(bf16[128,17,256]{2,1,0:T(8,128)(2,1)} %all-to-all-done), slice={[0:128], [0:16], [0:256]} | slice | bytes 2097152 | tf_op jit(solution)/shard_map/slice | solution.py:375
  54.8 14.2 %shard_map.114 = (f32[2,4,512,256]{3,2,1,0:T(8,128)}, f32[8,56,128]{2,1,0:T(8,128)}) custom-call(f32[56,128]{1,0:T(8,128)} %maximum_bitcast_fusion.2.block_ref, bf16[2,4,512,256]{3,2,1,0:T(8,128)(2,1)} %pad_maximum_fusion.1.src_ref, bf16[2,1,512,256]{3,2,1,0:T(8,128)(2,1)} %collective-permute-done.before_ref, bf16[2,1,512,256]{3,2,1,0:T(8,128)(2,1)} %copy-done.6, ...), custom_call_target="tpu_custom_call" | custom-call | tf_op jit(solution)/shard_map/pallas_call | solution.py:229
  69.0 1.0 copy.201
  70.0 0.6 gather_fusion
  70.7 0.1 broadcast_select_fusion.1
  71.3 0.1 convolution_bitcast_fusion.1
  71.4 0.1 convolution_bitcast_fusion
  71.6 0.1 convolution_bitcast_fusion.3
  71.7 0.1 convolution_bitcast_fusion.2
  71.9 6.8 %multiply_convert_fusion = (bf16[2,4,512,256]{3,2,1,0:T(8,128)(2,1)S(1)}, bf16[2,4,512,256]{3,2,1,0:T(8,128)(2,1)S(1)}) fusion(f32[2,4,512,256]{3,2,1,0:T(8,128)} %get-tuple-element.11, f32[256]{0:T(256)S(1)} %copy-done.10, f32[2,4,256]{2,1,0:T(4,128)S(1)} %get-tuple-element.47, f32[2,4,256]{2,1,0:T(4,128)S(1)} %get-tuple-element.46, ...), kind=kLoop, calls=%fused_computation.19 | loop fusion | flops 32505856 | bytes 12617728 | tf_op jit(solution)/shard_map/convert_element_type | solution.py:422
  78.7 0.0 copy-start.7
  78.7 0.2 fusion.13
  78.9 3.4 %collective-permute-start.3 = (bf16[2,1,512,512]{3,2,1,0:T(8,128)(2,1)S(1)}, bf16[2,1,512,512]{3,2,1,0:T(8,128)(2,1)S(1)}, u32[]{:S(2)}, u32[]{:S(2)}) collective-permute-start(bf16[2,1,512,512]{3,2,1,0:T(8,128)(2,1)S(1)} %get-tuple-element.20), channel_id=1, source_target_pairs={{1,0},{2,1},{3,2},{4,3},{5,4},{6,5},{7,6},{8,7},{9,8},{10,9},{11,1... | collective-permute-start | bytes 3145736 | tf_op jit(solution)/shard_map/ppermute | solution.py:289
  82.3 2.1 %collective-permute-start.2 = (bf16[2,1,512,512]{3,2,1,0:T(8,128)(2,1)S(1)}, bf16[2,1,512,512]{3,2,1,0:T(8,128)(2,1)S(1)}, u32[]{:S(2)}, u32[]{:S(2)}) collective-permute-start(bf16[2,1,512,512]{3,2,1,0:T(8,128)(2,1)S(1)} %get-tuple-element.21), channel_id=1, source_target_pairs={{0,1},{1,2},{2,3},{3,4},{4,5},{5,6},{6,7},{7,8},{8,9},{9,10},{10,1... | collective-permute-start | bytes 3145736 | tf_op jit(solution)/shard_map/ppermute | solution.py:288
  84.5 2.3 %pad_maximum_fusion.src_ref = bf16[2,4,512,512]{3,2,1,0:T(8,128)(2,1)} fusion(bf16[2,4,512,256]{3,2,1,0:T(8,128)(2,1)S(1)} %get-tuple-element.19, bf16[2,4,512,256]{3,2,1,0:T(8,128)(2,1)S(1)} %get-tuple-element.18), kind=kLoop, calls=%fused_computation.9 | loop fusion | flops 8388608 | bytes 8388608 | tf_op jit(solution)/shard_map/concatenate | solution.py:426
  86.8 16.9 %collective-permute-done.3 = bf16[2,1,512,512]{3,2,1,0:T(8,128)(2,1)S(1)} collective-permute-done((bf16[2,1,512,512]{3,2,1,0:T(8,128)(2,1)S(1)}, bf16[2,1,512,512]{3,2,1,0:T(8,128)(2,1)S(1)}, u32[]{:S(2)}, u32[]{:S(2)}) %collective-permute-start.3) | collective-permute-done | bytes 1048608 | tf_op jit(solution)/shard_map/ppermute | solution.py:289
  103.7 0.3 reverse_select_fusion.after_ref
  104.0 3.1 %collective-permute-done.2.before_ref = bf16[2,1,512,512]{3,2,1,0:T(8,128)(2,1)S(1)} collective-permute-done((bf16[2,1,512,512]{3,2,1,0:T(8,128)(2,1)S(1)}, bf16[2,1,512,512]{3,2,1,0:T(8,128)(2,1)S(1)}, u32[]{:S(2)}, u32[]{:S(2)}) %collective-permute-start.2) | collective-permute-done | bytes 1048608 | tf_op jit(solution)/shard_map/ppermute | solution.py:288
  107.2 0.9 copy-done.5
  108.1 6.3 %shard_map.115 = (f32[2,4,512,128]{3,2,1,0:T(8,128)}, f32[2,2,4,128]{3,2,1,0:T(4,128)}) custom-call(bf16[2,4,512,512]{3,2,1,0:T(8,128)(2,1)} %pad_maximum_fusion.src_ref, bf16[2,1,512,512]{3,2,1,0:T(8,128)(2,1)} %copy-done.5, bf16[2,1,512,512]{3,2,1,0:T(8,128)(2,1)} %copy-done.2, bf16[9,128,256]{2,1,0:T(8,128)(2,1)} %k_ref.6), custom_call_target="tpu_custom_call" | custom-call | tf_op jit(solution)/shard_map/pallas_call | solution.py:123
  114.4 0.7 copy.133
  115.1 0.6 maximum_bitcast_fusion.1.block_ref
  115.7 9.9 %shard_map.116 = (f32[2,4,512,128]{3,2,1,0:T(8,128)}, f32[8,64,128]{2,1,0:T(8,128)}) custom-call(f32[64,128]{1,0:T(8,128)} %maximum_bitcast_fusion.1.block_ref, bf16[2,4,512,512]{3,2,1,0:T(8,128)(2,1)} %pad_maximum_fusion.src_ref, bf16[2,1,512,512]{3,2,1,0:T(8,128)(2,1)} %copy-done.5, bf16[2,1,512,512]{3,2,1,0:T(8,128)(2,1)} %copy-done.2, ...), custom_call_target="tpu_custom_call" | custom-call | tf_op jit(solution)/shard_map/pallas_call | solution.py:229
  125.7 1.2 copy.200
  126.9 0.6 gather_fusion.1
  127.5 0.1 broadcast_select_fusion
  127.7 0.1 constant_dynamic-slice_fusion.3
  127.8 0.1 rev.36
  128.0 0.1 rev.37
  128.4 0.1 convolution_bitcast_fusion.5
  128.5 0.1 convolution_bitcast_fusion.4
  128.7 0.2 convolution_bitcast_fusion.7
  128.8 0.2 convolution_bitcast_fusion.6
  129.0 5.2 %add_bitcast_fusion = (f32[1,1,2,4,512,128]{5,4,3,2,1,0:T(8,128)}, bf16[1,1,2,4,512,128]{5,4,3,2,1,0:T(8,128)(2,1)}) fusion(f32[2,4,512,128]{3,2,1,0:T(8,128)} %get-tuple-element.17, f32[2,4,128]{2,1,0:T(4,128)S(1)} %reverse_select_fusion.4, f32[2,4,128]{2,1,0:T(4,128)S(1)} %reverse_select_fusion.5, pred[512]{0:T(512)(128)(4,1)S(1)} %get-tuple-element.86, ...), kind=kLoop, calls=%fused_computation.31 | loop fusion | flops 7340032 | bytes 9455104 | tf_op jit(solution)/shard_map/broadcast_in_dim | solution.py:436
  (98 shorter events, 0.9 us)
Async XLA Ops:
  0.6 12.9 %copy-start = (bf16[1024,256]{1,0:T(8,128)(2,1)S(1)}, bf16[1024,256]{1,0:T(8,128)(2,1)}, u32[]{:S(2)}) copy-start(bf16[1024,256]{1,0:T(8,128)(2,1)} %param.11) | copy-start | bytes 1572868
  3.0 33.9 %collective-permute-start.1 = (bf16[2,1,512,256]{3,2,1,0:T(8,128)(2,1)}, bf16[2,1,512,256]{3,2,1,0:T(8,128)(2,1)}, u32[]{:S(2)}, u32[]{:S(2)}) collective-permute-start(bf16[2,1,512,256]{3,2,1,0:T(8,128)(2,1)} %get-tuple-element.22), channel_id=1, source_target_pairs={{1,0},{2,1},{3,2},{4,3},{5,4},{6,5},{7,6},{8,7},{9,8},{10,9},{11,1... | collective-permute-start | bytes 1572872 | tf_op jit(solution)/shard_map/ppermute | solution.py:289
  7.6 30.8 %collective-permute-start = (bf16[2,1,512,256]{3,2,1,0:T(8,128)(2,1)}, bf16[2,1,512,256]{3,2,1,0:T(8,128)(2,1)}, u32[]{:S(2)}, u32[]{:S(2)}) collective-permute-start(bf16[2,1,512,256]{3,2,1,0:T(8,128)(2,1)} %get-tuple-element.23), channel_id=1, source_target_pairs={{0,1},{1,2},{2,3},{3,4},{4,5},{5,6},{6,7},{7,8},{8,9},{9,10},{10,1... | collective-permute-start | bytes 1572872 | tf_op jit(solution)/shard_map/ppermute | solution.py:288
  15.2 13.0 %copy-start.9 = (s32[8,2,3]{0,1,2:T(2,128)S(1)}, s32[8,2,3]{0,1,2:T(2,128)}, u32[]{:S(2)}) copy-start(s32[8,2,3]{0,1,2:T(2,128)} %param.14) | copy-start | bytes 580
  15.2 13.9 %copy-start.1 = (bf16[1,1,2,4,512,128]{5,4,3,2,1,0:T(8,128)(2,1)S(1)}, bf16[1,1,2,4,512,128]{5,4,3,2,1,0:T(8,128)(2,1)}, u32[]{:S(2)}) copy-start(bf16[1,1,2,4,512,128]{5,4,3,2,1,0:T(8,128)(2,1)} %param.10) | copy-start | bytes 3145732
  15.2 13.9 %copy-start.3 = (bf16[1,1,2,4,512,128]{5,4,3,2,1,0:T(8,128)(2,1)S(1)}, bf16[1,1,2,4,512,128]{5,4,3,2,1,0:T(8,128)(2,1)}, u32[]{:S(2)}) copy-start(bf16[1,1,2,4,512,128]{5,4,3,2,1,0:T(8,128)(2,1)} %param.19) | copy-start | bytes 3145732
  16.6 20.4 %copy-start.8 = (bf16[9,128,256]{2,1,0:T(8,128)(2,1)S(1)}, bf16[9,128,256]{2,1,0:T(8,128)(2,1)}, u32[]{:S(2)}) copy-start(bf16[9,128,256]{2,1,0:T(8,128)(2,1)} %k_ref.6) | copy-start | bytes 1769476
  16.6 33.9 %all-to-all-start = ((bf16[128,17,256]{2,1,0:T(8,128)(2,1)}), bf16[128,17,256]{2,1,0:T(8,128)(2,1)}, u32[]{:S(2)}, u32[]{:S(2)}) async-start(bf16[128,17,256]{2,1,0:T(8,128)(2,1)} %pad_maximum_fusion.2), calls=%async_computation | async-start | bytes 3145728 | tf_op jit(solution)/shard_map/all_to_all | solution.py:374
  38.3 0.8 copy-start.6
  54.8 17.1 %copy-start.10 = (f32[256]{0:T(256)S(1)}, f32[256]{0:T(256)}, u32[]{:S(2)}) copy-start(f32[256]{0:T(256)} %param.16) | copy-start | bytes 3076
  78.7 5.7 %copy-start.7 = (bf16[9,256,128]{2,1,0:T(8,128)(2,1)S(1)}, bf16[9,256,128]{2,1,0:T(8,128)(2,1)}, u32[]{:S(2)}) copy-start(bf16[9,256,128]{2,1,0:T(8,128)(2,1)} %k_ref.7) | copy-start | bytes 1769476
  78.9 24.7 %collective-permute-start.3 = (bf16[2,1,512,512]{3,2,1,0:T(8,128)(2,1)S(1)}, bf16[2,1,512,512]{3,2,1,0:T(8,128)(2,1)S(1)}, u32[]{:S(2)}, u32[]{:S(2)}) collective-permute-start(bf16[2,1,512,512]{3,2,1,0:T(8,128)(2,1)S(1)} %get-tuple-element.20), channel_id=1, source_target_pairs={{1,0},{2,1},{3,2},{4,3},{5,4},{6,5},{7,6},{8,7},{9,8},{10,9},{11,1... | collective-permute-start | bytes 3145736 | tf_op jit(solution)/shard_map/ppermute | solution.py:289
  82.3 24.8 %collective-permute-start.2 = (bf16[2,1,512,512]{3,2,1,0:T(8,128)(2,1)S(1)}, bf16[2,1,512,512]{3,2,1,0:T(8,128)(2,1)S(1)}, u32[]{:S(2)}, u32[]{:S(2)}) collective-permute-start(bf16[2,1,512,512]{3,2,1,0:T(8,128)(2,1)S(1)} %get-tuple-element.21), channel_id=1, source_target_pairs={{0,1},{1,2},{2,3},{3,4},{4,5},{5,6},{6,7},{7,8},{8,9},{9,10},{10,1... | collective-permute-start | bytes 3145736 | tf_op jit(solution)/shard_map/ppermute | solution.py:288
  104.0 4.1 %copy-start.2 = (bf16[2,1,512,512]{3,2,1,0:T(8,128)(2,1)}, bf16[2,1,512,512]{3,2,1,0:T(8,128)(2,1)S(1)}, u32[]{:S(2)}) copy-start(bf16[2,1,512,512]{3,2,1,0:T(8,128)(2,1)S(1)} %reverse_select_fusion.after_ref) | copy-start | bytes 3145732
  107.1 1.0 copy-start.5
  125.7 3.3 %copy-start.4 = (bf16[1,1,2,4,512,128]{5,4,3,2,1,0:T(8,128)(2,1)S(1)}, bf16[1,1,2,4,512,128]{5,4,3,2,1,0:T(8,128)(2,1)}, u32[]{:S(2)}) copy-start(bf16[1,1,2,4,512,128]{5,4,3,2,1,0:T(8,128)(2,1)} %param.19) | copy-start | bytes 3145732

commit v12 on v9

--- a/solution.py
+++ b/solution.py
@@ -393,6 +393,8 @@
         (jnp.concatenate([base_field, cot_field], axis=3), got_values)
     )
     both = extend_rows(fields, last_tile)
+    gridded, cot_before = lax.optimization_barrier((gridded, both[1]))
+    both = (both[0], cot_before, both[2])
     cot_back, cot_margins = conv_back(both, channels, channels, kernel_two)
     parts = [edge_cols(both, 0, channels), jnp.swapaxes(cot_margins, 1, 2)]
     first_out, landed = conv_gather(both, 0, channels, pack_parts(parts), kernel_one, 0)

time: 129 us -> 149 us (1.16)
  waiting for transfers between devices: 19.6 us -> 26.5 us
  other arithmetic: 22.4 us -> 28.8 us
  starting transfers between devices: 23.9 us -> 27.3 us
  matrix products: 8.13 us -> 9.81 us
    ppermute x2, waiting for transfers between devices: 16.1 us -> 22.9 us  [extend_rows(): after = lax.ppermute(head, 'tile', [(i + 1, i) for i in range(count - 1)])]
    ppermute x2, starting transfers between devices: 8.23 us -> 12.4 us  [extend_rows(): after = lax.ppermute(head, 'tile', [(i + 1, i) for i in range(count - 1)])]
    convert_element_type x1, other arithmetic: 5.04 us -> 7.61 us  [per_device(): inner = activation(pre_act).astype(jnp.bfloat16)]
    dot_general x1, matrix products: 5.34 us -> 7.01 us  [per_device(): gridded = jnp.dot(onehot, got_values, preferred_element_type=jnp.float32)]
    unnamed x60 -> x62, local copies, waits for them, and re-layouts: 4.04 us -> 3.3 us
  transfers between devices with their start and end apart: 5 -> 5, of which waited for: 2 -> 3; matrix products, arithmetic and copies ran while one was open for 12% -> 14% of each run, Pallas kernels for 14% -> 0%
where the time goes in v12:
time: 149 us; the launch traced here: 148 us
  Pallas kernels  34.6 us (23%)
  other arithmetic  28.8 us (19%)
  starting transfers between devices  27.3 us (18%)
  waiting for transfers between devices  26.5 us (18%)
  local copies, waits for them, and re-layouts  13.5 us (9%)
  matrix products  9.81 us (7%)
  between operations  7.58 us (5%)
    ppermute x2, waiting for transfers between devices, extend_rows(): after = lax.ppermute(head, 'tile', [(i + 1, i) for i in range(count - 1)])  22.9 us
    pallas_call x2, Pallas kernels, conv_gather(): pl.pallas_call(functools.partial(conv_gather_kernel, count), grid=(bands,...  21.8 us
    pallas_call x2, Pallas kernels, conv_back(): pl.pallas_call(back_kernel, grid=(bands,), in_specs=[pl.BlockSpec((1, row...  12.8 us
    ppermute x2, starting transfers between devices, extend_rows(): after = lax.ppermute(head, 'tile', [(i + 1, i) for i in range(count - 1)])  12.4 us
    all_to_all x1, starting transfers between devices, route_observations(): lax.all_to_all(payload, ('face', 'tile'), split_axis=0, concat_axis=0, ti...  10.7 us
    convert_element_type x1, other arithmetic, per_device(): inner = activation(pre_act).astype(jnp.bfloat16)  7.61 us
    dot_general x1, matrix products, per_device(): gridded = jnp.dot(onehot, got_values, preferred_element_type=jnp.float32)  7.01 us
    broadcast_in_dim x1, other arithmetic, per_device(): return (analysis[None, None], grad_base[None, None])  5.14 us
  transfers between devices with their start and end apart: 5, of which 3 were waited for; matrix products, arithmetic and copies ran while one was open for 14% of the time, Pallas kernels for 0%

profile of v12, /device:TPU:24, one launch (start us, length us, event | category | flops | bytes accessed | tf_op | source)
XLA Modules:
  0.0 148.0 jit_solution(16027909876916632936)
XLA Ops:
  0.6 1.3 convert_reduce_fusion
  1.9 0.7 multiply_add_fusion.1
  2.6 1.6 %select_reduce_fusion = s32[2048]{0:T(1024)S(1)} fusion(s32[1024]{0:T(1024)} %param.13, s32[1024]{0:T(1024)S(1)} %multiply_add_fusion.1), kind=kLoop, calls=%fused_computation.6 | loop fusion | flops 6289408 | bytes 16384 | tf_op jit(solution)/shard_map/reduce_sum | solution.py:340
  4.2 0.1 reduce_sum.22
  4.3 0.1 fusion.50
  4.4 0.1 pad.82.clone
  4.5 0.1 maximum_bitcast_fusion
  4.6 0.1 copy.113
  4.7 1.6 %fusion.14 = bf16[2048,256]{1,0:T(8,128)(2,1)S(1)} fusion(bf16[1024,256]{1,0:T(8,128)(2,1)S(1)} %copy-done, s32[1024]{0:T(1024)S(1)} %multiply_add_fusion.1), kind=kOutput, calls=%fused_computation.29 | convolution fusion | flops 1076363264 | bytes 1576960 | tf_op jit(solution)/shard_map/dot_general | solution.py:337
  6.3 1.4 pad_maximum_fusion.2
  7.7 10.7 %all-to-all-start = ((bf16[128,17,256]{2,1,0:T(8,128)(2,1)}), bf16[128,17,256]{2,1,0:T(8,128)(2,1)}, u32[]{:S(2)}, u32[]{:S(2)}) async-start(bf16[128,17,256]{2,1,0:T(8,128)(2,1)} %pad_maximum_fusion.2), calls=%async_computation | async-start | bytes 3145728 | tf_op jit(solution)/shard_map/all_to_all | solution.py:349
  18.4 1.9 %pad_maximum_fusion.1.src_ref = bf16[2,4,512,256]{3,2,1,0:T(8,128)(2,1)S(1)} fusion(bf16[2,4,512,128]{3,2,1,0:T(8,128)(2,1)} %bitcast.235, bf16[2,4,512,128]{3,2,1,0:T(8,128)(2,1)} %bitcast.236), kind=kLoop, calls=%fused_computation.30 | loop fusion | flops 4194304 | bytes 4194304 | tf_op jit(solution)/shard_map/concatenate | solution.py:393
  20.3 1.1 fusion.147
  21.4 2.0 %collective-permute-start = (bf16[2,1,512,256]{3,2,1,0:T(8,128)(2,1)}, bf16[2,1,512,256]{3,2,1,0:T(8,128)(2,1)}, u32[]{:S(2)}, u32[]{:S(2)}) collective-permute-start(bf16[2,1,512,256]{3,2,1,0:T(8,128)(2,1)} %get-tuple-element.29), channel_id=1, source_target_pairs={{0,1},{1,2},{2,3},{3,4},{4,5},{5,6},{6,7},{7,8},{8,9},{9,10},{10,1... | collective-permute-start | bytes 1572872 | tf_op jit(solution)/shard_map/ppermute | solution.py:263
  23.4 6.1 %collective-permute-start.1 = (bf16[2,1,512,256]{3,2,1,0:T(8,128)(2,1)}, bf16[2,1,512,256]{3,2,1,0:T(8,128)(2,1)}, u32[]{:S(2)}, u32[]{:S(2)}) collective-permute-start(bf16[2,1,512,256]{3,2,1,0:T(8,128)(2,1)} %get-tuple-element.28), channel_id=1, source_target_pairs={{1,0},{2,1},{3,2},{4,3},{5,4},{6,5},{7,6},{8,7},{9,8},{10,9},{11,1... | collective-permute-start | bytes 1572872 | tf_op jit(solution)/shard_map/ppermute | solution.py:264
  29.5 0.1 constant_dynamic-slice_fusion.8
  29.6 0.1 copy.115
  29.7 0.7 fusion.152
  36.4 0.6 iota_compare_fusion.9
  37.0 0.6 compare_and_fusion
  37.6 0.6 pad_clamp_fusion
  38.2 0.6 slice_bitcast_fusion.9
  38.8 7.2 %collective-permute-done.1 = bf16[2,1,512,256]{3,2,1,0:T(8,128)(2,1)} collective-permute-done((bf16[2,1,512,256]{3,2,1,0:T(8,128)(2,1)}, bf16[2,1,512,256]{3,2,1,0:T(8,128)(2,1)}, u32[]{:S(2)}, u32[]{:S(2)}) %collective-permute-start.1) | collective-permute-done | bytes 524320 | tf_op jit(solution)/shard_map/ppermute | solution.py:264
  46.0 1.3 reverse_select_fusion.1.after_ref
  47.4 1.6 %fusion.53 = s32[128,16]{1,0:T(8,128)S(1)} fusion(bf16[128,17,256]{2,1,0:T(8,128)(2,1)} %all-to-all-done), kind=kLoop, calls=%fused_computation.92 | loop fusion | flops 8192 | bytes 16384 | tf_op jit(solution)/shard_map/add | solution.py:353
  49.0 0.7 add.147
  49.6 1.3 slice.388
  51.0 7.0 %fusion = f32[2,4,512,256]{3,2,1,0:T(8,128)} fusion(bf16[2048,256,1,1]{1,0,3,2:T(8,128)(2,1)S(1)} %bitcast.237, s32[2048]{0:T(1024)} %add.147, s32[2,4,512]{2,1,0:T(4,128)S(1)} %multiply_add_fusion), kind=kOutput, calls=%fused_computation.2 | convolution fusion | flops 4303355904 | bytes 5267456 | tf_op jit(solution)/shard_map/dot_general | solution.py:385
  58.0 1.1 slice.304
  59.1 6.5 %shard_map.113 = (f32[2,4,512,256]{3,2,1,0:T(8,128)}, f32[2,2,4,256]{3,2,1,0:T(4,128)}) custom-call(bf16[2,4,512,256]{3,2,1,0:T(8,128)(2,1)} %copy-done.1, bf16[2,1,512,256]{3,2,1,0:T(8,128)(2,1)} %collective-permute-done.before_ref, bf16[2,1,512,256]{3,2,1,0:T(8,128)(2,1)} %copy-done.4, bf16[9,256,128]{2,1,0:T(8,128)(2,1)} %k_ref.7), custom_call_target="tpu_custom_call" | custom-call | tf_op jit(solution)/shard_map/pallas_call | solution.py:123
  65.5 0.7 copy.114
  66.4 0.6 maximum_bitcast_fusion.2.block_ref
  67.0 11.4 %shard_map.114 = (f32[2,4,512,256]{3,2,1,0:T(8,128)}, f32[8,56,128]{2,1,0:T(8,128)}) custom-call(f32[56,128]{1,0:T(8,128)} %maximum_bitcast_fusion.2.block_ref, bf16[2,4,512,256]{3,2,1,0:T(8,128)(2,1)} %copy-done.1, bf16[2,1,512,256]{3,2,1,0:T(8,128)(2,1)} %collective-permute-done.before_ref, bf16[2,1,512,256]{3,2,1,0:T(8,128)(2,1)} %copy-done.4, ...), custom_call_target="tpu_custom_call" | custom-call | tf_op jit(solution)/shard_map/pallas_call | solution.py:205
  78.4 1.0 copy.189
  79.4 0.7 gather_fusion
  80.2 0.1 broadcast_select_fusion.1
  80.8 0.1 convolution_bitcast_fusion.1
  80.9 0.1 convolution_bitcast_fusion
  81.1 0.1 convolution_bitcast_fusion.3
  81.2 0.2 convolution_bitcast_fusion.2
  81.4 7.6 %multiply_convert_fusion = (bf16[2,4,512,256]{3,2,1,0:T(8,128)(2,1)S(1)}, bf16[2,4,512,256]{3,2,1,0:T(8,128)(2,1)S(1)}) fusion(f32[2,4,512,256]{3,2,1,0:T(8,128)} %fusion, f32[256]{0:T(256)S(1)} %copy-done.15, f32[2,4,256]{2,1,0:T(4,128)S(1)} %get-tuple-element.53, pred[512]{0:T(512)(128)(4,1)S(1)} %copy-done.12, f32[2,4,512,256]{3,2,1,0:T(8,128)} %get-tuple-element.16, ...), kind=kLoop, calls=%fused_computation.23 | loop fusion | flops 33554432 | bytes 16812032 | tf_op jit(solution)/shard_map/convert_element_type | solution.py:405
  89.1 0.2 fusion.17
  89.2 6.3 %collective-permute-start.3 = (bf16[2,1,512,512]{3,2,1,0:T(8,128)(2,1)S(1)}, bf16[2,1,512,512]{3,2,1,0:T(8,128)(2,1)S(1)}, u32[]{:S(2)}, u32[]{:S(2)}) collective-permute-start(bf16[2,1,512,512]{3,2,1,0:T(8,128)(2,1)S(1)} %get-tuple-element.26), channel_id=1, source_target_pairs={{1,0},{2,1},{3,2},{4,3},{5,4},{6,5},{7,6},{8,7},{9,8},{10,9},{11,1... | collective-permute-start | bytes 3145736 | tf_op jit(solution)/shard_map/ppermute | solution.py:264
  95.6 2.1 %collective-permute-start.2 = (bf16[2,1,512,512]{3,2,1,0:T(8,128)(2,1)S(1)}, bf16[2,1,512,512]{3,2,1,0:T(8,128)(2,1)S(1)}, u32[]{:S(2)}, u32[]{:S(2)}) collective-permute-start(bf16[2,1,512,512]{3,2,1,0:T(8,128)(2,1)S(1)} %get-tuple-element.27), channel_id=1, source_target_pairs={{0,1},{1,2},{2,3},{3,4},{4,5},{5,6},{6,7},{7,8},{8,9},{9,10},{10,1... | collective-permute-start | bytes 3145736 | tf_op jit(solution)/shard_map/ppermute | solution.py:263
  97.7 0.7 slice_bitcast_fusion.3
  98.4 2.3 %pad_maximum_fusion.src_ref = bf16[2,4,512,512]{3,2,1,0:T(8,128)(2,1)} fusion(bf16[2,4,512,256]{3,2,1,0:T(8,128)(2,1)S(1)} %get-tuple-element.25, bf16[2,4,512,256]{3,2,1,0:T(8,128)(2,1)S(1)} %get-tuple-element.24), kind=kLoop, calls=%fused_computation.13 | loop fusion | flops 8388608 | bytes 8388608 | tf_op jit(solution)/shard_map/concatenate | solution.py:409
  100.7 15.7 %collective-permute-done.3 = bf16[2,1,512,512]{3,2,1,0:T(8,128)(2,1)S(1)} collective-permute-done((bf16[2,1,512,512]{3,2,1,0:T(8,128)(2,1)S(1)}, bf16[2,1,512,512]{3,2,1,0:T(8,128)(2,1)S(1)}, u32[]{:S(2)}, u32[]{:S(2)}) %collective-permute-start.3) | collective-permute-done | bytes 1048608 | tf_op jit(solution)/shard_map/ppermute | solution.py:264
  116.4 0.3 reverse_select_fusion.after_ref
  116.8 3.6 %collective-permute-done.2.before_ref = bf16[2,1,512,512]{3,2,1,0:T(8,128)(2,1)S(1)} collective-permute-done((bf16[2,1,512,512]{3,2,1,0:T(8,128)(2,1)S(1)}, bf16[2,1,512,512]{3,2,1,0:T(8,128)(2,1)S(1)}, u32[]{:S(2)}, u32[]{:S(2)}) %collective-permute-start.2) | collective-permute-done | bytes 1048608 | tf_op jit(solution)/shard_map/ppermute | solution.py:263
  120.5 0.9 copy-done.3
  121.4 6.3 %shard_map.115 = (f32[2,4,512,128]{3,2,1,0:T(8,128)}, f32[2,2,4,128]{3,2,1,0:T(4,128)}) custom-call(bf16[2,4,512,512]{3,2,1,0:T(8,128)(2,1)} %pad_maximum_fusion.src_ref, bf16[2,1,512,512]{3,2,1,0:T(8,128)(2,1)} %copy-done.3, bf16[2,1,512,512]{3,2,1,0:T(8,128)(2,1)} %copy-done.2, bf16[9,128,256]{2,1,0:T(8,128)(2,1)} %k_ref.6), custom_call_target="tpu_custom_call" | custom-call | tf_op jit(solution)/shard_map/pallas_call | solution.py:123
  127.6 0.7 copy.120
  128.3 0.6 maximum_bitcast_fusion.1.block_ref
  128.9 10.4 %shard_map.116 = (f32[2,4,512,128]{3,2,1,0:T(8,128)}, f32[8,64,128]{2,1,0:T(8,128)}) custom-call(f32[64,128]{1,0:T(8,128)} %maximum_bitcast_fusion.1.block_ref, bf16[2,4,512,512]{3,2,1,0:T(8,128)(2,1)} %pad_maximum_fusion.src_ref, bf16[2,1,512,512]{3,2,1,0:T(8,128)(2,1)} %copy-done.3, bf16[2,1,512,512]{3,2,1,0:T(8,128)(2,1)} %copy-done.2, ...), custom_call_target="tpu_custom_call" | custom-call | tf_op jit(solution)/shard_map/pallas_call | solution.py:205
  139.4 1.3 copy.188
  140.6 0.8 gather_fusion.1
  141.4 0.1 broadcast_select_fusion
  141.6 0.1 rev.36
  141.9 0.1 rev.37
  142.2 0.1 convolution_bitcast_fusion.5
  142.4 0.2 convolution_bitcast_fusion.4
  142.5 0.2 convolution_bitcast_fusion.7
  142.7 0.2 convolution_bitcast_fusion.6
  142.9 5.1 %add_bitcast_fusion = (f32[1,1,2,4,512,128]{5,4,3,2,1,0:T(8,128)}, bf16[1,1,2,4,512,128]{5,4,3,2,1,0:T(8,128)(2,1)}) fusion(f32[2,4,512,128]{3,2,1,0:T(8,128)} %get-tuple-element.23, f32[2,4,128]{2,1,0:T(4,128)S(1)} %reverse_select_fusion.4, f32[2,4,128]{2,1,0:T(4,128)S(1)} %reverse_select_fusion.5, pred[512]{0:T(512)(128)(4,1)S(1)} %copy-done.12, ...), kind=kLoop, calls=%fused_computation.31 | loop fusion | flops 7340032 | bytes 9455104 | tf_op jit(solution)/shard_map/broadcast_in_dim | solution.py:419
  (115 shorter events, 0.9 us)
Async XLA Ops:
  0.6 4.1 %copy-start = (bf16[1024,256]{1,0:T(8,128)(2,1)S(1)}, bf16[1024,256]{1,0:T(8,128)(2,1)}, u32[]{:S(2)}) copy-start(bf16[1024,256]{1,0:T(8,128)(2,1)} %param.11) | copy-start | bytes 1572868
  7.7 39.7 %all-to-all-start = ((bf16[128,17,256]{2,1,0:T(8,128)(2,1)}), bf16[128,17,256]{2,1,0:T(8,128)(2,1)}, u32[]{:S(2)}, u32[]{:S(2)}) async-start(bf16[128,17,256]{2,1,0:T(8,128)(2,1)} %pad_maximum_fusion.2), calls=%async_computation | async-start | bytes 3145728 | tf_op jit(solution)/shard_map/all_to_all | solution.py:349
  18.4 11.2 %copy-start.11 = (s32[8,2,3]{0,1,2:T(2,128)S(1)}, s32[8,2,3]{0,1,2:T(2,128)}, u32[]{:S(2)}) copy-start(s32[8,2,3]{0,1,2:T(2,128)} %param.14) | copy-start | bytes 580
  18.4 19.8 %copy-start.8 = (bf16[9,128,256]{2,1,0:T(8,128)(2,1)S(1)}, bf16[9,128,256]{2,1,0:T(8,128)(2,1)}, u32[]{:S(2)}) copy-start(bf16[9,128,256]{2,1,0:T(8,128)(2,1)} %k_ref.6) | copy-start | bytes 1769476
  20.3 30.7 %copy-start.1 = (bf16[2,4,512,256]{3,2,1,0:T(8,128)(2,1)}, bf16[2,4,512,256]{3,2,1,0:T(8,128)(2,1)S(1)}, u32[]{:S(2)}) copy-start(bf16[2,4,512,256]{3,2,1,0:T(8,128)(2,1)S(1)} %pad_maximum_fusion.1.src_ref) | copy-start | bytes 6291460
  21.4 36.6 %collective-permute-start = (bf16[2,1,512,256]{3,2,1,0:T(8,128)(2,1)}, bf16[2,1,512,256]{3,2,1,0:T(8,128)(2,1)}, u32[]{:S(2)}, u32[]{:S(2)}) collective-permute-start(bf16[2,1,512,256]{3,2,1,0:T(8,128)(2,1)} %get-tuple-element.29), channel_id=1, source_target_pairs={{0,1},{1,2},{2,3},{3,4},{4,5},{5,6},{6,7},{7,8},{8,9},{9,10},{10,1... | collective-permute-start | bytes 1572872 | tf_op jit(solution)/shard_map/ppermute | solution.py:263
  23.4 22.6 %collective-permute-start.1 = (bf16[2,1,512,256]{3,2,1,0:T(8,128)(2,1)}, bf16[2,1,512,256]{3,2,1,0:T(8,128)(2,1)}, u32[]{:S(2)}, u32[]{:S(2)}) collective-permute-start(bf16[2,1,512,256]{3,2,1,0:T(8,128)(2,1)} %get-tuple-element.28), channel_id=1, source_target_pairs={{1,0},{2,1},{3,2},{4,3},{5,4},{6,5},{7,6},{8,7},{9,8},{10,9},{11,1... | collective-permute-start | bytes 1572872 | tf_op jit(solution)/shard_map/ppermute | solution.py:264
  47.4 10.6 %copy-start.4 = (bf16[2,1,512,256]{3,2,1,0:T(8,128)(2,1)}, bf16[2,1,512,256]{3,2,1,0:T(8,128)(2,1)S(1)}, u32[]{:S(2)}) copy-start(bf16[2,1,512,256]{3,2,1,0:T(8,128)(2,1)S(1)} %reverse_select_fusion.1.after_ref) | copy-start | bytes 1572868
  58.0 8.3 %slice-start = ((bf16[2,4,512,256]{3,2,1,0:T(8,128)(2,1)}), bf16[2,4,512,128]{3,2,1,0:T(8,128)(2,1)S(1)}, s32[]{:S(2)}) async-start(bf16[2,4,512,256]{3,2,1,0:T(8,128)(2,1)} %copy-done.1), calls=%async_computation.1 | async-start | bytes 2097152 | tf_op jit(solution)/shard_map/slice | solution.py:270
  58.0 8.3 %slice-start.1 = ((bf16[2,1,512,256]{3,2,1,0:T(8,128)(2,1)}), bf16[2,1,512,128]{3,2,1,0:T(8,128)(2,1)S(1)}, s32[]{:S(2)}) async-start(bf16[2,1,512,256]{3,2,1,0:T(8,128)(2,1)} %copy-done.4), calls=%async_computation.2 | async-start | bytes 524288 | tf_op jit(solution)/shard_map/slice | solution.py:270
  65.5 14.6 %copy-start.14 = (pred[8]{0:T(512)(128)(4,1)S(1)}, pred[8]{0:T(512)(128)(4,1)}, u32[]{:S(2)}) copy-start(pred[8]{0:T(512)(128)(4,1)} %compare_and_fusion) | copy-start | bytes 28
  66.3 14.4 %copy-start.9 = (bf16[128,256]{1,0:T(8,128)(2,1)S(1)}, bf16[128,256]{1,0:T(8,128)(2,1)}, u32[]{:S(2)}) copy-start(bf16[128,256]{1,0:T(8,128)(2,1)} %get-tuple-element.40) | copy-start | bytes 196612
  67.0 14.4 %copy-start.12 = (pred[512]{0:T(512)(128)(4,1)S(1)}, pred[512]{0:T(512)(128)(4,1)}, u32[]{:S(2)}) copy-start(pred[512]{0:T(512)(128)(4,1)} %get-tuple-element.92) | copy-start | bytes 1540
  67.0 14.5 %copy-start.13 = (pred[512]{0:T(512)(128)(4,1)S(1)}, pred[512]{0:T(512)(128)(4,1)}, u32[]{:S(2)}) copy-start(pred[512]{0:T(512)(128)(4,1)} %get-tuple-element.93) | copy-start | bytes 1540
  67.0 14.5 %copy-start.15 = (f32[256]{0:T(256)S(1)}, f32[256]{0:T(256)}, u32[]{:S(2)}) copy-start(f32[256]{0:T(256)} %param.16) | copy-start | bytes 3076
  89.1 8.7 %copy-start.5 = (bf16[9,256,128]{2,1,0:T(8,128)(2,1)S(1)}, bf16[9,256,128]{2,1,0:T(8,128)(2,1)}, u32[]{:S(2)}) copy-start(bf16[9,256,128]{2,1,0:T(8,128)(2,1)} %k_ref.7) | copy-start | bytes 1769476
  89.2 27.2 %collective-permute-start.3 = (bf16[2,1,512,512]{3,2,1,0:T(8,128)(2,1)S(1)}, bf16[2,1,512,512]{3,2,1,0:T(8,128)(2,1)S(1)}, u32[]{:S(2)}, u32[]{:S(2)}) collective-permute-start(bf16[2,1,512,512]{3,2,1,0:T(8,128)(2,1)S(1)} %get-tuple-element.26), channel_id=1, source_target_pairs={{1,0},{2,1},{3,2},{4,3},{5,4},{6,5},{7,6},{8,7},{9,8},{10,9},{11,1... | collective-permute-start | bytes 3145736 | tf_op jit(solution)/shard_map/ppermute | solution.py:264
  95.6 24.8 %collective-permute-start.2 = (bf16[2,1,512,512]{3,2,1,0:T(8,128)(2,1)S(1)}, bf16[2,1,512,512]{3,2,1,0:T(8,128)(2,1)S(1)}, u32[]{:S(2)}, u32[]{:S(2)}) collective-permute-start(bf16[2,1,512,512]{3,2,1,0:T(8,128)(2,1)S(1)} %get-tuple-element.27), channel_id=1, source_target_pairs={{0,1},{1,2},{2,3},{3,4},{4,5},{5,6},{6,7},{7,8},{8,9},{9,10},{10,1... | collective-permute-start | bytes 3145736 | tf_op jit(solution)/shard_map/ppermute | solution.py:263
  116.7 3.8 %copy-start.2 = (bf16[2,1,512,512]{3,2,1,0:T(8,128)(2,1)}, bf16[2,1,512,512]{3,2,1,0:T(8,128)(2,1)S(1)}, u32[]{:S(2)}) copy-start(bf16[2,1,512,512]{3,2,1,0:T(8,128)(2,1)S(1)} %reverse_select_fusion.after_ref) | copy-start | bytes 3145732
  120.4 1.0 copy-start.3
  128.9 13.3 %copy-start.10 = (bf16[256,128]{1,0:T(8,128)(2,1)S(1)}, bf16[256,128]{1,0:T(8,128)(2,1)}, u32[]{:S(2)}) copy-start(bf16[256,128]{1,0:T(8,128)(2,1)} %get-tuple-element.33) | copy-start | bytes 196612
  139.3 3.6 %copy-start.6 = (bf16[1,1,2,4,512,128]{5,4,3,2,1,0:T(8,128)(2,1)S(1)}, bf16[1,1,2,4,512,128]{5,4,3,2,1,0:T(8,128)(2,1)}, u32[]{:S(2)}) copy-start(bf16[1,1,2,4,512,128]{5,4,3,2,1,0:T(8,128)(2,1)} %param.19) | copy-start | bytes 3145732
  139.3 3.6 %copy-start.7 = (bf16[1,1,2,4,512,128]{5,4,3,2,1,0:T(8,128)(2,1)S(1)}, bf16[1,1,2,4,512,128]{5,4,3,2,1,0:T(8,128)(2,1)}, u32[]{:S(2)}) copy-start(bf16[1,1,2,4,512,128]{5,4,3,2,1,0:T(8,128)(2,1)} %param.10) | copy-start | bytes 3145732
  139.3 3.5 %copy-start.16 = (f32[128]{0:T(128)S(1)}, f32[128]{0:T(128)}, u32[]{:S(2)}) copy-start(f32[128]{0:T(128)} %param.18) | copy-start | bytes 1540

commit v13 on v9

--- a/solution.py
+++ b/solution.py
@@ -92,7 +92,9 @@
     return out, margins
 
 
-def back_kernel(src_ref, before_ref, after_ref, k_ref, out_ref, margin_ref):
+def back_kernel(src_ref, before_ref, after_ref, k_ref, *rest):
+    residual_ref = rest[0] if len(rest) == 3 else None
+    out_ref, margin_ref = rest[-2:]
     band = pl.program_id(0)
     _, rows, cols, cout = out_ref.shape
     width = src_ref.shape[3]
@@ -110,16 +112,24 @@
     z_left, z_mid, z_right = [joined[:, i * cout : (i + 1) * cout] for i in range(3)]
     from_left = jnp.where(col == 0, 0.0, pltpu.roll(z_left, 1, 0))
     from_right = jnp.where(col == cols - 1, 0.0, pltpu.roll(z_right, pixels - 1, 0))
-    out_ref[0] = (z_mid + from_left + from_right).reshape(rows, cols, cout)
+    total = (z_mid + from_left + from_right).reshape(rows, cols, cout)
+    if residual_ref is not None:
+        total = total + residual_ref[0].astype(jnp.float32)
+    out_ref[0] = total
     margin_ref[0, 0] = z_right.reshape(rows, cols, cout)[:, 0, :]
     margin_ref[0, 1] = z_left.reshape(rows, cols, cout)[:, cols - 1, :]
 
 
-def conv_back(pieces, first, width, kernel):
+def conv_back(pieces, first, width, kernel, residual=None):
     source, before, after = pieces
     bands, rows, cols, _ = source.shape
     cout = kernel.shape[1]
     block = first // width
+    extra_specs = []
+    extra_args = ()
+    if residual is not None:
+        extra_specs = [pl.BlockSpec((1, rows, cols, cout), lambda b: (b, 0, 0, 0))]
+        extra_args = (residual,)
     return pl.pallas_call(
         back_kernel,
         grid=(bands,),
@@ -128,7 +138,8 @@
             pl.BlockSpec((1, 1, cols, width), lambda b: (b, 0, 0, block)),
             pl.BlockSpec((1, 1, cols, width), lambda b: (b, 0, 0, block)),
             pl.BlockSpec(kernel.shape, lambda b: (0, 0, 0)),
-        ],
+        ]
+        + extra_specs,
         out_specs=[
             pl.BlockSpec((1, rows, cols, cout), lambda b: (b, 0, 0, 0)),
             pl.BlockSpec((1, 2, rows, cout), lambda b: (b, 0, 0, 0)),
@@ -138,11 +149,15 @@
             jax.ShapeDtypeStruct((bands, 2, rows, cout), jnp.float32),
         ],
         compiler_params=pltpu.CompilerParams(vmem_limit_bytes=60 * 1024 * 1024),
-    )(source, before, after, kernel)
-
-
-def conv_gather_kernel(count, block_ref, src_ref, before_ref, after_ref, k_ref,
-                       out_ref, gathered_ref, landed, send_sems, recv_sems):
+    )(source, before, after, kernel, *extra_args)
+
+
+def conv_gather_kernel(count, block_ref, src_ref, before_ref, after_ref, k_ref, *rest):
+    if len(rest) == 7:
+        residual_ref, bias_ref = rest[:2]
+    else:
+        residual_ref = None
+    out_ref, gathered_ref, landed, send_sems, recv_sems = rest[-5:]
     step_at = pl.program_id(0)
     face = lax.axis_index("face")
     tile = lax.axis_index("tile")
@@ -185,7 +200,10 @@
     z_left, z_mid, z_right = [joined[:, i * cout : (i + 1) * cout] for i in range(3)]
     from_left = jnp.where(col == 0, 0.0, pltpu.roll(z_left, 1, 0))
     from_right = jnp.where(col == cols - 1, 0.0, pltpu.roll(z_right, pixels - 1, 0))
-    out_ref[0] = (z_mid + from_left + from_right).reshape(rows, cols, cout)
+    total = (z_mid + from_left + from_right).reshape(rows, cols, cout)
+    if residual_ref is not None:
+        total = total + residual_ref[0].astype(jnp.float32) + bias_ref[...]
+    out_ref[0] = total
 
     @pl.when(step_at == pl.num_programs(0) - 1)
     def _():
@@ -195,10 +213,18 @@
             gathered_ref[step] = landed[step]
 
 
-def conv_gather(pieces, first, width, block, kernel, gather_id):
+def conv_gather(pieces, first, width, block, kernel, gather_id, residual=None, bias=None):
     source, before, after = pieces
     bands, rows, cols, _ = source.shape
     cout = kernel.shape[2]
+    extra_specs = []
+    extra_args = ()
+    if residual is not None:
+        extra_specs = [
+            pl.BlockSpec((1, rows, cols, cout), lambda b: (b, 0, 0, 0)),
+            pl.BlockSpec((1, cout), lambda b: (0, 0)),
+        ]
+        extra_args = (residual, bias.reshape(1, cout))
     count = lax.axis_size("face")
     block_rows, lanes = block.shape
     lane_block = first // width
@@ -211,7 +237,8 @@
             pl.BlockSpec((1, 1, cols, width), lambda b: (b, 0, 0, lane_block)),
             pl.BlockSpec((1, 1, cols, width), lambda b: (b, 0, 0, lane_block)),
             pl.BlockSpec(kernel.shape, lambda b: (0, 0, 0)),
-        ],
+        ]
+        + extra_specs,
         out_specs=[
             pl.BlockSpec((1, rows, cols, cout), lambda b: (b, 0, 0, 0)),
             pl.BlockSpec((count, block_rows, lanes), lambda b: (0, 0, 0)),
@@ -228,7 +255,7 @@
         compiler_params=pltpu.CompilerParams(
             collective_id=gather_id, has_side_effects=True, vmem_limit_bytes=60 * 1024 * 1024
         ),
-    )(block, source, before, after, kernel)
+    )(block, source, before, after, kernel, *extra_args)
 
 
 def side_terms(sides, kernel):
@@ -405,15 +432,17 @@
     grad_pre = jax.vjp(activation, pre_act)[1](grad_inner)[0].astype(jnp.bfloat16)
 
     pair = extend_rows(jnp.concatenate([inner, grad_pre], axis=3), last_tile)
-    pre_back, pre_margins = conv_back(pair, lifted, lifted, kernel_one)
+    pre_back, pre_margins = conv_back(pair, lifted, lifted, kernel_one, cot_field)
     parts = [edge_cols(pair, 0, lifted), jnp.swapaxes(pre_margins, 1, 2)]
-    second_out, landed = conv_gather(pair, 0, lifted, pack_parts(parts), kernel_two, 1)
+    second_out, landed = conv_gather(
+        pair, 0, lifted, pack_parts(parts), kernel_two, 1, base_field, bias_two
+    )
     inner_edges, pre_gathered = unpack_parts(landed, parts)
     second_sides = side_terms(side_columns(inner_edges, matching_row), kernel_two)
 
     second_out = at_edges(second_out, second_sides[:, 0], second_sides[:, 1])
-    analysis = (base_field.astype(jnp.float32) + second_out + bias_two).astype(jnp.bfloat16)
-    grad_base = cot_field.astype(jnp.float32) + return_sides(pre_back, pre_gathered, matching_row)
+    analysis = second_out.astype(jnp.bfloat16)
+    grad_base = return_sides(pre_back, pre_gathered, matching_row)
     return (analysis[None, None], grad_base[None, None])
 
 

time: 129 us -> 129 us (level)
  other arithmetic: 22.4 us -> 21.1 us
    unnamed x60 -> x58, local copies, waits for them, and re-layouts: 4.04 us -> 4.04 us
where the time goes in v13:
time: 129 us; the launch traced here: 128 us
  Pallas kernels  34.5 us (27%)
  starting transfers between devices  23.9 us (19%)
  other arithmetic  21.1 us (16%)
  waiting for transfers between devices  19.7 us (15%)
  local copies, waits for them, and re-layouts  12.7 us (10%)
  matrix products  8.13 us (6%)
  between operations  7.79 us (6%)
    pallas_call x2, Pallas kernels, conv_gather(): pl.pallas_call(functools.partial(conv_gather_kernel, count), grid=(bands,...  21.7 us
    ppermute x2, waiting for transfers between devices, extend_rows(): after = lax.ppermute(head, 'tile', [(i + 1, i) for i in range(count - 1)])  16.1 us
    pallas_call x2, Pallas kernels, conv_back(): pl.pallas_call(back_kernel, grid=(bands,), in_specs=[pl.BlockSpec((1, row...  12.8 us
    all_to_all x1, starting transfers between devices, route_observations(): lax.all_to_all(payload, ('face', 'tile'), split_axis=0, concat_axis=0, ti...  11.6 us
    ppermute x2, starting transfers between devices, extend_rows(): after = lax.ppermute(head, 'tile', [(i + 1, i) for i in range(count - 1)])  8.23 us
    dot_general x1, matrix products, per_device(): gridded = jnp.dot(onehot, got_values, preferred_element_type=jnp.float32)  5.33 us
    convert_element_type x1, other arithmetic, per_device(): inner = activation(pre_act).astype(jnp.bfloat16)  5.04 us
    broadcast_in_dim x1, other arithmetic, per_device(): return (analysis[None, None], grad_base[None, None])  4.09 us
  transfers between devices with their start and end apart: 5, of which 2 were waited for; matrix products, arithmetic and copies ran while one was open for 12% of the time, Pallas kernels for 14%

profile of v13, /device:TPU:24, one launch (start us, length us, event | category | flops | bytes accessed | tf_op | source)
XLA Modules:
  0.0 127.8 jit_solution(5396907758564284299)
XLA Ops:
  0.6 0.0 copy-start
  0.7 1.8 %pad_maximum_fusion.1.src_ref = bf16[2,4,512,256]{3,2,1,0:T(8,128)(2,1)S(1)} fusion(bf16[2,4,512,128]{3,2,1,0:T(8,128)(2,1)} %bitcast.234, bf16[2,4,512,128]{3,2,1,0:T(8,128)(2,1)} %bitcast.236), kind=kLoop, calls=%fused_computation.30 | loop fusion | flops 4194304 | bytes 4194304 | tf_op jit(solution)/shard_map/concatenate | solution.py:420
  2.5 1.1 fusion.147
  3.7 4.5 %collective-permute-start.1 = (bf16[2,1,512,256]{3,2,1,0:T(8,128)(2,1)}, bf16[2,1,512,256]{3,2,1,0:T(8,128)(2,1)}, u32[]{:S(2)}, u32[]{:S(2)}) collective-permute-start(bf16[2,1,512,256]{3,2,1,0:T(8,128)(2,1)} %get-tuple-element.24), channel_id=1, source_target_pairs={{1,0},{2,1},{3,2},{4,3},{5,4},{6,5},{7,6},{8,7},{9,8},{10,9},{11,1... | collective-permute-start | bytes 1572872 | tf_op jit(solution)/shard_map/ppermute | solution.py:291
  8.2 1.9 %collective-permute-start = (bf16[2,1,512,256]{3,2,1,0:T(8,128)(2,1)}, bf16[2,1,512,256]{3,2,1,0:T(8,128)(2,1)}, u32[]{:S(2)}, u32[]{:S(2)}) collective-permute-start(bf16[2,1,512,256]{3,2,1,0:T(8,128)(2,1)} %get-tuple-element.25), channel_id=1, source_target_pairs={{0,1},{1,2},{2,3},{3,4},{4,5},{5,6},{6,7},{7,8},{8,9},{9,10},{10,1... | collective-permute-start | bytes 1572872 | tf_op jit(solution)/shard_map/ppermute | solution.py:290
  10.2 0.5 convert_reduce_fusion
  10.7 0.9 select_reduce_fusion
  11.6 0.1 reduce_sum.22
  11.7 0.1 fusion.50
  11.8 0.1 pad.43.clone
  11.9 0.1 maximum_bitcast_fusion
  12.0 0.1 copy.113
  12.1 1.6 %fusion.14 = bf16[2048,256]{1,0:T(8,128)(2,1)S(1)} fusion(bf16[1024,256]{1,0:T(8,128)(2,1)S(1)} %copy-done, s32[1024]{0:T(1024)S(1)} %multiply_add_fusion.1), kind=kOutput, calls=%fused_computation.29 | convolution fusion | flops 1076363264 | bytes 1576960 | tf_op jit(solution)/shard_map/dot_general | solution.py:364
  13.7 0.0 copy-start.12
  13.7 0.0 copy-start.8
  13.8 1.3 %pad_maximum_fusion.2 = bf16[128,17,256]{2,1,0:T(8,128)(2,1)} fusion(bf16[128,1,256]{2,1,0:T(2,128)(2,1)S(1)} %copy.113, bf16[128,16,256]{2,1,0:T(8,128)(2,1)S(1)} %bitcast.239), kind=kLoop, calls=%fused_computation.33 | loop fusion | flops 2228224 | bytes 2228224 | tf_op jit(solution)/shard_map/concatenate | solution.py:373
  15.1 11.6 %all-to-all-start = ((bf16[128,17,256]{2,1,0:T(8,128)(2,1)}), bf16[128,17,256]{2,1,0:T(8,128)(2,1)}, u32[]{:S(2)}, u32[]{:S(2)}) async-start(bf16[128,17,256]{2,1,0:T(8,128)(2,1)} %pad_maximum_fusion.2), calls=%async_computation | async-start | bytes 3145728 | tf_op jit(solution)/shard_map/all_to_all | solution.py:376
  26.8 0.1 constant_dynamic-slice_fusion.8
  26.8 0.1 copy.115
  27.0 0.6 fusion.152
  33.8 1.3 %reverse_select_fusion.1.after_ref = bf16[2,1,512,256]{3,2,1,0:T(8,128)(2,1)S(1)} fusion(bf16[2,1,512,256]{3,2,1,0:T(8,128)(2,1)} %collective-permute-done.1, bf16[2,1,512,256]{3,2,1,0:T(8,128)(2,1)} %get-tuple-element.25, pred[]{:T(512)S(6)} %eq.131), kind=kLoop, calls=%fused_computation.46 | loop fusion | flops 262144 | bytes 1572865 | tf_op jit(solution)/shard_map/jit(_where)/select_n | solution.py:292
  35.2 0.7 copy-done.4
  36.0 6.4 %shard_map.113 = (f32[2,4,512,256]{3,2,1,0:T(8,128)}, f32[2,2,4,256]{3,2,1,0:T(4,128)}) custom-call(bf16[2,4,512,256]{3,2,1,0:T(8,128)(2,1)} %copy-done.1, bf16[2,1,512,256]{3,2,1,0:T(8,128)(2,1)} %collective-permute-done.before_ref, bf16[2,1,512,256]{3,2,1,0:T(8,128)(2,1)} %copy-done.4, bf16[9,256,128]{2,1,0:T(8,128)(2,1)} %k_ref.7), custom_call_target="tpu_custom_call" | custom-call | tf_op jit(solution)/shard_map/pallas_call | solution.py:133
  42.4 0.7 copy.114
  43.1 1.0 slice.386
  44.1 0.6 maximum_bitcast_fusion.2.block_ref
  44.7 11.7 %shard_map.114 = (f32[2,4,512,256]{3,2,1,0:T(8,128)}, f32[8,56,128]{2,1,0:T(8,128)}) custom-call(f32[56,128]{1,0:T(8,128)} %maximum_bitcast_fusion.2.block_ref, bf16[2,4,512,256]{3,2,1,0:T(8,128)(2,1)} %copy-done.1, bf16[2,1,512,256]{3,2,1,0:T(8,128)(2,1)} %collective-permute-done.before_ref, bf16[2,1,512,256]{3,2,1,0:T(8,128)(2,1)} %copy-done.4, ...), custom_call_target="tpu_custom_call" | custom-call | tf_op jit(solution)/shard_map/pallas_call | solution.py:231
  56.5 1.0 copy.189
  57.5 0.6 gather_fusion
  58.1 0.1 broadcast_select_fusion.1
  58.6 0.1 convolution_bitcast_fusion.1
  58.8 0.1 convolution_bitcast_fusion
  58.9 0.1 convolution_bitcast_fusion.3
  59.1 0.1 convolution_bitcast_fusion.2
  59.4 1.4 %fusion.53 = s32[128,16]{1,0:T(8,128)S(1)} fusion(bf16[128,17,256]{2,1,0:T(8,128)(2,1)} %all-to-all-done), kind=kLoop, calls=%fused_computation.92 | loop fusion | flops 8192 | bytes 16384 | tf_op jit(solution)/shard_map/add | solution.py:380
  60.7 0.1 add.144
  60.8 1.3 %slice.409 = bf16[128,16,256]{2,1,0:T(8,128)(2,1)S(1)} slice(bf16[128,17,256]{2,1,0:T(8,128)(2,1)} %all-to-all-done), slice={[0:128], [0:16], [0:256]} | slice | bytes 2097152 | tf_op jit(solution)/shard_map/slice | solution.py:377
  62.2 0.0 copy-start.13
  62.2 5.3 %fusion = f32[2,4,512,256]{3,2,1,0:T(8,128)S(1)} fusion(bf16[2048,256,1,1]{1,0,3,2:T(8,128)(2,1)S(1)} %bitcast.238, s32[2048]{0:T(1024)S(1)} %add.144, s32[2,4,512]{2,1,0:T(4,128)S(1)} %multiply_add_fusion), kind=kOutput, calls=%fused_computation.2 | convolution fusion | flops 4303355904 | bytes 5267456 | tf_op jit(solution)/shard_map/dot_general | solution.py:412
  67.5 5.0 %multiply_convert_fusion = (bf16[2,4,512,256]{3,2,1,0:T(8,128)(2,1)S(1)}, bf16[2,4,512,256]{3,2,1,0:T(8,128)(2,1)S(1)}) fusion(f32[2,4,512,256]{3,2,1,0:T(8,128)S(1)} %fusion, f32[256]{0:T(256)S(1)} %copy-done.13, f32[2,4,256]{2,1,0:T(4,128)S(1)} %get-tuple-element.49, pred[512]{0:T(512)(128)(4,1)S(1)} %get-tuple-element.88, ...), kind=kLoop, calls=%fused_computation.23 | loop fusion | flops 33554432 | bytes 16812032 | tf_op jit(solution)/shard_map/convert_element_type | solution.py:430
  72.6 0.2 fusion.17
  72.8 3.7 %collective-permute-start.3 = (bf16[2,1,512,512]{3,2,1,0:T(8,128)(2,1)S(1)}, bf16[2,1,512,512]{3,2,1,0:T(8,128)(2,1)S(1)}, u32[]{:S(2)}, u32[]{:S(2)}) collective-permute-start(bf16[2,1,512,512]{3,2,1,0:T(8,128)(2,1)S(1)} %get-tuple-element.22), channel_id=1, source_target_pairs={{1,0},{2,1},{3,2},{4,3},{5,4},{6,5},{7,6},{8,7},{9,8},{10,9},{11,1... | collective-permute-start | bytes 3145736 | tf_op jit(solution)/shard_map/ppermute | solution.py:291
  76.5 2.1 %collective-permute-start.2 = (bf16[2,1,512,512]{3,2,1,0:T(8,128)(2,1)S(1)}, bf16[2,1,512,512]{3,2,1,0:T(8,128)(2,1)S(1)}, u32[]{:S(2)}, u32[]{:S(2)}) collective-permute-start(bf16[2,1,512,512]{3,2,1,0:T(8,128)(2,1)S(1)} %get-tuple-element.23), channel_id=1, source_target_pairs={{0,1},{1,2},{2,3},{3,4},{4,5},{5,6},{6,7},{7,8},{8,9},{9,10},{10,1... | collective-permute-start | bytes 3145736 | tf_op jit(solution)/shard_map/ppermute | solution.py:290
  78.6 0.6 slice_bitcast_fusion.3
  79.3 2.3 %pad_maximum_fusion.src_ref = bf16[2,4,512,512]{3,2,1,0:T(8,128)(2,1)} fusion(bf16[2,4,512,256]{3,2,1,0:T(8,128)(2,1)S(1)} %get-tuple-element.21, bf16[2,4,512,256]{3,2,1,0:T(8,128)(2,1)S(1)} %get-tuple-element.20), kind=kLoop, calls=%fused_computation.13 | loop fusion | flops 8388608 | bytes 8388608 | tf_op jit(solution)/shard_map/concatenate | solution.py:434
  81.6 16.1 %collective-permute-done.3 = bf16[2,1,512,512]{3,2,1,0:T(8,128)(2,1)S(1)} collective-permute-done((bf16[2,1,512,512]{3,2,1,0:T(8,128)(2,1)S(1)}, bf16[2,1,512,512]{3,2,1,0:T(8,128)(2,1)S(1)}, u32[]{:S(2)}, u32[]{:S(2)}) %collective-permute-start.3) | collective-permute-done | bytes 1048608 | tf_op jit(solution)/shard_map/ppermute | solution.py:291
  97.8 0.3 reverse_select_fusion.after_ref
  98.1 3.5 %collective-permute-done.2.before_ref = bf16[2,1,512,512]{3,2,1,0:T(8,128)(2,1)S(1)} collective-permute-done((bf16[2,1,512,512]{3,2,1,0:T(8,128)(2,1)S(1)}, bf16[2,1,512,512]{3,2,1,0:T(8,128)(2,1)S(1)}, u32[]{:S(2)}, u32[]{:S(2)}) %collective-permute-start.2) | collective-permute-done | bytes 1048608 | tf_op jit(solution)/shard_map/ppermute | solution.py:290
  101.7 0.9 copy-done.3
  102.6 6.4 %shard_map.115 = (f32[2,4,512,128]{3,2,1,0:T(8,128)}, f32[2,2,4,128]{3,2,1,0:T(4,128)}) custom-call(bf16[2,4,512,512]{3,2,1,0:T(8,128)(2,1)} %pad_maximum_fusion.src_ref, bf16[2,1,512,512]{3,2,1,0:T(8,128)(2,1)} %copy-done.3, bf16[2,1,512,512]{3,2,1,0:T(8,128)(2,1)} %copy-done.2, bf16[9,128,256]{2,1,0:T(8,128)(2,1)} %k_ref.6, bf16[2,4,512,128]{3,2,1,0:T(8,128)(2,1)} %bitcast.235), custom_call_target="tpu_custom_call" | custom-call | tf_op jit(solution)/shard_map/pallas_call | solution.py:133
  109.1 0.7 copy.120
  109.8 0.6 maximum_bitcast_fusion.1.block_ref
  110.4 9.9 %shard_map.116 = (f32[2,4,512,128]{3,2,1,0:T(8,128)}, f32[8,64,128]{2,1,0:T(8,128)}) custom-call(f32[64,128]{1,0:T(8,128)} %maximum_bitcast_fusion.1.block_ref, bf16[2,4,512,512]{3,2,1,0:T(8,128)(2,1)} %pad_maximum_fusion.src_ref, bf16[2,1,512,512]{3,2,1,0:T(8,128)(2,1)} %copy-done.3, bf16[2,1,512,512]{3,2,1,0:T(8,128)(2,1)} %copy-done.2, ...), custom_call_target="tpu_custom_call" | custom-call | tf_op jit(solution)/shard_map/pallas_call | solution.py:231
  120.3 1.3 copy.188
  121.6 0.6 gather_fusion.1
  122.2 0.1 broadcast_select_fusion
  122.4 0.1 constant_dynamic-slice_fusion.3
  122.5 0.1 rev.36
  122.7 0.1 rev.37
  123.1 0.1 convolution_bitcast_fusion.5
  123.2 0.1 convolution_bitcast_fusion.4
  123.4 0.2 convolution_bitcast_fusion.7
  123.6 0.2 convolution_bitcast_fusion.6
  123.8 4.1 %add_bitcast_fusion = (f32[1,1,2,4,512,128]{5,4,3,2,1,0:T(8,128)}, bf16[1,1,2,4,512,128]{5,4,3,2,1,0:T(8,128)(2,1)}) fusion(f32[2,4,512,128]{3,2,1,0:T(8,128)S(1)} %copy-done.9, f32[2,4,128]{2,1,0:T(4,128)S(1)} %reverse_select_fusion.4, f32[2,4,128]{2,1,0:T(4,128)S(1)} %reverse_select_fusion.5, pred[512]{0:T(512)(128)(4,1)S(1)} %get-tuple-element.88, ...), kind=kLoop, calls=%fused_computation.31 | loop fusion | flops 4718592 | bytes 7357440 | tf_op jit(solution)/shard_map/broadcast_in_dim | solution.py:446
  (110 shorter events, 0.9 us)
Async XLA Ops:
  0.6 11.5 %copy-start = (bf16[1024,256]{1,0:T(8,128)(2,1)S(1)}, bf16[1024,256]{1,0:T(8,128)(2,1)}, u32[]{:S(2)}) copy-start(bf16[1024,256]{1,0:T(8,128)(2,1)} %param.11) | copy-start | bytes 1572868
  0.6 9.5 %copy-start.11 = (s32[1024,1]{0,1:T(1,128)S(1)}, s32[1024,1]{0,1:T(1,128)}, u32[]{:S(2)}) copy-start(s32[1024,1]{0,1:T(1,128)} %param.12) | copy-start | bytes 12292
  0.7 10.0 %copy-start.14 = (s32[1024]{0:T(1024)S(1)}, s32[1024]{0:T(1024)}, u32[]{:S(2)}) copy-start(s32[1024]{0:T(1024)} %param.13) | copy-start | bytes 12292
  2.5 25.1 %copy-start.1 = (bf16[2,4,512,256]{3,2,1,0:T(8,128)(2,1)}, bf16[2,4,512,256]{3,2,1,0:T(8,128)(2,1)S(1)}, u32[]{:S(2)}) copy-start(bf16[2,4,512,256]{3,2,1,0:T(8,128)(2,1)S(1)} %pad_maximum_fusion.1.src_ref) | copy-start | bytes 6291460
  3.7 30.2 %collective-permute-start.1 = (bf16[2,1,512,256]{3,2,1,0:T(8,128)(2,1)}, bf16[2,1,512,256]{3,2,1,0:T(8,128)(2,1)}, u32[]{:S(2)}, u32[]{:S(2)}) collective-permute-start(bf16[2,1,512,256]{3,2,1,0:T(8,128)(2,1)} %get-tuple-element.24), channel_id=1, source_target_pairs={{1,0},{2,1},{3,2},{4,3},{5,4},{6,5},{7,6},{8,7},{9,8},{10,9},{11,1... | collective-permute-start | bytes 1572872 | tf_op jit(solution)/shard_map/ppermute | solution.py:291
  8.2 27.0 %collective-permute-start = (bf16[2,1,512,256]{3,2,1,0:T(8,128)(2,1)}, bf16[2,1,512,256]{3,2,1,0:T(8,128)(2,1)}, u32[]{:S(2)}, u32[]{:S(2)}) collective-permute-start(bf16[2,1,512,256]{3,2,1,0:T(8,128)(2,1)} %get-tuple-element.25), channel_id=1, source_target_pairs={{0,1},{1,2},{2,3},{3,4},{4,5},{5,6},{6,7},{7,8},{8,9},{9,10},{10,1... | collective-permute-start | bytes 1572872 | tf_op jit(solution)/shard_map/ppermute | solution.py:290
  13.7 13.0 %copy-start.12 = (s32[8,2,3]{0,1,2:T(2,128)S(1)}, s32[8,2,3]{0,1,2:T(2,128)}, u32[]{:S(2)}) copy-start(s32[8,2,3]{0,1,2:T(2,128)} %param.14) | copy-start | bytes 580
  13.7 20.0 %copy-start.8 = (bf16[9,128,256]{2,1,0:T(8,128)(2,1)S(1)}, bf16[9,128,256]{2,1,0:T(8,128)(2,1)}, u32[]{:S(2)}) copy-start(bf16[9,128,256]{2,1,0:T(8,128)(2,1)} %k_ref.6) | copy-start | bytes 1769476
  15.1 44.2 %all-to-all-start = ((bf16[128,17,256]{2,1,0:T(8,128)(2,1)}), bf16[128,17,256]{2,1,0:T(8,128)(2,1)}, u32[]{:S(2)}, u32[]{:S(2)}) async-start(bf16[128,17,256]{2,1,0:T(8,128)(2,1)} %pad_maximum_fusion.2), calls=%async_computation | async-start | bytes 3145728 | tf_op jit(solution)/shard_map/all_to_all | solution.py:376
  27.6 16.5 %slice-start = ((bf16[2,4,512,256]{3,2,1,0:T(8,128)(2,1)}), bf16[2,4,512,128]{3,2,1,0:T(8,128)(2,1)S(1)}, s32[]{:S(2)}) async-start(bf16[2,4,512,256]{3,2,1,0:T(8,128)(2,1)} %copy-done.1), calls=%async_computation.1 | async-start | bytes 2097152 | tf_op jit(solution)/shard_map/slice | solution.py:297
  35.2 0.8 copy-start.4
  62.1 5.4 %copy-start.6 = (f32[2,4,512,256]{3,2,1,0:T(8,128)S(1)}, f32[2,4,512,256]{3,2,1,0:T(8,128)}, u32[]{:S(2)}) copy-start(f32[2,4,512,256]{3,2,1,0:T(8,128)} %get-tuple-element.15) | copy-start | bytes 12582916
  62.1 5.4 %copy-start.7 = (f32[2,4,512,256]{3,2,1,0:T(8,128)S(1)}, f32[2,4,512,256]{3,2,1,0:T(8,128)}, u32[]{:S(2)}) copy-start(f32[2,4,512,256]{3,2,1,0:T(8,128)} %get-tuple-element.13) | copy-start | bytes 12582916
  62.2 5.4 %copy-start.13 = (f32[256]{0:T(256)S(1)}, f32[256]{0:T(256)}, u32[]{:S(2)}) copy-start(f32[256]{0:T(256)} %param.16) | copy-start | bytes 3076
  72.6 6.0 %copy-start.5 = (bf16[9,256,128]{2,1,0:T(8,128)(2,1)S(1)}, bf16[9,256,128]{2,1,0:T(8,128)(2,1)}, u32[]{:S(2)}) copy-start(bf16[9,256,128]{2,1,0:T(8,128)(2,1)} %k_ref.7) | copy-start | bytes 1769476
  72.8 25.0 %collective-permute-start.3 = (bf16[2,1,512,512]{3,2,1,0:T(8,128)(2,1)S(1)}, bf16[2,1,512,512]{3,2,1,0:T(8,128)(2,1)S(1)}, u32[]{:S(2)}, u32[]{:S(2)}) collective-permute-start(bf16[2,1,512,512]{3,2,1,0:T(8,128)(2,1)S(1)} %get-tuple-element.22), channel_id=1, source_target_pairs={{1,0},{2,1},{3,2},{4,3},{5,4},{6,5},{7,6},{8,7},{9,8},{10,9},{11,1... | collective-permute-start | bytes 3145736 | tf_op jit(solution)/shard_map/ppermute | solution.py:291
  76.5 25.2 %collective-permute-start.2 = (bf16[2,1,512,512]{3,2,1,0:T(8,128)(2,1)S(1)}, bf16[2,1,512,512]{3,2,1,0:T(8,128)(2,1)S(1)}, u32[]{:S(2)}, u32[]{:S(2)}) collective-permute-start(bf16[2,1,512,512]{3,2,1,0:T(8,128)(2,1)S(1)} %get-tuple-element.23), channel_id=1, source_target_pairs={{0,1},{1,2},{2,3},{3,4},{4,5},{5,6},{6,7},{7,8},{8,9},{9,10},{10,1... | collective-permute-start | bytes 3145736 | tf_op jit(solution)/shard_map/ppermute | solution.py:290
  98.1 3.7 %copy-start.2 = (bf16[2,1,512,512]{3,2,1,0:T(8,128)(2,1)}, bf16[2,1,512,512]{3,2,1,0:T(8,128)(2,1)S(1)}, u32[]{:S(2)}) copy-start(bf16[2,1,512,512]{3,2,1,0:T(8,128)(2,1)S(1)} %reverse_select_fusion.after_ref) | copy-start | bytes 3145732
  101.6 1.0 copy-start.3
  110.4 12.7 %copy-start.10 = (bf16[256,128]{1,0:T(8,128)(2,1)S(1)}, bf16[256,128]{1,0:T(8,128)(2,1)}, u32[]{:S(2)}) copy-start(bf16[256,128]{1,0:T(8,128)(2,1)} %get-tuple-element.29) | copy-start | bytes 196612
  120.3 3.4 %copy-start.9 = (f32[2,4,512,128]{3,2,1,0:T(8,128)S(1)}, f32[2,4,512,128]{3,2,1,0:T(8,128)}, u32[]{:S(2)}) copy-start(f32[2,4,512,128]{3,2,1,0:T(8,128)} %get-tuple-element.19) | copy-start | bytes 6291460

commit v14 on v13

--- a/solution.py
+++ b/solution.py
@@ -304,7 +304,9 @@
         partner = matching_row[side_number, 0]
         their_side = matching_row[side_number, 1]
         flipped = matching_row[side_number, 2]
-        chosen = lax.dynamic_index_in_dim(gathered, partner, 0, keepdims=False)
+        face_count = lax.axis_size("face")
+        slot = lax.rem(lax.axis_index("face") - partner + face_count, face_count)
+        chosen = lax.dynamic_index_in_dim(gathered, slot, 0, keepdims=False)
         column = jnp.where(their_side == 0, chosen[:, :, 0], chosen[:, :, 1])
         column = jnp.where(flipped == 1, column[::-1], column)
         picked_sides.append(column)
@@ -319,9 +321,7 @@
 def unpack_parts(landed, parts):
     face_count = lax.axis_size("face")
     face_at = lax.axis_index("face")
-    landed = landed.reshape(face_count, -1)
-    slot_of_face = lax.rem(face_at - lax.iota(jnp.int32, face_count) + face_count, face_count)
-    gathered = jnp.take(landed, slot_of_face, axis=0)
+    gathered = landed.reshape(face_count, -1)
     pieces = []
     offset = 0
     for part in parts:

time: 129 us -> 125 us (0.969)
  between operations: 7.79 us -> 5.24 us
  local copies, waits for them, and re-layouts: 12.7 us -> 11.2 us
    unnamed x58 -> x60, local copies, waits for them, and re-layouts: 4.04 us -> 3.92 us
  transfers between devices with their start and end apart: 5 -> 5, of which waited for: 2 -> 2; matrix products, arithmetic and copies ran while one was open for 12% -> 12% of each run, Pallas kernels for 14% -> 15%
where the time goes in v14:
time: 125 us; the launch traced here: 124 us
  Pallas kernels  34.7 us (28%)
  starting transfers between devices  23.9 us (19%)
  other arithmetic  21 us (17%)
  waiting for transfers between devices  19.7 us (16%)
  local copies, waits for them, and re-layouts  11.2 us (9%)
  matrix products  8.14 us (7%)
  between operations  5.24 us (4%)
    pallas_call x2, Pallas kernels, conv_gather(): pl.pallas_call(functools.partial(conv_gather_kernel, count), grid=(bands,...  21.8 us
    ppermute x2, waiting for transfers between devices, extend_rows(): after = lax.ppermute(head, 'tile', [(i + 1, i) for i in range(count - 1)])  16.1 us
    pallas_call x2, Pallas kernels, conv_back(): pl.pallas_call(back_kernel, grid=(bands,), in_specs=[pl.BlockSpec((1, row...  12.8 us
    all_to_all x1, starting transfers between devices, route_observations(): lax.all_to_all(payload, ('face', 'tile'), split_axis=0, concat_axis=0, ti...  11.6 us
    ppermute x2, starting transfers between devices, extend_rows(): after = lax.ppermute(head, 'tile', [(i + 1, i) for i in range(count - 1)])  8.23 us
    dot_general x1, matrix products, per_device(): gridded = jnp.dot(onehot, got_values, preferred_element_type=jnp.float32)  5.34 us
    convert_element_type x1, other arithmetic, per_device(): inner = activation(pre_act).astype(jnp.bfloat16)  5.04 us
    broadcast_in_dim x1, other arithmetic, per_device(): return (analysis[None, None], grad_base[None, None])  4.1 us
  transfers between devices with their start and end apart: 5, of which 2 were waited for; matrix products, arithmetic and copies ran while one was open for 12% of the time, Pallas kernels for 15%

profile of v14, /device:TPU:24, one launch (start us, length us, event | category | flops | bytes accessed | tf_op | source)
XLA Modules:
  0.0 123.8 jit_solution(14982279687141745884)
XLA Ops:
  0.6 0.0 copy-start
  0.7 1.8 %pad_maximum_fusion.1.src_ref = bf16[2,4,512,256]{3,2,1,0:T(8,128)(2,1)S(1)} fusion(bf16[2,4,512,128]{3,2,1,0:T(8,128)(2,1)} %bitcast.230, bf16[2,4,512,128]{3,2,1,0:T(8,128)(2,1)} %bitcast.232), kind=kLoop, calls=%fused_computation.28 | loop fusion | flops 4194304 | bytes 4194304 | tf_op jit(solution)/shard_map/concatenate | solution.py:420
  2.5 0.0 copy-start.1
  2.5 1.1 fusion.144
  3.7 4.5 %collective-permute-start.1 = (bf16[2,1,512,256]{3,2,1,0:T(8,128)(2,1)}, bf16[2,1,512,256]{3,2,1,0:T(8,128)(2,1)}, u32[]{:S(2)}, u32[]{:S(2)}) collective-permute-start(bf16[2,1,512,256]{3,2,1,0:T(8,128)(2,1)} %get-tuple-element.24), channel_id=1, source_target_pairs={{1,0},{2,1},{3,2},{4,3},{5,4},{6,5},{7,6},{8,7},{9,8},{10,9},{11,1... | collective-permute-start | bytes 1572872 | tf_op jit(solution)/shard_map/ppermute | solution.py:291
  8.2 1.9 %collective-permute-start = (bf16[2,1,512,256]{3,2,1,0:T(8,128)(2,1)}, bf16[2,1,512,256]{3,2,1,0:T(8,128)(2,1)}, u32[]{:S(2)}, u32[]{:S(2)}) collective-permute-start(bf16[2,1,512,256]{3,2,1,0:T(8,128)(2,1)} %get-tuple-element.25), channel_id=1, source_target_pairs={{0,1},{1,2},{2,3},{3,4},{4,5},{5,6},{6,7},{7,8},{8,9},{9,10},{10,1... | collective-permute-start | bytes 1572872 | tf_op jit(solution)/shard_map/ppermute | solution.py:290
  10.2 0.5 convert_reduce_fusion
  10.7 0.9 select_reduce_fusion
  11.6 0.1 reduce_sum.22
  11.7 0.1 fusion.50
  11.8 0.1 pad.43.clone
  11.9 0.1 maximum_bitcast_fusion
  12.0 0.1 copy.113
  12.1 1.6 %fusion.14 = bf16[2048,256]{1,0:T(8,128)(2,1)S(1)} fusion(bf16[1024,256]{1,0:T(8,128)(2,1)S(1)} %copy-done, s32[1024]{0:T(1024)S(1)} %multiply_add_fusion.1), kind=kOutput, calls=%fused_computation.27 | convolution fusion | flops 1076363264 | bytes 1576960 | tf_op jit(solution)/shard_map/dot_general | solution.py:364
  13.7 0.0 copy-start.12
  13.7 0.0 copy-start.8
  13.8 1.3 %pad_maximum_fusion.2 = bf16[128,17,256]{2,1,0:T(8,128)(2,1)} fusion(bf16[128,1,256]{2,1,0:T(2,128)(2,1)S(1)} %copy.113, bf16[128,16,256]{2,1,0:T(8,128)(2,1)S(1)} %bitcast.235), kind=kLoop, calls=%fused_computation.31 | loop fusion | flops 2228224 | bytes 2228224 | tf_op jit(solution)/shard_map/concatenate | solution.py:373
  15.1 11.6 %all-to-all-start = ((bf16[128,17,256]{2,1,0:T(8,128)(2,1)}), bf16[128,17,256]{2,1,0:T(8,128)(2,1)}, u32[]{:S(2)}, u32[]{:S(2)}) async-start(bf16[128,17,256]{2,1,0:T(8,128)(2,1)} %pad_maximum_fusion.2), calls=%async_computation | async-start | bytes 3145728 | tf_op jit(solution)/shard_map/all_to_all | solution.py:376
  26.7 0.1 constant_dynamic-slice_fusion.8
  26.8 0.1 copy.115
  26.9 0.6 fusion.149
  28.8 0.0 slice-start
  31.3 1.3 %reverse_select_fusion.1.after_ref = bf16[2,1,512,256]{3,2,1,0:T(8,128)(2,1)S(1)} fusion(bf16[2,1,512,256]{3,2,1,0:T(8,128)(2,1)} %collective-permute-done.1, bf16[2,1,512,256]{3,2,1,0:T(8,128)(2,1)} %get-tuple-element.25, pred[]{:T(512)S(6)} %eq.131), kind=kLoop, calls=%fused_computation.44 | loop fusion | flops 262144 | bytes 1572865 | tf_op jit(solution)/shard_map/jit(_where)/select_n | solution.py:292
  32.6 0.0 copy-start.4
  32.7 0.7 copy-done.4
  33.4 6.4 %shard_map.113 = (f32[2,4,512,256]{3,2,1,0:T(8,128)}, f32[2,2,4,256]{3,2,1,0:T(4,128)}) custom-call(bf16[2,4,512,256]{3,2,1,0:T(8,128)(2,1)} %copy-done.1, bf16[2,1,512,256]{3,2,1,0:T(8,128)(2,1)} %collective-permute-done.before_ref, bf16[2,1,512,256]{3,2,1,0:T(8,128)(2,1)} %copy-done.4, bf16[9,256,128]{2,1,0:T(8,128)(2,1)} %k_ref.7), custom_call_target="tpu_custom_call" | custom-call | tf_op jit(solution)/shard_map/pallas_call | solution.py:133
  39.8 0.7 copy.114
  40.6 1.0 slice.382
  41.6 0.6 maximum_bitcast_fusion.2.block_ref
  42.2 11.7 %shard_map.114 = (f32[2,4,512,256]{3,2,1,0:T(8,128)}, f32[8,56,128]{2,1,0:T(8,128)}) custom-call(f32[56,128]{1,0:T(8,128)} %maximum_bitcast_fusion.2.block_ref, bf16[2,4,512,256]{3,2,1,0:T(8,128)(2,1)} %copy-done.1, bf16[2,1,512,256]{3,2,1,0:T(8,128)(2,1)} %collective-permute-done.before_ref, bf16[2,1,512,256]{3,2,1,0:T(8,128)(2,1)} %copy-done.4, ...), custom_call_target="tpu_custom_call" | custom-call | tf_op jit(solution)/shard_map/pallas_call | solution.py:231
  53.9 1.0 copy.195
  55.4 0.1 convolution_bitcast_fusion.1
  55.5 0.1 convolution_bitcast_fusion
  55.7 0.1 convolution_bitcast_fusion.3
  55.8 0.1 convolution_bitcast_fusion.2
  56.1 1.4 %fusion.53 = s32[128,16]{1,0:T(8,128)S(1)} fusion(bf16[128,17,256]{2,1,0:T(8,128)(2,1)} %all-to-all-done), kind=kLoop, calls=%fused_computation.88 | loop fusion | flops 8192 | bytes 16384 | tf_op jit(solution)/shard_map/add | solution.py:380
  57.5 0.1 add.122
  57.6 1.3 %slice.405 = bf16[128,16,256]{2,1,0:T(8,128)(2,1)S(1)} slice(bf16[128,17,256]{2,1,0:T(8,128)(2,1)} %all-to-all-done), slice={[0:128], [0:16], [0:256]} | slice | bytes 2097152 | tf_op jit(solution)/shard_map/slice | solution.py:377
  58.9 0.0 copy-start.13
  58.9 5.3 %fusion = f32[2,4,512,256]{3,2,1,0:T(8,128)S(1)} fusion(bf16[2048,256,1,1]{1,0,3,2:T(8,128)(2,1)S(1)} %bitcast.234, s32[2048]{0:T(1024)S(1)} %add.122, s32[2,4,512]{2,1,0:T(4,128)S(1)} %multiply_add_fusion), kind=kOutput, calls=%fused_computation | convolution fusion | flops 4303355904 | bytes 5267456 | tf_op jit(solution)/shard_map/dot_general | solution.py:412
  64.3 5.0 %multiply_convert_fusion = (bf16[2,4,512,256]{3,2,1,0:T(8,128)(2,1)S(1)}, bf16[2,4,512,256]{3,2,1,0:T(8,128)(2,1)S(1)}) fusion(f32[2,4,512,256]{3,2,1,0:T(8,128)S(1)} %fusion, f32[256]{0:T(256)S(1)} %copy-done.13, f32[2,4,256]{2,1,0:T(4,128)S(1)} %get-tuple-element.49, pred[512]{0:T(512)(128)(4,1)S(1)} %get-tuple-element.88, ...), kind=kLoop, calls=%fused_computation.21 | loop fusion | flops 33554432 | bytes 16812032 | tf_op jit(solution)/shard_map/convert_element_type | solution.py:430
  69.3 0.0 copy-start.5
  69.3 0.2 fusion.17
  69.5 3.7 %collective-permute-start.3 = (bf16[2,1,512,512]{3,2,1,0:T(8,128)(2,1)S(1)}, bf16[2,1,512,512]{3,2,1,0:T(8,128)(2,1)S(1)}, u32[]{:S(2)}, u32[]{:S(2)}) collective-permute-start(bf16[2,1,512,512]{3,2,1,0:T(8,128)(2,1)S(1)} %get-tuple-element.22), channel_id=1, source_target_pairs={{1,0},{2,1},{3,2},{4,3},{5,4},{6,5},{7,6},{8,7},{9,8},{10,9},{11,1... | collective-permute-start | bytes 3145736 | tf_op jit(solution)/shard_map/ppermute | solution.py:291
  73.2 2.1 %collective-permute-start.2 = (bf16[2,1,512,512]{3,2,1,0:T(8,128)(2,1)S(1)}, bf16[2,1,512,512]{3,2,1,0:T(8,128)(2,1)S(1)}, u32[]{:S(2)}, u32[]{:S(2)}) collective-permute-start(bf16[2,1,512,512]{3,2,1,0:T(8,128)(2,1)S(1)} %get-tuple-element.23), channel_id=1, source_target_pairs={{0,1},{1,2},{2,3},{3,4},{4,5},{5,6},{6,7},{7,8},{8,9},{9,10},{10,1... | collective-permute-start | bytes 3145736 | tf_op jit(solution)/shard_map/ppermute | solution.py:290
  75.4 0.6 slice_bitcast_fusion.3
  76.0 2.3 %pad_maximum_fusion.src_ref = bf16[2,4,512,512]{3,2,1,0:T(8,128)(2,1)} fusion(bf16[2,4,512,256]{3,2,1,0:T(8,128)(2,1)S(1)} %get-tuple-element.21, bf16[2,4,512,256]{3,2,1,0:T(8,128)(2,1)S(1)} %get-tuple-element.20), kind=kLoop, calls=%fused_computation.11 | loop fusion | flops 8388608 | bytes 8388608 | tf_op jit(solution)/shard_map/concatenate | solution.py:434
  78.4 16.1 %collective-permute-done.3 = bf16[2,1,512,512]{3,2,1,0:T(8,128)(2,1)S(1)} collective-permute-done((bf16[2,1,512,512]{3,2,1,0:T(8,128)(2,1)S(1)}, bf16[2,1,512,512]{3,2,1,0:T(8,128)(2,1)S(1)}, u32[]{:S(2)}, u32[]{:S(2)}) %collective-permute-start.3) | collective-permute-done | bytes 1048608 | tf_op jit(solution)/shard_map/ppermute | solution.py:291
  94.5 0.3 reverse_select_fusion.after_ref
  94.8 3.5 %collective-permute-done.2.before_ref = bf16[2,1,512,512]{3,2,1,0:T(8,128)(2,1)S(1)} collective-permute-done((bf16[2,1,512,512]{3,2,1,0:T(8,128)(2,1)S(1)}, bf16[2,1,512,512]{3,2,1,0:T(8,128)(2,1)S(1)}, u32[]{:S(2)}, u32[]{:S(2)}) %collective-permute-start.2) | collective-permute-done | bytes 1048608 | tf_op jit(solution)/shard_map/ppermute | solution.py:290
  98.5 0.9 copy-done.3
  99.3 6.5 %shard_map.115 = (f32[2,4,512,128]{3,2,1,0:T(8,128)}, f32[2,2,4,128]{3,2,1,0:T(4,128)}) custom-call(bf16[2,4,512,512]{3,2,1,0:T(8,128)(2,1)} %pad_maximum_fusion.src_ref, bf16[2,1,512,512]{3,2,1,0:T(8,128)(2,1)} %copy-done.3, bf16[2,1,512,512]{3,2,1,0:T(8,128)(2,1)} %copy-done.2, bf16[9,128,256]{2,1,0:T(8,128)(2,1)} %k_ref.6, bf16[2,4,512,128]{3,2,1,0:T(8,128)(2,1)} %bitcast.231), custom_call_target="tpu_custom_call" | custom-call | tf_op jit(solution)/shard_map/pallas_call | solution.py:133
  105.8 0.7 copy.120
  106.5 0.6 maximum_bitcast_fusion.1.block_ref
  107.1 10.1 %shard_map.116 = (f32[2,4,512,128]{3,2,1,0:T(8,128)}, f32[8,64,128]{2,1,0:T(8,128)}) custom-call(f32[64,128]{1,0:T(8,128)} %maximum_bitcast_fusion.1.block_ref, bf16[2,4,512,512]{3,2,1,0:T(8,128)(2,1)} %pad_maximum_fusion.src_ref, bf16[2,1,512,512]{3,2,1,0:T(8,128)(2,1)} %copy-done.3, bf16[2,1,512,512]{3,2,1,0:T(8,128)(2,1)} %copy-done.2, ...), custom_call_target="tpu_custom_call" | custom-call | tf_op jit(solution)/shard_map/pallas_call | solution.py:231
  117.2 1.1 copy.194
  118.3 0.1 constant_dynamic-slice_fusion.3
  118.4 0.1 rev.36
  118.7 0.1 rev.37
  119.1 0.1 convolution_bitcast_fusion.5
  119.2 0.1 convolution_bitcast_fusion.4
  119.4 0.2 convolution_bitcast_fusion.7
  119.5 0.2 convolution_bitcast_fusion.6
  119.7 4.1 %add_bitcast_fusion = (f32[1,1,2,4,512,128]{5,4,3,2,1,0:T(8,128)}, bf16[1,1,2,4,512,128]{5,4,3,2,1,0:T(8,128)(2,1)}) fusion(f32[2,4,512,128]{3,2,1,0:T(8,128)S(1)} %copy-done.9, f32[2,4,128]{2,1,0:T(4,128)S(1)} %reverse_select_fusion.4, f32[2,4,128]{2,1,0:T(4,128)S(1)} %reverse_select_fusion.5, pred[512]{0:T(512)(128)(4,1)S(1)} %get-tuple-element.88, ...), kind=kLoop, calls=%fused_computation.29 | loop fusion | flops 4718592 | bytes 7357440 | tf_op jit(solution)/shard_map/broadcast_in_dim | solution.py:446
  (103 shorter events, 0.9 us)
Async XLA Ops:
  0.6 11.5 %copy-start = (bf16[1024,256]{1,0:T(8,128)(2,1)S(1)}, bf16[1024,256]{1,0:T(8,128)(2,1)}, u32[]{:S(2)}) copy-start(bf16[1024,256]{1,0:T(8,128)(2,1)} %param.11) | copy-start | bytes 1572868
  0.6 9.5 %copy-start.11 = (s32[1024,1]{0,1:T(1,128)S(1)}, s32[1024,1]{0,1:T(1,128)}, u32[]{:S(2)}) copy-start(s32[1024,1]{0,1:T(1,128)} %param.12) | copy-start | bytes 12292
  0.7 10.0 %copy-start.14 = (s32[1024]{0:T(1024)S(1)}, s32[1024]{0:T(1024)}, u32[]{:S(2)}) copy-start(s32[1024]{0:T(1024)} %param.13) | copy-start | bytes 12292
  2.5 26.2 %copy-start.1 = (bf16[2,4,512,256]{3,2,1,0:T(8,128)(2,1)}, bf16[2,4,512,256]{3,2,1,0:T(8,128)(2,1)S(1)}, u32[]{:S(2)}) copy-start(bf16[2,4,512,256]{3,2,1,0:T(8,128)(2,1)S(1)} %pad_maximum_fusion.1.src_ref) | copy-start | bytes 6291460
  3.7 27.6 %collective-permute-start.1 = (bf16[2,1,512,256]{3,2,1,0:T(8,128)(2,1)}, bf16[2,1,512,256]{3,2,1,0:T(8,128)(2,1)}, u32[]{:S(2)}, u32[]{:S(2)}) collective-permute-start(bf16[2,1,512,256]{3,2,1,0:T(8,128)(2,1)} %get-tuple-element.24), channel_id=1, source_target_pairs={{1,0},{2,1},{3,2},{4,3},{5,4},{6,5},{7,6},{8,7},{9,8},{10,9},{11,1... | collective-permute-start | bytes 1572872 | tf_op jit(solution)/shard_map/ppermute | solution.py:291
  8.2 24.5 %collective-permute-start = (bf16[2,1,512,256]{3,2,1,0:T(8,128)(2,1)}, bf16[2,1,512,256]{3,2,1,0:T(8,128)(2,1)}, u32[]{:S(2)}, u32[]{:S(2)}) collective-permute-start(bf16[2,1,512,256]{3,2,1,0:T(8,128)(2,1)} %get-tuple-element.25), channel_id=1, source_target_pairs={{0,1},{1,2},{2,3},{3,4},{4,5},{5,6},{6,7},{7,8},{8,9},{9,10},{10,1... | collective-permute-start | bytes 1572872 | tf_op jit(solution)/shard_map/ppermute | solution.py:290
  13.7 13.0 %copy-start.12 = (s32[8,2,3]{0,1,2:T(2,128)S(1)}, s32[8,2,3]{0,1,2:T(2,128)}, u32[]{:S(2)}) copy-start(s32[8,2,3]{0,1,2:T(2,128)} %param.14) | copy-start | bytes 580
  13.7 17.5 %copy-start.8 = (bf16[9,128,256]{2,1,0:T(8,128)(2,1)S(1)}, bf16[9,128,256]{2,1,0:T(8,128)(2,1)}, u32[]{:S(2)}) copy-start(bf16[9,128,256]{2,1,0:T(8,128)(2,1)} %k_ref.6) | copy-start | bytes 1769476
  15.1 41.0 %all-to-all-start = ((bf16[128,17,256]{2,1,0:T(8,128)(2,1)}), bf16[128,17,256]{2,1,0:T(8,128)(2,1)}, u32[]{:S(2)}, u32[]{:S(2)}) async-start(bf16[128,17,256]{2,1,0:T(8,128)(2,1)} %pad_maximum_fusion.2), calls=%async_computation | async-start | bytes 3145728 | tf_op jit(solution)/shard_map/all_to_all | solution.py:376
  28.8 12.8 %slice-start = ((bf16[2,4,512,256]{3,2,1,0:T(8,128)(2,1)}), bf16[2,4,512,128]{3,2,1,0:T(8,128)(2,1)S(1)}, s32[]{:S(2)}) async-start(bf16[2,4,512,256]{3,2,1,0:T(8,128)(2,1)} %copy-done.1), calls=%async_computation.1 | async-start | bytes 2097152 | tf_op jit(solution)/shard_map/slice | solution.py:297
  32.6 0.8 copy-start.4
  58.9 5.4 %copy-start.6 = (f32[2,4,512,256]{3,2,1,0:T(8,128)S(1)}, f32[2,4,512,256]{3,2,1,0:T(8,128)}, u32[]{:S(2)}) copy-start(f32[2,4,512,256]{3,2,1,0:T(8,128)} %get-tuple-element.15) | copy-start | bytes 12582916
  58.9 5.4 %copy-start.7 = (f32[2,4,512,256]{3,2,1,0:T(8,128)S(1)}, f32[2,4,512,256]{3,2,1,0:T(8,128)}, u32[]{:S(2)}) copy-start(f32[2,4,512,256]{3,2,1,0:T(8,128)} %get-tuple-element.13) | copy-start | bytes 12582916
  58.9 5.4 %copy-start.13 = (f32[256]{0:T(256)S(1)}, f32[256]{0:T(256)}, u32[]{:S(2)}) copy-start(f32[256]{0:T(256)} %param.16) | copy-start | bytes 3076
  69.3 6.0 %copy-start.5 = (bf16[9,256,128]{2,1,0:T(8,128)(2,1)S(1)}, bf16[9,256,128]{2,1,0:T(8,128)(2,1)}, u32[]{:S(2)}) copy-start(bf16[9,256,128]{2,1,0:T(8,128)(2,1)} %k_ref.7) | copy-start | bytes 1769476
  69.5 25.0 %collective-permute-start.3 = (bf16[2,1,512,512]{3,2,1,0:T(8,128)(2,1)S(1)}, bf16[2,1,512,512]{3,2,1,0:T(8,128)(2,1)S(1)}, u32[]{:S(2)}, u32[]{:S(2)}) collective-permute-start(bf16[2,1,512,512]{3,2,1,0:T(8,128)(2,1)S(1)} %get-tuple-element.22), channel_id=1, source_target_pairs={{1,0},{2,1},{3,2},{4,3},{5,4},{6,5},{7,6},{8,7},{9,8},{10,9},{11,1... | collective-permute-start | bytes 3145736 | tf_op jit(solution)/shard_map/ppermute | solution.py:291
  73.2 25.1 %collective-permute-start.2 = (bf16[2,1,512,512]{3,2,1,0:T(8,128)(2,1)S(1)}, bf16[2,1,512,512]{3,2,1,0:T(8,128)(2,1)S(1)}, u32[]{:S(2)}, u32[]{:S(2)}) collective-permute-start(bf16[2,1,512,512]{3,2,1,0:T(8,128)(2,1)S(1)} %get-tuple-element.23), channel_id=1, source_target_pairs={{0,1},{1,2},{2,3},{3,4},{4,5},{5,6},{6,7},{7,8},{8,9},{9,10},{10,1... | collective-permute-start | bytes 3145736 | tf_op jit(solution)/shard_map/ppermute | solution.py:290
  94.8 3.7 %copy-start.2 = (bf16[2,1,512,512]{3,2,1,0:T(8,128)(2,1)}, bf16[2,1,512,512]{3,2,1,0:T(8,128)(2,1)S(1)}, u32[]{:S(2)}) copy-start(bf16[2,1,512,512]{3,2,1,0:T(8,128)(2,1)S(1)} %reverse_select_fusion.after_ref) | copy-start | bytes 3145732
  98.4 1.0 copy-start.3
  107.1 12.0 %copy-start.10 = (bf16[256,128]{1,0:T(8,128)(2,1)S(1)}, bf16[256,128]{1,0:T(8,128)(2,1)}, u32[]{:S(2)}) copy-start(bf16[256,128]{1,0:T(8,128)(2,1)} %get-tuple-element.29) | copy-start | bytes 196612
  107.1 12.6 %copy-start.9 = (f32[2,4,512,128]{3,2,1,0:T(8,128)S(1)}, f32[2,4,512,128]{3,2,1,0:T(8,128)}, u32[]{:S(2)}) copy-start(f32[2,4,512,128]{3,2,1,0:T(8,128)} %get-tuple-element.19) | copy-start | bytes 6291460

commit v15 on v14

--- a/solution.py
+++ b/solution.py
@@ -306,7 +306,12 @@
         flipped = matching_row[side_number, 2]
         face_count = lax.axis_size("face")
         slot = lax.rem(lax.axis_index("face") - partner + face_count, face_count)
-        chosen = lax.dynamic_index_in_dim(gathered, slot, 0, keepdims=False)
+        landed, offset, shape = gathered
+        size = 1
+        for dim in shape:
+            size *= dim
+        row = lax.dynamic_index_in_dim(landed, slot, 0, keepdims=False).reshape(-1)
+        chosen = row[offset : offset + size].reshape(shape)
         column = jnp.where(their_side == 0, chosen[:, :, 0], chosen[:, :, 1])
         column = jnp.where(flipped == 1, column[::-1], column)
         picked_sides.append(column)
@@ -319,16 +324,11 @@
 
 
 def unpack_parts(landed, parts):
-    face_count = lax.axis_size("face")
-    face_at = lax.axis_index("face")
-    gathered = landed.reshape(face_count, -1)
     pieces = []
     offset = 0
     for part in parts:
-        size = part.size
-        piece = gathered[:, offset : offset + size].reshape((face_count,) + part.shape)
-        pieces.append(piece)
-        offset += size
+        pieces.append((landed, offset, part.shape))
+        offset += part.size
     return pieces
 
 

time: 125 us -> 129 us (1.032)
  other arithmetic: 21 us -> 25.4 us
  waiting for transfers between devices: 19.7 us -> 16.9 us
  local copies, waits for them, and re-layouts: 11.2 us -> 13.6 us
    slice x4 -> x10, local copies, waits for them, and re-layouts: 0.04 us -> 3.06 us  [the longest x4 2.97 us: pick_partner(): chosen = row[offset:offset + size].reshape(shape)]
    concatenate x2, other arithmetic: 2.51 us -> 5.36 us  [per_device(): pair = extend_rows(jnp.concatenate([inner, grad_pre], axis=3), last_tile)]
    unnamed x60 -> x50, local copies, waits for them, and re-layouts: 3.92 us -> 2.24 us
    select_n x2, other arithmetic: 1.62 us -> 3.16 us  [extend_rows(): after = jnp.where(last_tile, tail[::-1], after)]
    ppermute x2, waiting for transfers between devices: 3.51 us -> 1.98 us  [extend_rows(): before = lax.ppermute(tail, 'tile', [(i, i + 1) for i in range(count - 1)])]
  transfers between devices with their start and end apart: 5 -> 5, of which waited for: 2 -> 2; matrix products, arithmetic and copies ran while one was open for 12% -> 14% of each run, Pallas kernels for 15% -> 14%
where the time goes in v15:
time: 129 us; the launch traced here: 128 us
  Pallas kernels  34.7 us (27%)
  other arithmetic  25.4 us (20%)
  starting transfers between devices  23.9 us (19%)
  waiting for transfers between devices  16.9 us (13%)
  local copies, waits for them, and re-layouts  13.6 us (11%)
  matrix products  8.12 us (6%)
  between operations  5.33 us (4%)
    pallas_call x2, Pallas kernels, conv_gather(): pl.pallas_call(functools.partial(conv_gather_kernel, count), grid=(bands,...  21.8 us
    ppermute x2, waiting for transfers between devices, extend_rows(): after = lax.ppermute(head, 'tile', [(i + 1, i) for i in range(count - 1)])  14.9 us
    pallas_call x2, Pallas kernels, conv_back(): pl.pallas_call(back_kernel, grid=(bands,), in_specs=[pl.BlockSpec((1, row...  12.9 us
    all_to_all x1, starting transfers between devices, route_observations(): lax.all_to_all(payload, ('face', 'tile'), split_axis=0, concat_axis=0, ti...  11.6 us
    ppermute x2, starting transfers between devices, extend_rows(): after = lax.ppermute(head, 'tile', [(i + 1, i) for i in range(count - 1)])  8.23 us
    concatenate x2, other arithmetic, per_device(): pair = extend_rows(jnp.concatenate([inner, grad_pre], axis=3), last_tile)  5.36 us
    dot_general x1, matrix products, per_device(): gridded = jnp.dot(onehot, got_values, preferred_element_type=jnp.float32)  5.34 us
    convert_element_type x1, other arithmetic, per_device(): inner = activation(pre_act).astype(jnp.bfloat16)  5.09 us
  transfers between devices with their start and end apart: 5, of which 2 were waited for; matrix products, arithmetic and copies ran while one was open for 14% of the time, Pallas kernels for 14%

profile of v15, /device:TPU:24, one launch (start us, length us, event | category | flops | bytes accessed | tf_op | source)
XLA Modules:
  0.0 128.0 jit_solution(3620635503199084572)
XLA Ops:
  0.6 0.0 copy-start
  0.7 1.8 %pad_maximum_fusion.1.src_ref = bf16[2,4,512,256]{3,2,1,0:T(8,128)(2,1)S(1)} fusion(bf16[2,4,512,128]{3,2,1,0:T(8,128)(2,1)} %bitcast.180, bf16[2,4,512,128]{3,2,1,0:T(8,128)(2,1)} %bitcast.182), kind=kLoop, calls=%fused_computation.28 | loop fusion | flops 4194304 | bytes 4194304 | tf_op jit(solution)/shard_map/concatenate | solution.py:420
  2.5 0.0 copy-start.1
  2.5 1.1 fusion.142
  3.7 4.5 %collective-permute-start.1 = (bf16[2,1,512,256]{3,2,1,0:T(8,128)(2,1)}, bf16[2,1,512,256]{3,2,1,0:T(8,128)(2,1)}, u32[]{:S(2)}, u32[]{:S(2)}) collective-permute-start(bf16[2,1,512,256]{3,2,1,0:T(8,128)(2,1)} %get-tuple-element.24), channel_id=1, source_target_pairs={{1,0},{2,1},{3,2},{4,3},{5,4},{6,5},{7,6},{8,7},{9,8},{10,9},{11,1... | collective-permute-start | bytes 1572872 | tf_op jit(solution)/shard_map/ppermute | solution.py:291
  8.2 1.9 %collective-permute-start = (bf16[2,1,512,256]{3,2,1,0:T(8,128)(2,1)}, bf16[2,1,512,256]{3,2,1,0:T(8,128)(2,1)}, u32[]{:S(2)}, u32[]{:S(2)}) collective-permute-start(bf16[2,1,512,256]{3,2,1,0:T(8,128)(2,1)} %get-tuple-element.25), channel_id=1, source_target_pairs={{0,1},{1,2},{2,3},{3,4},{4,5},{5,6},{6,7},{7,8},{8,9},{9,10},{10,1... | collective-permute-start | bytes 1572872 | tf_op jit(solution)/shard_map/ppermute | solution.py:290
  10.2 0.5 convert_reduce_fusion
  10.7 0.9 select_reduce_fusion
  11.6 0.1 reduce_sum.22
  11.7 0.1 fusion.50
  11.8 0.1 pad.43.clone
  11.9 0.1 maximum_bitcast_fusion
  12.0 0.1 copy.141
  12.1 1.6 %fusion.14 = bf16[2048,256]{1,0:T(8,128)(2,1)S(1)} fusion(bf16[1024,256]{1,0:T(8,128)(2,1)S(1)} %copy-done, s32[1024]{0:T(1024)S(1)} %multiply_add_fusion.1), kind=kOutput, calls=%fused_computation.27 | convolution fusion | flops 1076363264 | bytes 1576960 | tf_op jit(solution)/shard_map/dot_general | solution.py:364
  13.7 0.0 copy-start.12
  13.8 0.0 copy-start.8
  13.8 1.3 %pad_maximum_fusion.2 = bf16[128,17,256]{2,1,0:T(8,128)(2,1)} fusion(bf16[128,1,256]{2,1,0:T(2,128)(2,1)S(1)} %copy.141, bf16[128,16,256]{2,1,0:T(8,128)(2,1)S(1)} %bitcast.185), kind=kLoop, calls=%fused_computation.31 | loop fusion | flops 2228224 | bytes 2228224 | tf_op jit(solution)/shard_map/concatenate | solution.py:373
  15.1 11.6 %all-to-all-start = ((bf16[128,17,256]{2,1,0:T(8,128)(2,1)}), bf16[128,17,256]{2,1,0:T(8,128)(2,1)}, u32[]{:S(2)}, u32[]{:S(2)}) async-start(bf16[128,17,256]{2,1,0:T(8,128)(2,1)} %pad_maximum_fusion.2), calls=%async_computation | async-start | bytes 3145728 | tf_op jit(solution)/shard_map/all_to_all | solution.py:376
  26.7 0.1 constant_dynamic-slice_fusion.8
  26.8 0.1 copy.143
  26.9 0.7 fusion.153
  31.5 1.3 %reverse_select_fusion.1.after_ref = bf16[2,1,512,256]{3,2,1,0:T(8,128)(2,1)S(1)} fusion(bf16[2,1,512,256]{3,2,1,0:T(8,128)(2,1)} %collective-permute-done.1, bf16[2,1,512,256]{3,2,1,0:T(8,128)(2,1)} %get-tuple-element.25, pred[]{:T(512)S(6)} %eq.131), kind=kLoop, calls=%fused_computation.44 | loop fusion | flops 262144 | bytes 1572865 | tf_op jit(solution)/shard_map/jit(_where)/select_n | solution.py:292
  32.9 0.7 copy-done.4
  33.7 6.4 %shard_map.113 = (f32[2,4,512,256]{3,2,1,0:T(8,128)}, f32[2,2,4,256]{3,2,1,0:T(4,128)}) custom-call(bf16[2,4,512,256]{3,2,1,0:T(8,128)(2,1)} %copy-done.1, bf16[2,1,512,256]{3,2,1,0:T(8,128)(2,1)} %collective-permute-done.before_ref, bf16[2,1,512,256]{3,2,1,0:T(8,128)(2,1)} %copy-done.4, bf16[9,256,128]{2,1,0:T(8,128)(2,1)} %k_ref.7), custom_call_target="tpu_custom_call" | custom-call | tf_op jit(solution)/shard_map/pallas_call | solution.py:133
  40.0 0.7 copy.142
  40.8 1.0 slice.406
  41.8 0.6 maximum_bitcast_fusion.2.block_ref
  42.4 11.8 %shard_map.114 = (f32[2,4,512,256]{3,2,1,0:T(8,128)}, f32[8,56,128]{2,1,0:T(8,128)}) custom-call(f32[56,128]{1,0:T(8,128)} %maximum_bitcast_fusion.2.block_ref, bf16[2,4,512,256]{3,2,1,0:T(8,128)(2,1)} %copy-done.1, bf16[2,1,512,256]{3,2,1,0:T(8,128)(2,1)} %collective-permute-done.before_ref, bf16[2,1,512,256]{3,2,1,0:T(8,128)(2,1)} %copy-done.4, ...), custom_call_target="tpu_custom_call" | custom-call | tf_op jit(solution)/shard_map/pallas_call | solution.py:231
  54.2 0.7 constant_dynamic-slice_fusion.3
  54.9 0.7 constant_dynamic-slice_fusion.7
  55.9 0.1 convolution_bitcast_fusion.1
  56.1 0.1 convolution_bitcast_fusion
  56.3 0.1 convolution_bitcast_fusion.3
  56.4 0.1 convolution_bitcast_fusion.2
  56.7 1.4 %fusion.53 = s32[128,16]{1,0:T(8,128)S(1)} fusion(bf16[128,17,256]{2,1,0:T(8,128)(2,1)} %all-to-all-done), kind=kLoop, calls=%fused_computation.86 | loop fusion | flops 8192 | bytes 16384 | tf_op jit(solution)/shard_map/add | solution.py:380
  58.1 0.1 add.120
  58.2 1.3 %slice.428 = bf16[128,16,256]{2,1,0:T(8,128)(2,1)S(1)} slice(bf16[128,17,256]{2,1,0:T(8,128)(2,1)} %all-to-all-done), slice={[0:128], [0:16], [0:256]} | slice | bytes 2097152 | tf_op jit(solution)/shard_map/slice | solution.py:377
  59.5 0.0 copy-start.13
  59.6 5.3 %fusion = f32[2,4,512,256]{3,2,1,0:T(8,128)S(1)} fusion(bf16[2048,256,1,1]{1,0,3,2:T(8,128)(2,1)S(1)} %bitcast.184, s32[2048]{0:T(1024)S(1)} %add.120, s32[2,4,512]{2,1,0:T(4,128)S(1)} %multiply_add_fusion), kind=kOutput, calls=%fused_computation | convolution fusion | flops 4303355904 | bytes 5267456 | tf_op jit(solution)/shard_map/dot_general | solution.py:412
  64.9 5.1 %multiply_convert_fusion = (bf16[2,4,512,256]{3,2,1,0:T(8,128)(2,1)S(1)}, bf16[2,4,512,256]{3,2,1,0:T(8,128)(2,1)S(1)}) fusion(f32[2,4,512,256]{3,2,1,0:T(8,128)S(1)} %fusion, f32[256]{0:T(256)S(1)} %copy-done.13, f32[2,4,256]{2,1,0:T(4,128)S(1)} %get-tuple-element.49, pred[512]{0:T(512)(128)(4,1)S(1)} %get-tuple-element.110, ...), kind=kLoop, calls=%fused_computation.21 | loop fusion | flops 33554432 | bytes 16812032 | tf_op jit(solution)/shard_map/convert_element_type | solution.py:430
  70.1 1.3 %copy-done.2 = bf16[2,4,512,256]{3,2,1,0:T(8,128)(2,1)} copy-done((bf16[2,4,512,256]{3,2,1,0:T(8,128)(2,1)}, bf16[2,4,512,256]{3,2,1,0:T(8,128)(2,1)S(1)}, u32[]{:S(2)}) %copy-start.2) | copy-done | bytes 2097176
  71.4 1.5 %fusion.17 = (bf16[2,1,512,512]{3,2,1,0:T(8,128)(2,1)}, bf16[2,1,512,512]{3,2,1,0:T(8,128)(2,1)}) fusion(bf16[2,4,512,256]{3,2,1,0:T(8,128)(2,1)S(1)} %get-tuple-element.20, bf16[2,4,512,256]{3,2,1,0:T(8,128)(2,1)S(1)} %get-tuple-element.21), kind=kLoop, calls=%fused_computation.42 | loop fusion | flops 4194304 | bytes 6291456 | tf_op jit(solution)/shard_map/concatenate | solution.py:434
  72.9 3.7 %collective-permute-start.3 = (bf16[2,1,512,512]{3,2,1,0:T(8,128)(2,1)}, bf16[2,1,512,512]{3,2,1,0:T(8,128)(2,1)}, u32[]{:S(2)}, u32[]{:S(2)}) collective-permute-start(bf16[2,1,512,512]{3,2,1,0:T(8,128)(2,1)} %get-tuple-element.22), channel_id=1, source_target_pairs={{1,0},{2,1},{3,2},{4,3},{5,4},{6,5},{7,6},{8,7},{9,8},{10,9},{11,1... | collective-permute-start | bytes 3145736 | tf_op jit(solution)/shard_map/ppermute | solution.py:291
  76.6 2.1 %collective-permute-start.2 = (bf16[2,1,512,512]{3,2,1,0:T(8,128)(2,1)}, bf16[2,1,512,512]{3,2,1,0:T(8,128)(2,1)}, u32[]{:S(2)}, u32[]{:S(2)}) collective-permute-start(bf16[2,1,512,512]{3,2,1,0:T(8,128)(2,1)} %get-tuple-element.23), channel_id=1, source_target_pairs={{0,1},{1,2},{2,3},{3,4},{4,5},{5,6},{6,7},{7,8},{8,9},{9,10},{10,1... | collective-permute-start | bytes 3145736 | tf_op jit(solution)/shard_map/ppermute | solution.py:290
  78.7 0.7 slice_bitcast_fusion.3
  79.4 3.9 %pad_maximum_fusion.src_ref = bf16[2,4,512,512]{3,2,1,0:T(8,128)(2,1)} fusion(bf16[2,4,512,256]{3,2,1,0:T(8,128)(2,1)} %copy-done.2, bf16[2,4,512,256]{3,2,1,0:T(8,128)(2,1)S(1)} %get-tuple-element.20), kind=kLoop, calls=%fused_computation.11 | loop fusion | flops 8388608 | bytes 8388608 | tf_op jit(solution)/shard_map/concatenate | solution.py:434
  83.2 14.9 %collective-permute-done.3 = bf16[2,1,512,512]{3,2,1,0:T(8,128)(2,1)} collective-permute-done((bf16[2,1,512,512]{3,2,1,0:T(8,128)(2,1)}, bf16[2,1,512,512]{3,2,1,0:T(8,128)(2,1)}, u32[]{:S(2)}, u32[]{:S(2)}) %collective-permute-start.3) | collective-permute-done | bytes 1048608 | tf_op jit(solution)/shard_map/ppermute | solution.py:291
  98.2 1.8 %reverse_select_fusion.after_ref = bf16[2,1,512,512]{3,2,1,0:T(8,128)(2,1)S(1)} fusion(bf16[2,1,512,512]{3,2,1,0:T(8,128)(2,1)} %collective-permute-done.3, bf16[2,1,512,512]{3,2,1,0:T(8,128)(2,1)} %get-tuple-element.23, pred[]{:T(512)S(6)} %eq.131), kind=kLoop, calls=%fused_computation.43 | loop fusion | flops 524288 | bytes 3145729 | tf_op jit(solution)/shard_map/jit(_where)/select_n | solution.py:292
  100.0 0.0 copy-start.3
  100.0 2.0 %collective-permute-done.2.before_ref = bf16[2,1,512,512]{3,2,1,0:T(8,128)(2,1)} collective-permute-done((bf16[2,1,512,512]{3,2,1,0:T(8,128)(2,1)}, bf16[2,1,512,512]{3,2,1,0:T(8,128)(2,1)}, u32[]{:S(2)}, u32[]{:S(2)}) %collective-permute-start.2) | collective-permute-done | bytes 1048608 | tf_op jit(solution)/shard_map/ppermute | solution.py:290
  102.0 1.1 slice.435
  103.2 6.5 %shard_map.115 = (f32[2,4,512,128]{3,2,1,0:T(8,128)}, f32[2,2,4,128]{3,2,1,0:T(4,128)}) custom-call(bf16[2,4,512,512]{3,2,1,0:T(8,128)(2,1)} %pad_maximum_fusion.src_ref, bf16[2,1,512,512]{3,2,1,0:T(8,128)(2,1)} %collective-permute-done.2.before_ref, bf16[2,1,512,512]{3,2,1,0:T(8,128)(2,1)} %copy-done.3, bf16[9,128,256]{2,1,0:T(8,128)(2,1)} %k_ref.6, ...), custom_call_target="tpu_custom_call" | custom-call | tf_op jit(solution)/shard_map/pallas_call | solution.py:133
  109.6 0.7 copy.152
  110.3 0.6 maximum_bitcast_fusion.1.block_ref
  111.0 10.1 %shard_map.116 = (f32[2,4,512,128]{3,2,1,0:T(8,128)}, f32[8,64,128]{2,1,0:T(8,128)}) custom-call(f32[64,128]{1,0:T(8,128)} %maximum_bitcast_fusion.1.block_ref, bf16[2,4,512,512]{3,2,1,0:T(8,128)(2,1)} %pad_maximum_fusion.src_ref, bf16[2,1,512,512]{3,2,1,0:T(8,128)(2,1)} %collective-permute-done.2.before_ref, bf16[2,1,512,512]{3,2,1,0:T(8,128)(2,1)} %copy-done.3, ...), custom_call_target="tpu_custom_call" | custom-call | tf_op jit(solution)/shard_map/pallas_call | solution.py:231
  121.1 0.8 constant_dynamic-slice_fusion.1
  121.9 0.1 rev.36
  122.2 0.1 rev.37
  122.4 0.7 constant_dynamic-slice_fusion.5
  123.2 0.1 convolution_bitcast_fusion.5
  123.4 0.1 convolution_bitcast_fusion.4
  123.5 0.2 convolution_bitcast_fusion.7
  123.7 0.2 convolution_bitcast_fusion.6
  123.9 4.1 %add_bitcast_fusion = (f32[1,1,2,4,512,128]{5,4,3,2,1,0:T(8,128)}, bf16[1,1,2,4,512,128]{5,4,3,2,1,0:T(8,128)(2,1)}) fusion(f32[2,4,512,128]{3,2,1,0:T(8,128)S(1)} %copy-done.9, f32[2,4,128]{2,1,0:T(4,128)S(1)} %reverse_select_fusion.4, f32[2,4,128]{2,1,0:T(4,128)S(1)} %reverse_select_fusion.5, pred[512]{0:T(512)(128)(4,1)S(1)} %get-tuple-element.110, ...), kind=kLoop, calls=%fused_computation.29 | loop fusion | flops 4718592 | bytes 7357440 | tf_op jit(solution)/shard_map/broadcast_in_dim | solution.py:446
  (94 shorter events, 0.8 us)
Async XLA Ops:
  0.6 11.5 %copy-start = (bf16[1024,256]{1,0:T(8,128)(2,1)S(1)}, bf16[1024,256]{1,0:T(8,128)(2,1)}, u32[]{:S(2)}) copy-start(bf16[1024,256]{1,0:T(8,128)(2,1)} %param.11) | copy-start | bytes 1572868
  0.6 9.5 %copy-start.11 = (s32[1024,1]{0,1:T(1,128)S(1)}, s32[1024,1]{0,1:T(1,128)}, u32[]{:S(2)}) copy-start(s32[1024,1]{0,1:T(1,128)} %param.12) | copy-start | bytes 12292
  0.7 10.0 %copy-start.14 = (s32[1024]{0:T(1024)S(1)}, s32[1024]{0:T(1024)}, u32[]{:S(2)}) copy-start(s32[1024]{0:T(1024)} %param.13) | copy-start | bytes 12292
  2.5 26.3 %copy-start.1 = (bf16[2,4,512,256]{3,2,1,0:T(8,128)(2,1)}, bf16[2,4,512,256]{3,2,1,0:T(8,128)(2,1)S(1)}, u32[]{:S(2)}) copy-start(bf16[2,4,512,256]{3,2,1,0:T(8,128)(2,1)S(1)} %pad_maximum_fusion.1.src_ref) | copy-start | bytes 6291460
  3.7 27.8 %collective-permute-start.1 = (bf16[2,1,512,256]{3,2,1,0:T(8,128)(2,1)}, bf16[2,1,512,256]{3,2,1,0:T(8,128)(2,1)}, u32[]{:S(2)}, u32[]{:S(2)}) collective-permute-start(bf16[2,1,512,256]{3,2,1,0:T(8,128)(2,1)} %get-tuple-element.24), channel_id=1, source_target_pairs={{1,0},{2,1},{3,2},{4,3},{5,4},{6,5},{7,6},{8,7},{9,8},{10,9},{11,1... | collective-permute-start | bytes 1572872 | tf_op jit(solution)/shard_map/ppermute | solution.py:291
  8.2 24.7 %collective-permute-start = (bf16[2,1,512,256]{3,2,1,0:T(8,128)(2,1)}, bf16[2,1,512,256]{3,2,1,0:T(8,128)(2,1)}, u32[]{:S(2)}, u32[]{:S(2)}) collective-permute-start(bf16[2,1,512,256]{3,2,1,0:T(8,128)(2,1)} %get-tuple-element.25), channel_id=1, source_target_pairs={{0,1},{1,2},{2,3},{3,4},{4,5},{5,6},{6,7},{7,8},{8,9},{9,10},{10,1... | collective-permute-start | bytes 1572872 | tf_op jit(solution)/shard_map/ppermute | solution.py:290
  13.7 13.0 %copy-start.12 = (s32[8,2,3]{0,1,2:T(2,128)S(1)}, s32[8,2,3]{0,1,2:T(2,128)}, u32[]{:S(2)}) copy-start(s32[8,2,3]{0,1,2:T(2,128)} %param.14) | copy-start | bytes 580
  13.8 17.7 %copy-start.8 = (bf16[9,128,256]{2,1,0:T(8,128)(2,1)S(1)}, bf16[9,128,256]{2,1,0:T(8,128)(2,1)}, u32[]{:S(2)}) copy-start(bf16[9,128,256]{2,1,0:T(8,128)(2,1)} %k_ref.6) | copy-start | bytes 1769476
  15.1 41.6 %all-to-all-start = ((bf16[128,17,256]{2,1,0:T(8,128)(2,1)}), bf16[128,17,256]{2,1,0:T(8,128)(2,1)}, u32[]{:S(2)}, u32[]{:S(2)}) async-start(bf16[128,17,256]{2,1,0:T(8,128)(2,1)} %pad_maximum_fusion.2), calls=%async_computation | async-start | bytes 3145728 | tf_op jit(solution)/shard_map/all_to_all | solution.py:376
  28.9 12.9 %slice-start = ((bf16[2,4,512,256]{3,2,1,0:T(8,128)(2,1)}), bf16[2,4,512,128]{3,2,1,0:T(8,128)(2,1)S(1)}, s32[]{:S(2)}) async-start(bf16[2,4,512,256]{3,2,1,0:T(8,128)(2,1)} %copy-done.1), calls=%async_computation.1 | async-start | bytes 2097152 | tf_op jit(solution)/shard_map/slice | solution.py:297
  32.9 0.8 copy-start.4
  59.5 5.4 %copy-start.6 = (f32[2,4,512,256]{3,2,1,0:T(8,128)S(1)}, f32[2,4,512,256]{3,2,1,0:T(8,128)}, u32[]{:S(2)}) copy-start(f32[2,4,512,256]{3,2,1,0:T(8,128)} %get-tuple-element.15) | copy-start | bytes 12582916
  59.5 5.4 %copy-start.7 = (f32[2,4,512,256]{3,2,1,0:T(8,128)S(1)}, f32[2,4,512,256]{3,2,1,0:T(8,128)}, u32[]{:S(2)}) copy-start(f32[2,4,512,256]{3,2,1,0:T(8,128)} %get-tuple-element.13) | copy-start | bytes 12582916
  59.5 5.4 %copy-start.13 = (f32[256]{0:T(256)S(1)}, f32[256]{0:T(256)}, u32[]{:S(2)}) copy-start(f32[256]{0:T(256)} %param.16) | copy-start | bytes 3076
  70.0 1.3 %copy-start.2 = (bf16[2,4,512,256]{3,2,1,0:T(8,128)(2,1)}, bf16[2,4,512,256]{3,2,1,0:T(8,128)(2,1)S(1)}, u32[]{:S(2)}) copy-start(bf16[2,4,512,256]{3,2,1,0:T(8,128)(2,1)S(1)} %get-tuple-element.21) | copy-start | bytes 6291460
  70.0 8.7 %copy-start.5 = (bf16[9,256,128]{2,1,0:T(8,128)(2,1)S(1)}, bf16[9,256,128]{2,1,0:T(8,128)(2,1)}, u32[]{:S(2)}) copy-start(bf16[9,256,128]{2,1,0:T(8,128)(2,1)} %k_ref.7) | copy-start | bytes 1769476
  72.9 25.3 %collective-permute-start.3 = (bf16[2,1,512,512]{3,2,1,0:T(8,128)(2,1)}, bf16[2,1,512,512]{3,2,1,0:T(8,128)(2,1)}, u32[]{:S(2)}, u32[]{:S(2)}) collective-permute-start(bf16[2,1,512,512]{3,2,1,0:T(8,128)(2,1)} %get-tuple-element.22), channel_id=1, source_target_pairs={{1,0},{2,1},{3,2},{4,3},{5,4},{6,5},{7,6},{8,7},{9,8},{10,9},{11,1... | collective-permute-start | bytes 3145736 | tf_op jit(solution)/shard_map/ppermute | solution.py:291
  76.6 25.5 %collective-permute-start.2 = (bf16[2,1,512,512]{3,2,1,0:T(8,128)(2,1)}, bf16[2,1,512,512]{3,2,1,0:T(8,128)(2,1)}, u32[]{:S(2)}, u32[]{:S(2)}) collective-permute-start(bf16[2,1,512,512]{3,2,1,0:T(8,128)(2,1)} %get-tuple-element.23), channel_id=1, source_target_pairs={{0,1},{1,2},{2,3},{3,4},{4,5},{5,6},{6,7},{7,8},{8,9},{9,10},{10,1... | collective-permute-start | bytes 3145736 | tf_op jit(solution)/shard_map/ppermute | solution.py:290
  100.0 3.1 %copy-start.3 = (bf16[2,1,512,512]{3,2,1,0:T(8,128)(2,1)}, bf16[2,1,512,512]{3,2,1,0:T(8,128)(2,1)S(1)}, u32[]{:S(2)}) copy-start(bf16[2,1,512,512]{3,2,1,0:T(8,128)(2,1)S(1)} %reverse_select_fusion.after_ref) | copy-start | bytes 3145732
  111.0 12.3 %copy-start.10 = (bf16[256,128]{1,0:T(8,128)(2,1)S(1)}, bf16[256,128]{1,0:T(8,128)(2,1)}, u32[]{:S(2)}) copy-start(bf16[256,128]{1,0:T(8,128)(2,1)} %get-tuple-element.29) | copy-start | bytes 196612
  111.0 12.9 %copy-start.9 = (f32[2,4,512,128]{3,2,1,0:T(8,128)S(1)}, f32[2,4,512,128]{3,2,1,0:T(8,128)}, u32[]{:S(2)}) copy-start(f32[2,4,512,128]{3,2,1,0:T(8,128)} %get-tuple-element.19) | copy-start | bytes 6291460

commit v16 on v14

--- a/solution.py
+++ b/solution.py
@@ -361,12 +361,16 @@
     slot_index = target * capacity + rank_within
     slot_ids = lax.iota(jnp.int32, device_count * capacity)
     hits = slot_ids[:, None] == slot_index[None, :]
-    value_slots = jnp.dot(
-        hits.astype(jnp.bfloat16), obs_values, preferred_element_type=jnp.float32
+    codes = jnp.stack([obs_pixel // 16, obs_pixel % 16], axis=1).astype(jnp.bfloat16)
+    widened = jnp.concatenate(
+        [obs_values, codes, jnp.zeros((obs_rows, 126), jnp.bfloat16)], axis=1
+    )
+    slots = jnp.dot(
+        hits.astype(jnp.bfloat16), widened, preferred_element_type=jnp.float32
     ).astype(jnp.bfloat16)
-    pixel_slots = jnp.sum(jnp.where(hits, obs_pixel[None, :], 0), axis=1)
-    high = (pixel_slots // 16).astype(jnp.bfloat16).reshape(device_count, capacity)
-    low = (pixel_slots % 16).astype(jnp.bfloat16).reshape(device_count, capacity)
+    value_slots = slots[:, :obs_width]
+    high = slots[:, obs_width].reshape(device_count, capacity)
+    low = slots[:, obs_width + 1].reshape(device_count, capacity)
     pixel_row = jnp.concatenate(
         [high, low, jnp.zeros((device_count, obs_width - 2 * capacity), jnp.bfloat16)], axis=1
     )

time: 125 us -> 128 us (1.024)
  local copies, waits for them, and re-layouts: 11.2 us -> 12.7 us
    slice x0 -> x3, local copies, waits for them, and re-layouts: none -> 1.43 us  [the longest x2 1.38 us: route_observations(): value_slots = slots[:, :obs_width]]
    concatenate x1, other arithmetic: 1.34 us -> 2.63 us  [route_observations(): jnp.concatenate([value_slots.reshape(device_count, capacity, obs_width),...]
    unnamed x60 -> x58, local copies, waits for them, and re-layouts: 3.92 us -> 3.91 us
  transfers between devices with their start and end apart: 5 -> 5, of which waited for: 2 -> 2; matrix products, arithmetic and copies ran while one was open for 12% -> 13% of each run, Pallas kernels for 15% -> 14%
where the time goes in v16:
time: 128 us; the launch traced here: 127 us
  Pallas kernels  34.6 us (27%)
  starting transfers between devices  24 us (19%)
  other arithmetic  21.2 us (17%)
  waiting for transfers between devices  20.3 us (16%)
  local copies, waits for them, and re-layouts  12.7 us (10%)
  matrix products  8.65 us (7%)
  between operations  5.41 us (4%)
    pallas_call x2, Pallas kernels, conv_gather(): pl.pallas_call(functools.partial(conv_gather_kernel, count), grid=(bands,...  21.8 us
    ppermute x2, waiting for transfers between devices, extend_rows(): after = lax.ppermute(head, 'tile', [(i + 1, i) for i in range(count - 1)])  16.8 us
    pallas_call x2, Pallas kernels, conv_back(): pl.pallas_call(back_kernel, grid=(bands,), in_specs=[pl.BlockSpec((1, row...  12.8 us
    all_to_all x1, starting transfers between devices, route_observations(): lax.all_to_all(payload, ('face', 'tile'), split_axis=0, concat_axis=0, ti...  11.6 us
    ppermute x2, starting transfers between devices, extend_rows(): after = lax.ppermute(head, 'tile', [(i + 1, i) for i in range(count - 1)])  8.36 us
    dot_general x1, matrix products, per_device(): gridded = jnp.dot(onehot, got_values, preferred_element_type=jnp.float32)  5.35 us
    convert_element_type x1, other arithmetic, per_device(): inner = activation(pre_act).astype(jnp.bfloat16)  5.02 us
    broadcast_in_dim x1, other arithmetic, per_device(): return (analysis[None, None], grad_base[None, None])  4.14 us
  transfers between devices with their start and end apart: 5, of which 2 were waited for; matrix products, arithmetic and copies ran while one was open for 13% of the time, Pallas kernels for 14%

profile of v16, /device:TPU:24, one launch (start us, length us, event | category | flops | bytes accessed | tf_op | source)
XLA Modules:
  0.0 126.9 jit_solution(18015196500948769728)
XLA Ops:
  0.6 0.0 copy-start
  0.7 1.9 %pad_maximum_fusion.1.src_ref = bf16[2,4,512,256]{3,2,1,0:T(8,128)(2,1)S(1)} fusion(bf16[2,4,512,128]{3,2,1,0:T(8,128)(2,1)} %bitcast.229, bf16[2,4,512,128]{3,2,1,0:T(8,128)(2,1)} %bitcast.231), kind=kLoop, calls=%fused_computation.27 | loop fusion | flops 4194304 | bytes 4194304 | tf_op jit(solution)/shard_map/concatenate | solution.py:424
  2.5 0.0 copy-start.1
  2.5 1.1 fusion.152
  3.7 4.5 %collective-permute-start.1 = (bf16[2,1,512,256]{3,2,1,0:T(8,128)(2,1)}, bf16[2,1,512,256]{3,2,1,0:T(8,128)(2,1)}, u32[]{:S(2)}, u32[]{:S(2)}) collective-permute-start(bf16[2,1,512,256]{3,2,1,0:T(8,128)(2,1)} %get-tuple-element.26), channel_id=1, source_target_pairs={{1,0},{2,1},{3,2},{4,3},{5,4},{6,5},{7,6},{8,7},{9,8},{10,9},{11,1... | collective-permute-start | bytes 1572872 | tf_op jit(solution)/shard_map/ppermute | solution.py:291
  8.2 1.9 %collective-permute-start = (bf16[2,1,512,256]{3,2,1,0:T(8,128)(2,1)}, bf16[2,1,512,256]{3,2,1,0:T(8,128)(2,1)}, u32[]{:S(2)}, u32[]{:S(2)}) collective-permute-start(bf16[2,1,512,256]{3,2,1,0:T(8,128)(2,1)} %get-tuple-element.27), channel_id=1, source_target_pairs={{0,1},{1,2},{2,3},{3,4},{4,5},{5,6},{6,7},{7,8},{8,9},{9,10},{10,1... | collective-permute-start | bytes 1572872 | tf_op jit(solution)/shard_map/ppermute | solution.py:290
  10.2 0.5 convert_reduce_fusion
  10.7 0.2 stack.116
  10.9 0.2 stack.117
  11.2 0.1 pad.47.clone
  11.2 2.1 %fusion.14 = bf16[2048,384]{0,1:T(8,128)(2,1)S(1)} fusion(s32[1024]{0:T(1024)S(1)} %multiply_add_fusion.1, bf16[1024,1]{1,0:T(8,128)(2,1)S(1)} %stack.117, bf16[1024,1]{1,0:T(8,128)(2,1)S(1)} %stack.116, bf16[1024,256]{1,0:T(8,128)(2,1)S(1)} %copy-done.13, bf16[384]{0:T(512)(128)(2,1)S(1)} %pad.47.clone), kind=kOutput, calls=%fused_computation.26 | convolution fusion | flops 1616642048 | bytes 2106112 | tf_op jit(solution)/shard_map/dot_general | solution.py:368
  13.4 0.1 slice_reduce_fusion.1
  13.4 0.1 slice.415
  13.5 0.1 reshape_squeeze.6
  13.6 0.1 reshape_squeeze.7
  13.7 0.1 pad.43.clone
  13.8 0.1 maximum_bitcast_fusion
  13.9 0.1 copy.115
  14.0 1.3 %copy.114 = bf16[2048,256]{1,0:T(8,128)(2,1)} copy(bf16[2048,256]{0,1:T(8,128)(2,1)S(1)} %slice.415) | data formatting | bytes 2097152 | tf_op jit(solution)/shard_map/slice | solution.py:371
  15.3 2.6 %pad_maximum_fusion.2 = bf16[128,17,256]{2,1,0:T(8,128)(2,1)} fusion(bf16[128,1,256]{2,1,0:T(2,128)(2,1)S(1)} %copy.115, bf16[128,16,256]{2,1,0:T(8,128)(2,1)} %bitcast.233), kind=kLoop, calls=%fused_computation.30 | loop fusion | flops 2228224 | bytes 2228224 | tf_op jit(solution)/shard_map/concatenate | solution.py:377
  17.9 11.6 %all-to-all-start = ((bf16[128,17,256]{2,1,0:T(8,128)(2,1)}), bf16[128,17,256]{2,1,0:T(8,128)(2,1)}, u32[]{:S(2)}, u32[]{:S(2)}) async-start(bf16[128,17,256]{2,1,0:T(8,128)(2,1)} %pad_maximum_fusion.2), calls=%async_computation | async-start | bytes 3145728 | tf_op jit(solution)/shard_map/all_to_all | solution.py:380
  29.6 0.1 constant_dynamic-slice_fusion.8
  29.6 0.1 copy.117
  29.8 0.7 fusion.157
  31.7 0.0 slice-start
  34.3 1.3 %reverse_select_fusion.1.after_ref = bf16[2,1,512,256]{3,2,1,0:T(8,128)(2,1)S(1)} fusion(bf16[2,1,512,256]{3,2,1,0:T(8,128)(2,1)} %collective-permute-done.1, bf16[2,1,512,256]{3,2,1,0:T(8,128)(2,1)} %get-tuple-element.27, pred[]{:T(512)S(6)} %eq.131), kind=kLoop, calls=%fused_computation.49 | loop fusion | flops 262144 | bytes 1572865 | tf_op jit(solution)/shard_map/jit(_where)/select_n | solution.py:292
  35.7 0.0 copy-start.4
  35.7 0.7 copy-done.4
  36.5 6.4 %shard_map.113 = (f32[2,4,512,256]{3,2,1,0:T(8,128)}, f32[2,2,4,256]{3,2,1,0:T(4,128)}) custom-call(bf16[2,4,512,256]{3,2,1,0:T(8,128)(2,1)} %copy-done.1, bf16[2,1,512,256]{3,2,1,0:T(8,128)(2,1)} %collective-permute-done.before_ref, bf16[2,1,512,256]{3,2,1,0:T(8,128)(2,1)} %copy-done.4, bf16[9,256,128]{2,1,0:T(8,128)(2,1)} %k_ref.7), custom_call_target="tpu_custom_call" | custom-call | tf_op jit(solution)/shard_map/pallas_call | solution.py:133
  42.8 0.7 copy.116
  43.6 1.0 slice.394
  44.6 0.6 maximum_bitcast_fusion.2.block_ref
  45.2 11.8 %shard_map.114 = (f32[2,4,512,256]{3,2,1,0:T(8,128)}, f32[8,56,128]{2,1,0:T(8,128)}) custom-call(f32[56,128]{1,0:T(8,128)} %maximum_bitcast_fusion.2.block_ref, bf16[2,4,512,256]{3,2,1,0:T(8,128)(2,1)} %copy-done.1, bf16[2,1,512,256]{3,2,1,0:T(8,128)(2,1)} %collective-permute-done.before_ref, bf16[2,1,512,256]{3,2,1,0:T(8,128)(2,1)} %copy-done.4, ...), custom_call_target="tpu_custom_call" | custom-call | tf_op jit(solution)/shard_map/pallas_call | solution.py:231
  57.0 1.0 copy.197
  58.4 0.1 convolution_bitcast_fusion.1
  58.5 0.1 convolution_bitcast_fusion
  58.7 0.2 convolution_bitcast_fusion.3
  58.8 0.2 convolution_bitcast_fusion.2
  59.1 1.4 %fusion.58 = s32[128,16]{1,0:T(8,128)S(1)} fusion(bf16[128,17,256]{2,1,0:T(8,128)(2,1)} %all-to-all-done), kind=kLoop, calls=%fused_computation.87 | loop fusion | flops 8192 | bytes 16384 | tf_op jit(solution)/shard_map/add | solution.py:384
  60.5 0.1 add.120
  60.6 1.3 %slice.420 = bf16[128,16,256]{2,1,0:T(8,128)(2,1)S(1)} slice(bf16[128,17,256]{2,1,0:T(8,128)(2,1)} %all-to-all-done), slice={[0:128], [0:16], [0:256]} | slice | bytes 2097152 | tf_op jit(solution)/shard_map/slice | solution.py:381
  61.9 5.3 %fusion = f32[2,4,512,256]{3,2,1,0:T(8,128)S(1)} fusion(bf16[2048,256,1,1]{1,0,3,2:T(8,128)(2,1)S(1)} %bitcast.234, s32[2048]{0:T(1024)S(1)} %add.120, s32[2,4,512]{2,1,0:T(4,128)S(1)} %multiply_add_fusion), kind=kOutput, calls=%fused_computation | convolution fusion | flops 4303355904 | bytes 5267456 | tf_op jit(solution)/shard_map/dot_general | solution.py:416
  67.3 5.0 %multiply_convert_fusion = (bf16[2,4,512,256]{3,2,1,0:T(8,128)(2,1)S(1)}, bf16[2,4,512,256]{3,2,1,0:T(8,128)(2,1)S(1)}) fusion(f32[2,4,512,256]{3,2,1,0:T(8,128)S(1)} %fusion, f32[256]{0:T(256)S(1)} %copy-done.12, f32[2,4,256]{2,1,0:T(4,128)S(1)} %get-tuple-element.49, pred[512]{0:T(512)(128)(4,1)S(1)} %get-tuple-element.90, ...), kind=kLoop, calls=%fused_computation.20 | loop fusion | flops 33554432 | bytes 16812032 | tf_op jit(solution)/shard_map/convert_element_type | solution.py:434
  72.4 0.1 fusion.17
  72.5 3.8 %collective-permute-start.3 = (bf16[2,1,512,512]{3,2,1,0:T(8,128)(2,1)S(1)}, bf16[2,1,512,512]{3,2,1,0:T(8,128)(2,1)S(1)}, u32[]{:S(2)}, u32[]{:S(2)}) collective-permute-start(bf16[2,1,512,512]{3,2,1,0:T(8,128)(2,1)S(1)} %get-tuple-element.24), channel_id=1, source_target_pairs={{1,0},{2,1},{3,2},{4,3},{5,4},{6,5},{7,6},{8,7},{9,8},{10,9},{11,1... | collective-permute-start | bytes 3145736 | tf_op jit(solution)/shard_map/ppermute | solution.py:291
  76.3 2.1 %collective-permute-start.2 = (bf16[2,1,512,512]{3,2,1,0:T(8,128)(2,1)S(1)}, bf16[2,1,512,512]{3,2,1,0:T(8,128)(2,1)S(1)}, u32[]{:S(2)}, u32[]{:S(2)}) collective-permute-start(bf16[2,1,512,512]{3,2,1,0:T(8,128)(2,1)S(1)} %get-tuple-element.25), channel_id=1, source_target_pairs={{0,1},{1,2},{2,3},{3,4},{4,5},{5,6},{6,7},{7,8},{8,9},{9,10},{10,1... | collective-permute-start | bytes 3145736 | tf_op jit(solution)/shard_map/ppermute | solution.py:290
  78.5 2.3 %pad_maximum_fusion.src_ref = bf16[2,4,512,512]{3,2,1,0:T(8,128)(2,1)} fusion(bf16[2,4,512,256]{3,2,1,0:T(8,128)(2,1)S(1)} %get-tuple-element.23, bf16[2,4,512,256]{3,2,1,0:T(8,128)(2,1)S(1)} %get-tuple-element.22), kind=kLoop, calls=%fused_computation.10 | loop fusion | flops 8388608 | bytes 8388608 | tf_op jit(solution)/shard_map/concatenate | solution.py:438
  80.9 16.8 %collective-permute-done.3 = bf16[2,1,512,512]{3,2,1,0:T(8,128)(2,1)S(1)} collective-permute-done((bf16[2,1,512,512]{3,2,1,0:T(8,128)(2,1)S(1)}, bf16[2,1,512,512]{3,2,1,0:T(8,128)(2,1)S(1)}, u32[]{:S(2)}, u32[]{:S(2)}) %collective-permute-start.3) | collective-permute-done | bytes 1048608 | tf_op jit(solution)/shard_map/ppermute | solution.py:291
  97.6 0.3 reverse_select_fusion.after_ref
  98.0 3.5 %collective-permute-done.2.before_ref = bf16[2,1,512,512]{3,2,1,0:T(8,128)(2,1)S(1)} collective-permute-done((bf16[2,1,512,512]{3,2,1,0:T(8,128)(2,1)S(1)}, bf16[2,1,512,512]{3,2,1,0:T(8,128)(2,1)S(1)}, u32[]{:S(2)}, u32[]{:S(2)}) %collective-permute-start.2) | collective-permute-done | bytes 1048608 | tf_op jit(solution)/shard_map/ppermute | solution.py:290
  101.6 0.9 copy-done.3
  102.5 6.5 %shard_map.115 = (f32[2,4,512,128]{3,2,1,0:T(8,128)}, f32[2,2,4,128]{3,2,1,0:T(4,128)}) custom-call(bf16[2,4,512,512]{3,2,1,0:T(8,128)(2,1)} %pad_maximum_fusion.src_ref, bf16[2,1,512,512]{3,2,1,0:T(8,128)(2,1)} %copy-done.3, bf16[2,1,512,512]{3,2,1,0:T(8,128)(2,1)} %copy-done.2, bf16[9,128,256]{2,1,0:T(8,128)(2,1)} %k_ref.6, bf16[2,4,512,128]{3,2,1,0:T(8,128)(2,1)} %bitcast.230), custom_call_target="tpu_custom_call" | custom-call | tf_op jit(solution)/shard_map/pallas_call | solution.py:133
  108.9 0.7 copy.122
  109.6 0.6 maximum_bitcast_fusion.1.block_ref
  110.2 10.0 %shard_map.116 = (f32[2,4,512,128]{3,2,1,0:T(8,128)}, f32[8,64,128]{2,1,0:T(8,128)}) custom-call(f32[64,128]{1,0:T(8,128)} %maximum_bitcast_fusion.1.block_ref, bf16[2,4,512,512]{3,2,1,0:T(8,128)(2,1)} %pad_maximum_fusion.src_ref, bf16[2,1,512,512]{3,2,1,0:T(8,128)(2,1)} %copy-done.3, bf16[2,1,512,512]{3,2,1,0:T(8,128)(2,1)} %copy-done.2, ...), custom_call_target="tpu_custom_call" | custom-call | tf_op jit(solution)/shard_map/pallas_call | solution.py:231
  120.3 1.1 copy.196
  121.4 0.1 constant_dynamic-slice_fusion.3
  121.5 0.1 rev.36
  121.8 0.1 rev.37
  122.1 0.1 convolution_bitcast_fusion.5
  122.3 0.1 convolution_bitcast_fusion.4
  122.4 0.2 convolution_bitcast_fusion.7
  122.6 0.2 convolution_bitcast_fusion.6
  122.8 4.1 %add_bitcast_fusion = (f32[1,1,2,4,512,128]{5,4,3,2,1,0:T(8,128)}, bf16[1,1,2,4,512,128]{5,4,3,2,1,0:T(8,128)(2,1)}) fusion(f32[2,4,512,128]{3,2,1,0:T(8,128)S(1)} %copy-done.9, f32[2,4,128]{2,1,0:T(4,128)S(1)} %reverse_select_fusion.4, f32[2,4,128]{2,1,0:T(4,128)S(1)} %reverse_select_fusion.5, pred[512]{0:T(512)(128)(4,1)S(1)} %get-tuple-element.90, ...), kind=kLoop, calls=%fused_computation.28 | loop fusion | flops 4718592 | bytes 7357440 | tf_op jit(solution)/shard_map/broadcast_in_dim | solution.py:450
  (108 shorter events, 0.9 us)
Async XLA Ops:
  0.6 28.9 %copy-start = (s32[8,2,3]{0,1,2:T(2,128)S(1)}, s32[8,2,3]{0,1,2:T(2,128)}, u32[]{:S(2)}) copy-start(s32[8,2,3]{0,1,2:T(2,128)} %param.14) | copy-start | bytes 580
  0.6 9.5 %copy-start.10 = (s32[1024,1]{0,1:T(1,128)S(1)}, s32[1024,1]{0,1:T(1,128)}, u32[]{:S(2)}) copy-start(s32[1024,1]{0,1:T(1,128)} %param.12) | copy-start | bytes 12292
  0.7 10.1 %copy-start.11 = (s32[1024]{0:T(1024)S(1)}, s32[1024]{0:T(1024)}, u32[]{:S(2)}) copy-start(s32[1024]{0:T(1024)} %param.13) | copy-start | bytes 12292
  0.7 10.6 %copy-start.13 = (bf16[1024,256]{1,0:T(8,128)(2,1)S(1)}, bf16[1024,256]{1,0:T(8,128)(2,1)}, u32[]{:S(2)}) copy-start(bf16[1024,256]{1,0:T(8,128)(2,1)} %param.11) | copy-start | bytes 1572868
  2.5 29.1 %copy-start.1 = (bf16[2,4,512,256]{3,2,1,0:T(8,128)(2,1)}, bf16[2,4,512,256]{3,2,1,0:T(8,128)(2,1)S(1)}, u32[]{:S(2)}) copy-start(bf16[2,4,512,256]{3,2,1,0:T(8,128)(2,1)S(1)} %pad_maximum_fusion.1.src_ref) | copy-start | bytes 6291460
  3.7 30.6 %collective-permute-start.1 = (bf16[2,1,512,256]{3,2,1,0:T(8,128)(2,1)}, bf16[2,1,512,256]{3,2,1,0:T(8,128)(2,1)}, u32[]{:S(2)}, u32[]{:S(2)}) collective-permute-start(bf16[2,1,512,256]{3,2,1,0:T(8,128)(2,1)} %get-tuple-element.26), channel_id=1, source_target_pairs={{1,0},{2,1},{3,2},{4,3},{5,4},{6,5},{7,6},{8,7},{9,8},{10,9},{11,1... | collective-permute-start | bytes 1572872 | tf_op jit(solution)/shard_map/ppermute | solution.py:291
  8.2 27.5 %collective-permute-start = (bf16[2,1,512,256]{3,2,1,0:T(8,128)(2,1)}, bf16[2,1,512,256]{3,2,1,0:T(8,128)(2,1)}, u32[]{:S(2)}, u32[]{:S(2)}) collective-permute-start(bf16[2,1,512,256]{3,2,1,0:T(8,128)(2,1)} %get-tuple-element.27), channel_id=1, source_target_pairs={{0,1},{1,2},{2,3},{3,4},{4,5},{5,6},{6,7},{7,8},{8,9},{9,10},{10,1... | collective-permute-start | bytes 1572872 | tf_op jit(solution)/shard_map/ppermute | solution.py:290
  15.3 19.0 %copy-start.8 = (bf16[9,128,256]{2,1,0:T(8,128)(2,1)S(1)}, bf16[9,128,256]{2,1,0:T(8,128)(2,1)}, u32[]{:S(2)}) copy-start(bf16[9,128,256]{2,1,0:T(8,128)(2,1)} %k_ref.6) | copy-start | bytes 1769476
  17.9 41.2 %all-to-all-start = ((bf16[128,17,256]{2,1,0:T(8,128)(2,1)}), bf16[128,17,256]{2,1,0:T(8,128)(2,1)}, u32[]{:S(2)}, u32[]{:S(2)}) async-start(bf16[128,17,256]{2,1,0:T(8,128)(2,1)} %pad_maximum_fusion.2), calls=%async_computation | async-start | bytes 3145728 | tf_op jit(solution)/shard_map/all_to_all | solution.py:380
  31.7 12.9 %slice-start = ((bf16[2,4,512,256]{3,2,1,0:T(8,128)(2,1)}), bf16[2,4,512,128]{3,2,1,0:T(8,128)(2,1)S(1)}, s32[]{:S(2)}) async-start(bf16[2,4,512,256]{3,2,1,0:T(8,128)(2,1)} %copy-done.1), calls=%async_computation.1 | async-start | bytes 2097152 | tf_op jit(solution)/shard_map/slice | solution.py:297
  35.7 0.8 copy-start.4
  61.9 5.4 %copy-start.6 = (f32[2,4,512,256]{3,2,1,0:T(8,128)S(1)}, f32[2,4,512,256]{3,2,1,0:T(8,128)}, u32[]{:S(2)}) copy-start(f32[2,4,512,256]{3,2,1,0:T(8,128)} %get-tuple-element.15) | copy-start | bytes 12582916
  61.9 5.4 %copy-start.7 = (f32[2,4,512,256]{3,2,1,0:T(8,128)S(1)}, f32[2,4,512,256]{3,2,1,0:T(8,128)}, u32[]{:S(2)}) copy-start(f32[2,4,512,256]{3,2,1,0:T(8,128)} %get-tuple-element.13) | copy-start | bytes 12582916
  61.9 5.4 %copy-start.12 = (f32[256]{0:T(256)S(1)}, f32[256]{0:T(256)}, u32[]{:S(2)}) copy-start(f32[256]{0:T(256)} %param.16) | copy-start | bytes 3076
  72.3 6.1 %copy-start.5 = (bf16[9,256,128]{2,1,0:T(8,128)(2,1)S(1)}, bf16[9,256,128]{2,1,0:T(8,128)(2,1)}, u32[]{:S(2)}) copy-start(bf16[9,256,128]{2,1,0:T(8,128)(2,1)} %k_ref.7) | copy-start | bytes 1769476
  72.5 25.1 %collective-permute-start.3 = (bf16[2,1,512,512]{3,2,1,0:T(8,128)(2,1)S(1)}, bf16[2,1,512,512]{3,2,1,0:T(8,128)(2,1)S(1)}, u32[]{:S(2)}, u32[]{:S(2)}) collective-permute-start(bf16[2,1,512,512]{3,2,1,0:T(8,128)(2,1)S(1)} %get-tuple-element.24), channel_id=1, source_target_pairs={{1,0},{2,1},{3,2},{4,3},{5,4},{6,5},{7,6},{8,7},{9,8},{10,9},{11,1... | collective-permute-start | bytes 3145736 | tf_op jit(solution)/shard_map/ppermute | solution.py:291
  76.3 25.1 %collective-permute-start.2 = (bf16[2,1,512,512]{3,2,1,0:T(8,128)(2,1)S(1)}, bf16[2,1,512,512]{3,2,1,0:T(8,128)(2,1)S(1)}, u32[]{:S(2)}, u32[]{:S(2)}) collective-permute-start(bf16[2,1,512,512]{3,2,1,0:T(8,128)(2,1)S(1)} %get-tuple-element.25), channel_id=1, source_target_pairs={{0,1},{1,2},{2,3},{3,4},{4,5},{5,6},{6,7},{7,8},{8,9},{9,10},{10,1... | collective-permute-start | bytes 3145736 | tf_op jit(solution)/shard_map/ppermute | solution.py:290
  97.9 3.7 %copy-start.2 = (bf16[2,1,512,512]{3,2,1,0:T(8,128)(2,1)}, bf16[2,1,512,512]{3,2,1,0:T(8,128)(2,1)S(1)}, u32[]{:S(2)}) copy-start(bf16[2,1,512,512]{3,2,1,0:T(8,128)(2,1)S(1)} %reverse_select_fusion.after_ref) | copy-start | bytes 3145732
  101.5 1.0 copy-start.3
  110.2 12.5 %copy-start.9 = (f32[2,4,512,128]{3,2,1,0:T(8,128)S(1)}, f32[2,4,512,128]{3,2,1,0:T(8,128)}, u32[]{:S(2)}) copy-start(f32[2,4,512,128]{3,2,1,0:T(8,128)} %get-tuple-element.19) | copy-start | bytes 6291460

commit v17 on v14

--- a/solution.py
+++ b/solution.py
@@ -416,10 +416,7 @@
     matching_row = lax.dynamic_index_in_dim(matching, face_at, 0, keepdims=False)
 
     lifted = kernel_one.shape[2]
-    fields, got_values = lax.optimization_barrier(
-        (jnp.concatenate([base_field, cot_field], axis=3), got_values)
-    )
-    both = extend_rows(fields, last_tile)
+    both = extend_rows(jnp.concatenate([base_field, cot_field], axis=3), last_tile)
     cot_back, cot_margins = conv_back(both, channels, channels, kernel_two)
     parts = [edge_cols(both, 0, channels), jnp.swapaxes(cot_margins, 1, 2)]
     first_out, landed = conv_gather(both, 0, channels, pack_parts(parts), kernel_one, 0)

time: 125 us -> 128 us (1.024)
  other arithmetic: 21 us -> 25.1 us
  local copies, waits for them, and re-layouts: 11.2 us -> 9.47 us
    concatenate x1 -> x2, other arithmetic: 1.84 us -> 3.88 us  [per_device(): jnp.concatenate([base_field, cot_field], axis=3)]
    unnamed x60 -> x56, local copies, waits for them, and re-layouts: 3.92 us -> 3.91 us
  transfers between devices with their start and end apart: 5 -> 5, of which waited for: 2 -> 2; matrix products, arithmetic and copies ran while one was open for 12% -> 14% of each run, Pallas kernels for 15% -> 14%
where the time goes in v17:
time: 128 us; the launch traced here: 127 us
  Pallas kernels  34.6 us (27%)
  other arithmetic  25.1 us (20%)
  starting transfers between devices  23.9 us (19%)
  waiting for transfers between devices  20.3 us (16%)
  local copies, waits for them, and re-layouts  9.47 us (7%)
  matrix products  8.13 us (6%)
  between operations  5.29 us (4%)
    pallas_call x2, Pallas kernels, conv_gather(): pl.pallas_call(functools.partial(conv_gather_kernel, count), grid=(bands,...  21.7 us
    ppermute x2, waiting for transfers between devices, extend_rows(): after = lax.ppermute(head, 'tile', [(i + 1, i) for i in range(count - 1)])  16.8 us
    pallas_call x2, Pallas kernels, conv_back(): pl.pallas_call(back_kernel, grid=(bands,), in_specs=[pl.BlockSpec((1, row...  12.8 us
    all_to_all x1, starting transfers between devices, route_observations(): lax.all_to_all(payload, ('face', 'tile'), split_axis=0, concat_axis=0, ti...  11.6 us
    ppermute x2, starting transfers between devices, extend_rows(): after = lax.ppermute(head, 'tile', [(i + 1, i) for i in range(count - 1)])  8.24 us
    dot_general x1, matrix products, per_device(): gridded = jnp.dot(onehot, got_values, preferred_element_type=jnp.float32)  5.33 us
    convert_element_type x1, other arithmetic, per_device(): inner = activation(pre_act).astype(jnp.bfloat16)  5.04 us
    broadcast_in_dim x1, other arithmetic, per_device(): return (analysis[None, None], grad_base[None, None])  4.11 us
  transfers between devices with their start and end apart: 5, of which 2 were waited for; matrix products, arithmetic and copies ran while one was open for 14% of the time, Pallas kernels for 14%

profile of v17, /device:TPU:24, one launch (start us, length us, event | category | flops | bytes accessed | tf_op | source)
XLA Modules:
  0.0 126.8 jit_solution(3508890983462563047)
XLA Ops:
  0.6 0.0 copy-start
  0.6 2.3 %fusion.19 = (bf16[2,1,512,256]{3,2,1,0:T(8,128)(2,1)}, bf16[2,1,512,256]{3,2,1,0:T(8,128)(2,1)}) fusion(bf16[2,4,512,128]{3,2,1,0:T(8,128)(2,1)} %bitcast.230, bf16[2,4,512,128]{3,2,1,0:T(8,128)(2,1)} %bitcast.234), kind=kLoop, calls=%fused_computation.49 | loop fusion | flops 2097152 | bytes 3145728 | tf_op jit(solution)/shard_map/concatenate | solution.py:419
  3.0 4.5 %collective-permute-start.1 = (bf16[2,1,512,256]{3,2,1,0:T(8,128)(2,1)}, bf16[2,1,512,256]{3,2,1,0:T(8,128)(2,1)}, u32[]{:S(2)}, u32[]{:S(2)}) collective-permute-start(bf16[2,1,512,256]{3,2,1,0:T(8,128)(2,1)} %get-tuple-element.22), channel_id=1, source_target_pairs={{1,0},{2,1},{3,2},{4,3},{5,4},{6,5},{7,6},{8,7},{9,8},{10,9},{11,1... | collective-permute-start | bytes 1572872 | tf_op jit(solution)/shard_map/ppermute | solution.py:291
  7.5 1.9 %collective-permute-start = (bf16[2,1,512,256]{3,2,1,0:T(8,128)(2,1)}, bf16[2,1,512,256]{3,2,1,0:T(8,128)(2,1)}, u32[]{:S(2)}, u32[]{:S(2)}) collective-permute-start(bf16[2,1,512,256]{3,2,1,0:T(8,128)(2,1)} %get-tuple-element.23), channel_id=1, source_target_pairs={{0,1},{1,2},{2,3},{3,4},{4,5},{5,6},{6,7},{7,8},{8,9},{9,10},{10,1... | collective-permute-start | bytes 1572872 | tf_op jit(solution)/shard_map/ppermute | solution.py:290
  9.4 1.3 %convert_reduce_fusion = s32[1024]{0:T(1024)S(1)} fusion(s32[1024]{0:T(1024)} %bitcast.264), kind=kLoop, calls=%fused_computation.23 | loop fusion | flops 5241856 | bytes 8192 | tf_op jit(solution)/shard_map/reduce_sum | solution.py:360
  10.7 0.7 multiply_add_fusion.1
  11.4 1.6 %select_reduce_fusion = s32[2048]{0:T(1024)S(1)} fusion(s32[1024]{0:T(1024)} %param.13, s32[1024]{0:T(1024)S(1)} %multiply_add_fusion.1), kind=kLoop, calls=%fused_computation.4 | loop fusion | flops 6289408 | bytes 16384 | tf_op jit(solution)/shard_map/reduce_sum | solution.py:367
  13.0 0.1 reduce_sum.22
  13.1 0.1 fusion.52
  13.2 0.1 pad.43.clone
  13.3 0.1 maximum_bitcast_fusion
  13.4 0.1 copy.117
  13.5 1.6 %fusion.14 = bf16[2048,256]{1,0:T(8,128)(2,1)S(1)} fusion(bf16[1024,256]{1,0:T(8,128)(2,1)S(1)} %copy-done, s32[1024]{0:T(1024)S(1)} %multiply_add_fusion.1), kind=kOutput, calls=%fused_computation.32 | convolution fusion | flops 1076363264 | bytes 1576960 | tf_op jit(solution)/shard_map/dot_general | solution.py:364
  15.1 0.0 copy-start.11
  15.1 0.0 copy-start.1
  15.2 0.0 copy-start.3
  15.2 1.4 %pad_maximum_fusion.2 = bf16[128,17,256]{2,1,0:T(8,128)(2,1)} fusion(bf16[128,1,256]{2,1,0:T(2,128)(2,1)S(1)} %copy.117, bf16[128,16,256]{2,1,0:T(8,128)(2,1)S(1)} %bitcast.238), kind=kLoop, calls=%fused_computation.35 | loop fusion | flops 2228224 | bytes 2228224 | tf_op jit(solution)/shard_map/concatenate | solution.py:373
  16.5 11.6 %all-to-all-start = ((bf16[128,17,256]{2,1,0:T(8,128)(2,1)}), bf16[128,17,256]{2,1,0:T(8,128)(2,1)}, u32[]{:S(2)}, u32[]{:S(2)}) async-start(bf16[128,17,256]{2,1,0:T(8,128)(2,1)} %pad_maximum_fusion.2), calls=%async_computation | async-start | bytes 3145728 | tf_op jit(solution)/shard_map/all_to_all | solution.py:376
  28.2 0.1 constant_dynamic-slice_fusion.8
  28.3 0.1 copy.114
  28.4 0.6 fusion.150
  29.0 1.6 %pad_maximum_fusion.1.src_ref = bf16[2,4,512,256]{3,2,1,0:T(8,128)(2,1)} fusion(bf16[2,4,512,128]{3,2,1,0:T(8,128)(2,1)S(1)} %bitcast.236, bf16[2,4,512,128]{3,2,1,0:T(8,128)(2,1)S(1)} %bitcast.232), kind=kLoop, calls=%fused_computation.29 | loop fusion | flops 4194304 | bytes 4194304 | tf_op jit(solution)/shard_map/concatenate | solution.py:419
  34.4 0.0 collective-permute-done.1
  34.4 1.3 %reverse_select_fusion.1.after_ref = bf16[2,1,512,256]{3,2,1,0:T(8,128)(2,1)S(1)} fusion(bf16[2,1,512,256]{3,2,1,0:T(8,128)(2,1)} %collective-permute-done.1, bf16[2,1,512,256]{3,2,1,0:T(8,128)(2,1)} %get-tuple-element.23, pred[]{:T(512)S(6)} %eq.125), kind=kLoop, calls=%fused_computation.50 | loop fusion | flops 262144 | bytes 1572865 | tf_op jit(solution)/shard_map/jit(_where)/select_n | solution.py:292
  35.7 0.0 copy-start.5
  35.8 0.7 copy-done.5
  36.5 6.4 %shard_map.113 = (f32[2,4,512,256]{3,2,1,0:T(8,128)}, f32[2,2,4,256]{3,2,1,0:T(4,128)}) custom-call(bf16[2,4,512,256]{3,2,1,0:T(8,128)(2,1)} %pad_maximum_fusion.1.src_ref, bf16[2,1,512,256]{3,2,1,0:T(8,128)(2,1)} %collective-permute-done.before_ref, bf16[2,1,512,256]{3,2,1,0:T(8,128)(2,1)} %copy-done.5, bf16[9,256,128]{2,1,0:T(8,128)(2,1)} %k_ref.7), custom_call_target="tpu_custom_call" | custom-call | tf_op jit(solution)/shard_map/pallas_call | solution.py:133
  42.9 0.7 copy.113
  43.6 1.0 slice.380
  44.7 0.6 maximum_bitcast_fusion.2.block_ref
  45.3 11.7 %shard_map.114 = (f32[2,4,512,256]{3,2,1,0:T(8,128)}, f32[8,56,128]{2,1,0:T(8,128)}) custom-call(f32[56,128]{1,0:T(8,128)} %maximum_bitcast_fusion.2.block_ref, bf16[2,4,512,256]{3,2,1,0:T(8,128)(2,1)} %pad_maximum_fusion.1.src_ref, bf16[2,1,512,256]{3,2,1,0:T(8,128)(2,1)} %collective-permute-done.before_ref, bf16[2,1,512,256]{3,2,1,0:T(8,128)(2,1)} %copy-done.5, ...), custom_call_target="tpu_custom_call" | custom-call | tf_op jit(solution)/shard_map/pallas_call | solution.py:231
  57.0 1.0 copy.195
  58.4 0.1 convolution_bitcast_fusion.1
  58.6 0.1 convolution_bitcast_fusion
  58.7 0.2 convolution_bitcast_fusion.3
  58.9 0.1 convolution_bitcast_fusion.2
  59.1 1.4 %fusion.55 = s32[128,16]{1,0:T(8,128)S(1)} fusion(bf16[128,17,256]{2,1,0:T(8,128)(2,1)} %all-to-all-done), kind=kLoop, calls=%fused_computation.94 | loop fusion | flops 8192 | bytes 16384 | tf_op jit(solution)/shard_map/add | solution.py:380
  60.5 0.1 add.122
  60.6 1.3 %slice.405 = bf16[128,16,256]{2,1,0:T(8,128)(2,1)S(1)} slice(bf16[128,17,256]{2,1,0:T(8,128)(2,1)} %all-to-all-done), slice={[0:128], [0:16], [0:256]} | slice | bytes 2097152 | tf_op jit(solution)/shard_map/slice | solution.py:377
  62.0 0.0 copy-start.12
  62.0 5.3 %fusion = f32[2,4,512,256]{3,2,1,0:T(8,128)S(1)} fusion(bf16[2048,256,1,1]{1,0,3,2:T(8,128)(2,1)S(1)} %bitcast.237, s32[2048]{0:T(1024)S(1)} %add.122, s32[2,4,512]{2,1,0:T(4,128)S(1)} %multiply_add_fusion), kind=kOutput, calls=%fused_computation | convolution fusion | flops 4303355904 | bytes 5267456 | tf_op jit(solution)/shard_map/dot_general | solution.py:412
  67.3 5.0 %multiply_convert_fusion = (bf16[2,4,512,256]{3,2,1,0:T(8,128)(2,1)S(1)}, bf16[2,4,512,256]{3,2,1,0:T(8,128)(2,1)S(1)}) fusion(f32[2,4,512,256]{3,2,1,0:T(8,128)S(1)} %fusion, f32[256]{0:T(256)S(1)} %copy-done.12, f32[2,4,256]{2,1,0:T(4,128)S(1)} %get-tuple-element.47, pred[512]{0:T(512)(128)(4,1)S(1)} %get-tuple-element.86, ...), kind=kLoop, calls=%fused_computation.21 | loop fusion | flops 33554432 | bytes 16812032 | tf_op jit(solution)/shard_map/convert_element_type | solution.py:427
  72.4 0.0 copy-start.6
  72.4 0.2 fusion.17
  72.6 3.7 %collective-permute-start.3 = (bf16[2,1,512,512]{3,2,1,0:T(8,128)(2,1)S(1)}, bf16[2,1,512,512]{3,2,1,0:T(8,128)(2,1)S(1)}, u32[]{:S(2)}, u32[]{:S(2)}) collective-permute-start(bf16[2,1,512,512]{3,2,1,0:T(8,128)(2,1)S(1)} %get-tuple-element.20), channel_id=1, source_target_pairs={{1,0},{2,1},{3,2},{4,3},{5,4},{6,5},{7,6},{8,7},{9,8},{10,9},{11,1... | collective-permute-start | bytes 3145736 | tf_op jit(solution)/shard_map/ppermute | solution.py:291
  76.3 2.1 %collective-permute-start.2 = (bf16[2,1,512,512]{3,2,1,0:T(8,128)(2,1)S(1)}, bf16[2,1,512,512]{3,2,1,0:T(8,128)(2,1)S(1)}, u32[]{:S(2)}, u32[]{:S(2)}) collective-permute-start(bf16[2,1,512,512]{3,2,1,0:T(8,128)(2,1)S(1)} %get-tuple-element.21), channel_id=1, source_target_pairs={{0,1},{1,2},{2,3},{3,4},{4,5},{5,6},{6,7},{7,8},{8,9},{9,10},{10,1... | collective-permute-start | bytes 3145736 | tf_op jit(solution)/shard_map/ppermute | solution.py:290
  78.5 2.3 %pad_maximum_fusion.src_ref = bf16[2,4,512,512]{3,2,1,0:T(8,128)(2,1)} fusion(bf16[2,4,512,256]{3,2,1,0:T(8,128)(2,1)S(1)} %get-tuple-element.19, bf16[2,4,512,256]{3,2,1,0:T(8,128)(2,1)S(1)} %get-tuple-element.18), kind=kLoop, calls=%fused_computation.11 | loop fusion | flops 8388608 | bytes 8388608 | tf_op jit(solution)/shard_map/concatenate | solution.py:431
  80.8 16.8 %collective-permute-done.3 = bf16[2,1,512,512]{3,2,1,0:T(8,128)(2,1)S(1)} collective-permute-done((bf16[2,1,512,512]{3,2,1,0:T(8,128)(2,1)S(1)}, bf16[2,1,512,512]{3,2,1,0:T(8,128)(2,1)S(1)}, u32[]{:S(2)}, u32[]{:S(2)}) %collective-permute-start.3) | collective-permute-done | bytes 1048608 | tf_op jit(solution)/shard_map/ppermute | solution.py:291
  97.6 0.3 reverse_select_fusion.after_ref
  97.9 3.5 %collective-permute-done.2.before_ref = bf16[2,1,512,512]{3,2,1,0:T(8,128)(2,1)S(1)} collective-permute-done((bf16[2,1,512,512]{3,2,1,0:T(8,128)(2,1)S(1)}, bf16[2,1,512,512]{3,2,1,0:T(8,128)(2,1)S(1)}, u32[]{:S(2)}, u32[]{:S(2)}) %collective-permute-start.2) | collective-permute-done | bytes 1048608 | tf_op jit(solution)/shard_map/ppermute | solution.py:290
  101.5 0.9 copy-done.4
  102.4 6.5 %shard_map.115 = (f32[2,4,512,128]{3,2,1,0:T(8,128)}, f32[2,2,4,128]{3,2,1,0:T(4,128)}) custom-call(bf16[2,4,512,512]{3,2,1,0:T(8,128)(2,1)} %pad_maximum_fusion.src_ref, bf16[2,1,512,512]{3,2,1,0:T(8,128)(2,1)} %copy-done.4, bf16[2,1,512,512]{3,2,1,0:T(8,128)(2,1)} %copy-done.2, bf16[9,128,256]{2,1,0:T(8,128)(2,1)} %k_ref.6, bf16[2,4,512,128]{3,2,1,0:T(8,128)(2,1)} %bitcast.235), custom_call_target="tpu_custom_call" | custom-call | tf_op jit(solution)/shard_map/pallas_call | solution.py:133
  108.9 0.7 copy.120
  109.6 0.6 maximum_bitcast_fusion.1.block_ref
  110.2 10.0 %shard_map.116 = (f32[2,4,512,128]{3,2,1,0:T(8,128)}, f32[8,64,128]{2,1,0:T(8,128)}) custom-call(f32[64,128]{1,0:T(8,128)} %maximum_bitcast_fusion.1.block_ref, bf16[2,4,512,512]{3,2,1,0:T(8,128)(2,1)} %pad_maximum_fusion.src_ref, bf16[2,1,512,512]{3,2,1,0:T(8,128)(2,1)} %copy-done.4, bf16[2,1,512,512]{3,2,1,0:T(8,128)(2,1)} %copy-done.2, ...), custom_call_target="tpu_custom_call" | custom-call | tf_op jit(solution)/shard_map/pallas_call | solution.py:231
  120.2 1.1 copy.194
  121.3 0.1 constant_dynamic-slice_fusion.3
  121.4 0.1 rev.36
  121.7 0.1 rev.37
  122.1 0.1 convolution_bitcast_fusion.5
  122.2 0.2 convolution_bitcast_fusion.4
  122.4 0.2 convolution_bitcast_fusion.7
  122.5 0.2 convolution_bitcast_fusion.6
  122.7 4.1 %add_bitcast_fusion = (f32[1,1,2,4,512,128]{5,4,3,2,1,0:T(8,128)}, bf16[1,1,2,4,512,128]{5,4,3,2,1,0:T(8,128)(2,1)}) fusion(f32[2,4,512,128]{3,2,1,0:T(8,128)S(1)} %copy-done.10, f32[2,4,128]{2,1,0:T(4,128)S(1)} %reverse_select_fusion.4, f32[2,4,128]{2,1,0:T(4,128)S(1)} %reverse_select_fusion.5, pred[512]{0:T(512)(128)(4,1)S(1)} %get-tuple-element.86, ...), kind=kLoop, calls=%fused_computation.33 | loop fusion | flops 4718592 | bytes 7357440 | tf_op jit(solution)/shard_map/broadcast_in_dim | solution.py:443
  (97 shorter events, 0.9 us)
Async XLA Ops:
  0.6 12.9 %copy-start = (bf16[1024,256]{1,0:T(8,128)(2,1)S(1)}, bf16[1024,256]{1,0:T(8,128)(2,1)}, u32[]{:S(2)}) copy-start(bf16[1024,256]{1,0:T(8,128)(2,1)} %param.11) | copy-start | bytes 1572868
  3.0 31.4 %collective-permute-start.1 = (bf16[2,1,512,256]{3,2,1,0:T(8,128)(2,1)}, bf16[2,1,512,256]{3,2,1,0:T(8,128)(2,1)}, u32[]{:S(2)}, u32[]{:S(2)}) collective-permute-start(bf16[2,1,512,256]{3,2,1,0:T(8,128)(2,1)} %get-tuple-element.22), channel_id=1, source_target_pairs={{1,0},{2,1},{3,2},{4,3},{5,4},{6,5},{7,6},{8,7},{9,8},{10,9},{11,1... | collective-permute-start | bytes 1572872 | tf_op jit(solution)/shard_map/ppermute | solution.py:291
  7.5 28.2 %collective-permute-start = (bf16[2,1,512,256]{3,2,1,0:T(8,128)(2,1)}, bf16[2,1,512,256]{3,2,1,0:T(8,128)(2,1)}, u32[]{:S(2)}, u32[]{:S(2)}) collective-permute-start(bf16[2,1,512,256]{3,2,1,0:T(8,128)(2,1)} %get-tuple-element.23), channel_id=1, source_target_pairs={{0,1},{1,2},{2,3},{3,4},{4,5},{5,6},{6,7},{7,8},{8,9},{9,10},{10,1... | collective-permute-start | bytes 1572872 | tf_op jit(solution)/shard_map/ppermute | solution.py:290
  15.1 13.0 %copy-start.11 = (s32[8,2,3]{0,1,2:T(2,128)S(1)}, s32[8,2,3]{0,1,2:T(2,128)}, u32[]{:S(2)}) copy-start(s32[8,2,3]{0,1,2:T(2,128)} %param.14) | copy-start | bytes 580
  15.1 13.8 %copy-start.1 = (bf16[1,1,2,4,512,128]{5,4,3,2,1,0:T(8,128)(2,1)S(1)}, bf16[1,1,2,4,512,128]{5,4,3,2,1,0:T(8,128)(2,1)}, u32[]{:S(2)}) copy-start(bf16[1,1,2,4,512,128]{5,4,3,2,1,0:T(8,128)(2,1)} %param.10) | copy-start | bytes 3145732
  15.2 13.8 %copy-start.3 = (bf16[1,1,2,4,512,128]{5,4,3,2,1,0:T(8,128)(2,1)S(1)}, bf16[1,1,2,4,512,128]{5,4,3,2,1,0:T(8,128)(2,1)}, u32[]{:S(2)}) copy-start(bf16[1,1,2,4,512,128]{5,4,3,2,1,0:T(8,128)(2,1)} %param.19) | copy-start | bytes 3145732
  16.5 17.8 %copy-start.9 = (bf16[9,128,256]{2,1,0:T(8,128)(2,1)S(1)}, bf16[9,128,256]{2,1,0:T(8,128)(2,1)}, u32[]{:S(2)}) copy-start(bf16[9,128,256]{2,1,0:T(8,128)(2,1)} %k_ref.6) | copy-start | bytes 1769476
  16.5 42.6 %all-to-all-start = ((bf16[128,17,256]{2,1,0:T(8,128)(2,1)}), bf16[128,17,256]{2,1,0:T(8,128)(2,1)}, u32[]{:S(2)}, u32[]{:S(2)}) async-start(bf16[128,17,256]{2,1,0:T(8,128)(2,1)} %pad_maximum_fusion.2), calls=%async_computation | async-start | bytes 3145728 | tf_op jit(solution)/shard_map/all_to_all | solution.py:376
  35.7 0.8 copy-start.5
  61.9 5.4 %copy-start.7 = (f32[2,4,512,256]{3,2,1,0:T(8,128)S(1)}, f32[2,4,512,256]{3,2,1,0:T(8,128)}, u32[]{:S(2)}) copy-start(f32[2,4,512,256]{3,2,1,0:T(8,128)} %get-tuple-element.13) | copy-start | bytes 12582916
  61.9 5.4 %copy-start.8 = (f32[2,4,512,256]{3,2,1,0:T(8,128)S(1)}, f32[2,4,512,256]{3,2,1,0:T(8,128)}, u32[]{:S(2)}) copy-start(f32[2,4,512,256]{3,2,1,0:T(8,128)} %get-tuple-element.11) | copy-start | bytes 12582916
  62.0 5.4 %copy-start.12 = (f32[256]{0:T(256)S(1)}, f32[256]{0:T(256)}, u32[]{:S(2)}) copy-start(f32[256]{0:T(256)} %param.16) | copy-start | bytes 3076
  72.4 6.0 %copy-start.6 = (bf16[9,256,128]{2,1,0:T(8,128)(2,1)S(1)}, bf16[9,256,128]{2,1,0:T(8,128)(2,1)}, u32[]{:S(2)}) copy-start(bf16[9,256,128]{2,1,0:T(8,128)(2,1)} %k_ref.7) | copy-start | bytes 1769476
  72.6 25.0 %collective-permute-start.3 = (bf16[2,1,512,512]{3,2,1,0:T(8,128)(2,1)S(1)}, bf16[2,1,512,512]{3,2,1,0:T(8,128)(2,1)S(1)}, u32[]{:S(2)}, u32[]{:S(2)}) collective-permute-start(bf16[2,1,512,512]{3,2,1,0:T(8,128)(2,1)S(1)} %get-tuple-element.20), channel_id=1, source_target_pairs={{1,0},{2,1},{3,2},{4,3},{5,4},{6,5},{7,6},{8,7},{9,8},{10,9},{11,1... | collective-permute-start | bytes 3145736 | tf_op jit(solution)/shard_map/ppermute | solution.py:291
  76.3 25.1 %collective-permute-start.2 = (bf16[2,1,512,512]{3,2,1,0:T(8,128)(2,1)S(1)}, bf16[2,1,512,512]{3,2,1,0:T(8,128)(2,1)S(1)}, u32[]{:S(2)}, u32[]{:S(2)}) collective-permute-start(bf16[2,1,512,512]{3,2,1,0:T(8,128)(2,1)S(1)} %get-tuple-element.21), channel_id=1, source_target_pairs={{0,1},{1,2},{2,3},{3,4},{4,5},{5,6},{6,7},{7,8},{8,9},{9,10},{10,1... | collective-permute-start | bytes 3145736 | tf_op jit(solution)/shard_map/ppermute | solution.py:290
  97.9 3.7 %copy-start.2 = (bf16[2,1,512,512]{3,2,1,0:T(8,128)(2,1)}, bf16[2,1,512,512]{3,2,1,0:T(8,128)(2,1)S(1)}, u32[]{:S(2)}) copy-start(bf16[2,1,512,512]{3,2,1,0:T(8,128)(2,1)S(1)} %reverse_select_fusion.after_ref) | copy-start | bytes 3145732
  101.4 1.0 copy-start.4
  110.2 12.5 %copy-start.10 = (f32[2,4,512,128]{3,2,1,0:T(8,128)S(1)}, f32[2,4,512,128]{3,2,1,0:T(8,128)}, u32[]{:S(2)}) copy-start(f32[2,4,512,128]{3,2,1,0:T(8,128)} %get-tuple-element.17) | copy-start | bytes 6291460
